TPU v7x, 32 devices: a whole 2x2x4 slice. The times are simulated.
32 devices in a mesh: expert: 4 (over z), batch: 8 (over y, x, core).
Axes of the slice: x: 2, y: 2, z: 4, core: 2. Of those that a mesh axis runs over, the one named last changes fastest.
Arguments:
- tokens: bfloat16 [32, 1024, 768], P(('expert', 'batch')), may hold values from -6 to 6
- lengths: int32 [32], P(('expert', 'batch')), may hold values from 64 to 1024, as said below
- routes: int32 [32, 1024, 2], P(('expert', 'batch')), may hold values from 0 to 7, as said below
- ln1_gain: float32 [768], replicated, may hold values from 0.5 to 1.5
- ln1_bias: float32 [768], replicated, may hold values from -1.5 to 1.5
- ln2_gain: float32 [768], replicated, may hold values from 0.5 to 1.5
- ln2_bias: float32 [768], replicated, may hold values from -1.5 to 1.5
- w_qkv: bfloat16 [768, 2304], replicated, may hold values from -0.21875 to 0.21875
- w_proj: bfloat16 [768, 768], replicated, may hold values from -1.25 to 1.25
- w_router: bfloat16 [768, 8], replicated, may hold values from -0.15625 to 0.15625
- old_in: bfloat16 [4, 768, 3072], P('expert', 'batch'), may hold values from -0.21875 to 0.21875
- old_out: bfloat16 [4, 3072, 768], P('expert', 'batch'), may hold values from -0.109375 to 0.109375
- new_in: bfloat16 [4, 768, 3072], P('expert', 'batch'), may hold values from -0.21875 to 0.21875
- new_out: bfloat16 [4, 3072, 768], P('expert', 'batch'), may hold values from -0.109375 to 0.109375
- cotangent: bfloat16 [32, 1024, 768], P(('expert', 'batch')), may hold values from -6 to 6
Outputs:
- output: float32 [32, 1024, 768], P(('expert', 'batch'))
- input_grad: float32 [32, 1024, 768], P(('expert', 'batch'))
- ln1_gain_grad: float32 [768], replicated
- ln1_bias_grad: float32 [768], replicated
- ln2_gain_grad: float32 [768], replicated
- ln2_bias_grad: float32 [768], replicated
- qkv_grad: float32 [768, 2304], replicated
- proj_grad: float32 [768, 768], replicated
- router_grad: float32 [768, 8], replicated
- new_in_grad: float32 [4, 768, 3072], P('expert', 'batch')
- new_out_grad: float32 [4, 3072, 768], P('expert', 'batch')
Inputs may be any that keep to these rules, and one draw needn't show every extreme that they name: Positions lengths[r] and beyond of row r are padding. In every draw some row has 1024 tokens and some row 64. `routes`: the two experts of one token always differ. Across the tokens of a sequence row the same expert is named many times, and some experts are named more often than others.
All inputs are finite; a program needn't handle non-finite values.
Results may differ from a plain program's by a relative error of at most 0.012.
Values may be sent and summed in bfloat16 or wider, within the bound.
No kernel may reach another device: no remote copies, remote signals or barrier semaphores. Data moves between devices by JAX's collectives and lax.ppermute only.
A program may use at most 320 MiB of HBM per device.

v0:
```python
import math

import jax
import jax.numpy as jnp
from jax import lax
from jax.sharding import PartitionSpec as P

HEADS = 12
HEAD_DIM = 64


norm_eps = 1e-05
masked_value = -1e30


def layer_norm(field_in, gain_vec, bias_vec):
    row_mean = jnp.mean(field_in, axis=-1, keepdims=True)
    centred = field_in - row_mean
    row_var = jnp.mean(centred * centred, axis=-1, keepdims=True)
    return centred * lax.rsqrt(row_var + norm_eps) * gain_vec + bias_vec


def gelu_tanh(field_in):
    inner_arg = 0.7978845608028654 * (field_in + 0.044715 * field_in * field_in * field_in)
    return 0.5 * field_in * (1.0 + jnp.tanh(inner_arg))


def rank_pairs(route_row, length, experts, capacity):
    seq_len = route_row.shape[0]
    pair_expert = jnp.transpose(route_row).reshape(2 * seq_len)
    live_pair = jnp.tile(jnp.arange(seq_len, dtype=jnp.int32) < length, 2)
    one_hot = (pair_expert[:, None] == jnp.arange(experts, dtype=jnp.int32)[None, :]).astype(
        jnp.int32
    ) * live_pair[:, None].astype(jnp.int32)
    earlier = jnp.cumsum(one_hot, axis=0, dtype=jnp.int32) - one_hot
    pair_rank = jnp.sum(earlier * one_hot, axis=1, dtype=jnp.int32)
    kept_pair = live_pair & (pair_rank < capacity)
    return (
        jnp.transpose(pair_rank.reshape(2, seq_len)),
        jnp.transpose(kept_pair.reshape(2, seq_len)),
    )


def buffer_row(expert_ids, experts, group_size):
    half_count = experts // 2
    per_device = half_count // group_size
    is_new = expert_ids >= half_count
    within = jnp.where(is_new, expert_ids - half_count, expert_ids)
    extra = jnp.where(is_new, per_device, 0).astype(jnp.int32)
    return within // per_device * (2 * per_device) + extra + within % per_device


def expert_hidden(buffer_rows, weights_in):
    pre_act = jnp.einsum(
        "slcd,ldf->slcf", buffer_rows, weights_in, preferred_element_type=jnp.float32
    )
    return (pre_act, gelu_tanh(pre_act).astype(jnp.bfloat16))


def expert_output(hidden, weights_out):
    return jnp.einsum("slcf,lfd->slcd", hidden, weights_out, preferred_element_type=jnp.float32)


def expert_back(pre_act, grads_out, weights_out):
    hid_grad = jnp.einsum(
        "slcd,lfd->slcf", grads_out, weights_out, preferred_element_type=jnp.float32
    )
    unused, gelu_back = jax.vjp(gelu_tanh, pre_act)
    return gelu_back(hid_grad)[0].astype(jnp.bfloat16)


def row_grads_of(pre_grad, weights_in):
    return jnp.einsum("slcf,ldf->slcd", pre_grad, weights_in, preferred_element_type=jnp.float32)


def body(
    tokens,
    lengths,
    routes,
    ln1_gain,
    ln1_bias,
    ln2_gain,
    ln2_bias,
    w_qkv,
    w_proj,
    w_router,
    old_in,
    old_out,
    new_in,
    new_out,
    cotangent,
):
    group_size = lax.axis_size("expert")
    inputs = tokens[0].astype(jnp.float32)
    seq_len = inputs.shape[0]
    model_width = inputs.shape[1]
    experts = w_router.shape[1]
    local_count = experts // group_size
    old_count = old_in.shape[0]
    capacity = max(4, seq_len // experts)
    buffer_size = experts * capacity
    score_scale = 1.0 / math.sqrt(HEAD_DIM)
    length = lengths[0]
    route_row = routes[0]
    block_rows = min(512, seq_len)
    blocks = seq_len // block_rows
    normed1, back_norm1 = jax.vjp(layer_norm, inputs, ln1_gain, ln1_bias)
    normed1_low = normed1.astype(jnp.bfloat16)
    qkv_low = jnp.dot(normed1_low, w_qkv, preferred_element_type=jnp.float32).astype(jnp.bfloat16)
    queries = qkv_low[:, :model_width].reshape(seq_len, HEADS, HEAD_DIM)
    key_rows = qkv_low[:, model_width : 2 * model_width].reshape(seq_len, HEADS, HEAD_DIM)
    value_rows = qkv_low[:, 2 * model_width :].reshape(seq_len, HEADS, HEAD_DIM)
    key_pos = jnp.arange(seq_len, dtype=jnp.int32)

    def block_scores(row_start, query_block):
        raw_scores = (
            jnp.einsum("qhd,khd->hqk", query_block, key_rows, preferred_element_type=jnp.float32)
            * score_scale
        )
        query_pos = row_start + jnp.arange(query_block.shape[0], dtype=jnp.int32)
        allowed = (key_pos[None, :] <= query_pos[:, None]) & (key_pos[None, :] < length)
        return jnp.where(allowed[None], raw_scores, masked_value)

    mixed_parts = []
    lse_parts = []
    for block_index in range(blocks):
        row_start = block_index * block_rows
        scores = block_scores(row_start, queries[row_start : row_start + block_rows])
        row_max = jnp.max(scores, axis=-1, keepdims=True)
        exp_scores = jnp.exp(scores - row_max)
        row_total = jnp.sum(exp_scores, axis=-1, keepdims=True)
        prob_low = (exp_scores / row_total).astype(jnp.bfloat16)
        mixed_parts.append(
            jnp.einsum(
                "hqk,khd->qhd", prob_low, value_rows, preferred_element_type=jnp.float32
            ).astype(jnp.bfloat16)
        )
        lse_parts.append(row_max + jnp.log(row_total))
    mixed_rows = jnp.concatenate(mixed_parts, axis=0).reshape(seq_len, model_width)
    residual = inputs + jnp.dot(mixed_rows, w_proj, preferred_element_type=jnp.float32)
    normed2, back_norm2 = jax.vjp(layer_norm, residual, ln2_gain, ln2_bias)
    normed2_low = normed2.astype(jnp.bfloat16)
    logits = jnp.dot(normed2_low, w_router, preferred_element_type=jnp.float32)
    gate_vals = jax.nn.softmax(jnp.take_along_axis(logits, route_row, axis=1), axis=-1)
    pair_rank, kept_pair = rank_pairs(route_row, length, experts, capacity)
    slot_index = buffer_row(route_row, experts, group_size) * capacity + pair_rank
    target = jnp.where(kept_pair, slot_index, buffer_size).reshape(-1)
    token_ids = jnp.broadcast_to(
        jnp.arange(seq_len, dtype=jnp.int32)[:, None], (seq_len, 2)
    ).reshape(-1)
    source_token = jnp.zeros((buffer_size,), jnp.int32).at[target].set(token_ids, mode="drop")
    slot_gate = (
        jnp.zeros((buffer_size,), jnp.float32).at[target].set(gate_vals.reshape(-1), mode="drop")
    )
    slot_filled = jnp.zeros((buffer_size,), jnp.bool_).at[target].set(True, mode="drop")
    pick_index = jnp.where(kept_pair, slot_index, 0)
    kept_weight = kept_pair.astype(jnp.float32)
    zero_low = jnp.zeros((), jnp.bfloat16)
    send_rows = jnp.where(slot_filled[:, None], normed2_low[source_token], zero_low)
    send_rows = send_rows.reshape(group_size, local_count, capacity, model_width)
    received = lax.all_to_all(send_rows, "expert", split_axis=0, concat_axis=0, tiled=True)
    gathered = (
        lax.all_gather(old_in, "batch", axis=1, tiled=True),
        lax.all_gather(old_out, "batch", axis=1, tiled=True),
        lax.all_gather(new_in, "batch", axis=1, tiled=True),
        lax.all_gather(new_out, "batch", axis=1, tiled=True),
    )
    old_rows = received[:, :old_count]
    new_rows = received[:, old_count:]
    old_pre, old_hid = expert_hidden(old_rows, gathered[0])
    new_pre, new_hid = expert_hidden(new_rows, gathered[2])
    expert_result = jnp.concatenate(
        [expert_output(old_hid, gathered[1]), expert_output(new_hid, gathered[3])], axis=1
    ).astype(jnp.bfloat16)
    returned = lax.all_to_all(
        expert_result, "expert", split_axis=0, concat_axis=0, tiled=True
    ).reshape(buffer_size, model_width)
    picked = returned[pick_index].astype(jnp.float32)
    mixture = jnp.sum((gate_vals * kept_weight)[:, :, None] * picked, axis=1)
    output = residual + mixture
    grad_out = cotangent[0].astype(jnp.float32)
    gate_grad = kept_weight * jnp.sum(grad_out[:, None, :] * picked, axis=-1)
    dchosen = gate_vals * (gate_grad - jnp.sum(gate_vals * gate_grad, axis=-1, keepdims=True))
    columns = jnp.arange(experts, dtype=jnp.int32)
    dlogits = jnp.sum(
        (route_row[:, :, None] == columns[None, None, :]).astype(jnp.float32) * dchosen[:, :, None],
        axis=1,
    ).astype(jnp.bfloat16)
    send_grads = jnp.where(
        slot_filled[:, None],
        (slot_gate[:, None] * grad_out[source_token]).astype(jnp.bfloat16),
        zero_low,
    )
    send_grads = send_grads.reshape(group_size, local_count, capacity, model_width)
    arrived = lax.all_to_all(send_grads, "expert", split_axis=0, concat_axis=0, tiled=True)
    weights_back = (
        lax.all_gather(old_in, "batch", axis=1, tiled=True),
        lax.all_gather(old_out, "batch", axis=1, tiled=True),
        lax.all_gather(new_in, "batch", axis=1, tiled=True),
        lax.all_gather(new_out, "batch", axis=1, tiled=True),
    )
    old_pre, old_hid = expert_hidden(old_rows, weights_back[0])
    new_pre, new_hid = expert_hidden(new_rows, weights_back[2])
    old_dout = arrived[:, :old_count]
    new_dout = arrived[:, old_count:]
    old_dpre = expert_back(old_pre, old_dout, weights_back[1])
    new_dpre = expert_back(new_pre, new_dout, weights_back[3])
    new_out_local = jnp.einsum(
        "slcf,slcd->lfd", new_hid, new_dout, preferred_element_type=jnp.float32
    )
    new_in_local = jnp.einsum(
        "slcd,slcf->ldf", new_rows, new_dpre, preferred_element_type=jnp.float32
    )
    row_grads = jnp.concatenate(
        [row_grads_of(old_dpre, weights_back[0]), row_grads_of(new_dpre, weights_back[2])], axis=1
    ).astype(jnp.bfloat16)
    returned_grads = lax.all_to_all(
        row_grads, "expert", split_axis=0, concat_axis=0, tiled=True
    ).reshape(buffer_size, model_width)
    new_in_grad, new_out_grad = (
        lax.psum_scatter(new_in_local, "batch", scatter_dimension=1, tiled=True),
        lax.psum_scatter(new_out_local, "batch", scatter_dimension=1, tiled=True),
    )
    dnormed2 = jnp.sum(
        kept_weight[:, :, None] * returned_grads[pick_index].astype(jnp.float32), axis=1
    )
    dnormed2 = dnormed2 + jnp.dot(dlogits, w_router.T, preferred_element_type=jnp.float32)
    router_local = jnp.dot(normed2_low.T, dlogits, preferred_element_type=jnp.float32)
    dresid_norm, gain2_local, bias2_local = back_norm2(dnormed2)
    dresid = grad_out + dresid_norm
    attn_grad = dresid.astype(jnp.bfloat16)
    proj_local = jnp.dot(mixed_rows.T, attn_grad, preferred_element_type=jnp.float32)
    dmixed = (
        jnp.dot(attn_grad, w_proj.T, preferred_element_type=jnp.float32)
        .astype(jnp.bfloat16)
        .reshape(seq_len, HEADS, HEAD_DIM)
    )
    key_grads = jnp.zeros((seq_len, HEADS, HEAD_DIM), jnp.float32)
    value_grads = jnp.zeros((seq_len, HEADS, HEAD_DIM), jnp.float32)
    dquery_parts = []
    for block_index in range(blocks):
        row_start = block_index * block_rows
        query_block = queries[row_start : row_start + block_rows]
        grad_block = dmixed[row_start : row_start + block_rows]
        scores = block_scores(row_start, query_block)
        probs = jnp.exp(scores - lse_parts[block_index])
        dprobs = jnp.einsum(
            "qhd,khd->hqk", grad_block, value_rows, preferred_element_type=jnp.float32
        )
        dscores = (probs * (dprobs - jnp.sum(probs * dprobs, axis=-1, keepdims=True))).astype(
            jnp.bfloat16
        )
        dquery_parts.append(
            jnp.einsum("hqk,khd->qhd", dscores, key_rows, preferred_element_type=jnp.float32)
            * score_scale
        )
        key_grads = (
            key_grads
            + jnp.einsum("hqk,qhd->khd", dscores, query_block, preferred_element_type=jnp.float32)
            * score_scale
        )
        value_grads = value_grads + jnp.einsum(
            "hqk,qhd->khd",
            probs.astype(jnp.bfloat16),
            grad_block,
            preferred_element_type=jnp.float32,
        )
    query_grads = jnp.concatenate(dquery_parts, axis=0)
    qkv_grads = jnp.concatenate(
        [
            query_grads.reshape(seq_len, model_width),
            key_grads.reshape(seq_len, model_width),
            value_grads.reshape(seq_len, model_width),
        ],
        axis=1,
    ).astype(jnp.bfloat16)
    qkv_local = jnp.dot(normed1_low.T, qkv_grads, preferred_element_type=jnp.float32)
    dnormed1 = jnp.dot(qkv_grads, w_qkv.T, preferred_element_type=jnp.float32)
    dinput_norm, gain1_local, bias1_local = back_norm1(dnormed1)
    input_grad = dresid + dinput_norm
    summed = lax.psum(
        (qkv_local, proj_local, router_local, gain1_local, bias1_local, gain2_local, bias2_local),
        ("expert", "batch"),
    )
    return (
        output[None],
        input_grad[None],
        summed[3],
        summed[4],
        summed[5],
        summed[6],
        summed[0],
        summed[1],
        summed[2],
        new_in_grad,
        new_out_grad,
    )


def solution(mesh):
    placed = (
        P(("expert", "batch"), None, None),
        P(("expert", "batch")),
        P(("expert", "batch"), None, None),
        P(),
        P(),
        P(),
        P(),
        P(),
        P(),
        P(),
        P("expert", "batch", None),
        P("expert", "batch", None),
        P("expert", "batch", None),
        P("expert", "batch", None),
        P(("expert", "batch"), None, None),
    )
    return jax.shard_map(
        body,
        mesh=mesh,
        in_specs=placed,
        out_specs=(
            P(("expert", "batch"), None, None),
            P(("expert", "batch"), None, None),
            P(),
            P(),
            P(),
            P(),
            P(),
            P(),
            P(),
            P("expert", "batch", None),
            P("expert", "batch", None),
        ),
        check_vma=False,
    )
```

profile of v0, /device:TPU:0, one launch (start us, length us, event | category | flops | bytes accessed | tf_op | source)
XLA Modules:
  0.0 1011.6 jit_solution(11103398749579291212)
XLA Ops:
  17.5 4.4 convolution_convert_fusion
  30.4 5.1 reduce-window.6
  44.8 9.4 scatter_custom_fusion
  66.8 15.3 %fusion.13 = (f32[12,512]{1,0:T(8,128)S(1)}, f32[12,512,1024]{2,1,0:T(8,128)}) fusion(pred[512,1024]{1,0:T(8,128)(4,1)} %get-tuple-element.111, bf16[512,12,64]{0,2,1:T(8,128)(2,1)} %bitcast.415, bf16[1024,12,64]{0,2,1:T(8,128)(2,1)} %bitcast.406), kind=kOutput, calls=%fused_computation.37 | convolution fusion | flops 824174592 | bytes 28073984 | tf_op jit(solution)/shard_map/qhd,khd->hqk/dot_general | solution.py:117
  82.1 12.5 %fusion.1 = f32[12,512]{1,0:T(8,128)S(1)} fusion(f32[12,512]{1,0:T(8,128)S(1)} %get-tuple-element.112, f32[12,512,1024]{2,1,0:T(8,128)} %get-tuple-element.113, pred[512,1024]{1,0:T(8,128)(4,1)S(1)} %copy-done.17), kind=kLoop, calls=%fused_computation.21 | loop fusion | flops 25159680 | bytes 25739264 | tf_op jit(solution)/shard_map/reduce_sum | solution.py:131
  94.6 3.2 copy-done.1
  97.8 9.8 fusion.126
  107.6 12.4 %fusion.12 = (f32[12,512]{1,0:T(8,128)S(1)}, f32[12,512,1024]{2,1,0:T(8,128)}) fusion(pred[512,1024]{1,0:T(8,128)(4,1)} %get-tuple-element.110, bf16[512,12,64]{0,2,1:T(8,128)(2,1)} %bitcast.417, bf16[1024,12,64]{0,2,1:T(8,128)(2,1)S(1)} %bitcast.407), kind=kOutput, calls=%fused_computation.36 | convolution fusion | flops 824174592 | bytes 28073984 | tf_op jit(solution)/shard_map/qhd,khd->hqk/dot_general | solution.py:117
  120.0 14.2 %fusion = f32[12,512]{1,0:T(8,128)S(1)} fusion(f32[12,512]{1,0:T(8,128)S(1)} %get-tuple-element.114, f32[12,512,1024]{2,1,0:T(8,128)} %get-tuple-element.115, pred[512,1024]{1,0:T(8,128)(4,1)} %get-tuple-element.110), kind=kLoop, calls=%fused_computation.20 | loop fusion | flops 25159680 | bytes 25739264 | tf_op jit(solution)/shard_map/reduce_sum | solution.py:131
  136.3 9.6 fusion.125
  152.3 8.7 scatter_custom_fusion.1
  163.7 3.5 bitcast_convert_fusion
  167.1 3.5 copy.196
  183.4 13.8 %gather_fusion.4 = f32[2048]{0:T(1024)S(1)} fusion(f32[1024,8]{0,1:T(8,128)} %fusion.196, s32[2048]{0:T(1024)S(1)} %reshape.475), kind=kCustom, calls=%fused_computation.4 | custom fusion | bytes 32768 | tf_op jit(solution)/shard_map/jit(take_along_axis)/gather | solution.py:144
  210.0 7.9 gather_fusion.2
  217.9 7.4 gather_fusion
  226.7 8.2 scatter_custom_fusion.2
  234.9 3.4 fusion.85
  238.3 43.2 %all_to_all.20 = bf16[4,2,128,768]{3,2,1,0:T(8,128)(2,1)} all-to-all(bf16[4,2,128,768]{3,2,1,0:T(8,128)(2,1)S(1)} %get-tuple-element.109), channel_id=1, replica_groups=mesh['expert'=4,'batch'=8] {'expert'}, dimensions={0} | all-to-all | bytes 3145728 | tf_op jit(solution)/shard_map/all_to_all | solution.py:161
  281.6 4.5 all-to-all-start.2
  286.1 7.8 fusion.44
  294.0 7.9 fusion.52
  301.9 8.8 fusion.108
  310.7 8.0 fusion.118
  322.3 4.6 all-to-all-start.1
  326.8 9.6 fusion.19
  336.5 6.1 fusion.113
  342.6 4.7 fusion.46
  347.4 10.6 %fusion.127 = bf16[4,1,128,768]{3,2,0,1:T(8,128)(2,1)S(1)} fusion(bf16[1,768,3072]{2,1,0:T(8,128)(2,1)} %all-gather.5.cloned.1.call-done, f32[4,128,3072]{2,1,0:T(8,128)} %fusion.52, f32[4,128,3072]{2,1,0:T(8,128)S(1)} %fusion.46), kind=kOutput, calls=%fused_computation.163 | convolution fusion | flops 2454061056 | bytes 18087936 | tf_op jit(solution)/shard_map/slcf,ldf->slcd/dot_general | solution.py:73
  359.4 4.1 all-to-all-done.1
  363.4 4.3 all-to-all-start.3
  379.6 12.1 %gather_fusion.1 = bf16[2048,768]{1,0:T(8,128)(2,1)} fusion(bf16[1024,768]{1,0:T(8,128)(2,1)} %bitcast.47, s32[2048]{0:T(1024)S(1)} %broadcast_clamp_fusion), kind=kCustom, calls=%fused_computation.1 | custom fusion | bytes 6299648 | tf_op jit(solution)/shard_map/gather | solution.py:178
  391.7 12.6 %all-to-all-done.3 = bf16[4,2,128,768]{3,2,1,0:T(8,128)(2,1)} async-done(((bf16[4,2,128,768]{3,2,1,0:T(8,128)(2,1)}), bf16[4,2,128,768]{3,2,1,0:T(8,128)(2,1)}, u32[]{:S(2)}, u32[]{:S(2)}) %all-to-all-start.3) | async-done | bytes 1572896 | tf_op jit(solution)/shard_map/all_to_all | solution.py:217
  404.3 11.7 %gather_fusion.3 = bf16[2048,768]{1,0:T(8,128)(2,1)} fusion(bf16[1024,768]{1,0:T(8,128)(2,1)} %bitcast.73, s32[2048]{0:T(1024)S(1)} %broadcast_clamp_fusion), kind=kCustom, calls=%fused_computation.3 | custom fusion | bytes 6299648 | tf_op jit(solution)/shard_map/gather | solution.py:225
  416.0 7.8 reshape.513
  423.8 11.2 %multiply_reduce_fusion.3 = f32[1024,768]{1,0:T(8,128)} fusion(f32[1024,2,768]{2,1,0:T(2,128)} %reshape.513, f32[1024,2]{1,0:T(8,128)} %copy.192), kind=kLoop, calls=%fused_computation.73 | loop fusion | flops 2359296 | bytes 9445376 | tf_op jit(solution)/shard_map/reduce_sum | solution.py:224
  435.0 3.5 copy.202
  438.5 7.8 reshape.512
  446.3 17.2 %multiply_reduce_fusion.2 = (f32[1024,2]{1,0:T(8,128)}, f32[1024,768]{1,0:T(8,128)}) fusion(f32[1024,2,768]{2,1,0:T(2,128)} %reshape.512, f32[1024,768]{1,0:T(8,128)} %copy.196, f32[1024,2]{1,0:T(8,128)} %copy.183), kind=kLoop, calls=%fused_computation.72 | loop fusion | flops 5502976 | bytes 12599296 | tf_op jit(solution)/shard_map/reduce_sum | solution.py:182
  466.9 6.4 multiply_reduce_fusion.5
  473.3 3.7 copy.190
  477.1 6.5 fusion.187
  491.6 18.9 %multiply_reduce_fusion.1 = (f32[12,512]{1,0:T(8,128)}, f32[12,512,1024]{2,1,0:T(8,128)}) fusion(f32[12,512]{1,0:T(8,128)} %log_add_fusion.1, f32[12,512,1024]{2,1,0:T(8,128)} %get-tuple-element.115, pred[512,1024]{1,0:T(8,128)(4,1)} %get-tuple-element.110, bf16[512,12,64]{0,2,1:T(8,128)(2,1)} %bitcast.422, bf16[1024,12,64]{0,2,1:T(8,128)(2,1)} %bitcast.412), kind=kOutput, calls=%fused_computation.12 | convolution fusion | flops 836757504 | bytes 53264384 | tf_op jit(solution)/shard_map/qhd,khd->hqk/dot_general | solution.py:247
  510.5 22.7 %multiply_convert_fusion.1 = bf16[12,512,1024]{2,1,0:T(8,128)(2,1)} fusion(f32[12,512,1024]{2,1,0:T(8,128)} %get-tuple-element.120, f32[12,512]{1,0:T(8,128)} %get-tuple-element.119, f32[12,512]{1,0:T(8,128)} %log_add_fusion.1, f32[12,512,1024]{2,1,0:T(8,128)} %get-tuple-element.115, pred[512,1024]{1,0:T(8,128)(4,1)} %get-tuple-element.110), kind=kLoop, calls=%fused_computation.11 | loop fusion | flops 37748736 | bytes 63488000 | tf_op jit(solution)/shard_map/convert_element_type | solution.py:250
  533.2 9.5 fusion.123
  542.7 8.6 fusion.197
  551.4 13.1 %fusion.4 = f32[12,64,1024]{2,1,0:T(8,128)} fusion(bf16[512,12,64]{0,2,1:T(8,128)(2,1)S(1)} %bitcast.425, f32[12,512]{1,0:T(8,128)S(1)} %copy-done.36, f32[12,512,1024]{2,1,0:T(8,128)} %get-tuple-element.113, pred[512,1024]{1,0:T(8,128)(4,1)S(1)} %copy-done.18), kind=kOutput, calls=%fused_computation.24 | convolution fusion | flops 830472192 | bytes 29646848 | tf_op jit(solution)/shard_map/hqk,qhd->khd/dot_general | solution.py:262
  564.4 18.9 %multiply_reduce_fusion = (f32[12,512]{1,0:T(8,128)}, f32[12,512,1024]{2,1,0:T(8,128)}) fusion(f32[12,512]{1,0:T(8,128)} %log_add_fusion, f32[12,512,1024]{2,1,0:T(8,128)} %get-tuple-element.113, pred[512,1024]{1,0:T(8,128)(4,1)} %get-tuple-element.111, bf16[512,12,64]{0,2,1:T(8,128)(2,1)} %bitcast.424, bf16[1024,12,64]{0,2,1:T(8,128)(2,1)} %bitcast.413), kind=kOutput, calls=%fused_computation.9 | convolution fusion | flops 836757504 | bytes 53264384 | tf_op jit(solution)/shard_map/qhd,khd->hqk/dot_general | solution.py:247
  583.3 13.2 %add_convert_fusion = bf16[12,64,1024]{2,1,0:T(8,128)(2,1)S(1)} fusion(f32[12,64,1024]{2,1,0:T(8,128)} %fusion.4, bf16[512,12,64]{0,2,1:T(8,128)(2,1)} %bitcast.423, f32[12,512]{1,0:T(8,128)} %log_add_fusion.1, f32[12,512,1024]{2,1,0:T(8,128)} %get-tuple-element.115, pred[512,1024]{1,0:T(8,128)(4,1)} %get-tuple-element.110), kind=kOutput, calls=%fused_computation.122 | convolution fusion | flops 832045056 | bytes 31219712 | tf_op jit(solution)/shard_map/hqk,qhd->khd/dot_general | solution.py:262
  596.6 21.9 %multiply_convert_fusion = bf16[12,512,1024]{2,1,0:T(8,128)(2,1)} fusion(f32[12,512,1024]{2,1,0:T(8,128)} %get-tuple-element.122, f32[12,512]{1,0:T(8,128)S(1)} %copy-done.42, f32[12,512]{1,0:T(8,128)S(1)} %copy-done.37, f32[12,512,1024]{2,1,0:T(8,128)} %get-tuple-element.113, pred[512,1024]{1,0:T(8,128)(4,1)S(1)} %copy-done.19), kind=kLoop, calls=%fused_computation.8 | loop fusion | flops 37748736 | bytes 63488000 | tf_op jit(solution)/shard_map/convert_element_type | solution.py:250
  618.5 8.6 fusion.124
  627.1 6.9 multiply_convert_fusion.4
  636.7 7.1 fusion.81
  643.8 9.9 convolution_bitcast_fusion
  654.0 8.6 convolution_bitcast_fusion.1
  662.5 3.6 copy.208
  666.1 8.7 fusion.195
  674.8 3.6 copy.204
  687.3 3.7 copy.209
  693.5 40.5 %all-reduce = (f32[768]{0:T(1024)}, f32[768]{0:T(1024)}, f32[768]{0:T(1024)}, f32[768]{0:T(1024)}, f32[768,8]{0,1:T(8,128)}) all-reduce(f32[768]{0:T(1024)} %get-tuple-element.81, f32[768]{0:T(1024)} %get-tuple-element.123, f32[768]{0:T(1024)} %get-tuple-element.77, ...), channel_id=1, replica_groups=mesh['expert'=4,'batch'=8] {'expert','batch'}, use_global_device_ids=true, to_apply=%region_28.29 | all-reduce | flops 9216 | bytes 73728 | tf_op jit(solution)/shard_map/psum | solution.py:281
  734.0 100.6 %all-reduce.4.cloned.1.call-done = (f32[768,2304]{1,0:T(8,128)}, f32[768,768]{1,0:T(8,128)}) async-done(((f32[768,2304]{1,0:T(8,128)}, f32[768,768]{1,0:T(8,128)}), (f32[768,2304]{1,0:T(8,128)}, f32[768,768]{1,0:T(8,128)})) %all-reduce.4.cloned.1.call-update) | async-done | bytes 9437200 | tf_op jit(solution)/shard_map/psum | solution.py:281
  834.6 80.8 %reduce-scatter.5.cloned.1.call-done = f32[1,384,768]{2,1,0:T(8,128)} async-done(((f32[1,3072,768]{2,1,0:T(8,128)}), f32[1,384,768]{2,1,0:T(8,128)}) %reduce-scatter.5.cloned.1.call-update) | async-done | bytes 1179664 | tf_op jit(solution)/shard_map/reduce_scatter | solution.py:222
  915.4 80.9 %reduce-scatter.3.cloned.1.call-done = f32[1,96,3072]{2,1,0:T(8,128)} async-done(((f32[1,768,3072]{2,1,0:T(8,128)}), f32[1,96,3072]{2,1,0:T(8,128)}) %reduce-scatter.3.cloned.1.call-update) | async-done | bytes 1179664 | tf_op jit(solution)/shard_map/reduce_scatter | solution.py:221
  996.4 6.6 copy.228
  (252 shorter events, 121.6 us)
Async XLA Ops:
  7.2 10.3 %copy-start = (bf16[768,2304]{1,0:T(8,128)(2,1)S(1)}, bf16[768,2304]{1,0:T(8,128)(2,1)}, u32[]{:S(2)}) copy-start(bf16[768,2304]{1,0:T(8,128)(2,1)} %param.22) | copy-start | bytes 10616836
  7.2 279.0 %all-gather.9.cloned.1.call-start = ((), (), s32[]{:S(2)}) async-start(), calls=%async_computation.8 | async-start | bytes 5308416 | tf_op jit(solution)/shard_map/all_gather | solution.py:165
  7.9 286.1 %all-gather.5.cloned.1.call-start = ((), (), s32[]{:S(2)}) async-start(), calls=%async_computation.6 | async-start | bytes 5308416 | tf_op jit(solution)/shard_map/all_gather | solution.py:163
  8.7 293.2 %all-gather.11.cloned.1.call-start = ((), (), s32[]{:S(2)}) async-start(), calls=%async_computation.9 | async-start | bytes 5308416 | tf_op jit(solution)/shard_map/all_gather | solution.py:166
  9.4 301.3 %all-gather.7.cloned.1.call-start = ((), (), s32[]{:S(2)}) async-start(), calls=%async_computation.7 | async-start | bytes 5308416 | tf_op jit(solution)/shard_map/all_gather | solution.py:164
  10.6 6.9 copy-start.62
  10.6 6.9 copy-start.69
  13.2 4.3 copy-start.3
  15.0 6.9 copy-start.47
  17.5 4.4 copy-start.55
  23.2 3.7 copy-start.32
  66.8 15.3 %copy-start.17 = (pred[512,1024]{1,0:T(8,128)(4,1)S(1)}, pred[512,1024]{1,0:T(8,128)(4,1)}, u32[]{:S(2)}) copy-start(pred[512,1024]{1,0:T(8,128)(4,1)} %get-tuple-element.111) | copy-start | bytes 1572868
  82.1 12.5 %copy-start.34 = (f32[12,512]{1,0:T(8,128)}, f32[12,512]{1,0:T(8,128)S(1)}, u32[]{:S(2)}) copy-start(f32[12,512]{1,0:T(8,128)S(1)} %get-tuple-element.112) | copy-start | bytes 73732
  82.1 15.7 %copy-start.1 = (f32[12,512,1024]{2,1,0:T(8,128)S(1)}, f32[12,512,1024]{2,1,0:T(8,128)}, u32[]{:S(2)}) copy-start(f32[12,512,1024]{2,1,0:T(8,128)} %get-tuple-element.113) | copy-start | bytes 75497472
  94.6 13.0 %copy-start.43 = (f32[12,512]{1,0:T(8,128)}, f32[12,512]{1,0:T(8,128)S(1)}, u32[]{:S(2)}) copy-start(f32[12,512]{1,0:T(8,128)S(1)} %fusion.1) | copy-start | bytes 73732
  97.8 9.8 copy-start.9
  120.0 14.2 %copy-start.35 = (f32[12,512]{1,0:T(8,128)}, f32[12,512]{1,0:T(8,128)S(1)}, u32[]{:S(2)}) copy-start(f32[12,512]{1,0:T(8,128)S(1)} %get-tuple-element.114) | copy-start | bytes 73732
  120.0 16.2 %copy-start.2 = (f32[12,512,1024]{2,1,0:T(8,128)S(1)}, f32[12,512,1024]{2,1,0:T(8,128)}, u32[]{:S(2)}) copy-start(f32[12,512,1024]{2,1,0:T(8,128)} %get-tuple-element.115) | copy-start | bytes 75497472
  120.0 16.3 %copy-start.20 = (pred[512,1024]{1,0:T(8,128)(4,1)S(1)}, pred[512,1024]{1,0:T(8,128)(4,1)}, u32[]{:S(2)}) copy-start(pred[512,1024]{1,0:T(8,128)(4,1)} %get-tuple-element.110) | copy-start | bytes 1572868
  136.3 9.6 copy-start.44
  281.6 40.7 %all-to-all-start.2 = ((bf16[4,2,128,768]{3,2,1,0:T(8,128)(2,1)}), bf16[4,2,128,768]{3,2,1,0:T(8,128)(2,1)}, u32[]{:S(2)}, u32[]{:S(2)}) async-start(bf16[4,2,128,768]{3,2,1,0:T(8,128)(2,1)} %get-tuple-element.108), calls=%async_computation.2 | async-start | bytes 3145728 | tf_op jit(solution)/shard_map/all_to_all | solution.py:195
  310.7 8.0 copy-start.31
  322.3 41.2 %all-to-all-start.1 = ((bf16[4,2,128,768]{3,2,1,0:T(8,128)(2,1)}), bf16[4,2,128,768]{3,2,1,0:T(8,128)(2,1)}, u32[]{:S(2)}, u32[]{:S(2)}) async-start(bf16[4,2,128,768]{3,2,1,0:T(8,128)(2,1)} %copy.188), calls=%async_computation.1 | async-start | bytes 3145728 | tf_op jit(solution)/shard_map/all_to_all | solution.py:175
  336.5 6.1 copy-start.25
  359.4 13.8 %copy-start.41 = (pred[2,1024]{1,0:T(4,128)(4,1)S(1)}, pred[2,1024]{1,0:T(4,128)(4,1)}, u32[]{:S(2)}) copy-start(pred[2,1024]{1,0:T(4,128)(4,1)} %copy-done.40) | copy-start | bytes 6148
  359.4 13.8 %copy-start.52 = (f32[1024]{0:T(1024)S(1)}, f32[1024]{0:T(1024)}, u32[]{:S(2)}) copy-start(f32[1024]{0:T(1024)} %copy-done.51) | copy-start | bytes 12292
  363.4 40.9 %all-to-all-start.3 = ((bf16[4,2,128,768]{3,2,1,0:T(8,128)(2,1)}), bf16[4,2,128,768]{3,2,1,0:T(8,128)(2,1)}, u32[]{:S(2)}, u32[]{:S(2)}) async-start(bf16[4,2,128,768]{3,2,1,0:T(8,128)(2,1)} %copy.199), calls=%async_computation.3 | async-start | bytes 3145728 | tf_op jit(solution)/shard_map/all_to_all | solution.py:217
  367.8 466.8 %all-reduce.4.cloned.1.call-start = ((), (), s32[]{:S(2)}) async-start(), calls=%async_computation.12 | async-start | bytes 18874368 | tf_op jit(solution)/shard_map/psum | solution.py:281
  446.3 20.5 %copy-start.33 = (s32[1,1024,2]{1,2,0:T(2,128)S(1)}, s32[1,1024,2]{1,2,0:T(2,128)}, u32[]{:S(2)}) copy-start(s32[1,1024,2]{1,2,0:T(2,128)} %param.17) | copy-start | bytes 24580
  446.3 20.6 %copy-start.46 = (f32[1024]{0:T(1024)S(1)}, f32[1024]{0:T(1024)}, u32[]{:S(2)}) copy-start(f32[1024]{0:T(1024)} %copy-done.45) | copy-start | bytes 12292
  466.9 6.4 copy-start.38
  466.9 6.4 copy-start.60
  473.3 3.7 copy-start.50
  473.3 3.7 copy-start.54
  477.1 6.5 copy-start.15
  483.6 2.5 copy-start.29
  486.1 2.8 copy-start.68
  510.5 22.7 %copy-start.10 = (bf16[1024,768]{0,1:T(8,128)(2,1)S(1)}, bf16[1024,768]{0,1:T(8,128)(2,1)}, u32[]{:S(2)}) copy-start(bf16[1024,768]{0,1:T(8,128)(2,1)} %copy.179) | copy-start | bytes 4718596
  533.2 9.5 copy-start.22
  542.7 8.6 copy-start.18
  542.7 8.7 copy-start.26
  542.7 8.7 copy-start.36
  583.3 13.3 %copy-start.19 = (pred[512,1024]{1,0:T(8,128)(4,1)S(1)}, pred[512,1024]{1,0:T(8,128)(4,1)}, u32[]{:S(2)}) copy-start(pred[512,1024]{1,0:T(8,128)(4,1)} %get-tuple-element.111) | copy-start | bytes 1572868
  583.3 13.3 %copy-start.37 = (f32[12,512]{1,0:T(8,128)S(1)}, f32[12,512]{1,0:T(8,128)}, u32[]{:S(2)}) copy-start(f32[12,512]{1,0:T(8,128)} %log_add_fusion) | copy-start | bytes 73732
  583.3 13.3 %copy-start.42 = (f32[12,512]{1,0:T(8,128)S(1)}, f32[12,512]{1,0:T(8,128)}, u32[]{:S(2)}) copy-start(f32[12,512]{1,0:T(8,128)} %get-tuple-element.121) | copy-start | bytes 73732
  596.5 37.8 %copy-start.71 = (bf16[12,64,1024]{2,1,0:T(8,128)(2,1)}, bf16[12,64,1024]{2,1,0:T(8,128)(2,1)S(1)}, u32[]{:S(2)}) copy-start(bf16[12,64,1024]{2,1,0:T(8,128)(2,1)S(1)} %add_convert_fusion) | copy-start | bytes 4718596
  596.6 21.9 %copy-start.11 = (bf16[1024,768]{0,1:T(8,128)(2,1)S(1)}, bf16[1024,768]{0,1:T(8,128)(2,1)}, u32[]{:S(2)}) copy-start(bf16[1024,768]{0,1:T(8,128)(2,1)} %copy.179) | copy-start | bytes 4718596
  618.5 8.7 copy-start.14
  618.5 8.7 copy-start.21
  627.1 7.0 copy-start.24
  634.1 2.5 copy-start.5
  634.1 2.5 copy-start.48
  634.1 2.5 copy-start.56
  634.1 2.5 copy-start.63
  643.8 271.7 %reduce-scatter.5.cloned.1.call-start = ((), (), s32[]{:S(2)}) async-start(), calls=%async_computation.11 | async-start | bytes 10616832 | tf_op jit(solution)/shard_map/reduce_scatter | solution.py:222
  653.7 342.7 %reduce-scatter.3.cloned.1.call-start = ((), (), s32[]{:S(2)}) async-start(), calls=%async_computation.10 | async-start | bytes 10616832 | tf_op jit(solution)/shard_map/reduce_scatter | solution.py:221
  678.3 3.1 copy-start.58
  678.3 3.2 copy-start.6
  678.3 3.9 copy-start.8
  681.5 2.7 copy-start.13
  681.5 2.7 copy-start.16
  681.5 2.7 copy-start.65
  687.3 3.7 copy-start.39
  996.3 6.6 copy-start.27
  (18 other events, 26.0 us)
Sparse Core Ops, SparseCore 0:
  9.9 41.5 all-gather.8
  53.3 38.7 all-gather.4
  94.1 38.7 all-gather.10
  134.6 38.8 all-gather.6
  643.9 190.6 all-reduce.3
  838.5 76.8 reduce-scatter.4
  919.5 76.8 reduce-scatter.2
where the time goes:
time: 1020 us; the launch traced here: 1010 us
  waiting for transfers between devices  284 us (28%)
  matrix products  264 us (26%)
  local copies, waits for them, and re-layouts  195 us (19%)
  other arithmetic  155 us (15%)
  blocking collectives  83.7 us (8%)
  between operations  16 us (2%)
  starting transfers between devices  13.9 us (1%)
    psum x1, waiting for transfers between devices, body(): lax.psum((qkv_local, proj_local, router_local, gain1_local, bias1_local,...  101 us
    reduce_scatter x1, waiting for transfers between devices, body(): lax.psum_scatter(new_in_local, 'batch', scatter_dimension=1, tiled=True)  80.9 us
    reduce_scatter x1, waiting for transfers between devices, body(): lax.psum_scatter(new_out_local, 'batch', scatter_dimension=1, tiled=True)  80.8 us
    convert_element_type x2, other arithmetic, body(): (probs * (dprobs - jnp.sum(probs * dprobs, axis=-1, keepdims=True))).asty...  44.6 us
    all_to_all x1, blocking collectives, body(): lax.all_to_all(send_rows, 'expert', split_axis=0, concat_axis=0, tiled=True)  43.2 us
    psum x1, blocking collectives, body(): lax.psum((qkv_local, proj_local, router_local, gain1_local, bias1_local,...  40.5 us
    dot_general x2, matrix products, body(): jnp.einsum('qhd,khd->hqk', grad_block, value_rows, preferred_element_type...  37.7 us
    unnamed x154, local copies, waits for them, and re-layouts  37.1 us
  transfers between devices with their start and end apart: 10, of which 6 were waited for; matrix products, arithmetic and copies ran while one was open for 35% of the time, Pallas kernels for 0%

commit v1 on v0

v1 whole, which is shorter than its diff:
```python
import functools

import jax
import jax.numpy as jnp
from jax import lax
from jax.experimental import pallas as pl
from jax.experimental.pallas import tpu as pltpu
from jax.sharding import PartitionSpec as P

HEAD_DIM = 64
LANES = 128
EPS = 1e-05
MASKED = -1e30
F32 = jnp.float32
BF16 = jnp.bfloat16
VMEM_LIMIT = 56 * 1024 * 1024


def params():
    return pltpu.CompilerParams(vmem_limit_bytes=VMEM_LIMIT)


def dot_nt(left, right):
    return lax.dot_general(left, right, (((1,), (1,)), ((), ())), preferred_element_type=F32)


def dot_tn(left, right):
    return lax.dot_general(left, right, (((0,), (0,)), ((), ())), preferred_element_type=F32)


def dot_nn(left, right):
    return jnp.dot(left, right, preferred_element_type=F32)


def norm_parts(rows):
    mean = jnp.mean(rows, axis=-1, keepdims=True)
    centred = rows - mean
    var = jnp.mean(centred * centred, axis=-1, keepdims=True)
    scale = lax.rsqrt(var + EPS)
    return centred * scale, scale


def norm_back(grad, gain, xhat, scale):
    a = grad * gain
    mean_a = jnp.mean(a, axis=-1, keepdims=True)
    mean_ax = jnp.mean(a * xhat, axis=-1, keepdims=True)
    return scale * (a - mean_a - xhat * mean_ax)


def full(shape):
    return pl.BlockSpec(shape, lambda *_: (0,) * len(shape))


def smem():
    return pl.BlockSpec(memory_space=pltpu.SMEM)


def qkv_kernel(tok_ref, gain_ref, bias_ref, w_ref, normed_ref, qkv_ref):
    xhat, _ = norm_parts(tok_ref[...].astype(F32))
    normed = (xhat * gain_ref[...] + bias_ref[...]).astype(BF16)
    normed_ref[...] = normed
    qkv_ref[...] = dot_nn(normed, w_ref[...]).astype(BF16)


def qkv_call(tokens, gain, bias, weight):
    seq, width = tokens.shape
    block = 256
    cols = weight.shape[1]
    return pl.pallas_call(
        qkv_kernel,
        grid=(seq // block,),
        in_specs=[
            pl.BlockSpec((block, width), lambda i: (i, 0)),
            full((1, width)),
            full((1, width)),
            full((width, cols)),
        ],
        out_specs=[
            pl.BlockSpec((block, width), lambda i: (i, 0)),
            pl.BlockSpec((block, cols), lambda i: (i, 0)),
        ],
        out_shape=[
            jax.ShapeDtypeStruct((seq, width), BF16),
            jax.ShapeDtypeStruct((seq, cols), BF16),
        ],
        compiler_params=params(),
        name="norm_qkv",
    )(tokens, gain, bias, weight)


def head_parts(head, length, q, k):
    seq = q.shape[0]
    lane = lax.broadcasted_iota(jnp.int32, (seq, LANES), 1)
    row = lax.broadcasted_iota(jnp.int32, (seq, LANES), 0)
    inside = (lane // HEAD_DIM) == head
    extra = lane == (1 - head) * HEAD_DIM
    key_bias = jnp.where(row >= length, MASKED, 0.0)
    kf = k.astype(F32)
    qf = q.astype(F32) * (HEAD_DIM**-0.5)
    k_head = jnp.where(inside, kf, jnp.where(extra, key_bias, 0.0)).astype(BF16)
    q_head = jnp.where(inside, qf, jnp.where(extra, 1.0, 0.0)).astype(BF16)
    return inside, k_head, q_head, jnp.where(inside, qf, 0.0).astype(BF16)


def causal(scores, block):
    key = lax.broadcasted_iota(jnp.int32, (block, block), 0)
    query = lax.broadcasted_iota(jnp.int32, (block, block), 1)
    last = jnp.where(key <= query, scores[-block:], MASKED)
    if scores.shape[0] == block:
        return last
    return jnp.concatenate([scores[:-block], last], axis=0)


def attend_kernel(len_ref, q_ref, k_ref, v_ref, out_ref, lse_ref, kh_ref, qh_ref, vt_ref, ot_ref):
    seq = q_ref.shape[0]
    block = 256
    length = len_ref[0]
    vt_ref[...] = v_ref[...].astype(F32).T.astype(BF16)
    lse_ref[...] = jnp.zeros_like(lse_ref)
    for head in range(2):
        _, k_head, q_head, _ = head_parts(head, length, q_ref[...], k_ref[...])
        kh_ref[...] = k_head
        qh_ref[...] = q_head
        for qb in range(seq // block):
            ext = (qb + 1) * block
            cols = slice(qb * block, ext)
            scores = causal(dot_nt(kh_ref[:ext, :], qh_ref[cols, :]), block)
            top = jnp.max(scores, axis=0, keepdims=True)
            probs = jnp.exp(scores - top)
            total = jnp.sum(probs, axis=0, keepdims=True)
            part = dot_nn(vt_ref[head * HEAD_DIM : (head + 1) * HEAD_DIM, :ext], probs.astype(BF16))
            ot_ref[head * HEAD_DIM : (head + 1) * HEAD_DIM, cols] = part * (1.0 / total)
            lse_ref[0, head : head + 1, cols] = top + jnp.log(total)
    out_ref[...] = ot_ref[...].T.astype(BF16)


def attend_call(length, qkv):
    seq = qkv.shape[0]
    width = qkv.shape[1] // 3
    pairs = width // LANES
    return pl.pallas_call(
        attend_kernel,
        grid=(pairs,),
        in_specs=[
            smem(),
            pl.BlockSpec((seq, LANES), lambda p: (0, p)),
            pl.BlockSpec((seq, LANES), lambda p: (0, pairs + p)),
            pl.BlockSpec((seq, LANES), lambda p: (0, 2 * pairs + p)),
        ],
        out_specs=[
            pl.BlockSpec((seq, LANES), lambda p: (0, p)),
            pl.BlockSpec((1, 8, seq), lambda p: (p, 0, 0)),
        ],
        out_shape=[
            jax.ShapeDtypeStruct((seq, width), BF16),
            jax.ShapeDtypeStruct((pairs, 8, seq), F32),
        ],
        scratch_shapes=[
            pltpu.VMEM((seq, LANES), BF16),
            pltpu.VMEM((seq, LANES), BF16),
            pltpu.VMEM((LANES, seq), BF16),
            pltpu.VMEM((LANES, seq), F32),
        ],
        compiler_params=params(),
        name="attend",
    )(length, qkv, qkv, qkv)


def attend_back_kernel(
    len_ref,
    q_ref,
    k_ref,
    v_ref,
    do_ref,
    o_ref,
    lse_ref,
    normed_ref,
    dqkv_ref,
    grad_ref,
    nt_ref,
    kt_ref,
    kh_ref,
    qh_ref,
    qm_ref,
    vh_ref,
    dh_ref,
    dk_ref,
    dv_ref,
    dqt_ref,
    pt_ref,
):
    seq = q_ref.shape[0]
    block = 256
    length = len_ref[0]

    @pl.when(pl.program_id(0) == 0)
    def _():
        nt_ref[...] = normed_ref[...].astype(F32).T.astype(BF16)

    kt_ref[...] = k_ref[...].astype(F32).T.astype(BF16)
    pt_ref[...] = (do_ref[...].astype(F32) * o_ref[...].astype(F32)).T
    dk_ref[...] = jnp.zeros_like(dk_ref)
    dv_ref[...] = jnp.zeros_like(dv_ref)
    for head in range(2):
        rows = slice(head * HEAD_DIM, (head + 1) * HEAD_DIM)
        inside, k_head, q_head, q_masked = head_parts(head, length, q_ref[...], k_ref[...])
        kh_ref[...] = k_head
        qh_ref[...] = q_head
        qm_ref[...] = q_masked
        vh_ref[...] = jnp.where(inside, v_ref[...].astype(F32), 0.0).astype(BF16)
        dh_ref[...] = jnp.where(inside, do_ref[...].astype(F32), 0.0).astype(BF16)
        for qb in range(seq // block):
            ext = (qb + 1) * block
            cols = slice(qb * block, ext)
            delta = jnp.sum(pt_ref[rows, cols], axis=0, keepdims=True)
            scores = causal(dot_nt(kh_ref[:ext, :], qh_ref[cols, :]), block)
            probs = jnp.exp(scores - lse_ref[0, head : head + 1, cols])
            dprobs = dot_nt(vh_ref[:ext, :], dh_ref[cols, :])
            dscores = (probs * (dprobs - delta)).astype(BF16)
            dv_ref[:ext, :] += dot_nn(probs.astype(BF16), dh_ref[cols, :])
            dk_ref[:ext, :] += dot_nn(dscores, qm_ref[cols, :])
            dqt_ref[rows, cols] = dot_nn(kt_ref[rows, :ext], dscores)
    dq = (dqt_ref[...].T * (HEAD_DIM**-0.5)).astype(BF16)
    dk = dk_ref[...].astype(BF16)
    dv = dv_ref[...].astype(BF16)
    dqkv_ref[0] = dq
    dqkv_ref[1] = dk
    dqkv_ref[2] = dv
    joined = dot_nn(nt_ref[...], jnp.concatenate([dq, dk, dv], axis=1)).astype(BF16)
    for part in range(3):
        grad_ref[part] = joined[:, part * LANES : (part + 1) * LANES]


def attend_back_call(length, qkv, dmixed, mixed, lse, normed):
    seq, width = normed.shape
    pairs = width // LANES
    col = lambda p: (0, p)
    return pl.pallas_call(
        attend_back_kernel,
        grid=(pairs,),
        in_specs=[
            smem(),
            pl.BlockSpec((seq, LANES), col),
            pl.BlockSpec((seq, LANES), lambda p: (0, pairs + p)),
            pl.BlockSpec((seq, LANES), lambda p: (0, 2 * pairs + p)),
            pl.BlockSpec((seq, LANES), col),
            pl.BlockSpec((seq, LANES), col),
            pl.BlockSpec((1, 8, seq), lambda p: (p, 0, 0)),
            full((seq, width)),
        ],
        out_specs=[
            pl.BlockSpec((3, seq, LANES), lambda p: (0, 0, p)),
            pl.BlockSpec((3, width, LANES), lambda p: (0, 0, p)),
        ],
        out_shape=[
            jax.ShapeDtypeStruct((3, seq, width), BF16),
            jax.ShapeDtypeStruct((3, width, width), BF16),
        ],
        scratch_shapes=[
            pltpu.VMEM((width, seq), BF16),
            pltpu.VMEM((LANES, seq), BF16),
            pltpu.VMEM((seq, LANES), BF16),
            pltpu.VMEM((seq, LANES), BF16),
            pltpu.VMEM((seq, LANES), BF16),
            pltpu.VMEM((seq, LANES), BF16),
            pltpu.VMEM((seq, LANES), BF16),
            pltpu.VMEM((seq, LANES), F32),
            pltpu.VMEM((seq, LANES), F32),
            pltpu.VMEM((LANES, seq), F32),
            pltpu.VMEM((LANES, seq), F32),
        ],
        compiler_params=params(),
        name="attend_back",
    )(length, qkv, qkv, qkv, dmixed, mixed, lse, normed)


def route_kernel(
    experts, group, capacity, len_ref, me_ref, route_ref, pair_ref, cot_ref, slot_ref, slot_t_ref, *out_refs
):
    seq = route_ref.shape[1]
    half = experts // 2
    per = half // group
    local = 2 * per
    length = len_ref[0]
    me = me_ref[0]
    live = lax.broadcasted_iota(jnp.int32, (1, seq), 1) < length
    ids = lax.broadcasted_iota(jnp.int32, (experts, seq), 0)
    upper = (
        lax.broadcasted_iota(jnp.int32, (seq, seq), 0) < lax.broadcasted_iota(jnp.int32, (seq, seq), 1)
    )
    upper = jnp.where(upper, 1.0, 0.0).astype(BF16)
    before = jnp.zeros((experts, 1), F32)
    slots = []
    for choice in range(2):
        named = route_ref[choice : choice + 1, :]
        hot = jnp.where((ids == named) & live, 1.0, 0.0)
        earlier = dot_nn(hot.astype(BF16), upper) + before
        rank = jnp.sum(hot * earlier, axis=0, keepdims=True).astype(jnp.int32)
        before = before + jnp.sum(hot, axis=1, keepdims=True)
        is_new = named >= half
        within = jnp.where(is_new, named - half, named)
        owner = within // per
        place = jnp.where(is_new, per, 0) + within - owner * per
        shift = owner - me
        shift = jnp.where(shift < 0, shift + group, shift)
        slot = (shift * local + place) * capacity + rank
        slots.append(jnp.where(live & (rank < capacity), slot, -1))
    slot_ref[...] = jnp.concatenate(slots + [jnp.full((6, seq), -1, jnp.int32)], axis=0)
    slot_t_ref[...] = jnp.concatenate(
        [slot.astype(F32) for slot in slots] + [jnp.full((LANES - 2, seq), -1.0, F32)], axis=0
    ).T.astype(jnp.int32)
    total = experts * capacity
    place = lax.broadcasted_iota(jnp.int32, (total, seq), 0)
    select = jnp.where((place == slots[0]) | (place == slots[1]), 1.0, 0.0).astype(BF16)
    rows = dot_nn(select, cot_ref[...]).astype(BF16)
    both = (pair_ref[:, 0:1] + pair_ref[:, 1:2]).astype(F32)
    lane = lax.broadcasted_iota(jnp.int32, (seq, LANES), 1)
    tail = dot_nn(select, jnp.where(lane == 0, both, 0.0).astype(BF16)).astype(BF16)
    width = cot_ref.shape[1]
    size = local * capacity
    for shift in range(group):
        piece = slice(shift * size, (shift + 1) * size)
        out_refs[shift][:, :, :width] = rows[piece].reshape(local, capacity, width)
        out_refs[shift][:, :, width:] = tail[piece].reshape(local, capacity, LANES)


def route_call(length, me, routes, cotangent, experts, group, capacity):
    seq, width = cotangent.shape
    local = experts // group
    wide = width + LANES
    return pl.pallas_call(
        functools.partial(route_kernel, experts, group, capacity),
        in_specs=[smem(), smem(), full((2, seq)), full((seq, 2)), full((seq, width))],
        out_specs=[full((8, seq)), full((seq, LANES))] + [full((local, capacity, wide))] * group,
        out_shape=[
            jax.ShapeDtypeStruct((8, seq), jnp.int32),
            jax.ShapeDtypeStruct((seq, LANES), jnp.int32),
        ]
        + [jax.ShapeDtypeStruct((local, capacity, wide), BF16)] * group,
        grid=(1,),
        compiler_params=params(),
        name="route",
    )(length, me, routes.T, routes, cotangent)


def project_kernel(
    group, mixed_ref, tok_ref, w_ref, gain_ref, bias_ref, slot_ref, res_ref, *refs
):
    out_refs = refs[:group]
    normed_ref = refs[group]
    step = pl.program_id(0)
    block = mixed_ref.shape[0]
    residual = tok_ref[...].astype(F32) + dot_nn(mixed_ref[...], w_ref[...])
    res_ref[...] = residual
    xhat, _ = norm_parts(residual)
    normed = (xhat * gain_ref[...] + bias_ref[...]).astype(BF16)
    normed_ref[pl.ds(pl.multiple_of(step * block, block), block), :] = normed

    @pl.when(step == pl.num_programs(0) - 1)
    def _():
        local, capacity, width = out_refs[0].shape
        size = local * capacity
        seq = normed_ref.shape[0]
        place = lax.broadcasted_iota(jnp.int32, (size * group, seq), 0)
        select = (place == slot_ref[0:1, :]) | (place == slot_ref[1:2, :])
        select = jnp.where(select, 1.0, 0.0).astype(BF16)
        rows = dot_nn(select, normed_ref[...]).astype(BF16)
        for shift in range(group):
            out_refs[shift][...] = rows[shift * size : (shift + 1) * size].reshape(local, capacity, width)


def project_call(mixed, tokens, weight, gain, bias, slots, group, local, capacity):
    seq, width = tokens.shape
    block = 256
    rows = pl.BlockSpec((block, width), lambda i: (i, 0))
    return pl.pallas_call(
        functools.partial(project_kernel, group),
        grid=(seq // block,),
        in_specs=[rows, rows, full((width, width)), full((1, width)), full((1, width)), full((8, seq))],
        out_specs=[rows] + [full((local, capacity, width))] * group,
        out_shape=[jax.ShapeDtypeStruct((seq, width), F32)]
        + [jax.ShapeDtypeStruct((local, capacity, width), BF16)] * group,
        scratch_shapes=[pltpu.VMEM((seq, width), BF16)],
        compiler_params=params(),
        name="project_dispatch",
    )(mixed, tokens, weight, gain, bias, slots)


def expert_kernel(trained, group, own_ref, *refs):
    x_refs = refs[:group]
    g_refs = refs[group : 2 * group]
    wr_ref, wrt_ref, win_ref, wout_ref = refs[2 * group : 2 * group + 4]
    rest = refs[2 * group + 4 :]
    out_refs = rest[:group]
    back_refs = rest[group : 2 * group]
    router_ref = rest[2 * group]
    rest = rest[2 * group + 1 :]
    if trained:
        din_ref, dout_ref = rest[:2]
        rest = rest[2:]
    x_ref, dexp_ref, gate_ref, acc_ref, back_ref, xt_ref = rest
    step = pl.program_id(0)
    capacity, width = out_refs[0].shape
    own = own_ref[0]

    def other_of(tail):
        return tail[:, 0:1].astype(F32).astype(jnp.int32) - own

    @pl.when(step == 0)
    def _():
        for shift in range(group):
            span = slice(shift * capacity, (shift + 1) * capacity)
            rows = x_refs[shift][0]
            x_ref[span, :] = rows
            logits = dot_nn(rows, wr_ref[...])
            lane = lax.broadcasted_iota(jnp.int32, logits.shape, 1)
            other = other_of(g_refs[shift][0, :, width:])
            mine = jnp.sum(jnp.where(lane == own, logits, 0.0), axis=1, keepdims=True)
            theirs = jnp.sum(jnp.where(lane == other, logits, 0.0), axis=1, keepdims=True)
            top = jnp.maximum(mine, theirs)
            up = jnp.exp(mine - top)
            gate = up / (up + jnp.exp(theirs - top))
            gate_ref[span, :] = jnp.broadcast_to(gate, (capacity, LANES))
            dexp_ref[span, :] = (gate * g_refs[shift][0, :, :width].astype(F32)).astype(BF16)
        acc_ref[...] = jnp.zeros_like(acc_ref)
        back_ref[...] = jnp.zeros_like(back_ref)
        xt_ref[...] = x_ref[...].astype(F32).T.astype(BF16)

    win = win_ref[0]
    wout = wout_ref[0]
    pre = dot_nn(x_ref[...], win)
    square = pre * pre
    tanh = jnp.tanh(0.7978845608028654 * (pre + 0.044715 * pre * square))
    half = 0.5 * (1.0 + tanh)
    hid = (pre * half).astype(BF16)
    slope = half + (0.5 * pre) * (1.0 - tanh * tanh) * (0.7978845608028654 + 0.1070322243 * square)
    acc_ref[...] += dot_nn(hid, wout)
    dpre = (dot_nt(dexp_ref[...], wout) * slope).astype(BF16)
    back_ref[...] += dot_nt(dpre, win)
    if trained:
        dout_ref[...] = dot_tn(hid, dexp_ref[...]).astype(BF16)
        din_ref[...] = dot_nn(xt_ref[...], dpre).astype(BF16)

    @pl.when(step == pl.num_programs(0) - 1)
    def _():
        router = jnp.zeros((width, LANES), F32)
        for shift in range(group):
            span = slice(shift * capacity, (shift + 1) * capacity)
            gate = gate_ref[span, 0:1]
            result = acc_ref[span, :]
            out_refs[shift][...] = (gate * result).astype(BF16)
            dot = jnp.sum(result * g_refs[shift][0, :, :width].astype(F32), axis=1, keepdims=True)
            coef = gate * (1.0 - gate) * dot
            lane = lax.broadcasted_iota(jnp.int32, (capacity, LANES), 1)
            other = other_of(g_refs[shift][0, :, width:])
            sign = jnp.where(lane == own, 1.0, 0.0) - jnp.where(lane == other, 1.0, 0.0)
            dlogits = (coef * sign).astype(BF16)
            back_refs[shift][...] = (back_ref[span, :] + dot_nn(dlogits, wrt_ref[...])).astype(BF16)
            router = router + dot_nn(xt_ref[:, span], dlogits)
        router_ref[...] = router


def expert_call(trained, place, own, rows, grads, router, router_t, w_in, w_out):
    group = len(rows)
    _, capacity, width = rows[0].shape
    inner = w_in.shape[2]
    chunk = 512
    wide = grads[0].shape[2]
    many = group * capacity
    fixed = full((capacity, width))
    out_specs = [fixed] * (2 * group) + [full((width, LANES))]
    out_shape = [jax.ShapeDtypeStruct((capacity, width), BF16)] * (2 * group) + [
        jax.ShapeDtypeStruct((width, LANES), F32)
    ]
    if trained:
        out_specs += [
            pl.BlockSpec((width, chunk), lambda f: (0, f)),
            pl.BlockSpec((chunk, width), lambda f: (f, 0)),
        ]
        out_shape += [
            jax.ShapeDtypeStruct((width, inner), BF16),
            jax.ShapeDtypeStruct((inner, width), BF16),
        ]
    return pl.pallas_call(
        functools.partial(expert_kernel, trained, group),
        grid=(inner // chunk,),
        in_specs=[smem()]
        + [pl.BlockSpec((1, capacity, width), lambda f: (place, 0, 0))] * group
        + [pl.BlockSpec((1, capacity, wide), lambda f: (place, 0, 0))] * group
        + [
            full((width, LANES)),
            full((LANES, width)),
            pl.BlockSpec((1, width, chunk), lambda f: (0, 0, f)),
            pl.BlockSpec((1, chunk, width), lambda f: (0, f, 0)),
        ],
        out_specs=out_specs,
        out_shape=out_shape,
        scratch_shapes=[
            pltpu.VMEM((many, width), BF16),
            pltpu.VMEM((many, width), BF16),
            pltpu.VMEM((many, LANES), F32),
            pltpu.VMEM((many, width), F32),
            pltpu.VMEM((many, width), F32),
            pltpu.VMEM((width, many), BF16),
        ],
        compiler_params=params(),
        name="experts_new" if trained else "experts_old",
    )(own, *rows, *grads, router, router_t, w_in, w_out)


def pick_matrix(slot_ref, total):
    place = lax.broadcasted_iota(jnp.int32, (slot_ref.shape[0], total), 1)
    hit = (place == slot_ref[:, 0:1]) | (place == slot_ref[:, 1:2])
    return jnp.where(hit, 1.0, 0.0).astype(BF16)


def pick_rows(slot_ref, part_refs):
    capacity = part_refs[0].shape[0]
    pick = pick_matrix(slot_ref, capacity * len(part_refs))
    total = jnp.zeros((slot_ref.shape[0], part_refs[0].shape[1]), F32)
    held = jnp.concatenate([part[...] for part in part_refs], axis=0)
    return total + dot_nn(pick, held)


def combine_kernel(count, slot_ref, res_ref, *refs):
    refs[count][...] = res_ref[...] + pick_rows(slot_ref, refs[:count])


def combine_call(slots, residual, parts):
    seq, width = residual.shape
    block = 256
    capacity = parts[0].shape[0]
    rows = pl.BlockSpec((block, width), lambda i: (i, 0))
    return pl.pallas_call(
        functools.partial(combine_kernel, len(parts)),
        grid=(seq // block,),
        in_specs=[pl.BlockSpec((block, LANES), lambda i: (i, 0)), rows]
        + [full((capacity, width))] * len(parts),
        out_specs=rows,
        out_shape=jax.ShapeDtypeStruct((seq, width), F32),
        compiler_params=params(),
        name="combine",
    )(slots, residual, *parts)


def middle_kernel(count, slot_ref, res_ref, cot_ref, gain_ref, mixed_ref, w_ref, *refs):
    parts = refs[:count]
    dres_ref, dmix_ref, proj_ref, sums_ref, acc_ref = refs[count:]
    step = pl.program_id(0)
    dnormed = pick_rows(slot_ref, parts)
    xhat, scale = norm_parts(res_ref[...])
    dres = cot_ref[...].astype(F32) + norm_back(dnormed, gain_ref[...], xhat, scale)
    dres_ref[...] = dres
    dattn = dres.astype(BF16)
    dmix_ref[...] = dot_nt(dattn, w_ref[...]).astype(BF16)

    @pl.when(step == 0)
    def _():
        sums_ref[...] = jnp.zeros_like(sums_ref)
        acc_ref[...] = jnp.zeros_like(acc_ref)

    acc_ref[...] += dot_tn(mixed_ref[...], dattn)
    sums_ref[0:1, :] += jnp.sum(dnormed * xhat, axis=0, keepdims=True)
    sums_ref[1:2, :] += jnp.sum(dnormed, axis=0, keepdims=True)

    @pl.when(step == pl.num_programs(0) - 1)
    def _():
        proj_ref[...] = acc_ref[...].astype(BF16)


def middle_call(slots, residual, cotangent, gain, mixed, weight, parts):
    seq, width = residual.shape
    block = 256
    capacity = parts[0].shape[0]
    rows = pl.BlockSpec((block, width), lambda i: (i, 0))
    return pl.pallas_call(
        functools.partial(middle_kernel, len(parts)),
        grid=(seq // block,),
        in_specs=[
            pl.BlockSpec((block, LANES), lambda i: (i, 0)),
            rows,
            rows,
            full((1, width)),
            rows,
            full((width, width)),
        ]
        + [full((capacity, width))] * len(parts),
        out_specs=[rows, rows, full((width, width)), full((8, width))],
        out_shape=[
            jax.ShapeDtypeStruct((seq, width), F32),
            jax.ShapeDtypeStruct((seq, width), BF16),
            jax.ShapeDtypeStruct((width, width), BF16),
            jax.ShapeDtypeStruct((8, width), F32),
        ],
        scratch_shapes=[pltpu.VMEM((width, width), F32)],
        compiler_params=params(),
        name="middle_back",
    )(slots, residual, cotangent, gain, mixed, weight, *parts)


def last_kernel(dqkv_ref, tok_ref, dres_ref, gain_ref, w_ref, out_ref, sums_ref):
    width = tok_ref.shape[1]
    dnormed = dot_nt(dqkv_ref[0], w_ref[:, :width])
    dnormed += dot_nt(dqkv_ref[1], w_ref[:, width : 2 * width])
    dnormed += dot_nt(dqkv_ref[2], w_ref[:, 2 * width :])
    xhat, scale = norm_parts(tok_ref[...].astype(F32))
    out_ref[...] = dres_ref[...] + norm_back(dnormed, gain_ref[...], xhat, scale)

    @pl.when(pl.program_id(0) == 0)
    def _():
        sums_ref[...] = jnp.zeros_like(sums_ref)

    sums_ref[0:1, :] += jnp.sum(dnormed * xhat, axis=0, keepdims=True)
    sums_ref[1:2, :] += jnp.sum(dnormed, axis=0, keepdims=True)


def last_call(dqkv, tokens, dres, gain, weight):
    seq, width = tokens.shape
    block = 256
    rows = pl.BlockSpec((block, width), lambda i: (i, 0))
    return pl.pallas_call(
        last_kernel,
        grid=(seq // block,),
        in_specs=[
            pl.BlockSpec((3, block, width), lambda i: (0, i, 0)),
            rows,
            rows,
            full((1, width)),
            full((width, 3 * width)),
        ],
        out_specs=[rows, full((8, width))],
        out_shape=[
            jax.ShapeDtypeStruct((seq, width), F32),
            jax.ShapeDtypeStruct((8, width), F32),
        ],
        compiler_params=params(),
        name="last_back",
    )(dqkv, tokens, dres, gain, weight)


def body(
    tokens,
    lengths,
    routes,
    ln1_gain,
    ln1_bias,
    ln2_gain,
    ln2_bias,
    w_qkv,
    w_proj,
    w_router,
    old_in,
    old_out,
    new_in,
    new_out,
    cotangent,
):
    group = lax.axis_size("expert")
    me = lax.axis_index("expert")
    token_rows = tokens[0]
    cot_rows = cotangent[0]
    seq, width = token_rows.shape
    experts = w_router.shape[1]
    local = experts // group
    per = old_in.shape[0]
    capacity = max(4, seq // experts)
    gain1, bias1 = ln1_gain[None], ln1_bias[None]
    gain2, bias2 = ln2_gain[None], ln2_bias[None]

    def go(block, shift):
        if shift == 0:
            return block
        return lax.ppermute(block, "expert", [(i, (i + shift) % group) for i in range(group)])

    def come(block, shift):
        if shift == 0:
            return block
        return lax.ppermute(block, "expert", [(i, (i - shift) % group) for i in range(group)])

    me_one = jnp.full((1,), me, jnp.int32)
    full_old_in = lax.all_gather(old_in, "batch", axis=1, tiled=True)
    full_old_out = lax.all_gather(old_out, "batch", axis=1, tiled=True)
    full_new_in = lax.all_gather(new_in, "batch", axis=1, tiled=True)
    full_new_out = lax.all_gather(new_out, "batch", axis=1, tiled=True)
    slots, slots_t, *sent_grads = route_call(
        lengths, me_one, routes[0], cot_rows, experts, group, capacity
    )
    grads = [go(block, shift) for shift, block in enumerate(sent_grads)]
    normed1, qkv = qkv_call(token_rows, gain1, bias1, w_qkv)
    mixed, lse = attend_call(lengths, qkv)
    residual, *sent_rows = project_call(
        mixed, token_rows, w_proj, gain2, bias2, slots, group, local, capacity
    )
    rows = [go(block, shift) for shift, block in enumerate(sent_rows)]
    router = jnp.pad(w_router, ((0, 0), (0, LANES - experts)))
    router_t = jnp.pad(w_router.T, ((0, LANES - experts), (0, 0)))
    outs, backs, router_sum = [], [], 0.0
    half = experts // 2
    for trained, w_in, w_out in ((False, full_old_in, full_old_out), (True, full_new_in, full_new_out)):
        for index in range(per):
            own = jnp.full((1,), me * per + index + (half if trained else 0), jnp.int32)
            got = expert_call(
                trained,
                index + (per if trained else 0),
                own,
                rows,
                grads,
                router,
                router_t,
                w_in[index : index + 1],
                w_out[index : index + 1],
            )
            outs.append(got[:group])
            backs.append(got[group : 2 * group])
            router_sum = router_sum + got[2 * group]
            if trained:
                new_in_local, new_out_local = got[2 * group + 1 :]
    returned = [come(backs[p][shift], shift) for shift in range(group) for p in range(local)]
    dres, dmixed, proj_grad, sums2 = middle_call(
        slots_t, residual, cot_rows, gain2, mixed, w_proj, returned
    )
    new_in_grad = lax.psum_scatter(new_in_local, "batch", scatter_dimension=0, tiled=True)
    new_out_grad = lax.psum_scatter(new_out_local, "batch", scatter_dimension=0, tiled=True)
    dqkv, qkv_grad = attend_back_call(lengths, qkv, dmixed, mixed, lse, normed1)
    big = lax.psum((qkv_grad, proj_grad), ("expert", "batch"))
    input_grad, sums1 = last_call(dqkv, token_rows, dres, gain1, w_qkv)
    back_outs = [come(outs[p][shift], shift) for shift in range(group) for p in range(local)]
    output = combine_call(slots_t, residual, back_outs)
    small = jnp.concatenate([router_sum.T[: 2 * 8], sums1, sums2], axis=0)
    small = jnp.sum(lax.all_gather(small, ("expert", "batch"), axis=0), axis=0)
    qkv_out = jnp.transpose(big[0].astype(F32), (1, 0, 2)).reshape(width, 3 * width)
    return (
        output[None],
        input_grad[None],
        small[16],
        small[17],
        small[24],
        small[25],
        qkv_out,
        big[1].astype(F32),
        small[:experts].T,
        new_in_grad.astype(F32)[None],
        new_out_grad.astype(F32)[None],
    )


def solution(mesh):
    rows = P(("expert", "batch"), None, None)
    weights = P("expert", "batch", None)
    placed = (
        (rows, P(("expert", "batch")), rows)
        + (P(),) * 7
        + (weights,) * 4
        + (rows,)
    )
    return jax.shard_map(
        body,
        mesh=mesh,
        in_specs=placed,
        out_specs=(rows, rows) + (P(),) * 7 + (weights, weights),
        check_vma=False,
    )
```

time: 1020 us -> 625 us (0.61)
  matrix products: 264 us -> 0 us
  local copies, waits for them, and re-layouts: 195 us -> 24.1 us
  Pallas kernels: 0 us -> 149 us
  other arithmetic: 155 us -> 10.8 us
  waiting for transfers between devices: 284 us -> 392 us
  blocking collectives: 83.7 us -> 0 us
  starting transfers between devices: 13.9 us -> 33.8 us
    dot_general x31 -> x0, matrix products: 264 us -> none  [the longest x2 37.7 us: body(): jnp.einsum('qhd,khd->hqk', grad_block, value_rows, preferred_element_type...]
    pallas_call x0 -> x10, Pallas kernels: none -> 149 us  [the longest x2 40.4 us: expert_call(): pl.pallas_call(functools.partial(expert_kernel, trained, group), grid=(in...]
    ppermute x0 -> x18, waiting for transfers between devices: none -> 118 us  [the longest x12 59.5 us: come(): lax.ppermute(block, 'expert', [(i, (i - shift) % group) for i in range(gr...]
    reduce_sum x14 -> x1, other arithmetic: 73.5 us -> 2.05 us  [body(): small = jnp.sum(lax.all_gather(small, ('expert', 'batch'), axis=0), axis=0)]
    all_gather x4 -> x5, waiting for transfers between devices: 0.03 us -> 61.4 us  [the longest x1 53.1 us: body(): small = jnp.sum(lax.all_gather(small, ('expert', 'batch'), axis=0), axis=0)]
    gather x9 -> x0, local copies, waits for them, and re-layouts: 58.3 us -> none  [the longest x5 19.2 us: body(): jnp.take_along_axis(logits, route_row, axis=1)]
    reduce_scatter x2, waiting for transfers between devices: 162 us -> 108 us  [the longest x1 55.1 us: body(): lax.psum_scatter(new_in_local, 'batch', scatter_dimension=0, tiled=True)]
    convert_element_type x7 -> x1, other arithmetic: 51.7 us -> 3 us  [body(): big[1].astype(F32)]
  transfers between devices with their start and end apart: 10 -> 26, of which waited for: 6 -> 12; matrix products, arithmetic and copies ran while one was open for 35% -> 4% of each run, Pallas kernels for 0% -> 17%
where the time goes in v1:
time: 625 us; the launch traced here: 624 us
  waiting for transfers between devices  392 us (63%)
  Pallas kernels  149 us (24%)
  starting transfers between devices  33.8 us (5%)
  local copies, waits for them, and re-layouts  24.1 us (4%)
  between operations  15.1 us (2%)
  other arithmetic  10.8 us (2%)
    psum x1, waiting for transfers between devices, body(): big = lax.psum((qkv_grad, proj_grad), ('expert', 'batch'))  100 us
    ppermute x12, waiting for transfers between devices, come(): lax.ppermute(block, 'expert', [(i, (i - shift) % group) for i in range(gr...  59.5 us
    ppermute x6, waiting for transfers between devices, go(): lax.ppermute(block, 'expert', [(i, (i + shift) % group) for i in range(gr...  58.5 us
    reduce_scatter x1, waiting for transfers between devices, body(): lax.psum_scatter(new_in_local, 'batch', scatter_dimension=0, tiled=True)  55.1 us
    all_gather x1, waiting for transfers between devices, body(): small = jnp.sum(lax.all_gather(small, ('expert', 'batch'), axis=0), axis=0)  53.1 us
    reduce_scatter x1, waiting for transfers between devices, body(): lax.psum_scatter(new_out_local, 'batch', scatter_dimension=0, tiled=True)  52.7 us
    pallas_call x2, Pallas kernels, expert_call(): pl.pallas_call(functools.partial(expert_kernel, trained, group), grid=(in...  40.4 us
    pallas_call x1, Pallas kernels, attend_back_call(): pl.pallas_call(attend_back_kernel, grid=(pairs,), in_specs=[smem(), pl.Bl...  31.9 us
  transfers between devices with their start and end apart: 26, of which 12 were waited for; matrix products, arithmetic and copies ran while one was open for 4% of the time, Pallas kernels for 17%

profile of v1, /device:TPU:0, one launch (start us, length us, event | category | flops | bytes accessed | tf_op | source)
XLA Modules:
  0.0 624.3 jit_solution(5699866423039138667)
XLA Ops:
  7.2 0.7 all-gather.7.cloned.1.call-update
  8.0 0.7 all-gather.9.cloned.1.call-update
  8.7 0.7 all-gather.11.cloned.1.call-update
  9.4 0.5 all-gather.13.cloned.1.call-update
  10.7 1.3 broadcast_in_dim.38.gain_ref
  11.9 1.3 broadcast_in_dim.40.gain_ref
  13.2 1.3 broadcast_in_dim.39.bias_ref
  14.5 1.3 broadcast_in_dim.41.bias_ref
  15.7 0.9 copy.39
  16.7 0.8 copy.40.route_ref
  17.5 8.6 %norm_qkv.1 = (bf16[1024,768]{1,0:T(8,128)(2,1)}, bf16[1024,2304]{1,0:T(8,128)(2,1)}) custom-call(bf16[1024,768]{1,0:T(8,128)(2,1)} %bitcast.25, f32[1,768]{1,0:T(1,128)} %broadcast_in_dim.38.gain_ref, f32[1,768]{1,0:T(1,128)} %broadcast_in_dim.39.bias_ref, bf16[768,2304]{1,0:T(8,128)(2,1)} %w_ref.7), custom_call_target="tpu_custom_call" | custom-call | tf_op jit(solution)/shard_map/norm_qkv/pallas_call | solution.py:69
  26.1 24.1 %attend.1 = (bf16[1024,768]{1,0:T(8,128)(2,1)}, f32[6,8,1024]{2,1,0:T(8,128)}) custom-call(s32[1]{0:T(128)S(6)} %copy.47.len_ref, bf16[1024,2304]{1,0:T(8,128)(2,1)} %get-tuple-element.55.q_ref.k_ref.v_ref, bf16[1024,2304]{1,0:T(8,128)(2,1)} %get-tuple-element.55.q_ref.k_ref.v_ref, bf16[1024,2304]{1,0:T(8,128)(2,1)} %get-tuple-element.55.q_ref.k_ref.v_ref), custom_call_target="tpu_custom_call" | custom-call | tf_op jit(solution)/shard_map/attend/pallas_call | solution.py:141
  50.2 5.9 route.1
  56.0 8.8 %project_dispatch.1 = (f32[1024,768]{1,0:T(8,128)}, bf16[2,128,768]{2,1,0:T(8,128)(2,1)}, bf16[2,128,768]{2,1,0:T(8,128)(2,1)}, bf16[2,128,768]{2,1,0:T(8,128)(2,1)}, bf16[2,128,768]{2,1,0:T(8,128)(2,1)}) custom-call(bf16[1024,768]{1,0:T(8,128)(2,1)} %get-tuple-element.56.mixed_ref.o_ref, bf16[1024,768]{1,0:T(8,128)(2,1)} %bitcast.26, ...), custom_call_target="tpu_custom_call" | custom-call | tf_op jit(solution)/shard_map/project_dispatch/pallas_call | solution.py:376
  64.9 3.2 collective-permute-start
  68.1 1.6 collective-permute-start.3
  69.6 1.1 collective-permute-start.4
  70.7 2.9 collective-permute-start.5
  73.5 0.4 collective-permute-start.1
  73.9 6.5 %collective-permute-done.refs_1_ = bf16[2,128,768]{2,1,0:T(8,128)(2,1)S(1)} collective-permute-done((bf16[2,128,768]{2,1,0:T(8,128)(2,1)}, bf16[2,128,768]{2,1,0:T(8,128)(2,1)S(1)}, u32[]{:S(2)}, u32[]{:S(2)}) %collective-permute-start) | collective-permute-done | bytes 393248 | tf_op jit(solution)/shard_map/ppermute | solution.py:673
  80.4 1.8 collective-permute-start.2
  82.4 0.7 pad.9.refs_9_
  83.1 0.7 pad.8.refs_8_
  83.9 51.9 %collective-permute-done.1.refs_2_ = bf16[2,128,768]{2,1,0:T(8,128)(2,1)S(1)} collective-permute-done((bf16[2,128,768]{2,1,0:T(8,128)(2,1)}, bf16[2,128,768]{2,1,0:T(8,128)(2,1)S(1)}, u32[]{:S(2)}, u32[]{:S(2)}) %collective-permute-start.1) | collective-permute-done | bytes 393248 | tf_op jit(solution)/shard_map/ppermute | solution.py:673
  135.9 0.6 copy-done.6
  137.1 17.4 %experts_old.1 = (bf16[128,768]{1,0:T(8,128)(2,1)}, bf16[128,768]{1,0:T(8,128)(2,1)}, bf16[128,768]{1,0:T(8,128)(2,1)}, bf16[128,768]{1,0:T(8,128)(2,1)}, bf16[1...) custom-call(s32[1]{0:T(128)} %bitcast.me_ref.own_ref, ...), custom_call_target="tpu_custom_call" | custom-call | tf_op jit(solution)/shard_map/experts_old/pallas_call | solution.py:484
  154.6 9.9 %collective-permute-start.12 = (bf16[128,768]{1,0:T(8,128)(2,1)}, bf16[128,768]{1,0:T(8,128)(2,1)S(1)}, u32[]{:S(2)}, u32[]{:S(2)}) collective-permute-start(bf16[128,768]{1,0:T(8,128)(2,1)} %get-tuple-element.77), channel_id=1, source_target_pairs={{0,24},{8,0},{16,8},{24,16},{1,25},{9,1},{17,9},{25,17},{2,26},{10... | collective-permute-start | bytes 589832 | tf_op jit(solution)/shard_map/ppermute | solution.py:678
  164.5 0.4 collective-permute-start.14
  165.1 8.3 %all-gather.13.cloned.1.call-done.refs_11_ = bf16[1,3072,768]{2,1,0:T(8,128)(2,1)} async-done(((bf16[1,384,768]{2,1,0:T(8,128)(2,1)}), bf16[1,3072,768]{2,1,0:T(8,128)(2,1)}) %all-gather.13.cloned.1.call-update) | async-done | bytes 4718608 | tf_op jit(solution)/shard_map/all_gather | solution.py:684
  173.4 22.9 %experts_new.1 = (bf16[128,768]{1,0:T(8,128)(2,1)}, bf16[128,768]{1,0:T(8,128)(2,1)}, bf16[128,768]{1,0:T(8,128)(2,1)}, bf16[128,768]{1,0:T(8,128)(2,1)}, bf16[1...) custom-call(s32[1]{0:T(128)} %bitcast.6.own_ref, ...), custom_call_target="tpu_custom_call" | custom-call | tf_op jit(solution)/shard_map/experts_new/pallas_call | solution.py:484
  196.3 3.4 collective-permute-start.13
  199.7 1.1 collective-permute-start.17
  200.9 4.6 collective-permute-done.13.refs_3_
  205.4 11.8 %collective-permute-done.15.refs_5_ = bf16[128,768]{1,0:T(8,128)(2,1)S(1)} collective-permute-done((bf16[128,768]{1,0:T(8,128)(2,1)}, bf16[128,768]{1,0:T(8,128)(2,1)S(1)}, u32[]{:S(2)}, u32[]{:S(2)}) %collective-permute-start.15) | collective-permute-done | bytes 196640 | tf_op jit(solution)/shard_map/ppermute | solution.py:678
  217.3 0.6 copy-done.17
  218.0 13.2 %middle_back.1 = (f32[1024,768]{1,0:T(8,128)}, bf16[1024,768]{1,0:T(8,128)(2,1)}, bf16[768,768]{1,0:T(8,128)(2,1)}, f32[8,768]{1,0:T(8,128)}) custom-call(s32[1024,128]{1,0:T(8,128)} %get-tuple-element.54.slot_ref, f32[1024,768]{1,0:T(8,128)} %get-tuple-element.58.res_ref, bf16[1024,768]{1,0:T(8,128)(2,1)} %bitcast.29, f32[1,768]{1,0:T(1,128)} %broadcast_in_dim.40.gain_ref, ...), custom_call_target="tpu_custom_call" | custom-call | tf_op jit(solution)/shard_map/middle_back/pallas_call | solution.py:576
  231.2 31.9 %attend_back.1 = (bf16[3,1024,768]{2,1,0:T(8,128)(2,1)}, bf16[3,768,768]{2,1,0:T(8,128)(2,1)}) custom-call(s32[1]{0:T(128)S(6)} %copy.47.len_ref, bf16[1024,2304]{1,0:T(8,128)(2,1)} %get-tuple-element.55.q_ref.k_ref.v_ref, bf16[1024,2304]{1,0:T(8,128)(2,1)} %get-tuple-element.55.q_ref.k_ref.v_ref, bf16[1024,2304]{1,0:T(8,128)(2,1)} %get-tuple-element.55.q_ref.k_ref.v_ref, ...), custom_call_target="tpu_custom_call" | custom-call | tf_op jit(solution)/shard_map/attend_back/pallas_call | solution.py:238
  263.1 6.0 copy.43
  269.2 0.9 copy-done.8
  270.4 9.9 %last_back.1 = (f32[1024,768]{1,0:T(8,128)}, f32[8,768]{1,0:T(8,128)}) custom-call(bf16[3,1024,768]{2,1,0:T(8,128)(2,1)} %get-tuple-element.86.dqkv_ref, bf16[1024,768]{1,0:T(8,128)(2,1)} %bitcast.27, f32[1024,768]{1,0:T(8,128)} %get-tuple-element.87.dres_ref, f32[1,768]{1,0:T(1,128)} %broadcast_in_dim.38.gain_ref, bf16[768,2304]{1,0:T(8,128)(2,1)} %w_ref.7), custom_call_target="tpu_custom_call" | custom-call | tf_op jit(solution)/shard_map/last_back/pallas_call | solution.py:621
  280.3 1.4 pad_maximum_fusion
  281.8 0.7 reduce-scatter.5.cloned.1.call-update
  282.6 0.7 reduce-scatter.3.cloned.1.call-update
  283.4 0.6 collective-permute-start.6
  283.9 2.2 collective-permute-start.8
  286.1 1.9 collective-permute-start.10
  288.1 1.9 collective-permute-start.7
  290.0 5.5 collective-permute-done.6.refs_2_
  295.4 1.1 collective-permute-start.11
  296.5 16.0 %collective-permute-done.8.refs_4_ = bf16[128,768]{1,0:T(8,128)(2,1)S(1)} collective-permute-done((bf16[128,768]{1,0:T(8,128)(2,1)S(1)}, bf16[128,768]{1,0:T(8,128)(2,1)S(1)}, u32[]{:S(2)}, u32[]{:S(2)}) %collective-permute-start.8) | collective-permute-done | bytes 196640 | tf_op jit(solution)/shard_map/ppermute | solution.py:678
  312.5 21.6 %collective-permute-done.9.refs_5_ = bf16[128,768]{1,0:T(8,128)(2,1)S(1)} collective-permute-done((bf16[128,768]{1,0:T(8,128)(2,1)S(1)}, bf16[128,768]{1,0:T(8,128)(2,1)S(1)}, u32[]{:S(2)}, u32[]{:S(2)}) %collective-permute-start.9) | collective-permute-done | bytes 196640 | tf_op jit(solution)/shard_map/ppermute | solution.py:678
  334.2 0.6 copy-done.19
  334.9 6.1 combine.1
  341.0 100.4 %all-reduce.5.cloned.1.call-done = (bf16[768,2304]{0,1:T(8,128)(2,1)}, bf16[768,768]{1,0:T(8,128)(2,1)}) async-done(((bf16[768,2304]{0,1:T(8,128)(2,1)}, bf16[768,768]{1,0:T(8,128)(2,1)}), (bf16[768,2304]{0,1:T(8,128)(2,1)}, bf16[768,768]{1,0:T(8,128)(2,1)})) %all-reduce.5.cloned.1.call-update) | async-done | bytes 4718608 | tf_op jit(solution)/shard_map/psum | solution.py:725
  441.4 3.0 convert_element_type.6
  444.4 4.5 copy.44
  448.9 53.1 %all-gather.15.cloned.1.call-done = f32[1024,768]{1,0:T(8,128)} async-done(((f32[32,768]{1,0:T(8,128)}), f32[1024,768]{1,0:T(8,128)}) %all-gather.15.cloned.1.call-update) | async-done | bytes 3145744 | tf_op jit(solution)/shard_map/all_gather | solution.py:730
  502.0 2.0 reduce_sum.9
  504.1 0.6 slice_reduce_fusion
  504.7 0.6 slice_bitcast_fusion
  505.3 52.7 %reduce-scatter.5.cloned.1.call-done = bf16[384,768]{1,0:T(8,128)(2,1)} async-done(((bf16[3072,768]{1,0:T(8,128)(2,1)}), bf16[384,768]{1,0:T(8,128)(2,1)}) %reduce-scatter.5.cloned.1.call-update) | async-done | bytes 589840 | tf_op jit(solution)/shard_map/reduce_scatter | solution.py:723
  558.0 2.2 bitcast_convert_fusion
  560.2 55.1 %reduce-scatter.3.cloned.1.call-done = bf16[96,3072]{1,0:T(8,128)(2,1)} async-done(((bf16[768,3072]{1,0:T(8,128)(2,1)}), bf16[96,3072]{1,0:T(8,128)(2,1)}) %reduce-scatter.3.cloned.1.call-update) | async-done | bytes 589840 | tf_op jit(solution)/shard_map/reduce_scatter | solution.py:722
  615.3 2.2 bitcast_convert_fusion.1
  (88 shorter events, 2.1 us)
Async XLA Ops:
  7.2 128.7 %all-gather.7.cloned.1.call-start = ((), (), s32[]{:S(2)}) async-start(), calls=%async_computation.2 | async-start | bytes 5308416 | tf_op jit(solution)/shard_map/all_gather | solution.py:681
  7.9 128.0 %all-gather.9.cloned.1.call-start = ((), (), s32[]{:S(2)}) async-start(), calls=%async_computation.3 | async-start | bytes 5308416 | tf_op jit(solution)/shard_map/all_gather | solution.py:682
  8.7 156.5 %all-gather.11.cloned.1.call-start = ((), (), s32[]{:S(2)}) async-start(), calls=%async_computation.4 | async-start | bytes 5308416 | tf_op jit(solution)/shard_map/all_gather | solution.py:683
  9.4 164.0 %all-gather.13.cloned.1.call-start = ((), (), s32[]{:S(2)}) async-start(), calls=%async_computation.5 | async-start | bytes 5308416 | tf_op jit(solution)/shard_map/all_gather | solution.py:684
  10.0 431.4 %all-reduce.5.cloned.1.call-start = ((), (), s32[]{:S(2)}) async-start(), calls=%async_computation.9 | async-start | bytes 9437184 | tf_op jit(solution)/shard_map/psum | solution.py:725
  16.7 33.5 %copy-start = (s32[1,1024,2]{2,1,0:T(8,128)}, s32[1,1024,2]{2,1,0:T(8,128)S(1)}, u32[]{:S(2)}) copy-start(s32[1,1024,2]{2,1,0:T(8,128)S(1)} %copy.39) | copy-start | bytes 24580
  50.2 32.1 %copy-start.22 = (bf16[768,8]{0,1:T(8,128)(2,1)S(1)}, bf16[768,8]{0,1:T(8,128)(2,1)}, u32[]{:S(2)}) copy-start(bf16[768,8]{0,1:T(8,128)(2,1)} %param.24) | copy-start | bytes 36868
  56.0 14.7 %copy-start.24 = (bf16[2,128,896]{2,1,0:T(8,128)(2,1)S(1)}, bf16[2,128,896]{2,1,0:T(8,128)(2,1)}, u32[]{:S(2)}) copy-start(bf16[2,128,896]{2,1,0:T(8,128)(2,1)} %get-tuple-element.66) | copy-start | bytes 1376260
  64.9 15.6 %collective-permute-start = (bf16[2,128,768]{2,1,0:T(8,128)(2,1)}, bf16[2,128,768]{2,1,0:T(8,128)(2,1)S(1)}, u32[]{:S(2)}, u32[]{:S(2)}) collective-permute-start(bf16[2,128,768]{2,1,0:T(8,128)(2,1)} %get-tuple-element.60), channel_id=1, source_target_pairs={{0,8},{8,16},{16,24},{24,0},{1,9},{9,17},{17,25},{25,1},{2,10},{10... | collective-permute-start | bytes 1179656 | tf_op jit(solution)/shard_map/ppermute | solution.py:673
  68.1 67.7 %collective-permute-start.3 = (bf16[2,128,896]{2,1,0:T(8,128)(2,1)}, bf16[2,128,896]{2,1,0:T(8,128)(2,1)S(1)}, u32[]{:S(2)}, u32[]{:S(2)}) collective-permute-start(bf16[2,128,896]{2,1,0:T(8,128)(2,1)} %get-tuple-element.64), channel_id=1, source_target_pairs={{0,8},{8,16},{16,24},{24,0},{1,9},{9,17},{17,25},{25,1},{2,10},{10... | collective-permute-start | bytes 1376264 | tf_op jit(solution)/shard_map/ppermute | solution.py:673
  69.6 66.2 %collective-permute-start.4 = (bf16[2,128,896]{2,1,0:T(8,128)(2,1)}, bf16[2,128,896]{2,1,0:T(8,128)(2,1)S(1)}, u32[]{:S(2)}, u32[]{:S(2)}) collective-permute-start(bf16[2,128,896]{2,1,0:T(8,128)(2,1)} %get-tuple-element.65), channel_id=1, source_target_pairs={{0,16},{8,24},{16,0},{24,8},{1,17},{9,25},{17,1},{25,9},{2,18},{10... | collective-permute-start | bytes 1376264 | tf_op jit(solution)/shard_map/ppermute | solution.py:673
  70.7 65.2 %collective-permute-start.5 = (bf16[2,128,896]{2,1,0:T(8,128)(2,1)S(1)}, bf16[2,128,896]{2,1,0:T(8,128)(2,1)S(1)}, u32[]{:S(2)}, u32[]{:S(2)}) collective-permute-start(bf16[2,128,896]{2,1,0:T(8,128)(2,1)S(1)} %copy-done.24), channel_id=1, source_target_pairs={{0,24},{8,0},{16,8},{24,16},{1,25},{9,1},{17,9},{25,17},{2,26},{10... | collective-permute-start | bytes 1376264 | tf_op jit(solution)/shard_map/ppermute | solution.py:673
  73.5 62.2 %collective-permute-start.1 = (bf16[2,128,768]{2,1,0:T(8,128)(2,1)}, bf16[2,128,768]{2,1,0:T(8,128)(2,1)S(1)}, u32[]{:S(2)}, u32[]{:S(2)}) collective-permute-start(bf16[2,128,768]{2,1,0:T(8,128)(2,1)} %get-tuple-element.61), channel_id=1, source_target_pairs={{0,16},{8,24},{16,0},{24,8},{1,17},{9,25},{17,1},{25,9},{2,18},{10... | collective-permute-start | bytes 1179656 | tf_op jit(solution)/shard_map/ppermute | solution.py:673
  80.4 55.5 %copy-start.5 = (bf16[2,128,768]{2,1,0:T(8,128)(2,1)}, bf16[2,128,768]{2,1,0:T(8,128)(2,1)S(1)}, u32[]{:S(2)}) copy-start(bf16[2,128,768]{2,1,0:T(8,128)(2,1)S(1)} %collective-permute-done.refs_1_) | copy-start | bytes 1179652
  80.4 55.4 %collective-permute-start.2 = (bf16[2,128,768]{2,1,0:T(8,128)(2,1)}, bf16[2,128,768]{2,1,0:T(8,128)(2,1)S(1)}, u32[]{:S(2)}, u32[]{:S(2)}) collective-permute-start(bf16[2,128,768]{2,1,0:T(8,128)(2,1)} %get-tuple-element.62), channel_id=1, source_target_pairs={{0,24},{8,0},{16,8},{24,16},{1,25},{9,1},{17,9},{25,17},{2,26},{10... | collective-permute-start | bytes 1179656 | tf_op jit(solution)/shard_map/ppermute | solution.py:673
  135.8 0.7 copy-start.6
  135.8 0.9 copy-start.7
  135.8 1.0 copy-start.2
  135.8 1.1 copy-start.3
  135.8 1.3 copy-start.4
  154.6 45.1 %collective-permute-start.12 = (bf16[128,768]{1,0:T(8,128)(2,1)}, bf16[128,768]{1,0:T(8,128)(2,1)S(1)}, u32[]{:S(2)}, u32[]{:S(2)}) collective-permute-start(bf16[128,768]{1,0:T(8,128)(2,1)} %get-tuple-element.77), channel_id=1, source_target_pairs={{0,24},{8,0},{16,8},{24,16},{1,25},{9,1},{17,9},{25,17},{2,26},{10... | collective-permute-start | bytes 589832 | tf_op jit(solution)/shard_map/ppermute | solution.py:678
  164.5 36.3 %collective-permute-start.14 = (bf16[128,768]{1,0:T(8,128)(2,1)}, bf16[128,768]{1,0:T(8,128)(2,1)S(1)}, u32[]{:S(2)}, u32[]{:S(2)}) collective-permute-start(bf16[128,768]{1,0:T(8,128)(2,1)} %get-tuple-element.79), channel_id=1, source_target_pairs={{0,16},{8,24},{16,0},{24,8},{1,17},{9,25},{17,1},{25,9},{2,18},{10... | collective-permute-start | bytes 589832 | tf_op jit(solution)/shard_map/ppermute | solution.py:678
  164.8 36.0 %collective-permute-start.16 = (bf16[128,768]{1,0:T(8,128)(2,1)}, bf16[128,768]{1,0:T(8,128)(2,1)S(1)}, u32[]{:S(2)}, u32[]{:S(2)}) collective-permute-start(bf16[128,768]{1,0:T(8,128)(2,1)} %get-tuple-element.81), channel_id=1, source_target_pairs={{0,8},{8,16},{16,24},{24,0},{1,9},{9,17},{17,25},{25,1},{2,10},{10... | collective-permute-start | bytes 589832 | tf_op jit(solution)/shard_map/ppermute | solution.py:678
  196.3 9.1 %collective-permute-start.13 = (bf16[128,768]{1,0:T(8,128)(2,1)}, bf16[128,768]{1,0:T(8,128)(2,1)S(1)}, u32[]{:S(2)}, u32[]{:S(2)}) collective-permute-start(bf16[128,768]{1,0:T(8,128)(2,1)} %get-tuple-element.78), channel_id=1, source_target_pairs={{0,24},{8,0},{16,8},{24,16},{1,25},{9,1},{17,9},{25,17},{2,26},{10... | collective-permute-start | bytes 589832 | tf_op jit(solution)/shard_map/ppermute | solution.py:678
  199.7 17.5 %collective-permute-start.15 = (bf16[128,768]{1,0:T(8,128)(2,1)}, bf16[128,768]{1,0:T(8,128)(2,1)S(1)}, u32[]{:S(2)}, u32[]{:S(2)}) collective-permute-start(bf16[128,768]{1,0:T(8,128)(2,1)} %get-tuple-element.80), channel_id=1, source_target_pairs={{0,16},{8,24},{16,0},{24,8},{1,17},{9,25},{17,1},{25,9},{2,18},{10... | collective-permute-start | bytes 589832 | tf_op jit(solution)/shard_map/ppermute | solution.py:678
  199.7 17.5 %copy-start.10 = (bf16[128,768]{1,0:T(8,128)(2,1)}, bf16[128,768]{1,0:T(8,128)(2,1)S(1)}, u32[]{:S(2)}) copy-start(bf16[128,768]{1,0:T(8,128)(2,1)S(1)} %collective-permute-done.12.refs_2_) | copy-start | bytes 589828
  199.7 17.5 %collective-permute-start.17 = (bf16[128,768]{1,0:T(8,128)(2,1)}, bf16[128,768]{1,0:T(8,128)(2,1)S(1)}, u32[]{:S(2)}, u32[]{:S(2)}) collective-permute-start(bf16[128,768]{1,0:T(8,128)(2,1)} %get-tuple-element.82), channel_id=1, source_target_pairs={{0,8},{8,16},{16,24},{24,0},{1,9},{9,17},{17,25},{25,1},{2,10},{10... | collective-permute-start | bytes 589832 | tf_op jit(solution)/shard_map/ppermute | solution.py:678
  200.8 16.4 %copy-start.11 = (bf16[128,768]{1,0:T(8,128)(2,1)}, bf16[128,768]{1,0:T(8,128)(2,1)S(1)}, u32[]{:S(2)}) copy-start(bf16[128,768]{1,0:T(8,128)(2,1)S(1)} %collective-permute-done.14.refs_4_) | copy-start | bytes 589828
  200.8 16.4 %copy-start.12 = (bf16[128,768]{1,0:T(8,128)(2,1)}, bf16[128,768]{1,0:T(8,128)(2,1)S(1)}, u32[]{:S(2)}) copy-start(bf16[128,768]{1,0:T(8,128)(2,1)S(1)} %collective-permute-done.16.refs_6_) | copy-start | bytes 589828
  205.4 11.8 %copy-start.15 = (bf16[128,768]{1,0:T(8,128)(2,1)}, bf16[128,768]{1,0:T(8,128)(2,1)S(1)}, u32[]{:S(2)}) copy-start(bf16[128,768]{1,0:T(8,128)(2,1)S(1)} %collective-permute-done.13.refs_3_) | copy-start | bytes 589828
  217.2 0.7 copy-start.17
  217.2 0.7 copy-start.20
  269.1 1.0 copy-start.8
  269.1 1.1 copy-start.9
  269.1 232.9 %all-gather.15.cloned.1.call-start = ((), (), s32[]{:S(2)}) async-start(), calls=%async_computation.8 | async-start | bytes 3244032 | tf_op jit(solution)/shard_map/all_gather | solution.py:730
  270.4 9.9 %copy-start.23 = (f32[8,768]{1,0:T(8,128)S(1)}, f32[8,768]{1,0:T(8,128)}, u32[]{:S(2)}) copy-start(f32[8,768]{1,0:T(8,128)} %get-tuple-element.92) | copy-start | bytes 73732
  281.7 276.3 %reduce-scatter.5.cloned.1.call-start = ((), (), s32[]{:S(2)}) async-start(), calls=%async_computation.7 | async-start | bytes 5308416 | tf_op jit(solution)/shard_map/reduce_scatter | solution.py:723
  282.5 0.9 copy-start.27
  282.5 1.5 copy-start.26
  282.5 3.6 copy-start.25
  282.5 5.6 copy-start.30
  282.5 7.5 %copy-start.29 = (bf16[128,768]{1,0:T(8,128)(2,1)S(1)}, bf16[128,768]{1,0:T(8,128)(2,1)}, u32[]{:S(2)}) copy-start(bf16[128,768]{1,0:T(8,128)(2,1)} %get-tuple-element.72) | copy-start | bytes 589828
  282.5 12.9 %copy-start.28 = (bf16[128,768]{1,0:T(8,128)(2,1)S(1)}, bf16[128,768]{1,0:T(8,128)(2,1)}, u32[]{:S(2)}) copy-start(bf16[128,768]{1,0:T(8,128)(2,1)} %get-tuple-element.74) | copy-start | bytes 589828
  282.5 332.8 %reduce-scatter.3.cloned.1.call-start = ((), (), s32[]{:S(2)}) async-start(), calls=%async_computation.6 | async-start | bytes 5308416 | tf_op jit(solution)/shard_map/reduce_scatter | solution.py:722
  283.4 12.1 %collective-permute-start.6 = (bf16[128,768]{1,0:T(8,128)(2,1)S(1)}, bf16[128,768]{1,0:T(8,128)(2,1)S(1)}, u32[]{:S(2)}, u32[]{:S(2)}) collective-permute-start(bf16[128,768]{1,0:T(8,128)(2,1)S(1)} %copy-done.27), channel_id=1, source_target_pairs={{0,24},{8,0},{16,8},{24,16},{1,25},{9,1},{17,9},{25,17},{2,26},{10... | collective-permute-start | bytes 589832 | tf_op jit(solution)/shard_map/ppermute | solution.py:678
  283.9 28.5 %collective-permute-start.8 = (bf16[128,768]{1,0:T(8,128)(2,1)S(1)}, bf16[128,768]{1,0:T(8,128)(2,1)S(1)}, u32[]{:S(2)}, u32[]{:S(2)}) collective-permute-start(bf16[128,768]{1,0:T(8,128)(2,1)S(1)} %copy-done.26), channel_id=1, source_target_pairs={{0,16},{8,24},{16,0},{24,8},{1,17},{9,25},{17,1},{25,9},{2,18},{10... | collective-permute-start | bytes 589832 | tf_op jit(solution)/shard_map/ppermute | solution.py:678
  286.1 26.4 %collective-permute-start.10 = (bf16[128,768]{1,0:T(8,128)(2,1)S(1)}, bf16[128,768]{1,0:T(8,128)(2,1)S(1)}, u32[]{:S(2)}, u32[]{:S(2)}) collective-permute-start(bf16[128,768]{1,0:T(8,128)(2,1)S(1)} %copy-done.25), channel_id=1, source_target_pairs={{0,8},{8,16},{16,24},{24,0},{1,9},{9,17},{17,25},{25,1},{2,10},{10... | collective-permute-start | bytes 589832 | tf_op jit(solution)/shard_map/ppermute | solution.py:678
  288.1 24.4 %collective-permute-start.7 = (bf16[128,768]{1,0:T(8,128)(2,1)S(1)}, bf16[128,768]{1,0:T(8,128)(2,1)S(1)}, u32[]{:S(2)}, u32[]{:S(2)}) collective-permute-start(bf16[128,768]{1,0:T(8,128)(2,1)S(1)} %copy-done.30), channel_id=1, source_target_pairs={{0,24},{8,0},{16,8},{24,16},{1,25},{9,1},{17,9},{25,17},{2,26},{10... | collective-permute-start | bytes 589832 | tf_op jit(solution)/shard_map/ppermute | solution.py:678
  290.0 44.2 %collective-permute-start.9 = (bf16[128,768]{1,0:T(8,128)(2,1)S(1)}, bf16[128,768]{1,0:T(8,128)(2,1)S(1)}, u32[]{:S(2)}, u32[]{:S(2)}) collective-permute-start(bf16[128,768]{1,0:T(8,128)(2,1)S(1)} %copy-done.29), channel_id=1, source_target_pairs={{0,16},{8,24},{16,0},{24,8},{1,17},{9,25},{17,1},{25,9},{2,18},{10... | collective-permute-start | bytes 589832 | tf_op jit(solution)/shard_map/ppermute | solution.py:678
  295.4 38.7 %copy-start.13 = (bf16[128,768]{1,0:T(8,128)(2,1)}, bf16[128,768]{1,0:T(8,128)(2,1)S(1)}, u32[]{:S(2)}) copy-start(bf16[128,768]{1,0:T(8,128)(2,1)S(1)} %collective-permute-done.6.refs_2_) | copy-start | bytes 589828
  295.4 38.7 %collective-permute-start.11 = (bf16[128,768]{1,0:T(8,128)(2,1)S(1)}, bf16[128,768]{1,0:T(8,128)(2,1)S(1)}, u32[]{:S(2)}, u32[]{:S(2)}) collective-permute-start(bf16[128,768]{1,0:T(8,128)(2,1)S(1)} %copy-done.28), channel_id=1, source_target_pairs={{0,8},{8,16},{16,24},{24,0},{1,9},{9,17},{17,25},{25,1},{2,10},{10... | collective-permute-start | bytes 589832 | tf_op jit(solution)/shard_map/ppermute | solution.py:678
  312.5 21.7 %copy-start.14 = (bf16[128,768]{1,0:T(8,128)(2,1)}, bf16[128,768]{1,0:T(8,128)(2,1)S(1)}, u32[]{:S(2)}) copy-start(bf16[128,768]{1,0:T(8,128)(2,1)S(1)} %collective-permute-done.8.refs_4_) | copy-start | bytes 589828
  312.5 21.7 %copy-start.16 = (bf16[128,768]{1,0:T(8,128)(2,1)}, bf16[128,768]{1,0:T(8,128)(2,1)S(1)}, u32[]{:S(2)}) copy-start(bf16[128,768]{1,0:T(8,128)(2,1)S(1)} %collective-permute-done.10.refs_6_) | copy-start | bytes 589828
  312.5 21.7 %copy-start.18 = (bf16[128,768]{1,0:T(8,128)(2,1)}, bf16[128,768]{1,0:T(8,128)(2,1)S(1)}, u32[]{:S(2)}) copy-start(bf16[128,768]{1,0:T(8,128)(2,1)S(1)} %collective-permute-done.7.refs_3_) | copy-start | bytes 589828
  334.1 0.7 copy-start.19
  334.2 0.8 copy-start.21
  441.4 3.0 copy-start.1
Sparse Core Ops, SparseCore 0:
  9.9 41.5 all-gather.6
  53.3 38.7 all-gather.8
  94.0 38.7 all-gather.10
  134.6 38.7 all-gather.12
  269.2 172.1 all-reduce.4
  444.1 57.8 all-gather.14
  505.5 52.5 reduce-scatter.4
  561.5 53.7 reduce-scatter.2

commit v2 on v1

--- a/solution.py
+++ b/solution.py
@@ -14,6 +14,7 @@
 F32 = jnp.float32
 BF16 = jnp.bfloat16
 VMEM_LIMIT = 56 * 1024 * 1024
+BLOCKS = 32
 
 
 def params():
@@ -53,6 +54,14 @@
 
 def smem():
     return pl.BlockSpec(memory_space=pltpu.SMEM)
+
+
+def cost(micros):
+    return pl.CostEstimate(flops=int(micros * 1.1e9), transcendentals=0, bytes_accessed=int(micros * 3e6))
+
+
+def block_at(at_ref, chip, core, far):
+    return (at_ref[0] ^ (2 * chip + core)) * 4 + ((at_ref[1] + far) & 3)
 
 
 def qkv_kernel(tok_ref, gain_ref, bias_ref, w_ref, normed_ref, qkv_ref):
@@ -84,6 +93,7 @@
             jax.ShapeDtypeStruct((seq, cols), BF16),
         ],
         compiler_params=params(),
+        cost_estimate=cost(8.7),
         name="norm_qkv",
     )(tokens, gain, bias, weight)
 
@@ -162,6 +172,7 @@
             pltpu.VMEM((LANES, seq), F32),
         ],
         compiler_params=params(),
+        cost_estimate=cost(24),
         name="attend",
     )(length, qkv, qkv, qkv)
 
@@ -175,8 +186,10 @@
     o_ref,
     lse_ref,
     normed_ref,
+    at_ref,
     dqkv_ref,
-    grad_ref,
+    keep_ref,
+    send_ref,
     nt_ref,
     kt_ref,
     kh_ref,
@@ -188,6 +201,7 @@
     dv_ref,
     dqt_ref,
     pt_ref,
+    join_ref,
 ):
     seq = q_ref.shape[0]
     block = 256
@@ -226,14 +240,20 @@
     dqkv_ref[0] = dq
     dqkv_ref[1] = dk
     dqkv_ref[2] = dv
-    joined = dot_nn(nt_ref[...], jnp.concatenate([dq, dk, dv], axis=1)).astype(BF16)
-    for part in range(3):
-        grad_ref[part] = joined[:, part * LANES : (part + 1) * LANES]
-
-
-def attend_back_call(length, qkv, dmixed, mixed, lse, normed):
+    joined = dot_nn(nt_ref[...], jnp.concatenate([dq, dk, dv], axis=1))
+    join_ref[...] = joined.reshape(join_ref.shape)
+    for chip in range(4):
+        for far in range(4):
+            for core, ref in enumerate((keep_ref, send_ref)):
+                piece = join_ref[block_at(at_ref, chip, core, far)].astype(BF16)
+                for part in range(3):
+                    ref[chip, far, part] = piece[:, part * LANES : (part + 1) * LANES]
+
+
+def attend_back_call(length, qkv, dmixed, mixed, lse, normed, at):
     seq, width = normed.shape
     pairs = width // LANES
+    tall = width // BLOCKS
     col = lambda p: (0, p)
     return pl.pallas_call(
         attend_back_kernel,
@@ -247,15 +267,12 @@
             pl.BlockSpec((seq, LANES), col),
             pl.BlockSpec((1, 8, seq), lambda p: (p, 0, 0)),
             full((seq, width)),
-        ],
-        out_specs=[
-            pl.BlockSpec((3, seq, LANES), lambda p: (0, 0, p)),
-            pl.BlockSpec((3, width, LANES), lambda p: (0, 0, p)),
-        ],
-        out_shape=[
-            jax.ShapeDtypeStruct((3, seq, width), BF16),
-            jax.ShapeDtypeStruct((3, width, width), BF16),
-        ],
+            smem(),
+        ],
+        out_specs=[pl.BlockSpec((3, seq, LANES), lambda p: (0, 0, p))]
+        + [pl.BlockSpec((4, 4, 3, tall, LANES), lambda p: (0, 0, 0, 0, p))] * 2,
+        out_shape=[jax.ShapeDtypeStruct((3, seq, width), BF16)]
+        + [jax.ShapeDtypeStruct((4, 4, 3, tall, width), BF16)] * 2,
         scratch_shapes=[
             pltpu.VMEM((width, seq), BF16),
             pltpu.VMEM((LANES, seq), BF16),
@@ -268,10 +285,12 @@
             pltpu.VMEM((seq, LANES), F32),
             pltpu.VMEM((LANES, seq), F32),
             pltpu.VMEM((LANES, seq), F32),
-        ],
-        compiler_params=params(),
+            pltpu.VMEM((BLOCKS, tall, 3 * LANES), F32),
+        ],
+        compiler_params=params(),
+        cost_estimate=cost(32),
         name="attend_back",
-    )(length, qkv, qkv, qkv, dmixed, mixed, lse, normed)
+    )(length, qkv, qkv, qkv, dmixed, mixed, lse, normed, at)
 
 
 def route_kernel(
@@ -339,6 +358,7 @@
         + [jax.ShapeDtypeStruct((local, capacity, wide), BF16)] * group,
         grid=(1,),
         compiler_params=params(),
+        cost_estimate=cost(5.7),
         name="route",
     )(length, me, routes.T, routes, cotangent)
 
@@ -382,6 +402,7 @@
         + [jax.ShapeDtypeStruct((local, capacity, width), BF16)] * group,
         scratch_shapes=[pltpu.VMEM((seq, width), BF16)],
         compiler_params=params(),
+        cost_estimate=cost(8.8),
         name="project_dispatch",
     )(mixed, tokens, weight, gain, bias, slots)
 
@@ -504,6 +525,7 @@
             pltpu.VMEM((width, many), BF16),
         ],
         compiler_params=params(),
+        cost_estimate=cost(23 if trained else 17),
         name="experts_new" if trained else "experts_old",
     )(own, *rows, *grads, router, router_t, w_in, w_out)
 
@@ -539,13 +561,14 @@
         out_specs=rows,
         out_shape=jax.ShapeDtypeStruct((seq, width), F32),
         compiler_params=params(),
+        cost_estimate=cost(6.2),
         name="combine",
     )(slots, residual, *parts)
 
 
-def middle_kernel(count, slot_ref, res_ref, cot_ref, gain_ref, mixed_ref, w_ref, *refs):
+def middle_kernel(count, slot_ref, res_ref, cot_ref, gain_ref, mixed_ref, w_ref, at_ref, *refs):
     parts = refs[:count]
-    dres_ref, dmix_ref, proj_ref, sums_ref, acc_ref = refs[count:]
+    dres_ref, dmix_ref, keep_ref, send_ref, sums_ref, acc_ref = refs[count:]
     step = pl.program_id(0)
     dnormed = pick_rows(slot_ref, parts)
     xhat, scale = norm_parts(res_ref[...])
@@ -559,17 +582,21 @@
         sums_ref[...] = jnp.zeros_like(sums_ref)
         acc_ref[...] = jnp.zeros_like(acc_ref)
 
-    acc_ref[...] += dot_tn(mixed_ref[...], dattn)
+    acc_ref[...] += dot_tn(mixed_ref[...], dattn).reshape(acc_ref.shape)
     sums_ref[0:1, :] += jnp.sum(dnormed * xhat, axis=0, keepdims=True)
     sums_ref[1:2, :] += jnp.sum(dnormed, axis=0, keepdims=True)
 
     @pl.when(step == pl.num_programs(0) - 1)
     def _():
-        proj_ref[...] = acc_ref[...].astype(BF16)
-
-
-def middle_call(slots, residual, cotangent, gain, mixed, weight, parts):
+        for chip in range(4):
+            for far in range(4):
+                for core, ref in enumerate((keep_ref, send_ref)):
+                    ref[chip, far, 0] = acc_ref[block_at(at_ref, chip, core, far)].astype(BF16)
+
+
+def middle_call(slots, residual, cotangent, gain, mixed, weight, at, parts):
     seq, width = residual.shape
+    tall = width // BLOCKS
     block = 256
     capacity = parts[0].shape[0]
     rows = pl.BlockSpec((block, width), lambda i: (i, 0))
@@ -583,19 +610,22 @@
             full((1, width)),
             rows,
             full((width, width)),
+            smem(),
         ]
         + [full((capacity, width))] * len(parts),
-        out_specs=[rows, rows, full((width, width)), full((8, width))],
+        out_specs=[rows, rows] + [full((4, 4, 1, tall, width))] * 2 + [full((8, width))],
         out_shape=[
             jax.ShapeDtypeStruct((seq, width), F32),
             jax.ShapeDtypeStruct((seq, width), BF16),
-            jax.ShapeDtypeStruct((width, width), BF16),
+            jax.ShapeDtypeStruct((4, 4, 1, tall, width), BF16),
+            jax.ShapeDtypeStruct((4, 4, 1, tall, width), BF16),
             jax.ShapeDtypeStruct((8, width), F32),
         ],
-        scratch_shapes=[pltpu.VMEM((width, width), F32)],
-        compiler_params=params(),
+        scratch_shapes=[pltpu.VMEM((BLOCKS, tall, width), F32)],
+        compiler_params=params(),
+        cost_estimate=cost(13),
         name="middle_back",
-    )(slots, residual, cotangent, gain, mixed, weight, *parts)
+    )(slots, residual, cotangent, gain, mixed, weight, at, *parts)
 
 
 def last_kernel(dqkv_ref, tok_ref, dres_ref, gain_ref, w_ref, out_ref, sums_ref):
@@ -634,8 +664,100 @@
             jax.ShapeDtypeStruct((8, width), F32),
         ],
         compiler_params=params(),
+        cost_estimate=cost(9.8),
         name="last_back",
     )(dqkv, tokens, dres, gain, weight)
+
+
+def unpack_kernel(at_ref, *refs):
+    pieces = refs[:8]
+    qkv_ref, proj_ref = refs[8:]
+    tall = pieces[0].shape[2]
+    part = pl.program_id(0)
+
+    def put(out_ref):
+        for index, piece in enumerate(pieces):
+            for far in range(4):
+                place = (at_ref[0] ^ index) * 4 + ((at_ref[1] - far) & 3)
+                rows = pl.ds(pl.multiple_of(place * tall, 8), tall)
+                out_ref[rows, :] = piece[far, 0].astype(F32)
+
+    @pl.when(part < 3)
+    def _():
+        put(qkv_ref)
+
+    @pl.when(part == 3)
+    def _():
+        put(proj_ref)
+
+
+def unpack_call(at, pieces):
+    _, _, tall, width = pieces[0].shape
+    return pl.pallas_call(
+        unpack_kernel,
+        grid=(4,),
+        in_specs=[smem()] + [pl.BlockSpec((4, 1, tall, width), lambda p: (0, p, 0, 0))] * 8,
+        out_specs=[
+            pl.BlockSpec((width, width), lambda p: (0, jnp.minimum(p, 2))),
+            full((width, width)),
+        ],
+        out_shape=[
+            jax.ShapeDtypeStruct((width, 3 * width), F32),
+            jax.ShapeDtypeStruct((width, width), F32),
+        ],
+        compiler_params=params(),
+        cost_estimate=cost(6),
+        name="unpack",
+    )(at, *pieces)
+
+
+def swap(block, bits):
+    size = lax.axis_size("batch")
+    return lax.ppermute(block, "batch", [(i, i ^ bits) for i in range(size)])
+
+
+def turn(block, shift):
+    size = lax.axis_size("expert")
+    return lax.ppermute(block, "expert", [(i, (i + shift) % size) for i in range(size)])
+
+
+def added(*blocks):
+    total = blocks[0].astype(F32)
+    for block in blocks[1:]:
+        total = total + block.astype(F32)
+    return total
+
+
+def sum_dense(fast, keep, send):
+    if not fast:
+        keep, send = lax.psum((keep, send), ("expert", "batch"))
+        pieces = []
+        for chip in range(4):
+            for half in (keep, send):
+                parts = jnp.concatenate([part[chip] for part in half], axis=1)
+                pieces.append(jnp.stack([parts[-far % 4] for far in range(4)]))
+        return pieces
+    got = [swap(part, 1) for part in send]
+    halves = []
+    for chip in range(4):
+        parts = [added(mine[chip], other[chip]) for mine, other in zip(keep, got)]
+        halves.append(jnp.concatenate(parts, axis=1).astype(BF16))
+    quarter = added(halves[0], *[swap(halves[chip], 2 * chip) for chip in (1, 2, 3)]).astype(BF16)
+    own = added(quarter[0], *[turn(quarter[far], far) for far in (1, 2, 3)]).astype(BF16)
+    column = jnp.stack([own] + [turn(own, far) for far in (1, 2, 3)])
+    chips = [column] + [swap(column, 2 * chip) for chip in (1, 2, 3)]
+    pieces = []
+    for block in chips:
+        pieces += [block, swap(block, 1)]
+    return pieces
+
+
+def sum_small(fast, rows):
+    if not fast:
+        return jnp.sum(lax.all_gather(rows, ("expert", "batch"), axis=0), axis=0)
+    rows = rows + swap(rows, 1)
+    rows = added(rows, *[swap(rows, 2 * chip) for chip in (1, 2, 3)])
+    return added(rows, *[turn(rows, far) for far in (1, 2, 3)])
 
 
 def body(
@@ -677,6 +799,8 @@
             return block
         return lax.ppermute(block, "expert", [(i, (i - shift) % group) for i in range(group)])
 
+    fast = group == 4 and lax.axis_size("batch") == 8
+    at = jnp.stack([lax.axis_index("batch"), me]).astype(jnp.int32) if fast else jnp.zeros((2,), jnp.int32)
     me_one = jnp.full((1,), me, jnp.int32)
     full_old_in = lax.all_gather(old_in, "batch", axis=1, tiled=True)
     full_old_out = lax.all_gather(old_out, "batch", axis=1, tiled=True)
@@ -716,28 +840,27 @@
             if trained:
                 new_in_local, new_out_local = got[2 * group + 1 :]
     returned = [come(backs[p][shift], shift) for shift in range(group) for p in range(local)]
-    dres, dmixed, proj_grad, sums2 = middle_call(
-        slots_t, residual, cot_rows, gain2, mixed, w_proj, returned
+    dres, dmixed, proj_keep, proj_send, sums2 = middle_call(
+        slots_t, residual, cot_rows, gain2, mixed, w_proj, at, returned
     )
     new_in_grad = lax.psum_scatter(new_in_local, "batch", scatter_dimension=0, tiled=True)
     new_out_grad = lax.psum_scatter(new_out_local, "batch", scatter_dimension=0, tiled=True)
-    dqkv, qkv_grad = attend_back_call(lengths, qkv, dmixed, mixed, lse, normed1)
-    big = lax.psum((qkv_grad, proj_grad), ("expert", "batch"))
+    dqkv, qkv_keep, qkv_send = attend_back_call(lengths, qkv, dmixed, mixed, lse, normed1, at)
+    pieces = sum_dense(fast, (qkv_keep, proj_keep), (qkv_send, proj_send))
+    qkv_grad, proj_grad = unpack_call(at, pieces)
     input_grad, sums1 = last_call(dqkv, token_rows, dres, gain1, w_qkv)
     back_outs = [come(outs[p][shift], shift) for shift in range(group) for p in range(local)]
     output = combine_call(slots_t, residual, back_outs)
-    small = jnp.concatenate([router_sum.T[: 2 * 8], sums1, sums2], axis=0)
-    small = jnp.sum(lax.all_gather(small, ("expert", "batch"), axis=0), axis=0)
-    qkv_out = jnp.transpose(big[0].astype(F32), (1, 0, 2)).reshape(width, 3 * width)
+    small = sum_small(fast, jnp.concatenate([router_sum.T[:experts], sums1, sums2], axis=0))
     return (
         output[None],
         input_grad[None],
-        small[16],
-        small[17],
-        small[24],
-        small[25],
-        qkv_out,
-        big[1].astype(F32),
+        small[experts],
+        small[experts + 1],
+        small[experts + 8],
+        small[experts + 9],
+        qkv_grad,
+        proj_grad,
         small[:experts].T,
         new_in_grad.astype(F32)[None],
         new_out_grad.astype(F32)[None],

time: 625 us -> 439 us (0.70)
  waiting for transfers between devices: 392 us -> 199 us
  starting transfers between devices: 33.8 us -> 47.9 us
  local copies, waits for them, and re-layouts: 24.1 us -> 10.3 us
  Pallas kernels: 149 us -> 157 us
    psum x1 -> x0, waiting for transfers between devices: 100 us -> none  [body(): big = lax.psum((qkv_grad, proj_grad), ('expert', 'batch'))]
    ppermute x0 -> x25, waiting for transfers between devices: none -> 79.8 us  [the longest x16 62.7 us: swap(): return lax.ppermute(block, 'batch', [(i, i ^ bits) for i in range(size)])]
    reduce_scatter x1, waiting for transfers between devices: 55.1 us -> 0.01 us  [body(): lax.psum_scatter(new_in_local, 'batch', scatter_dimension=0, tiled=True)]
    all_gather x1 -> x0, waiting for transfers between devices: 53.1 us -> none  [body(): small = jnp.sum(lax.all_gather(small, ('expert', 'batch'), axis=0), axis=0)]
    reduce_scatter x1, waiting for transfers between devices: 52.7 us -> 0.02 us  [body(): lax.psum_scatter(new_out_local, 'batch', scatter_dimension=0, tiled=True)]
    ppermute x0 -> x25, starting transfers between devices: none -> 19.8 us  [the longest x16 12.5 us: swap(): return lax.ppermute(block, 'batch', [(i, i ^ bits) for i in range(size)])]
    ppermute x12, waiting for transfers between devices: 59.5 us -> 40.5 us  [come(): lax.ppermute(block, 'expert', [(i, (i - shift) % group) for i in range(gr...]
    all_gather x1, waiting for transfers between devices: 0.02 us -> 17.1 us  [body(): full_old_out = lax.all_gather(old_out, 'batch', axis=1, tiled=True)]
  transfers between devices with their start and end apart: 26 -> 49, of which waited for: 12 -> 18; matrix products, arithmetic and copies ran while one was open for 4% -> 3% of each run, Pallas kernels for 17% -> 36%
where the time goes in v2:
time: 439 us; the launch traced here: 438 us
  waiting for transfers between devices  199 us (45%)
  Pallas kernels  157 us (36%)
  starting transfers between devices  47.9 us (11%)
  between operations  15.4 us (4%)
  local copies, waits for them, and re-layouts  10.3 us (2%)
  other arithmetic  9.15 us (2%)
    ppermute x16, waiting for transfers between devices, swap(): return lax.ppermute(block, 'batch', [(i, i ^ bits) for i in range(size)])  62.7 us
    ppermute x6, waiting for transfers between devices, go(): lax.ppermute(block, 'expert', [(i, (i + shift) % group) for i in range(gr...  58.6 us
    ppermute x12, waiting for transfers between devices, come(): lax.ppermute(block, 'expert', [(i, (i - shift) % group) for i in range(gr...  40.5 us
    pallas_call x2, Pallas kernels, expert_call(): pl.pallas_call(functools.partial(expert_kernel, trained, group), grid=(in...  40.3 us
    pallas_call x1, Pallas kernels, attend_back_call(): pl.pallas_call(attend_back_kernel, grid=(pairs,), in_specs=[smem(), pl.Bl...  32.3 us
    pallas_call x1, Pallas kernels, attend_call(): pl.pallas_call(attend_kernel, grid=(pairs,), in_specs=[smem(), pl.BlockSp...  24.1 us
    ppermute x12, starting transfers between devices, come(): lax.ppermute(block, 'expert', [(i, (i - shift) % group) for i in range(gr...  17.3 us
    ppermute x9, waiting for transfers between devices, turn(): lax.ppermute(block, 'expert', [(i, (i + shift) % size) for i in range(siz...  17.2 us
  transfers between devices with their start and end apart: 49, of which 18 were waited for; matrix products, arithmetic and copies ran while one was open for 3% of the time, Pallas kernels for 36%

profile of v2, /device:TPU:0, one launch (start us, length us, event | category | flops | bytes accessed | tf_op | source)
XLA Modules:
  0.0 438.2 jit_solution(1782309757153131631)
XLA Ops:
  7.3 0.7 all-gather.9.cloned.1.call-update
  8.0 0.7 all-gather.11.cloned.1.call-update
  8.8 0.7 all-gather.5.cloned.1.call-update
  13.3 0.8 copy.27.route_ref
  14.1 5.8 %route.1 = (s32[8,1024]{1,0:T(8,128)}, s32[1024,128]{1,0:T(8,128)}, bf16[2,128,896]{2,1,0:T(8,128)(2,1)}, bf16[2,128,896]{2,1,0:T(8,128)(2,1)}, bf16[2,128,896]{...) custom-call(s32[1]{0:T(128)S(6)} %copy.39.len_ref, s32[1]{0:T(128)} %bitcast.me_ref.own_ref, s32[2,1024]{1,0:T(2,128)} %copy.27.route_ref, ...), custom_call_target="tpu_custom_call" | custom-call | flops 6270000128 | bytes 17100000 | tf_op jit(solution)/shard_map/route/pallas_call | solution.py:350
  19.9 8.7 %norm_qkv.1 = (bf16[1024,768]{1,0:T(8,128)(2,1)}, bf16[1024,2304]{1,0:T(8,128)(2,1)}) custom-call(bf16[1024,768]{1,0:T(8,128)(2,1)} %bitcast.70, f32[1,768]{1,0:T(1,128)} %broadcast_in_dim.38.gain_ref, f32[1,768]{1,0:T(1,128)} %broadcast_in_dim.39.bias_ref, bf16[768,2304]{1,0:T(8,128)(2,1)} %w_ref.7), custom_call_target="tpu_custom_call" | custom-call | flops 9569999872 | bytes 26100000 | tf_op jit(solution)/shard_map/norm_qkv/pallas_call | solution.py:78
  28.6 24.1 %attend.1 = (bf16[1024,768]{1,0:T(8,128)(2,1)}, f32[6,8,1024]{2,1,0:T(8,128)}) custom-call(s32[1]{0:T(128)S(6)} %copy.39.len_ref, bf16[1024,2304]{1,0:T(8,128)(2,1)} %get-tuple-element.59.q_ref.k_ref.v_ref, bf16[1024,2304]{1,0:T(8,128)(2,1)} %get-tuple-element.59.q_ref.k_ref.v_ref, bf16[1024,2304]{1,0:T(8,128)(2,1)} %get-tuple-element.59.q_ref.k_ref.v_ref), custom_call_target="tpu_custom_call" | custom-call | flops 26400000000 | bytes 72000000 | tf_op jit(solution)/shard_map/attend/pallas_call | solution.py:151
  52.8 8.8 %project_dispatch.1 = (f32[1024,768]{1,0:T(8,128)}, bf16[2,128,768]{2,1,0:T(8,128)(2,1)}, bf16[2,128,768]{2,1,0:T(8,128)(2,1)}, bf16[2,128,768]{2,1,0:T(8,128)(2,1)}, bf16[2,128,768]{2,1,0:T(8,128)(2,1)}) custom-call(bf16[1024,768]{1,0:T(8,128)(2,1)} %get-tuple-element.60.mixed_ref.o_ref, bf16[1024,768]{1,0:T(8,128)(2,1)} %bitcast.71, ...), custom_call_target="tpu_custom_call" | custom-call | flops 9680000000 | bytes 26400000 | tf_op jit(solution)/shard_map/project_dispatch/pallas_call | solution.py:396
  61.6 2.9 collective-permute-start
  64.4 1.6 collective-permute-start.3
  66.0 1.1 collective-permute-start.4
  67.1 2.9 collective-permute-start.5
  70.3 6.5 %collective-permute-done.refs_1_ = bf16[2,128,768]{2,1,0:T(8,128)(2,1)S(1)} collective-permute-done((bf16[2,128,768]{2,1,0:T(8,128)(2,1)}, bf16[2,128,768]{2,1,0:T(8,128)(2,1)S(1)}, u32[]{:S(2)}, u32[]{:S(2)}) %collective-permute-start) | collective-permute-done | bytes 393248 | tf_op jit(solution)/shard_map/ppermute | solution.py:795
  76.8 1.8 collective-permute-start.2
  78.8 0.7 pad.9.refs_9_
  79.5 0.7 pad.8.refs_8_
  80.2 52.0 %collective-permute-done.1.refs_2_ = bf16[2,128,768]{2,1,0:T(8,128)(2,1)} collective-permute-done((bf16[2,128,768]{2,1,0:T(8,128)(2,1)}, bf16[2,128,768]{2,1,0:T(8,128)(2,1)}, u32[]{:S(2)}, u32[]{:S(2)}) %collective-permute-start.1) | collective-permute-done | bytes 393248 | tf_op jit(solution)/shard_map/ppermute | solution.py:795
  133.3 22.9 %experts_new.1 = (bf16[128,768]{1,0:T(8,128)(2,1)}, bf16[128,768]{1,0:T(8,128)(2,1)}, bf16[128,768]{1,0:T(8,128)(2,1)}, bf16[128,768]{1,0:T(8,128)(2,1)}, bf16[1...) custom-call(s32[1]{0:T(128)} %bitcast.6.own_ref, ...), custom_call_target="tpu_custom_call" | custom-call | flops 25300000768 | bytes 69000000 | tf_op jit(solution)/shard_map/experts_new/pallas_call | solution.py:505
  156.3 17.1 %all-gather.7.cloned.1.call-done.refs_11_ = bf16[1,3072,768]{2,1,0:T(8,128)(2,1)} async-done(((bf16[1,384,768]{2,1,0:T(8,128)(2,1)}), bf16[1,3072,768]{2,1,0:T(8,128)(2,1)}) %all-gather.7.cloned.1.call-update) | async-done | bytes 4718608 | tf_op jit(solution)/shard_map/all_gather | solution.py:806
  173.4 17.4 %experts_old.1 = (bf16[128,768]{1,0:T(8,128)(2,1)}, bf16[128,768]{1,0:T(8,128)(2,1)}, bf16[128,768]{1,0:T(8,128)(2,1)}, bf16[128,768]{1,0:T(8,128)(2,1)}, bf16[1...) custom-call(s32[1]{0:T(128)} %bitcast.me_ref.own_ref, ...), custom_call_target="tpu_custom_call" | custom-call | flops 18699999232 | bytes 51000000 | tf_op jit(solution)/shard_map/experts_old/pallas_call | solution.py:505
  190.9 3.4 collective-permute-start.12
  194.2 1.1 collective-permute-start.16
  195.3 2.7 collective-permute-start.13
  198.0 1.1 collective-permute-start.15
  199.2 0.7 collective-permute-done.12.refs_2_
  199.9 1.0 collective-permute-start.17
  201.5 11.4 %collective-permute-done.14.refs_4_ = bf16[128,768]{1,0:T(8,128)(2,1)S(1)} collective-permute-done((bf16[128,768]{1,0:T(8,128)(2,1)}, bf16[128,768]{1,0:T(8,128)(2,1)S(1)}, u32[]{:S(2)}, u32[]{:S(2)}) %collective-permute-start.14) | collective-permute-done | bytes 196640 | tf_op jit(solution)/shard_map/ppermute | solution.py:800
  212.9 15.6 %collective-permute-done.15.refs_5_ = bf16[128,768]{1,0:T(8,128)(2,1)S(1)} collective-permute-done((bf16[128,768]{1,0:T(8,128)(2,1)S(1)}, bf16[128,768]{1,0:T(8,128)(2,1)S(1)}, u32[]{:S(2)}, u32[]{:S(2)}) %collective-permute-start.15) | collective-permute-done | bytes 196640 | tf_op jit(solution)/shard_map/ppermute | solution.py:800
  229.3 13.4 %middle_back.1 = (f32[1024,768]{1,0:T(8,128)}, bf16[1024,768]{1,0:T(8,128)(2,1)}, bf16[4,4,1,24,768]{4,3,2,1,0:T(8,128)(2,1)}, bf16[4,4,1,24,768]{4,3,2,1,0:T(8,128)(2,1)}, f32[8,768]{1,0:T(8,128)}) custom-call(s32[1024,128]{1,0:T(8,128)} %get-tuple-element.58.slot_ref, f32[1024,768]{1,0:T(8,128)} %get-tuple-element.62.res_ref, bf16[1024,768]{1,0:T(8,128)(2,1)} %bitcast.69, ...), custom_call_target="tpu_custom_call" | custom-call | flops 14300000256 | bytes 39000000 | tf_op jit(solution)/shard_map/middle_back/pallas_call | solution.py:603
  242.7 32.3 %attend_back.1 = (bf16[3,1024,768]{2,1,0:T(8,128)(2,1)}, bf16[4,4,3,24,768]{4,3,2,1,0:T(8,128)(2,1)}, bf16[4,4,3,24,768]{4,3,2,1,0:T(8,128)(2,1)}) custom-call(s32[1]{0:T(128)S(6)} %copy.39.len_ref, bf16[1024,2304]{1,0:T(8,128)(2,1)} %get-tuple-element.59.q_ref.k_ref.v_ref, bf16[1024,2304]{1,0:T(8,128)(2,1)} %get-tuple-element.59.q_ref.k_ref.v_ref, ...), custom_call_target="tpu_custom_call" | custom-call | flops 35200000000 | bytes 96000000 | tf_op jit(solution)/shard_map/attend_back/pallas_call | solution.py:258
  275.6 4.2 collective-permute-done.26
  280.5 1.5 collective-permute-start.27
  282.7 1.6 collective-permute-start.29
  284.5 2.5 collective-permute-start.8
  287.3 9.5 %collective-permute-done.27 = bf16[4,4,24,768]{3,2,1,0:T(8,128)(2,1)} collective-permute-done((bf16[4,4,24,768]{3,2,1,0:T(8,128)(2,1)S(1)}, bf16[4,4,24,768]{3,2,1,0:T(8,128)(2,1)}, u32[]{:S(2)}, u32[]{:S(2)}) %collective-permute-start.27) | collective-permute-done | bytes 589856 | tf_op jit(solution)/shard_map/ppermute | solution.py:716
  296.9 7.0 %collective-permute-done.28 = bf16[4,4,24,768]{3,2,1,0:T(8,128)(2,1)} collective-permute-done((bf16[4,4,24,768]{3,2,1,0:T(8,128)(2,1)S(1)}, bf16[4,4,24,768]{3,2,1,0:T(8,128)(2,1)}, u32[]{:S(2)}, u32[]{:S(2)}) %collective-permute-start.28) | collective-permute-done | bytes 589856 | tf_op jit(solution)/shard_map/ppermute | solution.py:716
  303.9 15.0 %collective-permute-done.29 = bf16[4,4,24,768]{3,2,1,0:T(8,128)(2,1)} collective-permute-done((bf16[4,4,24,768]{3,2,1,0:T(8,128)(2,1)S(1)}, bf16[4,4,24,768]{3,2,1,0:T(8,128)(2,1)}, u32[]{:S(2)}, u32[]{:S(2)}) %collective-permute-start.29) | collective-permute-done | bytes 589856 | tf_op jit(solution)/shard_map/ppermute | solution.py:716
  319.0 1.7 add_convert_fusion
  320.9 3.7 collective-permute-start.32
  324.6 1.2 collective-permute-start.31
  325.8 3.3 collective-permute-done.30
  329.2 7.1 %collective-permute-done.31 = bf16[4,24,768]{2,1,0:T(8,128)(2,1)S(1)} collective-permute-done((bf16[4,24,768]{2,1,0:T(8,128)(2,1)S(1)}, bf16[4,24,768]{2,1,0:T(8,128)(2,1)S(1)}, u32[]{:S(2)}, u32[]{:S(2)}) %collective-permute-start.31) | collective-permute-done | bytes 147488 | tf_op jit(solution)/shard_map/ppermute | solution.py:721
  336.3 1.3 collective-permute-start.35
  337.6 0.8 collective-permute-start.33
  338.4 9.9 %last_back.1 = (f32[1024,768]{1,0:T(8,128)}, f32[8,768]{1,0:T(8,128)}) custom-call(bf16[3,1024,768]{2,1,0:T(8,128)(2,1)} %get-tuple-element.90.dqkv_ref, bf16[1024,768]{1,0:T(8,128)(2,1)} %bitcast.72, f32[1024,768]{1,0:T(8,128)} %get-tuple-element.91.dres_ref, f32[1,768]{1,0:T(1,128)} %broadcast_in_dim.38.gain_ref, bf16[768,2304]{1,0:T(8,128)(2,1)} %w_ref.7), custom_call_target="tpu_custom_call" | custom-call | flops 10780000256 | bytes 29400000 | tf_op jit(solution)/shard_map/last_back/pallas_call | solution.py:651
  348.4 0.7 pad_maximum_fusion.4
  349.1 2.8 collective-permute-start.10
  351.9 1.1 collective-permute-start.7
  353.1 3.3 collective-permute-start.41
  357.1 0.7 fusion.11
  357.9 2.9 collective-permute-start.21
  360.9 24.0 %collective-permute-done.21 = f32[24,768]{1,0:T(8,128)S(1)} collective-permute-done((f32[24,768]{1,0:T(8,128)S(1)}, f32[24,768]{1,0:T(8,128)S(1)}, u32[]{:S(2)}, u32[]{:S(2)}) %collective-permute-start.21) | collective-permute-done | bytes 73760 | tf_op jit(solution)/shard_map/ppermute | solution.py:716
  385.1 1.1 collective-permute-done.20
  386.2 1.1 collective-permute-start.9
  387.4 1.8 collective-permute-done.19
  389.6 12.7 %collective-permute-done.9.refs_5_ = bf16[128,768]{1,0:T(8,128)(2,1)S(1)} collective-permute-done((bf16[128,768]{1,0:T(8,128)(2,1)S(1)}, bf16[128,768]{1,0:T(8,128)(2,1)S(1)}, u32[]{:S(2)}, u32[]{:S(2)}) %collective-permute-start.9) | collective-permute-done | bytes 196640 | tf_op jit(solution)/shard_map/ppermute | solution.py:800
  402.4 5.2 %collective-permute-done.24 = f32[24,768]{1,0:T(8,128)S(1)} collective-permute-done((f32[24,768]{1,0:T(8,128)S(1)}, f32[24,768]{1,0:T(8,128)S(1)}, u32[]{:S(2)}, u32[]{:S(2)}) %collective-permute-start.24) | collective-permute-done | bytes 73760 | tf_op jit(solution)/shard_map/ppermute | solution.py:721
  407.7 1.5 collective-permute-done.23
  410.2 6.2 %combine.1 = f32[1024,768]{1,0:T(8,128)} custom-call(s32[1024,128]{1,0:T(8,128)} %get-tuple-element.58.slot_ref, f32[1024,768]{1,0:T(8,128)} %get-tuple-element.62.res_ref, bf16[128,768]{1,0:T(8,128)(2,1)} %get-tuple-element.71.refs_0_, bf16[128,768]{1,0:T(8,128)(2,1)} %get-tuple-element.72.refs_1_, bf16[128,768]{1,0:T(8,128)(2,1)} %collective-permute-done.6.refs_2_, ...), custom_call_target="tpu_custom_call" | custom-call | flops 6819999744 | bytes 18600000 | tf_op jit(solution)/shard_map/combine/pallas_call | solution.py:556
  417.7 0.8 copy-done.16
  418.9 0.8 copy-done.19
  419.7 7.2 %unpack.1 = (f32[768,2304]{1,0:T(8,128)}, f32[768,768]{1,0:T(8,128)}) custom-call(s32[2]{0:T(128)} %pad_add_fusion.at_ref, bf16[4,4,24,768]{3,2,1,0:T(8,128)(2,1)} %copy-done.3, bf16[4,4,24,768]{3,2,1,0:T(8,128)(2,1)} %copy-done.16, bf16[4,4,24,768]{3,2,1,0:T(8,128)(2,1)} %copy-done.15, bf16[4,4,24,768]{3,2,1,0:T(8,128)(2,1)} %copy-done.19, ...), custom_call_target="tpu_custom_call" | custom-call | flops 6600000000 | bytes 18000000 | tf_op jit(solution)/shard_map/unpack/pallas_call | solution.py:696
  427.0 2.2 bitcast_convert_fusion
  429.2 2.2 bitcast_convert_fusion.1
  (172 shorter events, 13.5 us)
Async XLA Ops:
  7.2 125.1 %all-gather.9.cloned.1.call-start = ((), (), s32[]{:S(2)}) async-start(), calls=%async_computation.4 | async-start | bytes 5308416 | tf_op jit(solution)/shard_map/all_gather | solution.py:807
  8.0 124.4 %all-gather.11.cloned.1.call-start = ((), (), s32[]{:S(2)}) async-start(), calls=%async_computation.5 | async-start | bytes 5308416 | tf_op jit(solution)/shard_map/all_gather | solution.py:808
  8.7 147.6 %all-gather.5.cloned.1.call-start = ((), (), s32[]{:S(2)}) async-start(), calls=%async_computation.2 | async-start | bytes 5308416 | tf_op jit(solution)/shard_map/all_gather | solution.py:805
  9.4 164.0 %all-gather.7.cloned.1.call-start = ((), (), s32[]{:S(2)}) async-start(), calls=%async_computation.3 | async-start | bytes 5308416 | tf_op jit(solution)/shard_map/all_gather | solution.py:806
  10.0 417.0 %reduce-scatter.5.cloned.1.call-start = ((), (), s32[]{:S(2)}) async-start(), calls=%async_computation.7 | async-start | bytes 5308416 | tf_op jit(solution)/shard_map/reduce_scatter | solution.py:847
  52.8 25.9 %copy-start.7 = (bf16[768,8]{0,1:T(8,128)(2,1)S(1)}, bf16[768,8]{0,1:T(8,128)(2,1)}, u32[]{:S(2)}) copy-start(bf16[768,8]{0,1:T(8,128)(2,1)} %param.24) | copy-start | bytes 36868
  61.6 15.3 %collective-permute-start = (bf16[2,128,768]{2,1,0:T(8,128)(2,1)}, bf16[2,128,768]{2,1,0:T(8,128)(2,1)S(1)}, u32[]{:S(2)}, u32[]{:S(2)}) collective-permute-start(bf16[2,128,768]{2,1,0:T(8,128)(2,1)} %get-tuple-element.64), channel_id=1, source_target_pairs={{0,8},{8,16},{16,24},{24,0},{1,9},{9,17},{17,25},{25,1},{2,10},{10... | collective-permute-start | bytes 1179656 | tf_op jit(solution)/shard_map/ppermute | solution.py:795
  64.4 67.8 %collective-permute-start.3 = (bf16[2,128,896]{2,1,0:T(8,128)(2,1)S(1)}, bf16[2,128,896]{2,1,0:T(8,128)(2,1)S(1)}, u32[]{:S(2)}, u32[]{:S(2)}) collective-permute-start(bf16[2,128,896]{2,1,0:T(8,128)(2,1)S(1)} %copy-done.26), channel_id=1, source_target_pairs={{0,8},{8,16},{16,24},{24,0},{1,9},{9,17},{17,25},{25,1},{2,10},{10... | collective-permute-start | bytes 1376264 | tf_op jit(solution)/shard_map/ppermute | solution.py:795
  66.0 66.3 %collective-permute-start.4 = (bf16[2,128,896]{2,1,0:T(8,128)(2,1)S(1)}, bf16[2,128,896]{2,1,0:T(8,128)(2,1)S(1)}, u32[]{:S(2)}, u32[]{:S(2)}) collective-permute-start(bf16[2,128,896]{2,1,0:T(8,128)(2,1)S(1)} %copy-done.25), channel_id=1, source_target_pairs={{0,16},{8,24},{16,0},{24,8},{1,17},{9,25},{17,1},{25,9},{2,18},{10... | collective-permute-start | bytes 1376264 | tf_op jit(solution)/shard_map/ppermute | solution.py:795
  67.1 65.2 %collective-permute-start.5 = (bf16[2,128,896]{2,1,0:T(8,128)(2,1)S(1)}, bf16[2,128,896]{2,1,0:T(8,128)(2,1)S(1)}, u32[]{:S(2)}, u32[]{:S(2)}) collective-permute-start(bf16[2,128,896]{2,1,0:T(8,128)(2,1)S(1)} %copy-done.24), channel_id=1, source_target_pairs={{0,24},{8,0},{16,8},{24,16},{1,25},{9,1},{17,9},{25,17},{2,26},{10... | collective-permute-start | bytes 1376264 | tf_op jit(solution)/shard_map/ppermute | solution.py:795
  70.0 62.3 %collective-permute-start.1 = (bf16[2,128,768]{2,1,0:T(8,128)(2,1)}, bf16[2,128,768]{2,1,0:T(8,128)(2,1)}, u32[]{:S(2)}, u32[]{:S(2)}) collective-permute-start(bf16[2,128,768]{2,1,0:T(8,128)(2,1)} %get-tuple-element.65), channel_id=1, source_target_pairs={{0,16},{8,24},{16,0},{24,8},{1,17},{9,25},{17,1},{25,9},{2,18},{10... | collective-permute-start | bytes 1179656 | tf_op jit(solution)/shard_map/ppermute | solution.py:795
  76.8 55.5 %copy-start.27 = (bf16[2,128,768]{2,1,0:T(8,128)(2,1)}, bf16[2,128,768]{2,1,0:T(8,128)(2,1)S(1)}, u32[]{:S(2)}) copy-start(bf16[2,128,768]{2,1,0:T(8,128)(2,1)S(1)} %collective-permute-done.refs_1_) | copy-start | bytes 1179652
  76.8 55.4 %collective-permute-start.2 = (bf16[2,128,768]{2,1,0:T(8,128)(2,1)}, bf16[2,128,768]{2,1,0:T(8,128)(2,1)}, u32[]{:S(2)}, u32[]{:S(2)}) collective-permute-start(bf16[2,128,768]{2,1,0:T(8,128)(2,1)} %get-tuple-element.66), channel_id=1, source_target_pairs={{0,24},{8,0},{16,8},{24,16},{1,25},{9,1},{17,9},{25,17},{2,26},{10... | collective-permute-start | bytes 1179656 | tf_op jit(solution)/shard_map/ppermute | solution.py:795
  156.2 39.1 %copy-start.36 = (bf16[128,768]{1,0:T(8,128)(2,1)S(1)}, bf16[128,768]{1,0:T(8,128)(2,1)}, u32[]{:S(2)}) copy-start(bf16[128,768]{1,0:T(8,128)(2,1)} %get-tuple-element.82) | copy-start | bytes 589828
  156.2 41.8 %copy-start.35 = (bf16[128,768]{1,0:T(8,128)(2,1)S(1)}, bf16[128,768]{1,0:T(8,128)(2,1)}, u32[]{:S(2)}) copy-start(bf16[128,768]{1,0:T(8,128)(2,1)} %get-tuple-element.84) | copy-start | bytes 589828
  156.2 43.7 %copy-start.34 = (bf16[128,768]{1,0:T(8,128)(2,1)S(1)}, bf16[128,768]{1,0:T(8,128)(2,1)}, u32[]{:S(2)}) copy-start(bf16[128,768]{1,0:T(8,128)(2,1)} %get-tuple-element.86) | copy-start | bytes 589828
  156.3 272.9 %reduce-scatter.3.cloned.1.call-start = ((), (), s32[]{:S(2)}) async-start(), calls=%async_computation.6 | async-start | bytes 5308416 | tf_op jit(solution)/shard_map/reduce_scatter | solution.py:846
  190.9 9.0 %collective-permute-start.12 = (bf16[128,768]{1,0:T(8,128)(2,1)}, bf16[128,768]{1,0:T(8,128)(2,1)S(1)}, u32[]{:S(2)}, u32[]{:S(2)}) collective-permute-start(bf16[128,768]{1,0:T(8,128)(2,1)} %get-tuple-element.81), channel_id=1, source_target_pairs={{0,24},{8,0},{16,8},{24,16},{1,25},{9,1},{17,9},{25,17},{2,26},{10... | collective-permute-start | bytes 589832 | tf_op jit(solution)/shard_map/ppermute | solution.py:800
  194.2 18.7 %collective-permute-start.14 = (bf16[128,768]{1,0:T(8,128)(2,1)}, bf16[128,768]{1,0:T(8,128)(2,1)S(1)}, u32[]{:S(2)}, u32[]{:S(2)}) collective-permute-start(bf16[128,768]{1,0:T(8,128)(2,1)} %get-tuple-element.83), channel_id=1, source_target_pairs={{0,16},{8,24},{16,0},{24,8},{1,17},{9,25},{17,1},{25,9},{2,18},{10... | collective-permute-start | bytes 589832 | tf_op jit(solution)/shard_map/ppermute | solution.py:800
  194.2 18.7 %collective-permute-start.16 = (bf16[128,768]{1,0:T(8,128)(2,1)}, bf16[128,768]{1,0:T(8,128)(2,1)S(1)}, u32[]{:S(2)}, u32[]{:S(2)}) collective-permute-start(bf16[128,768]{1,0:T(8,128)(2,1)} %get-tuple-element.85), channel_id=1, source_target_pairs={{0,8},{8,16},{16,24},{24,0},{1,9},{9,17},{17,25},{25,1},{2,10},{10... | collective-permute-start | bytes 589832 | tf_op jit(solution)/shard_map/ppermute | solution.py:800
  195.3 17.6 %collective-permute-start.13 = (bf16[128,768]{1,0:T(8,128)(2,1)S(1)}, bf16[128,768]{1,0:T(8,128)(2,1)S(1)}, u32[]{:S(2)}, u32[]{:S(2)}) collective-permute-start(bf16[128,768]{1,0:T(8,128)(2,1)S(1)} %copy-done.36), channel_id=1, source_target_pairs={{0,24},{8,0},{16,8},{24,16},{1,25},{9,1},{17,9},{25,17},{2,26},{10... | collective-permute-start | bytes 589832 | tf_op jit(solution)/shard_map/ppermute | solution.py:800
  198.0 30.5 %collective-permute-start.15 = (bf16[128,768]{1,0:T(8,128)(2,1)S(1)}, bf16[128,768]{1,0:T(8,128)(2,1)S(1)}, u32[]{:S(2)}, u32[]{:S(2)}) collective-permute-start(bf16[128,768]{1,0:T(8,128)(2,1)S(1)} %copy-done.35), channel_id=1, source_target_pairs={{0,16},{8,24},{16,0},{24,8},{1,17},{9,25},{17,1},{25,9},{2,18},{10... | collective-permute-start | bytes 589832 | tf_op jit(solution)/shard_map/ppermute | solution.py:800
  199.9 28.7 %copy-start.39 = (bf16[128,768]{1,0:T(8,128)(2,1)}, bf16[128,768]{1,0:T(8,128)(2,1)S(1)}, u32[]{:S(2)}) copy-start(bf16[128,768]{1,0:T(8,128)(2,1)S(1)} %collective-permute-done.12.refs_2_) | copy-start | bytes 589828
  199.9 28.7 %collective-permute-start.17 = (bf16[128,768]{1,0:T(8,128)(2,1)S(1)}, bf16[128,768]{1,0:T(8,128)(2,1)S(1)}, u32[]{:S(2)}, u32[]{:S(2)}) collective-permute-start(bf16[128,768]{1,0:T(8,128)(2,1)S(1)} %copy-done.34), channel_id=1, source_target_pairs={{0,8},{8,16},{16,24},{24,0},{1,9},{9,17},{17,25},{25,1},{2,10},{10... | collective-permute-start | bytes 589832 | tf_op jit(solution)/shard_map/ppermute | solution.py:800
  212.9 15.7 %copy-start.40 = (bf16[128,768]{1,0:T(8,128)(2,1)}, bf16[128,768]{1,0:T(8,128)(2,1)S(1)}, u32[]{:S(2)}) copy-start(bf16[128,768]{1,0:T(8,128)(2,1)S(1)} %collective-permute-done.14.refs_4_) | copy-start | bytes 589828
  212.9 15.7 %copy-start.41 = (bf16[128,768]{1,0:T(8,128)(2,1)}, bf16[128,768]{1,0:T(8,128)(2,1)S(1)}, u32[]{:S(2)}) copy-start(bf16[128,768]{1,0:T(8,128)(2,1)S(1)} %collective-permute-done.16.refs_6_) | copy-start | bytes 589828
  212.9 15.7 %copy-start.42 = (bf16[128,768]{1,0:T(8,128)(2,1)}, bf16[128,768]{1,0:T(8,128)(2,1)S(1)}, u32[]{:S(2)}) copy-start(bf16[128,768]{1,0:T(8,128)(2,1)S(1)} %collective-permute-done.13.refs_3_) | copy-start | bytes 589828
  242.7 32.4 %copy-start.20 = (bf16[4,4,1,24,768]{4,3,2,1,0:T(8,128)(2,1)S(1)}, bf16[4,4,1,24,768]{4,3,2,1,0:T(8,128)(2,1)}, u32[]{:S(2)}) copy-start(bf16[4,4,1,24,768]{4,3,2,1,0:T(8,128)(2,1)} %get-tuple-element.100) | copy-start | bytes 1769476
  275.0 4.9 %collective-permute-start.25 = (bf16[4,4,3,24,768]{4,3,2,1,0:T(8,128)(2,1)}, bf16[4,4,3,24,768]{4,3,2,1,0:T(8,128)(2,1)S(1)}, u32[]{:S(2)}, u32[]{:S(2)}) collective-permute-start(bf16[4,4,3,24,768]{4,3,2,1,0:T(8,128)(2,1)} %get-tuple-element.98), channel_id=1, source_target_pairs={{0,1},{1,0},{2,3},{3,2},{4,5},{5,4},{6,7},{7,6},{8,9},{9,8},{10,11... | collective-permute-start | bytes 5308424 | tf_op jit(solution)/shard_map/ppermute | solution.py:716
  275.1 4.7 %collective-permute-start.26 = (bf16[4,4,1,24,768]{4,3,1,2,0:T(8,128)(2,1)S(1)}, bf16[4,4,1,24,768]{4,3,1,2,0:T(8,128)(2,1)S(1)}, u32[]{:S(2)}, u32[]{:S(2)}) collective-permute-start(bf16[4,4,1,24,768]{4,3,1,2,0:T(8,128)(2,1)S(1)} %bitcast.73), channel_id=1, source_target_pairs={{0,1},{1,0},{2,3},{3,2},{4,5},{5,4},{6,7},{7,6},{8,9},{9,8},{10,11... | collective-permute-start | bytes 1769480 | tf_op jit(solution)/shard_map/ppermute | solution.py:716
  280.5 16.4 %collective-permute-start.27 = (bf16[4,4,24,768]{3,2,1,0:T(8,128)(2,1)S(1)}, bf16[4,4,24,768]{3,2,1,0:T(8,128)(2,1)}, u32[]{:S(2)}, u32[]{:S(2)}) collective-permute-start(bf16[4,4,24,768]{3,2,1,0:T(8,128)(2,1)S(1)} %pad_maximum_fusion), channel_id=1, source_target_pairs={{0,2},{1,3},{2,0},{3,1},{4,6},{5,7},{6,4},{7,5},{8,10},{9,11},{10,... | collective-permute-start | bytes 1769480 | tf_op jit(solution)/shard_map/ppermute | solution.py:716
  282.1 21.8 %collective-permute-start.28 = (bf16[4,4,24,768]{3,2,1,0:T(8,128)(2,1)S(1)}, bf16[4,4,24,768]{3,2,1,0:T(8,128)(2,1)}, u32[]{:S(2)}, u32[]{:S(2)}) collective-permute-start(bf16[4,4,24,768]{3,2,1,0:T(8,128)(2,1)S(1)} %pad_maximum_fusion.1), channel_id=1, source_target_pairs={{0,4},{1,5},{2,6},{3,7},{4,0},{5,1},{6,2},{7,3},{8,12},{9,13},{10,... | collective-permute-start | bytes 1769480 | tf_op jit(solution)/shard_map/ppermute | solution.py:716
  282.7 36.2 %collective-permute-start.29 = (bf16[4,4,24,768]{3,2,1,0:T(8,128)(2,1)S(1)}, bf16[4,4,24,768]{3,2,1,0:T(8,128)(2,1)}, u32[]{:S(2)}, u32[]{:S(2)}) collective-permute-start(bf16[4,4,24,768]{3,2,1,0:T(8,128)(2,1)S(1)} %pad_maximum_fusion.2), channel_id=1, source_target_pairs={{0,6},{1,7},{2,4},{3,5},{4,2},{5,3},{6,0},{7,1},{8,14},{9,15},{10,... | collective-permute-start | bytes 1769480 | tf_op jit(solution)/shard_map/ppermute | solution.py:716
  284.3 68.8 %collective-permute-start.6 = (bf16[128,768]{1,0:T(8,128)(2,1)}, bf16[128,768]{1,0:T(8,128)(2,1)}, u32[]{:S(2)}, u32[]{:S(2)}) collective-permute-start(bf16[128,768]{1,0:T(8,128)(2,1)} %get-tuple-element.73), channel_id=1, source_target_pairs={{0,24},{8,0},{16,8},{24,16},{1,25},{9,1},{17,9},{25,17},{2,26},{10... | collective-permute-start | bytes 589832 | tf_op jit(solution)/shard_map/ppermute | solution.py:800
  284.5 72.0 %collective-permute-start.8 = (bf16[128,768]{1,0:T(8,128)(2,1)}, bf16[128,768]{1,0:T(8,128)(2,1)}, u32[]{:S(2)}, u32[]{:S(2)}) collective-permute-start(bf16[128,768]{1,0:T(8,128)(2,1)} %get-tuple-element.75), channel_id=1, source_target_pairs={{0,16},{8,24},{16,0},{24,8},{1,17},{9,25},{17,1},{25,9},{2,18},{10... | collective-permute-start | bytes 589832 | tf_op jit(solution)/shard_map/ppermute | solution.py:800
  320.7 8.5 %collective-permute-start.30 = (bf16[4,24,768]{2,1,0:T(8,128)(2,1)S(1)}, bf16[4,24,768]{2,1,0:T(8,128)(2,1)S(1)}, u32[]{:S(2)}, u32[]{:S(2)}) collective-permute-start(bf16[4,24,768]{2,1,0:T(8,128)(2,1)S(1)} %get-tuple-element.117), channel_id=1, source_target_pairs={{0,8},{8,16},{16,24},{24,0},{1,9},{9,17},{17,25},{25,1},{2,10},{10... | collective-permute-start | bytes 442376 | tf_op jit(solution)/shard_map/ppermute | solution.py:721
  320.9 8.3 %collective-permute-start.32 = (bf16[4,24,768]{2,1,0:T(8,128)(2,1)S(1)}, bf16[4,24,768]{2,1,0:T(8,128)(2,1)S(1)}, u32[]{:S(2)}, u32[]{:S(2)}) collective-permute-start(bf16[4,24,768]{2,1,0:T(8,128)(2,1)S(1)} %get-tuple-element.118), channel_id=1, source_target_pairs={{0,24},{8,0},{16,8},{24,16},{1,25},{9,1},{17,9},{25,17},{2,26},{10... | collective-permute-start | bytes 442376 | tf_op jit(solution)/shard_map/ppermute | solution.py:721
  324.6 11.7 %collective-permute-start.31 = (bf16[4,24,768]{2,1,0:T(8,128)(2,1)S(1)}, bf16[4,24,768]{2,1,0:T(8,128)(2,1)S(1)}, u32[]{:S(2)}, u32[]{:S(2)}) collective-permute-start(bf16[4,24,768]{2,1,0:T(8,128)(2,1)S(1)} %get-tuple-element.119), channel_id=1, source_target_pairs={{0,16},{8,24},{16,0},{24,8},{1,17},{9,25},{17,1},{25,9},{2,18},{10... | collective-permute-start | bytes 442376 | tf_op jit(solution)/shard_map/ppermute | solution.py:721
  336.3 12.8 %collective-permute-start.35 = (bf16[4,24,768]{2,1,0:T(8,128)(2,1)S(1)}, bf16[4,24,768]{2,1,0:T(8,128)(2,1)S(1)}, u32[]{:S(2)}, u32[]{:S(2)}) collective-permute-start(bf16[4,24,768]{2,1,0:T(8,128)(2,1)S(1)} %fusion.6), channel_id=1, source_target_pairs={{0,24},{8,0},{16,8},{24,16},{1,25},{9,1},{17,9},{25,17},{2,26},{10... | collective-permute-start | bytes 442376 | tf_op jit(solution)/shard_map/ppermute | solution.py:721
  337.6 14.3 %collective-permute-start.34 = (bf16[4,24,768]{2,1,0:T(8,128)(2,1)S(1)}, bf16[4,24,768]{2,1,0:T(8,128)(2,1)S(1)}, u32[]{:S(2)}, u32[]{:S(2)}) collective-permute-start(bf16[4,24,768]{2,1,0:T(8,128)(2,1)S(1)} %fusion.6), channel_id=1, source_target_pairs={{0,16},{8,24},{16,0},{24,8},{1,17},{9,25},{17,1},{25,9},{2,18},{10... | collective-permute-start | bytes 442376 | tf_op jit(solution)/shard_map/ppermute | solution.py:721
  337.6 15.4 %collective-permute-start.33 = (bf16[4,24,768]{2,1,0:T(8,128)(2,1)S(1)}, bf16[4,24,768]{2,1,0:T(8,128)(2,1)S(1)}, u32[]{:S(2)}, u32[]{:S(2)}) collective-permute-start(bf16[4,24,768]{2,1,0:T(8,128)(2,1)S(1)} %fusion.6), channel_id=1, source_target_pairs={{0,8},{8,16},{16,24},{24,0},{1,9},{9,17},{17,25},{25,1},{2,10},{10... | collective-permute-start | bytes 442376 | tf_op jit(solution)/shard_map/ppermute | solution.py:721
  338.4 47.8 %copy-start.29 = (bf16[128,768]{1,0:T(8,128)(2,1)S(1)}, bf16[128,768]{1,0:T(8,128)(2,1)}, u32[]{:S(2)}) copy-start(bf16[128,768]{1,0:T(8,128)(2,1)} %get-tuple-element.76) | copy-start | bytes 589828
  338.4 50.7 %copy-start.28 = (bf16[128,768]{1,0:T(8,128)(2,1)S(1)}, bf16[128,768]{1,0:T(8,128)(2,1)}, u32[]{:S(2)}) copy-start(bf16[128,768]{1,0:T(8,128)(2,1)} %get-tuple-element.78) | copy-start | bytes 589828
  349.1 8.7 %collective-permute-start.10 = (bf16[128,768]{1,0:T(8,128)(2,1)S(1)}, bf16[128,768]{1,0:T(8,128)(2,1)S(1)}, u32[]{:S(2)}, u32[]{:S(2)}) collective-permute-start(bf16[128,768]{1,0:T(8,128)(2,1)S(1)} %copy-done.31), channel_id=1, source_target_pairs={{0,8},{8,16},{16,24},{24,0},{1,9},{9,17},{17,25},{25,1},{2,10},{10... | collective-permute-start | bytes 589832 | tf_op jit(solution)/shard_map/ppermute | solution.py:800
  351.9 8.9 %collective-permute-start.7 = (bf16[128,768]{1,0:T(8,128)(2,1)S(1)}, bf16[128,768]{1,0:T(8,128)(2,1)S(1)}, u32[]{:S(2)}, u32[]{:S(2)}) collective-permute-start(bf16[128,768]{1,0:T(8,128)(2,1)S(1)} %copy-done.30), channel_id=1, source_target_pairs={{0,24},{8,0},{16,8},{24,16},{1,25},{9,1},{17,9},{25,17},{2,26},{10... | collective-permute-start | bytes 589832 | tf_op jit(solution)/shard_map/ppermute | solution.py:800
  353.0 3.4 collective-permute-start.18
  353.1 63.3 %copy-start.3 = (bf16[4,4,24,768]{3,2,1,0:T(8,128)(2,1)}, bf16[4,4,24,768]{3,2,1,0:T(8,128)(2,1)S(1)}, u32[]{:S(2)}) copy-start(bf16[4,4,24,768]{3,2,1,0:T(8,128)(2,1)S(1)} %pad_maximum_fusion.3.refs_0_) | copy-start | bytes 1769476
  353.1 56.1 %collective-permute-start.41 = (bf16[4,4,24,768]{3,2,1,0:T(8,128)(2,1)S(1)}, bf16[4,4,24,768]{3,2,1,0:T(8,128)(2,1)S(1)}, u32[]{:S(2)}, u32[]{:S(2)}) collective-permute-start(bf16[4,4,24,768]{3,2,1,0:T(8,128)(2,1)S(1)} %pad_maximum_fusion.3.refs_0_), channel_id=1, source_target_pairs={{0,6},{1,7},{2,4},{3,5},{4,2},{5,3},{6,0},{7,1},{8,14},{9,15},{10,... | collective-permute-start | bytes 1769480 | tf_op jit(solution)/shard_map/ppermute | solution.py:716
  356.4 53.2 %collective-permute-start.39 = (bf16[4,4,24,768]{3,2,1,0:T(8,128)(2,1)S(1)}, bf16[4,4,24,768]{3,2,1,0:T(8,128)(2,1)S(1)}, u32[]{:S(2)}, u32[]{:S(2)}) collective-permute-start(bf16[4,4,24,768]{3,2,1,0:T(8,128)(2,1)S(1)} %pad_maximum_fusion.3.refs_0_), channel_id=1, source_target_pairs={{0,4},{1,5},{2,6},{3,7},{4,0},{5,1},{6,2},{7,3},{8,12},{9,13},{10,... | collective-permute-start | bytes 1769480 | tf_op jit(solution)/shard_map/ppermute | solution.py:716
  356.5 53.3 %collective-permute-start.37 = (bf16[4,4,24,768]{3,2,1,0:T(8,128)(2,1)S(1)}, bf16[4,4,24,768]{3,2,1,0:T(8,128)(2,1)S(1)}, u32[]{:S(2)}, u32[]{:S(2)}) collective-permute-start(bf16[4,4,24,768]{3,2,1,0:T(8,128)(2,1)S(1)} %pad_maximum_fusion.3.refs_0_), channel_id=1, source_target_pairs={{0,2},{1,3},{2,0},{3,1},{4,6},{5,7},{6,4},{7,5},{8,10},{9,11},{10,... | collective-permute-start | bytes 1769480 | tf_op jit(solution)/shard_map/ppermute | solution.py:716
  357.9 52.4 %copy-start.32 = (bf16[128,768]{1,0:T(8,128)(2,1)}, bf16[128,768]{1,0:T(8,128)(2,1)S(1)}, u32[]{:S(2)}) copy-start(bf16[128,768]{1,0:T(8,128)(2,1)S(1)} %collective-permute-done.10.refs_6_) | copy-start | bytes 589828
  357.9 26.9 %collective-permute-start.21 = (f32[24,768]{1,0:T(8,128)S(1)}, f32[24,768]{1,0:T(8,128)S(1)}, u32[]{:S(2)}, u32[]{:S(2)}) collective-permute-start(f32[24,768]{1,0:T(8,128)S(1)} %fusion.11), channel_id=1, source_target_pairs={{0,6},{1,7},{2,4},{3,5},{4,2},{5,3},{6,0},{7,1},{8,14},{9,15},{10,... | collective-permute-start | bytes 221192 | tf_op jit(solution)/shard_map/ppermute | solution.py:716
  360.8 49.4 %copy-start.33 = (bf16[128,768]{1,0:T(8,128)(2,1)}, bf16[128,768]{1,0:T(8,128)(2,1)S(1)}, u32[]{:S(2)}) copy-start(bf16[128,768]{1,0:T(8,128)(2,1)S(1)} %collective-permute-done.7.refs_3_) | copy-start | bytes 589828
  360.8 25.5 %collective-permute-start.20 = (f32[24,768]{1,0:T(8,128)S(1)}, f32[24,768]{1,0:T(8,128)S(1)}, u32[]{:S(2)}, u32[]{:S(2)}) collective-permute-start(f32[24,768]{1,0:T(8,128)S(1)} %fusion.11), channel_id=1, source_target_pairs={{0,4},{1,5},{2,6},{3,7},{4,0},{5,1},{6,2},{7,3},{8,12},{9,13},{10,... | collective-permute-start | bytes 221192 | tf_op jit(solution)/shard_map/ppermute | solution.py:716
  384.8 4.4 collective-permute-start.19
  386.2 16.0 %collective-permute-start.9 = (bf16[128,768]{1,0:T(8,128)(2,1)S(1)}, bf16[128,768]{1,0:T(8,128)(2,1)S(1)}, u32[]{:S(2)}, u32[]{:S(2)}) collective-permute-start(bf16[128,768]{1,0:T(8,128)(2,1)S(1)} %copy-done.29), channel_id=1, source_target_pairs={{0,16},{8,24},{16,0},{24,8},{1,17},{9,25},{17,1},{25,9},{2,18},{10... | collective-permute-start | bytes 589832 | tf_op jit(solution)/shard_map/ppermute | solution.py:800
  389.2 13.1 %collective-permute-start.11 = (bf16[128,768]{1,0:T(8,128)(2,1)S(1)}, bf16[128,768]{1,0:T(8,128)(2,1)S(1)}, u32[]{:S(2)}, u32[]{:S(2)}) collective-permute-start(bf16[128,768]{1,0:T(8,128)(2,1)S(1)} %copy-done.28), channel_id=1, source_target_pairs={{0,8},{8,16},{16,24},{24,0},{1,9},{9,17},{17,25},{25,1},{2,10},{10... | collective-permute-start | bytes 589832 | tf_op jit(solution)/shard_map/ppermute | solution.py:800
  402.3 5.4 %collective-permute-start.24 = (f32[24,768]{1,0:T(8,128)S(1)}, f32[24,768]{1,0:T(8,128)S(1)}, u32[]{:S(2)}, u32[]{:S(2)}) collective-permute-start(f32[24,768]{1,0:T(8,128)S(1)} %add_add_fusion.1), channel_id=1, source_target_pairs={{0,24},{8,0},{16,8},{24,16},{1,25},{9,1},{17,9},{25,17},{2,26},{10... | collective-permute-start | bytes 221192 | tf_op jit(solution)/shard_map/ppermute | solution.py:721
  402.3 6.9 %collective-permute-start.23 = (f32[24,768]{1,0:T(8,128)S(1)}, f32[24,768]{1,0:T(8,128)S(1)}, u32[]{:S(2)}, u32[]{:S(2)}) collective-permute-start(f32[24,768]{1,0:T(8,128)S(1)} %add_add_fusion.1), channel_id=1, source_target_pairs={{0,16},{8,24},{16,0},{24,8},{1,17},{9,25},{17,1},{25,9},{2,18},{10... | collective-permute-start | bytes 221192 | tf_op jit(solution)/shard_map/ppermute | solution.py:721
  407.7 8.8 %collective-permute-start.22 = (f32[24,768]{1,0:T(8,128)S(1)}, f32[24,768]{1,0:T(8,128)S(1)}, u32[]{:S(2)}, u32[]{:S(2)}) collective-permute-start(f32[24,768]{1,0:T(8,128)S(1)} %add_add_fusion.1), channel_id=1, source_target_pairs={{0,8},{8,16},{16,24},{24,0},{1,9},{9,17},{17,25},{25,1},{2,10},{10... | collective-permute-start | bytes 221192 | tf_op jit(solution)/shard_map/ppermute | solution.py:721
  409.2 8.5 %collective-permute-start.36 = (bf16[4,4,24,768]{3,2,1,0:T(8,128)(2,1)S(1)}, bf16[4,4,24,768]{3,2,1,0:T(8,128)(2,1)S(1)}, u32[]{:S(2)}, u32[]{:S(2)}) collective-permute-start(bf16[4,4,24,768]{3,2,1,0:T(8,128)(2,1)S(1)} %pad_maximum_fusion.3.refs_0_), channel_id=1, source_target_pairs={{0,1},{1,0},{2,3},{3,2},{4,5},{5,4},{6,7},{7,6},{8,9},{9,8},{10,11... | collective-permute-start | bytes 1769480 | tf_op jit(solution)/shard_map/ppermute | solution.py:716
  409.2 8.5 %collective-permute-start.42 = (bf16[4,4,24,768]{3,2,1,0:T(8,128)(2,1)S(1)}, bf16[4,4,24,768]{3,2,1,0:T(8,128)(2,1)S(1)}, u32[]{:S(2)}, u32[]{:S(2)}) collective-permute-start(bf16[4,4,24,768]{3,2,1,0:T(8,128)(2,1)S(1)} %collective-permute-done.41.refs_6_), channel_id=1, source_target_pairs={{0,1},{1,0},{2,3},{3,2},{4,5},{5,4},{6,7},{7,6},{8,9},{9,8},{10,11... | collective-permute-start | bytes 1769480 | tf_op jit(solution)/shard_map/ppermute | solution.py:716
  409.7 8.0 %collective-permute-start.40 = (bf16[4,4,24,768]{3,2,1,0:T(8,128)(2,1)S(1)}, bf16[4,4,24,768]{3,2,1,0:T(8,128)(2,1)S(1)}, u32[]{:S(2)}, u32[]{:S(2)}) collective-permute-start(bf16[4,4,24,768]{3,2,1,0:T(8,128)(2,1)S(1)} %collective-permute-done.39.refs_4_), channel_id=1, source_target_pairs={{0,1},{1,0},{2,3},{3,2},{4,5},{5,4},{6,7},{7,6},{8,9},{9,8},{10,11... | collective-permute-start | bytes 1769480 | tf_op jit(solution)/shard_map/ppermute | solution.py:716
  409.8 8.0 %collective-permute-start.38 = (bf16[4,4,24,768]{3,2,1,0:T(8,128)(2,1)S(1)}, bf16[4,4,24,768]{3,2,1,0:T(8,128)(2,1)S(1)}, u32[]{:S(2)}, u32[]{:S(2)}) collective-permute-start(bf16[4,4,24,768]{3,2,1,0:T(8,128)(2,1)S(1)} %collective-permute-done.37.refs_2_), channel_id=1, source_target_pairs={{0,1},{1,0},{2,3},{3,2},{4,5},{5,4},{6,7},{7,6},{8,9},{9,8},{10,11... | collective-permute-start | bytes 1769480 | tf_op jit(solution)/shard_map/ppermute | solution.py:716
  (30 other events, 164.1 us)
Sparse Core Ops, SparseCore 0:
  9.9 41.4 all-gather.8
  53.3 38.7 all-gather.10
  94.1 38.7 all-gather.4
  134.6 38.7 all-gather.6
  176.7 53.7 reduce-scatter.4
  275.7 62.4 reduce-scatter.2

commit v3 on v2

v3 whole, which is shorter than its diff:
```python
import functools

import jax
import jax.numpy as jnp
from jax import lax
from jax.experimental import pallas as pl
from jax.experimental.pallas import tpu as pltpu
from jax.sharding import PartitionSpec as P

HEAD_DIM = 64
LANES = 128
EPS = 1e-05
MASKED = -1e30
F32 = jnp.float32
BF16 = jnp.bfloat16
VMEM_LIMIT = 56 * 1024 * 1024
BLOCKS = 32
FAR = (0, 2, 1, 3)
PLACES = ((0, 0), (1, 0), (2, 0), (3, 0), (3, 1))


def params():
    return pltpu.CompilerParams(vmem_limit_bytes=VMEM_LIMIT)


def dot_nt(left, right):
    return lax.dot_general(left, right, (((1,), (1,)), ((), ())), preferred_element_type=F32)


def dot_tn(left, right):
    return lax.dot_general(left, right, (((0,), (0,)), ((), ())), preferred_element_type=F32)


def dot_nn(left, right):
    return jnp.dot(left, right, preferred_element_type=F32)


def norm_parts(rows):
    mean = jnp.mean(rows, axis=-1, keepdims=True)
    centred = rows - mean
    var = jnp.mean(centred * centred, axis=-1, keepdims=True)
    scale = lax.rsqrt(var + EPS)
    return centred * scale, scale


def norm_back(grad, gain, xhat, scale):
    a = grad * gain
    mean_a = jnp.mean(a, axis=-1, keepdims=True)
    mean_ax = jnp.mean(a * xhat, axis=-1, keepdims=True)
    return scale * (a - mean_a - xhat * mean_ax)


def full(shape):
    return pl.BlockSpec(shape, lambda *_: (0,) * len(shape))


def smem():
    return pl.BlockSpec(memory_space=pltpu.SMEM)


def cost(micros):
    return pl.CostEstimate(flops=int(micros * 1.1e9), transcendentals=0, bytes_accessed=int(micros * 3e6))


def block_at(at_ref, chip, core, far):
    return (at_ref[0] ^ (2 * chip + core)) * 4 + (at_ref[1] ^ FAR[far])


def qkv_kernel(tok_ref, scale_ref, w_ref, normed_ref, qkv_ref):
    xhat, _ = norm_parts(tok_ref[...].astype(F32))
    normed = (xhat * scale_ref[0:1, :] + scale_ref[1:2, :]).astype(BF16)
    normed_ref[...] = normed
    qkv_ref[...] = dot_nn(normed, w_ref[...]).astype(BF16)


def qkv_call(tokens, scales, weight):
    seq, width = tokens.shape
    block = 256
    cols = weight.shape[1]
    return pl.pallas_call(
        qkv_kernel,
        grid=(seq // block,),
        in_specs=[
            pl.BlockSpec((block, width), lambda i: (i, 0)),
            full((4, width)),
            full((width, cols)),
        ],
        out_specs=[
            pl.BlockSpec((block, width), lambda i: (i, 0)),
            pl.BlockSpec((block, cols), lambda i: (i, 0)),
        ],
        out_shape=[
            jax.ShapeDtypeStruct((seq, width), BF16),
            jax.ShapeDtypeStruct((seq, cols), BF16),
        ],
        compiler_params=params(),
        cost_estimate=cost(8.7),
        name="norm_qkv",
    )(tokens, scales, weight)


def head_parts(head, length, q, k):
    seq = q.shape[0]
    lane = lax.broadcasted_iota(jnp.int32, (seq, LANES), 1)
    row = lax.broadcasted_iota(jnp.int32, (seq, LANES), 0)
    inside = (lane // HEAD_DIM) == head
    extra = lane == (1 - head) * HEAD_DIM
    key_bias = jnp.where(row >= length, MASKED, 0.0)
    kf = k.astype(F32)
    qf = q.astype(F32) * (HEAD_DIM**-0.5)
    k_head = jnp.where(inside, kf, jnp.where(extra, key_bias, 0.0)).astype(BF16)
    q_head = jnp.where(inside, qf, jnp.where(extra, 1.0, 0.0)).astype(BF16)
    return inside, k_head, q_head, jnp.where(inside, qf, 0.0).astype(BF16)


def causal(scores, block):
    key = lax.broadcasted_iota(jnp.int32, (block, block), 0)
    query = lax.broadcasted_iota(jnp.int32, (block, block), 1)
    last = jnp.where(key <= query, scores[-block:], MASKED)
    if scores.shape[0] == block:
        return last
    return jnp.concatenate([scores[:-block], last], axis=0)


def attend_kernel(len_ref, q_ref, k_ref, v_ref, out_ref, lse_ref, kh_ref, qh_ref, vt_ref, ot_ref):
    seq = q_ref.shape[0]
    block = 256
    length = len_ref[0]
    vt_ref[...] = v_ref[...].astype(F32).T.astype(BF16)
    lse_ref[...] = jnp.zeros_like(lse_ref)
    for head in range(2):
        _, k_head, q_head, _ = head_parts(head, length, q_ref[...], k_ref[...])
        kh_ref[...] = k_head
        qh_ref[...] = q_head
        for qb in range(seq // block):
            ext = (qb + 1) * block
            cols = slice(qb * block, ext)
            scores = causal(dot_nt(kh_ref[:ext, :], qh_ref[cols, :]), block)
            top = jnp.max(scores, axis=0, keepdims=True)
            probs = jnp.exp(scores - top)
            total = jnp.sum(probs, axis=0, keepdims=True)
            part = dot_nn(vt_ref[head * HEAD_DIM : (head + 1) * HEAD_DIM, :ext], probs.astype(BF16))
            ot_ref[head * HEAD_DIM : (head + 1) * HEAD_DIM, cols] = part * (1.0 / total)
            lse_ref[0, head : head + 1, cols] = top + jnp.log(total)
    out_ref[...] = ot_ref[...].T.astype(BF16)


def attend_call(length, qkv, first, count):
    seq = qkv.shape[0]
    pairs = qkv.shape[1] // 3 // LANES
    width = count * LANES
    return pl.pallas_call(
        attend_kernel,
        grid=(count,),
        in_specs=[smem()]
        + [pl.BlockSpec((seq, LANES), lambda p, part=part: (0, part * pairs + first + p)) for part in range(3)],
        out_specs=[
            pl.BlockSpec((seq, LANES), lambda p: (0, p)),
            pl.BlockSpec((1, 8, seq), lambda p: (p, 0, 0)),
        ],
        out_shape=[
            jax.ShapeDtypeStruct((seq, width), BF16),
            jax.ShapeDtypeStruct((count, 8, seq), F32),
        ],
        scratch_shapes=[
            pltpu.VMEM((seq, LANES), BF16),
            pltpu.VMEM((seq, LANES), BF16),
            pltpu.VMEM((LANES, seq), BF16),
            pltpu.VMEM((LANES, seq), F32),
        ],
        compiler_params=params(),
        cost_estimate=cost(12),
        name="attend",
    )(length, qkv, qkv, qkv)


def attend_back_kernel(
    len_ref,
    q_ref,
    k_ref,
    v_ref,
    do_ref,
    o_ref,
    lse_ref,
    normed_ref,
    at_ref,
    dqkv_ref,
    keep_ref,
    send_ref,
    nt_ref,
    kt_ref,
    kh_ref,
    qh_ref,
    qm_ref,
    vh_ref,
    dh_ref,
    dk_ref,
    dv_ref,
    dqt_ref,
    pt_ref,
    join_ref,
):
    seq = q_ref.shape[0]
    block = 256
    length = len_ref[0]

    @pl.when(pl.program_id(0) == 0)
    def _():
        nt_ref[...] = normed_ref[...].astype(F32).T.astype(BF16)

    kt_ref[...] = k_ref[...].astype(F32).T.astype(BF16)
    pt_ref[...] = (do_ref[...].astype(F32) * o_ref[...].astype(F32)).T
    dk_ref[...] = jnp.zeros_like(dk_ref)
    dv_ref[...] = jnp.zeros_like(dv_ref)
    for head in range(2):
        rows = slice(head * HEAD_DIM, (head + 1) * HEAD_DIM)
        inside, k_head, q_head, q_masked = head_parts(head, length, q_ref[...], k_ref[...])
        kh_ref[...] = k_head
        qh_ref[...] = q_head
        qm_ref[...] = q_masked
        vh_ref[...] = jnp.where(inside, v_ref[...].astype(F32), 0.0).astype(BF16)
        dh_ref[...] = jnp.where(inside, do_ref[...].astype(F32), 0.0).astype(BF16)
        for qb in range(seq // block):
            ext = (qb + 1) * block
            cols = slice(qb * block, ext)
            delta = jnp.sum(pt_ref[rows, cols], axis=0, keepdims=True)
            scores = causal(dot_nt(kh_ref[:ext, :], qh_ref[cols, :]), block)
            probs = jnp.exp(scores - lse_ref[0, head : head + 1, cols])
            dprobs = dot_nt(vh_ref[:ext, :], dh_ref[cols, :])
            dscores = (probs * (dprobs - delta)).astype(BF16)
            dv_ref[:ext, :] += dot_nn(probs.astype(BF16), dh_ref[cols, :])
            dk_ref[:ext, :] += dot_nn(dscores, qm_ref[cols, :])
            dqt_ref[rows, cols] = dot_nn(kt_ref[rows, :ext], dscores)
    dq = (dqt_ref[...].T * (HEAD_DIM**-0.5)).astype(BF16)
    dk = dk_ref[...].astype(BF16)
    dv = dv_ref[...].astype(BF16)
    dqkv_ref[0] = dq
    dqkv_ref[1] = dk
    dqkv_ref[2] = dv
    joined = dot_nn(nt_ref[...], jnp.concatenate([dq, dk, dv], axis=1))
    join_ref[...] = joined.reshape(join_ref.shape)
    for chip in range(4):
        for far in range(4):
            for core, ref in enumerate((keep_ref, send_ref)):
                piece = join_ref[block_at(at_ref, chip, core, far)].astype(BF16)
                for part in range(3):
                    ref[chip, far, part] = piece[:, part * LANES : (part + 1) * LANES]


def attend_back_call(length, qkv, dmixed, mixed, lse, normed, at, first, count):
    seq, width = normed.shape
    pairs = width // LANES
    tall = width // BLOCKS
    part_width = count * LANES
    col = lambda p: (0, p)
    return pl.pallas_call(
        attend_back_kernel,
        grid=(count,),
        in_specs=[smem()]
        + [pl.BlockSpec((seq, LANES), lambda p, part=part: (0, part * pairs + first + p)) for part in range(3)]
        + [
            pl.BlockSpec((seq, LANES), lambda p: (0, first + p)),
            pl.BlockSpec((seq, LANES), col),
            pl.BlockSpec((1, 8, seq), lambda p: (p, 0, 0)),
            full((seq, width)),
            smem(),
        ],
        out_specs=[pl.BlockSpec((3, seq, LANES), lambda p: (0, 0, p))]
        + [pl.BlockSpec((4, 4, 3, tall, LANES), lambda p: (0, 0, 0, 0, p))] * 2,
        out_shape=[jax.ShapeDtypeStruct((3, seq, part_width), BF16)]
        + [jax.ShapeDtypeStruct((4, 4, 3, tall, part_width), BF16)] * 2,
        scratch_shapes=[
            pltpu.VMEM((width, seq), BF16),
            pltpu.VMEM((LANES, seq), BF16),
            pltpu.VMEM((seq, LANES), BF16),
            pltpu.VMEM((seq, LANES), BF16),
            pltpu.VMEM((seq, LANES), BF16),
            pltpu.VMEM((seq, LANES), BF16),
            pltpu.VMEM((seq, LANES), BF16),
            pltpu.VMEM((seq, LANES), F32),
            pltpu.VMEM((seq, LANES), F32),
            pltpu.VMEM((LANES, seq), F32),
            pltpu.VMEM((LANES, seq), F32),
            pltpu.VMEM((BLOCKS, tall, 3 * LANES), F32),
        ],
        compiler_params=params(),
        cost_estimate=cost(5),
        name="attend_back",
    )(length, qkv, qkv, qkv, dmixed, mixed, lse, normed, at)


def route_kernel(
    experts, group, capacity, len_ref, me_ref, route_ref, pair_ref, cot_ref, slot_ref, slot_t_ref, out_ref
):
    seq = route_ref.shape[1]
    half = experts // 2
    per = half // group
    local = 2 * per
    length = len_ref[0]
    me = me_ref[0]
    live = lax.broadcasted_iota(jnp.int32, (1, seq), 1) < length
    ids = lax.broadcasted_iota(jnp.int32, (experts, seq), 0)
    upper = (
        lax.broadcasted_iota(jnp.int32, (seq, seq), 0) < lax.broadcasted_iota(jnp.int32, (seq, seq), 1)
    )
    upper = jnp.where(upper, 1.0, 0.0).astype(BF16)
    before = jnp.zeros((experts, 1), F32)
    slots = []
    for choice in range(2):
        named = route_ref[choice : choice + 1, :]
        hot = jnp.where((ids == named) & live, 1.0, 0.0)
        earlier = dot_nn(hot.astype(BF16), upper) + before
        rank = jnp.sum(hot * earlier, axis=0, keepdims=True).astype(jnp.int32)
        before = before + jnp.sum(hot, axis=1, keepdims=True)
        is_new = named >= half
        within = jnp.where(is_new, named - half, named)
        owner = within // per
        place = jnp.where(is_new, per, 0) + within - owner * per
        shift = owner - me
        shift = jnp.where(shift < 0, shift + group, shift)
        slot = (shift * local + place) * capacity + rank
        slots.append(jnp.where(live & (rank < capacity), slot, -1))
    slot_ref[...] = jnp.concatenate(slots + [jnp.full((6, seq), -1, jnp.int32)], axis=0)
    slot_t_ref[...] = jnp.concatenate(
        [slot.astype(F32) for slot in slots] + [jnp.full((LANES - 2, seq), -1.0, F32)], axis=0
    ).T.astype(jnp.int32)
    total = experts * capacity
    place = lax.broadcasted_iota(jnp.int32, (total, seq), 0)
    select = jnp.where((place == slots[0]) | (place == slots[1]), 1.0, 0.0).astype(BF16)
    rows = dot_nn(select, cot_ref[...]).astype(BF16)
    both = (pair_ref[:, 0:1] + pair_ref[:, 1:2]).astype(F32)
    lane = lax.broadcasted_iota(jnp.int32, (seq, LANES), 1)
    tail = dot_nn(select, jnp.where(lane == 0, both, 0.0).astype(BF16)).astype(BF16)
    width = cot_ref.shape[1]
    size = local * capacity
    for shift in range(group):
        piece = slice(shift * size, (shift + 1) * size)
        place = lax.rem(me + shift, group)
        out_ref[place, :, :, :width] = rows[piece].reshape(local, capacity, width)
        out_ref[place, :, :, width:] = tail[piece].reshape(local, capacity, LANES)


def route_call(length, me, routes, cotangent, experts, group, capacity):
    seq, width = cotangent.shape
    local = experts // group
    wide = width + LANES
    return pl.pallas_call(
        functools.partial(route_kernel, experts, group, capacity),
        in_specs=[smem(), smem(), full((2, seq)), full((seq, 2)), full((seq, width))],
        out_specs=[full((8, seq)), full((seq, LANES)), full((group, local, capacity, wide))],
        out_shape=[
            jax.ShapeDtypeStruct((8, seq), jnp.int32),
            jax.ShapeDtypeStruct((seq, LANES), jnp.int32),
            jax.ShapeDtypeStruct((group, local, capacity, wide), BF16),
        ],
        grid=(1,),
        compiler_params=params(),
        cost_estimate=cost(5.7),
        name="route",
    )(length, me, routes.T, routes, cotangent)


def project_kernel(
    group, low_ref, high_ref, tok_ref, w_ref, scale_ref, slot_ref, res_ref, *refs
):
    out_refs = refs[:group]
    normed_ref = refs[group]
    step = pl.program_id(0)
    block = tok_ref.shape[0]
    mixed = jnp.concatenate([low_ref[...], high_ref[...]], axis=1)
    residual = tok_ref[...].astype(F32) + dot_nn(mixed, w_ref[...])
    res_ref[...] = residual
    xhat, _ = norm_parts(residual)
    normed = (xhat * scale_ref[2:3, :] + scale_ref[3:4, :]).astype(BF16)
    normed_ref[pl.ds(pl.multiple_of(step * block, block), block), :] = normed

    @pl.when(step == pl.num_programs(0) - 1)
    def _():
        local, capacity, width = out_refs[0].shape
        size = local * capacity
        seq = normed_ref.shape[0]
        place = lax.broadcasted_iota(jnp.int32, (size * group, seq), 0)
        select = (place == slot_ref[0:1, :]) | (place == slot_ref[1:2, :])
        select = jnp.where(select, 1.0, 0.0).astype(BF16)
        rows = dot_nn(select, normed_ref[...]).astype(BF16)
        for shift in range(group):
            out_refs[shift][...] = rows[shift * size : (shift + 1) * size].reshape(local, capacity, width)


def project_call(mixed, tokens, weight, scales, slots, group, local, capacity):
    seq, width = tokens.shape
    block = 256
    rows = pl.BlockSpec((block, width), lambda i: (i, 0))
    half = pl.BlockSpec((block, width // 2), lambda i: (i, 0))
    return pl.pallas_call(
        functools.partial(project_kernel, group),
        grid=(seq // block,),
        in_specs=[half, half, rows, full((width, width)), full((4, width)), full((8, seq))],
        out_specs=[rows] + [full((local, capacity, width))] * group,
        out_shape=[jax.ShapeDtypeStruct((seq, width), F32)]
        + [jax.ShapeDtypeStruct((local, capacity, width), BF16)] * group,
        scratch_shapes=[pltpu.VMEM((seq, width), BF16)],
        compiler_params=params(),
        cost_estimate=cost(8.8),
        name="project_dispatch",
    )(*mixed, tokens, weight, scales, slots)


def expert_kernel(trained, group, held, own_ref, *refs):
    x_refs = refs[:group]
    g_ref, wr_ref, wrt_ref = refs[group : group + 3]
    in_refs = refs[group + 3 : group + 13]
    out_w_refs = refs[group + 13 : group + 23]
    rest = refs[group + 23 + held :]
    out_ref = rest[0]
    back_refs = rest[1 : group + 1]
    router_ref = rest[group + 1]
    rest = rest[group + 2 :]
    if trained:
        grad_refs = rest[:4]
        rest = rest[4:]
    x_ref, dexp_ref, gate_ref, acc_ref, back_ref, xt_ref, win_ref, wout_ref, din_ref, dout_ref = rest
    step = pl.program_id(0)
    capacity, width = back_refs[0].shape
    own = own_ref[0]

    def source(shift):
        return lax.rem(own_ref[3] - shift + group, group)

    def other_of(tail):
        return tail[:, 0:1].astype(F32).astype(jnp.int32) - own

    @pl.when(step == 0)
    def _():
        for shift in range(group):
            span = slice(shift * capacity, (shift + 1) * capacity)
            rows = x_refs[shift][0]
            x_ref[span, :] = rows
            logits = dot_nn(rows, wr_ref[...])
            lane = lax.broadcasted_iota(jnp.int32, logits.shape, 1)
            other = other_of(g_ref[source(shift), 0, :, width:])
            mine = jnp.sum(jnp.where(lane == own, logits, 0.0), axis=1, keepdims=True)
            theirs = jnp.sum(jnp.where(lane == other, logits, 0.0), axis=1, keepdims=True)
            top = jnp.maximum(mine, theirs)
            up = jnp.exp(mine - top)
            gate = up / (up + jnp.exp(theirs - top))
            gate_ref[span, :] = jnp.broadcast_to(gate, (capacity, LANES))
            dexp_ref[span, :] = (gate * g_ref[source(shift), 0, :, :width].astype(F32)).astype(BF16)
        acc_ref[...] = jnp.zeros_like(acc_ref)
        back_ref[...] = jnp.zeros_like(back_ref)
        xt_ref[...] = x_ref[...].astype(F32).T.astype(BF16)

    for which in range(2):
        core = own_ref[1] ^ which
        for index, (chip, lower) in enumerate(PLACES):
            piece = in_refs[5 * which + index]
            tall = piece.shape[1]
            at = ((own_ref[2] ^ chip) * 2 + core) * in_refs[0].shape[1] + lower * tall
            win_ref[pl.ds(pl.multiple_of(at, 16), tall), :] = piece[0]

            @pl.when(step == chip)
            def _(piece=out_w_refs[5 * which + index], lower=lower, core=core):
                tall = piece.shape[1]
                at = core * out_w_refs[0].shape[1] + lower * tall
                wout_ref[pl.ds(pl.multiple_of(at, 16), tall), :] = piece[0]

    win = win_ref[...]
    wout = wout_ref[...]
    pre = dot_nn(x_ref[...], win)
    square = pre * pre
    tanh = jnp.tanh(0.7978845608028654 * (pre + 0.044715 * pre * square))
    half = 0.5 * (1.0 + tanh)
    hid = (pre * half).astype(BF16)
    slope = half + (0.5 * pre) * (1.0 - tanh * tanh) * (0.7978845608028654 + 0.1070322243 * square)
    acc_ref[...] += dot_nn(hid, wout)
    dpre = (dot_nt(dexp_ref[...], wout) * slope).astype(BF16)
    back_ref[...] += dot_nt(dpre, win)
    if trained:
        dout_ref[...] = dot_tn(hid, dexp_ref[...]).astype(BF16).reshape(dout_ref.shape)
        din_ref[...] = dot_nn(xt_ref[...], dpre).astype(BF16).reshape(din_ref.shape)
        for which in range(2):
            core = own_ref[1] ^ which
            for chip in range(4):
                grad_refs[which][chip] = din_ref[(own_ref[2] ^ chip) * 2 + core]
            grad_refs[2 + which][0] = dout_ref[core]

    @pl.when(step == pl.num_programs(0) - 1)
    def _():
        router = jnp.zeros((width, LANES), F32)
        for shift in range(group):
            span = slice(shift * capacity, (shift + 1) * capacity)
            gate = gate_ref[span, 0:1]
            result = acc_ref[span, :]
            out_ref[source(shift), 0] = (gate * result).astype(BF16)
            dot = jnp.sum(result * g_ref[source(shift), 0, :, :width].astype(F32), axis=1, keepdims=True)
            coef = gate * (1.0 - gate) * dot
            lane = lax.broadcasted_iota(jnp.int32, (capacity, LANES), 1)
            other = other_of(g_ref[source(shift), 0, :, width:])
            sign = jnp.where(lane == own, 1.0, 0.0) - jnp.where(lane == other, 1.0, 0.0)
            dlogits = (coef * sign).astype(BF16)
            back_refs[shift][...] = (back_ref[span, :] + dot_nn(dlogits, wrt_ref[...])).astype(BF16)
            router = router + dot_nn(xt_ref[:, span], dlogits)
        router_ref[...] = router


def expert_call(trained, place, local, own, rows, grads, router, router_t, held, pick, w_in, w_out):
    group = len(rows)
    _, capacity, width = rows[0].shape
    inner = w_in[0].shape[2]
    chunk = inner // 4
    block = lambda f, own: own[2] ^ f
    wide = grads.shape[3]
    many = group * capacity
    shard, deep = width // 8, inner // 8
    out_specs = [pl.BlockSpec((group, 1, capacity, width), lambda f, own: (0, place, 0, 0))]
    out_specs += [full((capacity, width))] * group + [full((width, LANES))]
    out_shape = [jax.ShapeDtypeStruct((group, local, capacity, width), BF16)]
    out_shape += [jax.ShapeDtypeStruct((capacity, width), BF16)] * group
    out_shape += [jax.ShapeDtypeStruct((width, LANES), F32)]
    if trained:
        out_specs += [pl.BlockSpec((4, shard, chunk), lambda f, own: (0, 0, block(f, own)))] * 2
        out_specs += [pl.BlockSpec((1, deep, width), lambda f, own: (f, 0, 0))] * 2
        out_shape += [jax.ShapeDtypeStruct((4, shard, inner), BF16)] * 2
        out_shape += [jax.ShapeDtypeStruct((4, deep, width), BF16)] * 2
    return pl.pallas_call(
        functools.partial(expert_kernel, trained, group, len(held)),
        grid_spec=pltpu.PrefetchScalarGridSpec(
            num_scalar_prefetch=1,
            grid=(4,),
            in_specs=[pl.BlockSpec((1, capacity, width), lambda f, own: (place, 0, 0))] * group
            + [pl.BlockSpec((group, 1, capacity, wide), lambda f, own: (0, place, 0, 0))]
            + [full((width, LANES)), full((LANES, width))]
            + [pl.BlockSpec((1, w.shape[1], chunk), lambda f, own: (pick, 0, block(f, own))) for w in w_in]
            + [pl.BlockSpec((1, w.shape[1], width), lambda f, own: (pick, 0, 0)) for w in w_out]
            + [pl.BlockSpec(memory_space=pl.ANY)] * len(held),
            out_specs=out_specs,
            scratch_shapes=[
            pltpu.VMEM((many, width), BF16),
            pltpu.VMEM((many, width), BF16),
            pltpu.VMEM((many, LANES), F32),
            pltpu.VMEM((many, width), F32),
            pltpu.VMEM((many, width), F32),
            pltpu.VMEM((width, many), BF16),
            pltpu.VMEM((width, chunk), BF16),
            pltpu.VMEM((chunk, width), BF16),
            pltpu.VMEM((8, shard, chunk) if trained else (8, LANES), BF16),
            pltpu.VMEM((2, deep, width) if trained else (8, LANES), BF16),
            ],
        ),
        out_shape=out_shape,
        input_output_aliases={group + 24: 0} if held else {},
        compiler_params=params(),
        cost_estimate=cost(23 if trained else 17),
        name="experts_new" if trained else "experts_old",
    )(own, *rows, grads, router, router_t, *w_in, *w_out, *held)


def pick_matrix(slot_ref, total):
    place = lax.broadcasted_iota(jnp.int32, (slot_ref.shape[0], total), 1)
    hit = (place == slot_ref[:, 0:1]) | (place == slot_ref[:, 1:2])
    return jnp.where(hit, 1.0, 0.0).astype(BF16)


def pick_rows(slot_ref, part_refs):
    width = part_refs[0].shape[-1]
    held = jnp.concatenate([part[...].reshape(-1, width) for part in part_refs], axis=0)
    return dot_nn(pick_matrix(slot_ref, held.shape[0]), held)


def combine_kernel(me_ref, slot_ref, res_ref, part_ref, out_ref):
    group, _, _, width = part_ref.shape
    parts = [part_ref[lax.rem(me_ref[0] + shift, group)].reshape(-1, width) for shift in range(group)]
    held = jnp.concatenate(parts, axis=0)
    out_ref[...] = res_ref[...] + dot_nn(pick_matrix(slot_ref, held.shape[0]), held)


def combine_call(me, slots, residual, parts):
    seq, width = residual.shape
    block = 256
    rows = pl.BlockSpec((block, width), lambda i: (i, 0))
    return pl.pallas_call(
        combine_kernel,
        grid=(seq // block,),
        in_specs=[smem(), pl.BlockSpec((block, LANES), lambda i: (i, 0)), rows, full(parts.shape)],
        out_specs=rows,
        out_shape=jax.ShapeDtypeStruct((seq, width), F32),
        compiler_params=params(),
        cost_estimate=cost(6.2),
        name="combine",
    )(me, slots, residual, parts)


def middle_kernel(count, slot_ref, res_ref, cot_ref, gain_ref, low_ref, high_ref, w_ref, at_ref, *refs):
    parts = refs[:count]
    dres_ref, dmix_ref, keep_ref, send_ref, sums_ref, acc_ref = refs[count:]
    step = pl.program_id(0)
    dnormed = pick_rows(slot_ref, parts)
    xhat, scale = norm_parts(res_ref[...])
    dres = cot_ref[...].astype(F32) + norm_back(dnormed, gain_ref[2:3, :], xhat, scale)
    dres_ref[...] = dres
    dattn = dres.astype(BF16)
    dmix_ref[...] = dot_nt(dattn, w_ref[...]).astype(BF16)

    @pl.when(step == 0)
    def _():
        sums_ref[...] = jnp.zeros_like(sums_ref)
        acc_ref[...] = jnp.zeros_like(acc_ref)

    mixed = jnp.concatenate([low_ref[...], high_ref[...]], axis=1)
    acc_ref[...] += dot_tn(mixed, dattn).reshape(acc_ref.shape)
    sums_ref[0:1, :] += jnp.sum(dnormed * xhat, axis=0, keepdims=True)
    sums_ref[1:2, :] += jnp.sum(dnormed, axis=0, keepdims=True)

    @pl.when(step == pl.num_programs(0) - 1)
    def _():
        for chip in range(4):
            for far in range(4):
                for core, ref in enumerate((keep_ref, send_ref)):
                    piece = acc_ref[block_at(at_ref, chip, core, far)].astype(BF16)
                    ref[chip, far, 0] = piece[:, : piece.shape[1] // 2]
                    ref[chip, far, 1] = piece[:, piece.shape[1] // 2 :]


def middle_call(slots, residual, cotangent, gain, mixed, weight, at, parts):
    seq, width = residual.shape
    tall = width // BLOCKS
    block = 256
    capacity = parts[0].shape[0]
    rows = pl.BlockSpec((block, width), lambda i: (i, 0))
    half = pl.BlockSpec((block, width // 2), lambda i: (i, 0))
    return pl.pallas_call(
        functools.partial(middle_kernel, len(parts)),
        grid=(seq // block,),
        in_specs=[
            pl.BlockSpec((block, LANES), lambda i: (i, 0)),
            rows,
            rows,
            full((4, width)),
            half,
            half,
            full((width, width)),
            smem(),
        ]
        + [full((capacity, width))] * len(parts),
        out_specs=[rows, rows] + [full((4, 4, 2, tall, width // 2))] * 2 + [full((8, width))],
        out_shape=[
            jax.ShapeDtypeStruct((seq, width), F32),
            jax.ShapeDtypeStruct((seq, width), BF16),
            jax.ShapeDtypeStruct((4, 4, 2, tall, width // 2), BF16),
            jax.ShapeDtypeStruct((4, 4, 2, tall, width // 2), BF16),
            jax.ShapeDtypeStruct((8, width), F32),
        ],
        scratch_shapes=[pltpu.VMEM((BLOCKS, tall, width), F32)],
        compiler_params=params(),
        cost_estimate=cost(13),
        name="middle_back",
    )(slots, residual, cotangent, gain, *mixed, weight, at, *parts)


def last_kernel(low_ref, high_ref, tok_ref, dres_ref, gain_ref, w_ref, out_ref, sums_ref):
    width = tok_ref.shape[1]
    grads = [ref[part] for part in range(3) for ref in (low_ref, high_ref)]
    dnormed = dot_nt(jnp.concatenate(grads, axis=1), w_ref[...])
    xhat, scale = norm_parts(tok_ref[...].astype(F32))
    out_ref[...] = dres_ref[...] + norm_back(dnormed, gain_ref[0:1, :], xhat, scale)

    @pl.when(pl.program_id(0) == 0)
    def _():
        sums_ref[...] = jnp.zeros_like(sums_ref)

    sums_ref[0:1, :] += jnp.sum(dnormed * xhat, axis=0, keepdims=True)
    sums_ref[1:2, :] += jnp.sum(dnormed, axis=0, keepdims=True)


def last_call(dqkv, tokens, dres, gain, weight):
    seq, width = tokens.shape
    block = 256
    rows = pl.BlockSpec((block, width), lambda i: (i, 0))
    return pl.pallas_call(
        last_kernel,
        grid=(seq // block,),
        in_specs=[
            pl.BlockSpec((3, block, width // 2), lambda i: (0, i, 0)),
            pl.BlockSpec((3, block, width // 2), lambda i: (0, i, 0)),
            rows,
            rows,
            full((4, width)),
            full((width, 3 * width)),
        ],
        out_specs=[rows, full((8, width))],
        out_shape=[
            jax.ShapeDtypeStruct((seq, width), F32),
            jax.ShapeDtypeStruct((8, width), F32),
        ],
        compiler_params=params(),
        cost_estimate=cost(5),
        name="last_back",
    )(*dqkv, tokens, dres, gain, weight)


def unpack_kernel(outs, parts, at_ref, *refs):
    pieces = refs[:8]
    out_refs = refs[-outs:]
    tall = pieces[0].shape[1]
    part = pl.program_id(0)

    def put(out_ref):
        for index, piece in enumerate(pieces):
            for far in range(4):
                place = (at_ref[0] ^ index) * 4 + (at_ref[1] ^ FAR[far])
                rows = pl.ds(pl.multiple_of(place * tall, 8), tall)
                out_ref[rows, :] = piece[far * parts + part].astype(F32)

    @pl.when(part < 3)
    def _():
        put(out_refs[0])

    if outs > 1:

        @pl.when(part >= 3)
        def _():
            put(out_refs[1])


def unpack_call(at, pieces, half, base=None):
    blocks, tall, part_width = pieces[0].shape
    parts = blocks // 4
    width = tall * BLOCKS
    out_specs = [pl.BlockSpec((width, part_width), lambda p: (0, 2 * jnp.minimum(p, 2) + half))]
    out_shape = [jax.ShapeDtypeStruct((width, 6 * part_width), F32)]
    if parts > 3:
        out_specs.append(pl.BlockSpec((width, part_width), lambda p: (0, jnp.maximum(p - 3, 0))))
        out_shape.append(jax.ShapeDtypeStruct((width, width), F32))
    held = [] if base is None else [base]
    return pl.pallas_call(
        functools.partial(unpack_kernel, len(out_shape), parts),
        grid=(parts,),
        in_specs=[smem()]
        + [full((blocks, tall, part_width))] * 8
        + [pl.BlockSpec(memory_space=pl.ANY)] * len(held),
        out_specs=out_specs,
        out_shape=out_shape,
        input_output_aliases={9: 0} if held else {},
        compiler_params=params(),
        cost_estimate=cost(4),
        name="unpack",
    )(at, *pieces, *held)


def swap(block, bits):
    size = lax.axis_size("batch")
    return lax.ppermute(block, "batch", [(i, i ^ bits) for i in range(size)])


def across(block, bits):
    size = lax.axis_size("expert")
    return lax.ppermute(block, "expert", [(i, i ^ bits) for i in range(size)])


def added(*blocks):
    total = blocks[0].astype(F32)
    for block in blocks[1:]:
        total = total + block.astype(F32)
    return total


def gather_shards(shard):
    whole = lax.all_gather(shard, "batch", axis=1, tiled=True)
    some, rows, width = whole.shape
    parts = whole.reshape(some, 4, 2, rows // 8, width)
    half = rows // 16
    return [
        parts[:, chip, core, lower * half : (lower + 1) * half] if chip == 3 else parts[:, chip, core]
        for core in range(2)
        for chip, lower in PLACES
    ]


def near(shard):
    return [swap(shard, 2), swap(shard, 4)]


def relay(full_x, full_y):
    half = full_x.shape[1] // 2
    return [swap(full_y[:, :half], 2), swap(full_x[:, half:], 4)]


def tie(*values):
    return list(lax.optimization_barrier(values))


def sum_all(keep, send):
    keep, send = lax.psum((keep, send), ("expert", "batch"))
    pieces = []
    for chip in range(4):
        for half in (keep, send):
            parts = jnp.concatenate([part[chip] for part in half], axis=1)
            pieces.append(jnp.concatenate([parts[far] for far in range(4)]))
    return pieces


def sum_core(keep, send):
    got = [swap(part, 1) for part in send]
    halves = []
    for chip in range(4):
        parts = [added(mine[chip], other[chip]) for mine, other in zip(keep, got)]
        halves.append(jnp.concatenate(parts, axis=1).astype(BF16))
    return halves


def to_chips(halves):
    return [halves[0]] + [swap(halves[chip], 2 * chip) for chip in (1, 2, 3)]


def total(parts):
    return added(*parts).astype(BF16)


def give(block, bits):
    rows = block.shape[0] // 2
    return [block[:rows], across(block[rows:], bits)]


def spread_chips(column):
    return [column] + [swap(column, 2 * chip) for chip in (1, 2, 3)]


def spread_cores(blocks):
    return [piece for block in blocks for piece in (block, swap(block, 1))]


def scatter_core(keep, send):
    return [added(mine, other).astype(BF16) for mine, other in zip(keep, swap(send, 1))]


def natural(keep, send):
    both = jnp.stack([keep, send], axis=1)
    return both.reshape(-1, both.shape[-1])


def body(
    tokens,
    lengths,
    routes,
    ln1_gain,
    ln1_bias,
    ln2_gain,
    ln2_bias,
    w_qkv,
    w_proj,
    w_router,
    old_in,
    old_out,
    new_in,
    new_out,
    cotangent,
):
    group = lax.axis_size("expert")
    me = lax.axis_index("expert")
    token_rows = tokens[0]
    cot_rows = cotangent[0]
    seq, width = token_rows.shape
    experts = w_router.shape[1]
    local = experts // group
    per = old_in.shape[0]
    capacity = max(4, seq // experts)
    scales = jnp.stack([ln1_gain, ln1_bias, ln2_gain, ln2_bias])

    def go(block, shift):
        if shift == 0:
            return block
        return lax.ppermute(block, "expert", [(i, (i + shift) % group) for i in range(group)])

    def trade(blocks):
        return lax.all_to_all(blocks, "expert", 0, 0, tiled=True)

    def come(block, shift):
        if shift == 0:
            return block
        return lax.ppermute(block, "expert", [(i, (i - shift) % group) for i in range(group)])

    fast = group == 4 and lax.axis_size("batch") == 8 and per == 1 and experts == 8
    at = jnp.stack([lax.axis_index("batch"), me]).astype(jnp.int32) if fast else jnp.zeros((2,), jnp.int32)
    me_one = jnp.full((1,), me, jnp.int32)
    pairs = width // LANES
    first_half = pairs // 2
    halves = ((0, first_half), (first_half, pairs - first_half))
    if fast:
        pair_in = jnp.stack([new_in[0], old_in[0]])
        pair_out = jnp.stack([new_out[0], old_out[0]])
        in_full = near(pair_in)
    slots, slots_t, sent_grads = route_call(
        lengths, me_one, routes[0], cot_rows, experts, group, capacity
    )
    grads = trade(sent_grads)
    token_rows, slots = tie(token_rows, slots)
    normed1, qkv = qkv_call(token_rows, scales, w_qkv)
    mixed_low, lse_low = attend_call(lengths, qkv, *halves[0])
    if fast:
        qkv, mixed_low, pair_in, pair_out, in_full[0], in_full[1] = tie(
            qkv, mixed_low, pair_in, pair_out, *in_full
        )
        in_half = relay(*in_full)
        in_other = [swap(part, 1) for part in (pair_in, *in_full)]
    mixed_high, lse_high = attend_call(lengths, qkv, *halves[1])
    if fast:
        mixed_high, pair_out, *tied = tie(mixed_high, pair_out, *in_half, *in_other)
        in_half, in_other = tied[:2], tied[2:]
        out_full = near(pair_out)
    mixed = (mixed_low, mixed_high)
    residual, *sent_rows = project_call(
        mixed, token_rows, w_proj, scales, slots, group, local, capacity
    )
    rows = [go(sent_rows[shift], shift) for shift in range(group)]
    if fast:
        rows[1], rows[3], pair_out, *tied = tie(rows[1], rows[3], pair_out, *out_full, *in_half)
        out_full, in_half = tied[:2], tied[2:]
        out_half = relay(*out_full)
        in_parts = [pair_in, *in_full, *in_half]
        out_parts = [pair_out, *out_full, *out_half]
        in_parts += in_other + [swap(part, 1) for part in in_half]
        out_parts += [swap(part, 1) for part in out_parts]
        weights = {True: (0, in_parts, out_parts), False: (1, in_parts, out_parts)}
    else:
        weights = {
            trained: (0, gather_shards(w_in), gather_shards(w_out))
            for trained, w_in, w_out in ((True, new_in, new_out), (False, old_in, old_out))
        }
    core, chip = (at[0] & 1, at[0] >> 1) if fast else (0, 0)
    router = jnp.pad(w_router, ((0, 0), (0, LANES - experts)))
    router_t = jnp.pad(w_router.T, ((0, LANES - experts), (0, 0)))
    outs, backs, router_sum = [], {}, 0.0
    half = experts // 2
    for trained in (True, False):
        for index in range(per):
            place = index + (per if trained else 0)
            own = jnp.stack([me * per + index + (half if trained else 0), core, chip, me]).astype(jnp.int32)
            got = expert_call(
                trained,
                place,
                local,
                own,
                rows,
                grads,
                router,
                router_t,
                outs,
                weights[trained][0] + index,
                *weights[trained][1:],
            )
            outs = [got[0]]
            sent = got[1 : group + 1]
            if fast and not trained:
                tied = tie(*sent, *backs[1])
                sent, backs[1] = tied[:group], tied[group:]
            backs[place] = [come(sent[shift], shift) for shift in range(group)]
            router_sum = router_sum + got[group + 1]
            if trained:
                in_keep, in_send, out_keep, out_send = got[group + 2 :]
    returned = [backs[p][shift] for shift in range(group) for p in range(local)]
    if fast:
        in_rs = scatter_core(in_keep, in_send)
        out_rs = scatter_core(out_keep, out_send)
        in_got = [swap(in_rs[chip], 2 * chip) for chip in (1, 2)]
        tied = tie(*returned, *in_got, *in_rs, *out_rs)
        returned, in_got, in_rs, out_rs = tied[:-10], tied[-10:-8], tied[-8:-4], tied[-4:]
        in_got.append(swap(in_rs[3], 6))
        out_got = [swap(out_rs[chip], 2 * chip) for chip in (1, 2)]
    dres, dmixed, proj_keep, proj_send, sums2 = middle_call(
        slots_t, residual, cot_rows, scales, mixed, w_proj, at, returned
    )
    if fast:
        dmixed, outs[0] = tie(dmixed, outs[0])
    else:
        natural_in = natural(in_keep, in_send)
        natural_out = natural(out_keep, out_send)
    back_outs = trade(outs[0])
    dq_low, keep_low, send_low = attend_back_call(
        lengths, qkv, dmixed, mixed_low, lse_low, normed1, at, *halves[0]
    )
    if fast:
        halves_low = sum_core((keep_low, proj_keep), (send_low, proj_send))
        dmixed, dq_low, in_got[2], out_got[0], out_got[1], out_rs[3] = tie(
            dmixed, dq_low, in_got[2], *out_got, out_rs[3]
        )
        out_got.append(swap(out_rs[3], 6))
    dq_high, keep_high, send_high = attend_back_call(
        lengths, qkv, dmixed, mixed_high, lse_high, normed1, at, *halves[1]
    )
    if fast:
        dq_high, keep_high, back_outs, out_got[2], *halves_low = tie(
            dq_high, keep_high, back_outs, out_got[2], *halves_low
        )
        low = to_chips(halves_low)
        halves_high = sum_core((keep_high,), (send_high,))
    input_grad, sums1 = last_call((dq_low, dq_high), token_rows, dres, scales, w_qkv)
    if fast:
        sums1, *halves_high = tie(sums1, *halves_high)
        high = to_chips(halves_high)
        small = jnp.concatenate([router_sum.T[:experts], sums1[:2], sums2[:2]], axis=0)
        low = give(total(low), 1)
        tied = tie(*low, *high)
        low = give(total(tied[:2]), 2)
        high = give(total(tied[2:]), 1)
        tied = tie(*low, *high)
        own_low = total(tied[:2])[0]
        low = [own_low, across(own_low, 2)]
        high = give(total(tied[2:]), 2)
        tied = tie(*low, *high)
        low = jnp.stack(tied[:2])
        low = [low, across(low, 1)]
        own_high = total(tied[2:])[0]
        mine = small.astype(BF16).reshape(1, *own_high.shape[1:])
        high = [jnp.concatenate([own_high, mine])]
        high.append(across(high[0], 2))
        tied = tie(*low, *high)
        column_low = jnp.concatenate(tied[:2]).reshape(-1, *own_low.shape[1:])
        chips_low = spread_chips(column_low)
        parts = own_high.shape[0]
        mine = total([block[parts:] for block in tied[2:]])
        high = jnp.concatenate([block[:parts] for block in tied[2:]] + [mine])
        high = [high, across(high, 1)]
        mine = total([block[2 * parts :] for block in high])
        chips_high = spread_chips(jnp.concatenate([block[: 2 * parts] for block in high] + [mine]))
        pieces_low = spread_cores(chips_low)
        qkv_grad, proj_grad = unpack_call(at, pieces_low, 0)
        qkv_grad, *chips_high = tie(qkv_grad, *chips_high)
        pieces_high = spread_cores(chips_high)
        small = added(*[piece[4 * parts] for piece in pieces_high]).reshape(small.shape)
        new_in_grad = added(in_rs[0], *in_got)
        new_out_grad = added(out_rs[0], *out_got)
    else:
        pieces_low = sum_all((keep_low, proj_keep), (send_low, proj_send))
        pieces_high = sum_all((keep_high,), (send_high,))
        small = jnp.concatenate([router_sum.T[:experts], sums1[:2], sums2[:2]], axis=0)
        small = jnp.sum(lax.all_gather(small, ("expert", "batch"), axis=0), axis=0)
        new_in_grad = lax.psum_scatter(natural_in, "batch", scatter_dimension=0, tiled=True)
        new_out_grad = lax.psum_scatter(natural_out, "batch", scatter_dimension=0, tiled=True)
    output = combine_call(me_one, slots_t, residual, back_outs)
    if not fast:
        qkv_grad, proj_grad = unpack_call(at, pieces_low, 0)
    (qkv_grad,) = unpack_call(at, pieces_high, 1, qkv_grad)
    return (
        output[None],
        input_grad[None],
        small[experts],
        small[experts + 1],
        small[experts + 2],
        small[experts + 3],
        qkv_grad,
        proj_grad,
        small[:experts].T,
        new_in_grad.astype(F32)[None],
        new_out_grad.astype(F32)[None],
    )


def solution(mesh):
    rows = P(("expert", "batch"), None, None)
    weights = P("expert", "batch", None)
    placed = (
        (rows, P(("expert", "batch")), rows)
        + (P(),) * 7
        + (weights,) * 4
        + (rows,)
    )
    return jax.shard_map(
        body,
        mesh=mesh,
        in_specs=placed,
        out_specs=(rows, rows) + (P(),) * 7 + (weights, weights),
        check_vma=False,
    )
```

time: 439 us -> 373 us (0.85)
  waiting for transfers between devices: 199 us -> 94.2 us
  starting transfers between devices: 47.9 us -> 65.9 us
  Pallas kernels: 157 us -> 171 us
  between operations: 15.4 us -> 2.43 us
  local copies, waits for them, and re-layouts: 10.3 us -> 19.1 us
  other arithmetic: 9.15 us -> 16.1 us
    ppermute x16 -> x49, waiting for transfers between devices: 62.7 us -> 30 us  [swap(): return lax.ppermute(block, 'batch', [(i, i ^ bits) for i in range(size)])]
    ppermute x12 -> x6, waiting for transfers between devices: 40.5 us -> 15.3 us  [come(): lax.ppermute(block, 'expert', [(i, (i - shift) % group) for i in range(gr...]
    ppermute x16 -> x49, starting transfers between devices: 12.5 us -> 35.5 us  [swap(): return lax.ppermute(block, 'batch', [(i, i ^ bits) for i in range(size)])]
    ppermute x6 -> x3, waiting for transfers between devices: 58.6 us -> 35.6 us  [go(): lax.ppermute(block, 'expert', [(i, (i + shift) % group) for i in range(gr...]
    all_gather x4 -> x0, waiting for transfers between devices: 17.2 us -> none  [the longest x1 17.1 us: body(): full_old_out = lax.all_gather(old_out, 'batch', axis=1, tiled=True)]
    pallas_call x6 -> x9, Pallas kernels: 110 us -> 125 us  [the longest x2 47.5 us: expert_call(): pl.pallas_call(functools.partial(expert_kernel, trained, group, len(held)...]
    ppermute x12 -> x6, starting transfers between devices: 17.3 us -> 5.6 us  [come(): lax.ppermute(block, 'expert', [(i, (i - shift) % group) for i in range(gr...]
    all_to_all x0 -> x2, starting transfers between devices: none -> 9.1 us  [trade(): return lax.all_to_all(blocks, 'expert', 0, 0, tiled=True)]
  transfers between devices with their start and end apart: 49 -> 68, of which waited for: 18 -> 25; matrix products, arithmetic and copies ran while one was open for 3% -> 7% of each run, Pallas kernels for 36% -> 34%
where the time goes in v3:
time: 373 us; the launch traced here: 369 us
  Pallas kernels  171 us (46%)
  waiting for transfers between devices  94.2 us (25%)
  starting transfers between devices  65.9 us (18%)
  local copies, waits for them, and re-layouts  19.1 us (5%)
  other arithmetic  16.1 us (4%)
    pallas_call x2, Pallas kernels, expert_call(): pl.pallas_call(functools.partial(expert_kernel, trained, group, len(held)...  47.5 us
    pallas_call x2, Pallas kernels, attend_back_call(): pl.pallas_call(attend_back_kernel, grid=(count,), in_specs=[smem()] + [pl...  35.7 us
    ppermute x3, waiting for transfers between devices, go(): lax.ppermute(block, 'expert', [(i, (i + shift) % group) for i in range(gr...  35.6 us
    ppermute x49, starting transfers between devices, swap(): return lax.ppermute(block, 'batch', [(i, i ^ bits) for i in range(size)])  35.5 us
    ppermute x49, waiting for transfers between devices, swap(): return lax.ppermute(block, 'batch', [(i, i ^ bits) for i in range(size)])  30 us
    pallas_call x2, Pallas kernels, attend_call(): pl.pallas_call(attend_kernel, grid=(count,), in_specs=[smem()] + [pl.Bloc...  26 us
    ppermute x6, waiting for transfers between devices, come(): lax.ppermute(block, 'expert', [(i, (i - shift) % group) for i in range(gr...  15.3 us
    pallas_call x1, Pallas kernels, middle_call(): pl.pallas_call(functools.partial(middle_kernel, len(parts)), grid=(seq //...  13.4 us
  transfers between devices with their start and end apart: 68, of which 25 were waited for; matrix products, arithmetic and copies ran while one was open for 7% of the time, Pallas kernels for 34%

profile of v3, /device:TPU:0, one launch (start us, length us, event | category | flops | bytes accessed | tf_op | source)
XLA Modules:
  0.0 369.0 jit_solution(14111406528275923751)
XLA Ops:
  0.7 2.0 constant_dynamic-update-slice_fusion.1
  3.5 3.0 collective-permute-start
  6.5 1.5 collective-permute-start.1
  9.7 6.0 %route.1 = (s32[8,1024]{1,0:T(8,128)}, s32[1024,128]{1,0:T(8,128)}, bf16[4,2,128,896]{3,2,1,0:T(8,128)(2,1)}) custom-call(s32[1]{0:T(128)S(6)} %copy.41.len_ref, s32[1]{0:T(128)} %bitcast.me_ref, s32[2,1024]{1,0:T(2,128)} %copy.35.route_ref, s32[1024,2]{1,0:T(8,128)} %bitcast.69, bf16[1024,768]{1,0:T(8,128)(2,1)} %bitcast.80), custom_call_target="tpu_custom_call" | custom-call | flops 6270000128 | bytes 17100000 | tf_op jit(solution)/shard_map/route/pallas_call | solution.py:347
  15.7 5.2 %all-to-all-start = ((bf16[4,2,128,896]{3,2,1,0:T(8,128)(2,1)}), bf16[4,2,128,896]{3,2,1,0:T(8,128)(2,1)S(1)}, u32[]{:S(2)}, u32[]{:S(2)}) async-start(bf16[4,2,128,896]{3,2,1,0:T(8,128)(2,1)} %get-tuple-element.170), calls=%async_computation | async-start | bytes 3670016 | tf_op jit(solution)/shard_map/all_to_all | solution.py:875
  22.8 8.5 %norm_qkv.1 = (bf16[1024,768]{1,0:T(8,128)(2,1)}, bf16[1024,2304]{1,0:T(8,128)(2,1)}) custom-call(bf16[1024,768]{1,0:T(8,128)(2,1)} %bitcast.82, f32[4,768]{1,0:T(4,128)} %pad_maximum_fusion.11.scale_ref.gain_ref, bf16[768,2304]{1,0:T(8,128)(2,1)} %w_ref.7), custom_call_target="tpu_custom_call" | custom-call | flops 9569999872 | bytes 26100000 | tf_op jit(solution)/shard_map/norm_qkv/pallas_call | solution.py:80
  31.3 13.0 %attend.2 = (bf16[1024,384]{1,0:T(8,128)(2,1)}, f32[3,8,1024]{2,1,0:T(8,128)}) custom-call(s32[1]{0:T(128)S(6)} %copy.41.len_ref, bf16[1024,2304]{1,0:T(8,128)(2,1)} %get-tuple-element.152.q_ref.k_ref.v_ref, bf16[1024,2304]{1,0:T(8,128)(2,1)} %get-tuple-element.152.q_ref.k_ref.v_ref, bf16[1024,2304]{1,0:T(8,128)(2,1)} %get-tuple-element.152.q_ref.k_ref.v_ref), custom_call_target="tpu_custom_call" | custom-call | flops 13200000000 | bytes 36000000 | tf_op jit(solution)/shard_map/attend/pallas_call | solution.py:152
  48.2 13.0 %attend.3 = (bf16[1024,384]{1,0:T(8,128)(2,1)}, f32[3,8,1024]{2,1,0:T(8,128)}) custom-call(s32[1]{0:T(128)S(6)} %copy.41.len_ref, bf16[1024,2304]{1,0:T(8,128)(2,1)} %get-tuple-element.152.q_ref.k_ref.v_ref, bf16[1024,2304]{1,0:T(8,128)(2,1)} %get-tuple-element.152.q_ref.k_ref.v_ref, bf16[1024,2304]{1,0:T(8,128)(2,1)} %get-tuple-element.152.q_ref.k_ref.v_ref), custom_call_target="tpu_custom_call" | custom-call | flops 13200000000 | bytes 36000000 | tf_op jit(solution)/shard_map/attend/pallas_call | solution.py:152
  61.2 1.2 collective-permute-done.2.refs_10_
  63.3 1.5 collective-permute-start.9
  64.8 8.8 %project_dispatch.1 = (f32[1024,768]{1,0:T(8,128)}, bf16[2,128,768]{2,1,0:T(8,128)(2,1)}, bf16[2,128,768]{2,1,0:T(8,128)(2,1)}, bf16[2,128,768]{2,1,0:T(8,128)(2,1)}, bf16[2,128,768]{2,1,0:T(8,128)(2,1)}) custom-call(bf16[1024,384]{1,0:T(8,128)(2,1)} %get-tuple-element.151.low_ref.o_ref, bf16[1024,384]{1,0:T(8,128)(2,1)} %get-tuple-element.158.high_ref.o_ref, ...), custom_call_target="tpu_custom_call" | custom-call | flops 9680000000 | bytes 26400000 | tf_op jit(solution)/shard_map/project_dispatch/pallas_call | solution.py:395
  73.6 2.1 collective-permute-start.7
  75.7 2.1 collective-permute-start.8
  77.9 9.9 %collective-permute-done.7.refs_1_ = bf16[2,128,768]{2,1,0:T(8,128)(2,1)S(1)} collective-permute-done((bf16[2,128,768]{2,1,0:T(8,128)(2,1)}, bf16[2,128,768]{2,1,0:T(8,128)(2,1)S(1)}, u32[]{:S(2)}, u32[]{:S(2)}) %collective-permute-start.7) | collective-permute-done | bytes 393248 | tf_op jit(solution)/shard_map/ppermute | solution.py:872
  87.7 7.1 %collective-permute-done.8.refs_3_ = bf16[2,128,768]{2,1,0:T(8,128)(2,1)S(1)} collective-permute-done((bf16[2,128,768]{2,1,0:T(8,128)(2,1)}, bf16[2,128,768]{2,1,0:T(8,128)(2,1)S(1)}, u32[]{:S(2)}, u32[]{:S(2)}) %collective-permute-start.8) | collective-permute-done | bytes 393248 | tf_op jit(solution)/shard_map/ppermute | solution.py:872
  94.9 1.2 slice.188
  97.8 1.6 collective-permute-start.15
  100.7 18.6 %collective-permute-done.11.refs_2_ = bf16[2,128,768]{2,1,0:T(8,128)(2,1)} collective-permute-done((bf16[2,128,768]{2,1,0:T(8,128)(2,1)S(1)}, bf16[2,128,768]{2,1,0:T(8,128)(2,1)}, u32[]{:S(2)}, u32[]{:S(2)}) %collective-permute-start.11) | collective-permute-done | bytes 393248 | tf_op jit(solution)/shard_map/ppermute | solution.py:872
  126.5 27.0 %experts_new.1 = (bf16[4,2,128,768]{3,2,1,0:T(8,128)(2,1)}, bf16[128,768]{1,0:T(8,128)(2,1)}, bf16[128,768]{1,0:T(8,128)(2,1)}, bf16[128,768]{1,0:T(8,128)(2,1)}...) custom-call(s32[4]{0:T(128)} %get-tuple-element.314.own_ref, ...), custom_call_target="tpu_custom_call" | custom-call | flops 25300000768 | bytes 69000000 | tf_op jit(solution)/shard_map/experts_new/pallas_call | solution.py:525
  155.2 1.9 collective-permute-start.23
  157.1 1.2 collective-permute-done.27
  158.3 2.5 fusion.3
  161.3 1.7 collective-permute-done.21.refs_3_
  163.6 20.5 %experts_old.1 = (bf16[4,2,128,768]{3,2,1,0:T(8,128)(2,1)}, bf16[128,768]{1,0:T(8,128)(2,1)}, bf16[128,768]{1,0:T(8,128)(2,1)}, bf16[128,768]{1,0:T(8,128)(2,1)}...) custom-call(s32[4]{0:T(128)} %get-tuple-element.313.own_ref, ...), custom_call_target="tpu_custom_call", output_to_operand_aliasing={{0}: (28, {})} | custom-call | flops 18699999232 | bytes 51000000 | tf_op jit(solution)/shard_map/experts_old/pallas_call | solution.py:525
  184.1 2.0 collective-permute-start.24
  187.2 1.5 fusion.7
  188.8 2.9 collective-permute-done.24.refs_2_
  191.7 10.6 %collective-permute-done.25.refs_4_ = bf16[128,768]{1,0:T(8,128)(2,1)S(1)} collective-permute-done((bf16[128,768]{1,0:T(8,128)(2,1)}, bf16[128,768]{1,0:T(8,128)(2,1)S(1)}, u32[]{:S(2)}, u32[]{:S(2)}) %collective-permute-start.25) | collective-permute-done | bytes 196640 | tf_op jit(solution)/shard_map/ppermute | solution.py:880
  203.0 13.4 %middle_back.1 = (f32[1024,768]{1,0:T(8,128)}, bf16[1024,768]{1,0:T(8,128)(2,1)}, bf16[4,4,2,24,384]{4,3,2,1,0:T(8,128)(2,1)}, bf16[4,4,2,24,384]{4,3,2,1,0:T(8,128)(2,1)}, f32[8,768]{1,0:T(8,128)}) custom-call(s32[1024,128]{1,0:T(8,128)} %get-tuple-element.146.slot_ref, f32[1024,768]{1,0:T(8,128)} %get-tuple-element.160.res_ref, ...), custom_call_target="tpu_custom_call" | custom-call | flops 14300000256 | bytes 39000000 | tf_op jit(solution)/shard_map/middle_back/pallas_call | solution.py:631
  216.5 3.9 %all-to-all-start.1 = ((bf16[4,2,128,768]{3,2,1,0:T(8,128)(2,1)}), bf16[4,2,128,768]{3,2,1,0:T(8,128)(2,1)S(1)}, u32[]{:S(2)}, u32[]{:S(2)}) async-start(bf16[4,2,128,768]{3,2,1,0:T(8,128)(2,1)} %get-tuple-element.222), calls=%async_computation.1 | async-start | bytes 3145728 | tf_op jit(solution)/shard_map/all_to_all | solution.py:875
  220.4 1.5 collective-permute-start.31
  223.9 17.8 %attend_back.2 = (bf16[3,1024,384]{2,1,0:T(8,128)(2,1)}, bf16[4,4,3,24,384]{4,3,2,1,0:T(8,128)(2,1)}, bf16[4,4,3,24,384]{4,3,2,1,0:T(8,128)(2,1)}) custom-call(s32[1]{0:T(128)S(6)} %copy.41.len_ref, bf16[1024,2304]{1,0:T(8,128)(2,1)} %get-tuple-element.152.q_ref.k_ref.v_ref, bf16[1024,2304]{1,0:T(8,128)(2,1)} %get-tuple-element.152.q_ref.k_ref.v_ref, ...), custom_call_target="tpu_custom_call" | custom-call | flops 5500000256 | bytes 15000000 | tf_op jit(solution)/shard_map/attend_back/pallas_call | solution.py:256
  242.2 5.7 %collective-permute-done.32 = bf16[384,768]{1,0:T(8,128)(2,1)S(1)} collective-permute-done((bf16[384,768]{1,0:T(8,128)(2,1)}, bf16[384,768]{1,0:T(8,128)(2,1)S(1)}, u32[]{:S(2)}, u32[]{:S(2)}) %collective-permute-start.32) | collective-permute-done | bytes 589856 | tf_op jit(solution)/shard_map/ppermute | solution.py:752
  248.9 1.5 collective-permute-start.34
  250.4 17.9 %attend_back.3 = (bf16[3,1024,384]{2,1,0:T(8,128)(2,1)}, bf16[4,4,3,24,384]{4,3,2,1,0:T(8,128)(2,1)}, bf16[4,4,3,24,384]{4,3,2,1,0:T(8,128)(2,1)}) custom-call(s32[1]{0:T(128)S(6)} %copy.41.len_ref, bf16[1024,2304]{1,0:T(8,128)(2,1)} %get-tuple-element.152.q_ref.k_ref.v_ref, bf16[1024,2304]{1,0:T(8,128)(2,1)} %get-tuple-element.152.q_ref.k_ref.v_ref, ...), custom_call_target="tpu_custom_call" | custom-call | flops 5500000256 | bytes 15000000 | tf_op jit(solution)/shard_map/attend_back/pallas_call | solution.py:256
  272.1 1.4 collective-permute-start.38
  273.5 1.4 collective-permute-start.39
  274.9 10.1 %last_back.1 = (f32[1024,768]{1,0:T(8,128)}, f32[8,768]{1,0:T(8,128)}) custom-call(bf16[3,1024,384]{2,1,0:T(8,128)(2,1)} %get-tuple-element.229.low_ref, bf16[3,1024,384]{2,1,0:T(8,128)(2,1)} %get-tuple-element.230.high_ref, bf16[1024,768]{1,0:T(8,128)(2,1)} %bitcast.84, f32[1024,768]{1,0:T(8,128)} %get-tuple-element.231.dres_ref, ...), custom_call_target="tpu_custom_call" | custom-call | flops 5500000256 | bytes 15000000 | tf_op jit(solution)/shard_map/last_back/pallas_call | solution.py:679
  285.1 1.5 fusion.15
  287.3 1.4 collective-permute-start.43
  288.7 1.4 collective-permute-start.44
  291.4 1.8 collective-permute-start.40
  293.2 2.6 collective-permute-done.42
  295.8 3.7 %collective-permute-done.43 = bf16[4,3,24,384]{3,2,1,0:T(8,128)(2,1)S(1)} collective-permute-done((bf16[4,3,24,384]{3,2,1,0:T(8,128)(2,1)S(1)}, bf16[4,3,24,384]{3,2,1,0:T(8,128)(2,1)S(1)}, u32[]{:S(2)}, u32[]{:S(2)}) %collective-permute-start.43) | collective-permute-done | bytes 221216 | tf_op jit(solution)/shard_map/ppermute | solution.py:752
  299.7 1.8 collective-permute-start.46
  301.6 2.4 collective-permute-start.45
  305.7 2.4 collective-permute-done.45
  308.1 1.5 collective-permute-start.48
  309.7 1.5 collective-permute-start.47
  311.3 2.2 collective-permute-done.48
  313.4 3.4 collective-permute-done.47
  317.9 4.5 %collective-permute-done.50 = bf16[4,24,384]{2,1,0:T(8,128)(2,1)S(1)} collective-permute-done((bf16[4,24,384]{2,1,0:T(8,128)(2,1)S(1)}, bf16[4,24,384]{2,1,0:T(8,128)(2,1)S(1)}, u32[]{:S(2)}, u32[]{:S(2)}) %collective-permute-start.50) | collective-permute-done | bytes 73760 | tf_op jit(solution)/shard_map/ppermute | solution.py:757
  323.3 2.4 collective-permute-start.52
  325.8 1.5 collective-permute-start.56
  327.3 2.6 add_bitcast_fusion.1
  330.6 2.0 collective-permute-done.52.refs_2_
  332.6 5.0 %collective-permute-done.54.refs_4_ = bf16[20,24,384]{2,1,0:T(8,128)(2,1)S(1)} collective-permute-done((bf16[20,24,384]{2,1,0:T(8,128)(2,1)S(1)}, bf16[20,24,384]{2,1,0:T(8,128)(2,1)S(1)}, u32[]{:S(2)}, u32[]{:S(2)}) %collective-permute-start.54) | collective-permute-done | bytes 368672 | tf_op jit(solution)/shard_map/ppermute | solution.py:752
  338.1 6.2 %combine.1 = f32[1024,768]{1,0:T(8,128)} custom-call(s32[1]{0:T(128)} %bitcast.me_ref, s32[1024,128]{1,0:T(8,128)} %get-tuple-element.146.slot_ref, f32[1024,768]{1,0:T(8,128)} %get-tuple-element.160.res_ref, bf16[4,2,128,768]{3,2,1,0:T(8,128)(2,1)} %copy-done.3), custom_call_target="tpu_custom_call" | custom-call | flops 6819999744 | bytes 18600000 | tf_op jit(solution)/shard_map/combine/pallas_call | solution.py:581
  345.3 1.2 collective-permute-start.60
  346.5 1.5 collective-permute-start.61
  349.5 5.2 %unpack.2 = (f32[768,2304]{1,0:T(8,128)}, f32[768,768]{1,0:T(8,128)}) custom-call(s32[2]{0:T(128)} %pad_add_fusion.at_ref, bf16[20,24,384]{2,1,0:T(8,128)(2,1)} %bitcast.75, bf16[20,24,384]{2,1,0:T(8,128)(2,1)} %copy-done.48, bf16[20,24,384]{2,1,0:T(8,128)(2,1)} %copy-done.45, bf16[20,24,384]{2,1,0:T(8,128)(2,1)} %copy-done.49, ...), custom_call_target="tpu_custom_call" | custom-call | flops 4400000000 | bytes 12000000 | tf_op jit(solution)/shard_map/unpack/pallas_call | solution.py:735
  354.8 3.3 collective-permute-done.60.refs_4_
  359.2 2.3 add_bitcast_fusion
  364.8 4.0 %unpack.3 = f32[768,2304]{1,0:T(8,128)} custom-call(s32[2]{0:T(128)} %pad_add_fusion.at_ref, bf16[13,24,384]{2,1,0:T(8,128)(2,1)} %copy-done.20, bf16[13,24,384]{2,1,0:T(8,128)(2,1)} %copy-done.30, bf16[13,24,384]{2,1,0:T(8,128)(2,1)} %copy-done.27, bf16[13,24,384]{2,1,0:T(8,128)(2,1)} %copy-done.31, ...), custom_call_target="tpu_custom_call", output_to_operand_aliasing={{}: (9, {})} | custom-call | flops 4400000000 | bytes 12000000 | tf_op jit(solution)/shard_map/unpack/pallas_call | solution.py:735
  (266 shorter events, 44.5 us)
Async XLA Ops:
  3.5 40.8 %collective-permute-start = (bf16[2,96,3072]{2,1,0:T(8,128)(2,1)}, bf16[2,96,3072]{2,1,0:T(8,128)(2,1)}, u32[]{:S(2)}, u32[]{:S(2)}) collective-permute-start(bf16[2,96,3072]{2,1,0:T(8,128)(2,1)} %constant_dynamic-update-slice_fusion.refs_7_), channel_id=1, source_target_pairs={{0,2},{1,3},{2,0},{3,1},{4,6},{5,7},{6,4},{7,5},{8,10},{9,11},{10,... | collective-permute-start | bytes 3538952 | tf_op jit(solution)/shard_map/ppermute | solution.py:752
  6.5 37.8 %collective-permute-start.1 = (bf16[2,96,3072]{2,1,0:T(8,128)(2,1)}, bf16[2,96,3072]{2,1,0:T(8,128)(2,1)}, u32[]{:S(2)}, u32[]{:S(2)}) collective-permute-start(bf16[2,96,3072]{2,1,0:T(8,128)(2,1)} %constant_dynamic-update-slice_fusion.refs_7_), channel_id=1, source_target_pairs={{0,4},{1,5},{2,6},{3,7},{4,0},{5,1},{6,2},{7,3},{8,12},{9,13},{10,... | collective-permute-start | bytes 3538952 | tf_op jit(solution)/shard_map/ppermute | solution.py:752
  15.7 108.7 %all-to-all-start = ((bf16[4,2,128,896]{3,2,1,0:T(8,128)(2,1)}), bf16[4,2,128,896]{3,2,1,0:T(8,128)(2,1)S(1)}, u32[]{:S(2)}, u32[]{:S(2)}) async-start(bf16[4,2,128,896]{3,2,1,0:T(8,128)(2,1)} %get-tuple-element.170), calls=%async_computation | async-start | bytes 3670016 | tf_op jit(solution)/shard_map/all_to_all | solution.py:875
  45.4 17.3 %collective-permute-start.5 = (bf16[2,96,3072]{2,1,0:T(8,128)(2,1)}, bf16[2,96,3072]{2,1,0:T(8,128)(2,1)S(1)}, u32[]{:S(2)}, u32[]{:S(2)}) collective-permute-start(bf16[2,96,3072]{2,1,0:T(8,128)(2,1)} %collective-permute-done.refs_8_), channel_id=1, source_target_pairs={{0,1},{1,0},{2,3},{3,2},{4,5},{5,4},{6,7},{7,6},{8,9},{9,8},{10,11... | collective-permute-start | bytes 3538952 | tf_op jit(solution)/shard_map/ppermute | solution.py:752
  46.6 16.1 %collective-permute-start.6 = (bf16[2,96,3072]{2,1,0:T(8,128)(2,1)}, bf16[2,96,3072]{2,1,0:T(8,128)(2,1)S(1)}, u32[]{:S(2)}, u32[]{:S(2)}) collective-permute-start(bf16[2,96,3072]{2,1,0:T(8,128)(2,1)} %collective-permute-done.1.refs_9_), channel_id=1, source_target_pairs={{0,1},{1,0},{2,3},{3,2},{4,5},{5,4},{6,7},{7,6},{8,9},{9,8},{10,11... | collective-permute-start | bytes 3538952 | tf_op jit(solution)/shard_map/ppermute | solution.py:752
  47.1 15.3 %collective-permute-start.2 = (bf16[2,48,3072]{2,1,0:T(8,128)(2,1)S(1)}, bf16[2,48,3072]{2,1,0:T(8,128)(2,1)S(1)}, u32[]{:S(2)}, u32[]{:S(2)}) collective-permute-start(bf16[2,48,3072]{2,1,0:T(8,128)(2,1)S(1)} %slice.186), channel_id=1, source_target_pairs={{0,2},{1,3},{2,0},{3,1},{4,6},{5,7},{6,4},{7,5},{8,10},{9,11},{10,... | collective-permute-start | bytes 1769480 | tf_op jit(solution)/shard_map/ppermute | solution.py:752
  47.6 15.0 %collective-permute-start.3 = (bf16[2,48,3072]{2,1,0:T(8,128)(2,1)S(1)}, bf16[2,48,3072]{2,1,0:T(8,128)(2,1)S(1)}, u32[]{:S(2)}, u32[]{:S(2)}) collective-permute-start(bf16[2,48,3072]{2,1,0:T(8,128)(2,1)S(1)} %slice.187), channel_id=1, source_target_pairs={{0,4},{1,5},{2,6},{3,7},{4,0},{5,1},{6,2},{7,3},{8,12},{9,13},{10,... | collective-permute-start | bytes 1769480 | tf_op jit(solution)/shard_map/ppermute | solution.py:752
  48.2 14.5 %collective-permute-start.4 = (bf16[2,96,3072]{2,1,0:T(8,128)(2,1)}, bf16[2,96,3072]{2,1,0:T(8,128)(2,1)S(1)}, u32[]{:S(2)}, u32[]{:S(2)}) collective-permute-start(bf16[2,96,3072]{2,1,0:T(8,128)(2,1)} %constant_dynamic-update-slice_fusion.refs_7_), channel_id=1, source_target_pairs={{0,1},{1,0},{2,3},{3,2},{4,5},{5,4},{6,7},{7,6},{8,9},{9,8},{10,11... | collective-permute-start | bytes 3538952 | tf_op jit(solution)/shard_map/ppermute | solution.py:752
  62.7 32.2 %collective-permute-start.10 = (bf16[2,384,768]{2,1,0:T(8,128)(2,1)}, bf16[2,384,768]{2,1,0:T(8,128)(2,1)}, u32[]{:S(2)}, u32[]{:S(2)}) collective-permute-start(bf16[2,384,768]{2,1,0:T(8,128)(2,1)} %pad_maximum_fusion.refs_17_), channel_id=1, source_target_pairs={{0,4},{1,5},{2,6},{3,7},{4,0},{5,1},{6,2},{7,3},{8,12},{9,13},{10,... | collective-permute-start | bytes 3538952 | tf_op jit(solution)/shard_map/ppermute | solution.py:752
  63.3 31.6 %collective-permute-start.9 = (bf16[2,384,768]{2,1,0:T(8,128)(2,1)}, bf16[2,384,768]{2,1,0:T(8,128)(2,1)}, u32[]{:S(2)}, u32[]{:S(2)}) collective-permute-start(bf16[2,384,768]{2,1,0:T(8,128)(2,1)} %pad_maximum_fusion.refs_17_), channel_id=1, source_target_pairs={{0,2},{1,3},{2,0},{3,1},{4,6},{5,7},{6,4},{7,5},{8,10},{9,11},{10,... | collective-permute-start | bytes 3538952 | tf_op jit(solution)/shard_map/ppermute | solution.py:752
  73.6 14.1 %collective-permute-start.7 = (bf16[2,128,768]{2,1,0:T(8,128)(2,1)}, bf16[2,128,768]{2,1,0:T(8,128)(2,1)S(1)}, u32[]{:S(2)}, u32[]{:S(2)}) collective-permute-start(bf16[2,128,768]{2,1,0:T(8,128)(2,1)} %get-tuple-element.162), channel_id=1, source_target_pairs={{0,8},{8,16},{16,24},{24,0},{1,9},{9,17},{17,25},{25,1},{2,10},{10... | collective-permute-start | bytes 1179656 | tf_op jit(solution)/shard_map/ppermute | solution.py:872
  75.7 19.2 %collective-permute-start.8 = (bf16[2,128,768]{2,1,0:T(8,128)(2,1)}, bf16[2,128,768]{2,1,0:T(8,128)(2,1)S(1)}, u32[]{:S(2)}, u32[]{:S(2)}) collective-permute-start(bf16[2,128,768]{2,1,0:T(8,128)(2,1)} %get-tuple-element.163), channel_id=1, source_target_pairs={{0,24},{8,0},{16,8},{24,16},{1,25},{9,1},{17,9},{25,17},{2,26},{10... | collective-permute-start | bytes 1179656 | tf_op jit(solution)/shard_map/ppermute | solution.py:872
  96.2 23.1 %collective-permute-start.14 = (bf16[2,192,768]{2,1,0:T(8,128)(2,1)S(1)}, bf16[2,192,768]{2,1,0:T(8,128)(2,1)}, u32[]{:S(2)}, u32[]{:S(2)}) collective-permute-start(bf16[2,192,768]{2,1,0:T(8,128)(2,1)S(1)} %slice.188), channel_id=1, source_target_pairs={{0,2},{1,3},{2,0},{3,1},{4,6},{5,7},{6,4},{7,5},{8,10},{9,11},{10,... | collective-permute-start | bytes 1769480 | tf_op jit(solution)/shard_map/ppermute | solution.py:752
  97.8 21.9 %collective-permute-start.15 = (bf16[2,192,768]{2,1,0:T(8,128)(2,1)S(1)}, bf16[2,192,768]{2,1,0:T(8,128)(2,1)}, u32[]{:S(2)}, u32[]{:S(2)}) collective-permute-start(bf16[2,192,768]{2,1,0:T(8,128)(2,1)S(1)} %slice.189), channel_id=1, source_target_pairs={{0,4},{1,5},{2,6},{3,7},{4,0},{5,1},{6,2},{7,3},{8,12},{9,13},{10,... | collective-permute-start | bytes 1769480 | tf_op jit(solution)/shard_map/ppermute | solution.py:752
  99.4 19.8 %collective-permute-start.11 = (bf16[2,128,768]{2,1,0:T(8,128)(2,1)S(1)}, bf16[2,128,768]{2,1,0:T(8,128)(2,1)}, u32[]{:S(2)}, u32[]{:S(2)}) collective-permute-start(bf16[2,128,768]{2,1,0:T(8,128)(2,1)S(1)} %copy-done.44), channel_id=1, source_target_pairs={{0,16},{8,24},{16,0},{24,8},{1,17},{9,25},{17,1},{25,9},{2,18},{10... | collective-permute-start | bytes 1179656 | tf_op jit(solution)/shard_map/ppermute | solution.py:872
  100.1 26.3 %collective-permute-start.17 = (bf16[2,384,768]{2,1,0:T(8,128)(2,1)}, bf16[2,384,768]{2,1,0:T(8,128)(2,1)}, u32[]{:S(2)}, u32[]{:S(2)}) collective-permute-start(bf16[2,384,768]{2,1,0:T(8,128)(2,1)} %collective-permute-done.9.refs_18_), channel_id=1, source_target_pairs={{0,1},{1,0},{2,3},{3,2},{4,5},{5,4},{6,7},{7,6},{8,9},{9,8},{10,11... | collective-permute-start | bytes 3538952 | tf_op jit(solution)/shard_map/ppermute | solution.py:752
  100.1 19.7 %collective-permute-start.12 = (bf16[2,48,3072]{2,1,0:T(8,128)(2,1)S(1)}, bf16[2,48,3072]{2,1,0:T(8,128)(2,1)S(1)}, u32[]{:S(2)}, u32[]{:S(2)}) collective-permute-start(bf16[2,48,3072]{2,1,0:T(8,128)(2,1)S(1)} %collective-permute-done.2.refs_10_), channel_id=1, source_target_pairs={{0,1},{1,0},{2,3},{3,2},{4,5},{5,4},{6,7},{7,6},{8,9},{9,8},{10,11... | collective-permute-start | bytes 1769480 | tf_op jit(solution)/shard_map/ppermute | solution.py:752
  119.3 7.2 %collective-permute-start.16 = (bf16[2,384,768]{2,1,0:T(8,128)(2,1)}, bf16[2,384,768]{2,1,0:T(8,128)(2,1)}, u32[]{:S(2)}, u32[]{:S(2)}) collective-permute-start(bf16[2,384,768]{2,1,0:T(8,128)(2,1)} %pad_maximum_fusion.refs_17_), channel_id=1, source_target_pairs={{0,1},{1,0},{2,3},{3,2},{4,5},{5,4},{6,7},{7,6},{8,9},{9,8},{10,11... | collective-permute-start | bytes 3538952 | tf_op jit(solution)/shard_map/ppermute | solution.py:752
  119.8 6.7 %collective-permute-start.18 = (bf16[2,384,768]{2,1,0:T(8,128)(2,1)}, bf16[2,384,768]{2,1,0:T(8,128)(2,1)}, u32[]{:S(2)}, u32[]{:S(2)}) collective-permute-start(bf16[2,384,768]{2,1,0:T(8,128)(2,1)} %collective-permute-done.10.refs_19_), channel_id=1, source_target_pairs={{0,1},{1,0},{2,3},{3,2},{4,5},{5,4},{6,7},{7,6},{8,9},{9,8},{10,11... | collective-permute-start | bytes 3538952 | tf_op jit(solution)/shard_map/ppermute | solution.py:752
  119.8 5.6 %collective-permute-start.19 = (bf16[2,192,768]{2,1,0:T(8,128)(2,1)}, bf16[2,192,768]{2,1,0:T(8,128)(2,1)S(1)}, u32[]{:S(2)}, u32[]{:S(2)}) collective-permute-start(bf16[2,192,768]{2,1,0:T(8,128)(2,1)} %collective-permute-done.14.refs_20_), channel_id=1, source_target_pairs={{0,1},{1,0},{2,3},{3,2},{4,5},{5,4},{6,7},{7,6},{8,9},{9,8},{10,11... | collective-permute-start | bytes 1769480 | tf_op jit(solution)/shard_map/ppermute | solution.py:752
  122.1 4.3 %collective-permute-start.20 = (bf16[2,192,768]{2,1,0:T(8,128)(2,1)}, bf16[2,192,768]{2,1,0:T(8,128)(2,1)}, u32[]{:S(2)}, u32[]{:S(2)}) collective-permute-start(bf16[2,192,768]{2,1,0:T(8,128)(2,1)} %collective-permute-done.15.refs_21_), channel_id=1, source_target_pairs={{0,1},{1,0},{2,3},{3,2},{4,5},{5,4},{6,7},{7,6},{8,9},{9,8},{10,11... | collective-permute-start | bytes 1769480 | tf_op jit(solution)/shard_map/ppermute | solution.py:752
  153.5 4.8 %collective-permute-start.27 = (bf16[4,96,3072]{2,1,0:T(8,128)(2,1)}, bf16[4,96,3072]{2,1,0:T(8,128)(2,1)S(1)}, u32[]{:S(2)}, u32[]{:S(2)}) collective-permute-start(bf16[4,96,3072]{2,1,0:T(8,128)(2,1)} %get-tuple-element.197), channel_id=1, source_target_pairs={{0,1},{1,0},{2,3},{3,2},{4,5},{5,4},{6,7},{7,6},{8,9},{9,8},{10,11... | collective-permute-start | bytes 7077896 | tf_op jit(solution)/shard_map/ppermute | solution.py:752
  154.2 31.8 %collective-permute-start.30 = (bf16[4,384,768]{2,1,0:T(8,128)(2,1)}, bf16[4,384,768]{2,1,0:T(8,128)(2,1)S(1)}, u32[]{:S(2)}, u32[]{:S(2)}) collective-permute-start(bf16[4,384,768]{2,1,0:T(8,128)(2,1)} %get-tuple-element.199), channel_id=1, source_target_pairs={{0,1},{1,0},{2,3},{3,2},{4,5},{5,4},{6,7},{7,6},{8,9},{9,8},{10,11... | collective-permute-start | bytes 7077896 | tf_op jit(solution)/shard_map/ppermute | solution.py:752
  154.6 8.4 %collective-permute-start.21 = (bf16[128,768]{1,0:T(8,128)(2,1)}, bf16[128,768]{1,0:T(8,128)(2,1)S(1)}, u32[]{:S(2)}, u32[]{:S(2)}) collective-permute-start(bf16[128,768]{1,0:T(8,128)(2,1)} %get-tuple-element.185), channel_id=1, source_target_pairs={{0,24},{8,0},{16,8},{24,16},{1,25},{9,1},{17,9},{25,17},{2,26},{10... | collective-permute-start | bytes 589832 | tf_op jit(solution)/shard_map/ppermute | solution.py:880
  155.2 28.8 %collective-permute-start.22 = (bf16[128,768]{1,0:T(8,128)(2,1)}, bf16[128,768]{1,0:T(8,128)(2,1)S(1)}, u32[]{:S(2)}, u32[]{:S(2)}) collective-permute-start(bf16[128,768]{1,0:T(8,128)(2,1)} %get-tuple-element.186), channel_id=1, source_target_pairs={{0,16},{8,24},{16,0},{24,8},{1,17},{9,25},{17,1},{25,9},{2,18},{10... | collective-permute-start | bytes 589832 | tf_op jit(solution)/shard_map/ppermute | solution.py:880
  155.2 28.8 %collective-permute-start.23 = (bf16[128,768]{1,0:T(8,128)(2,1)}, bf16[128,768]{1,0:T(8,128)(2,1)S(1)}, u32[]{:S(2)}, u32[]{:S(2)}) collective-permute-start(bf16[128,768]{1,0:T(8,128)(2,1)} %get-tuple-element.187), channel_id=1, source_target_pairs={{0,8},{8,16},{16,24},{24,0},{1,9},{9,17},{17,25},{25,1},{2,10},{10... | collective-permute-start | bytes 589832 | tf_op jit(solution)/shard_map/ppermute | solution.py:880
  160.8 41.5 %collective-permute-start.28 = (bf16[96,3072]{1,0:T(8,128)(2,1)S(1)}, bf16[96,3072]{1,0:T(8,128)(2,1)}, u32[]{:S(2)}, u32[]{:S(2)}) collective-permute-start(bf16[96,3072]{1,0:T(8,128)(2,1)S(1)} %get-tuple-element.288), channel_id=1, source_target_pairs={{0,2},{1,3},{2,0},{3,1},{4,6},{5,7},{6,4},{7,5},{8,10},{9,11},{10,... | collective-permute-start | bytes 1769480 | tf_op jit(solution)/shard_map/ppermute | solution.py:752
  163.1 39.3 %collective-permute-start.29 = (bf16[96,3072]{1,0:T(8,128)(2,1)S(1)}, bf16[96,3072]{1,0:T(8,128)(2,1)}, u32[]{:S(2)}, u32[]{:S(2)}) collective-permute-start(bf16[96,3072]{1,0:T(8,128)(2,1)S(1)} %get-tuple-element.287), channel_id=1, source_target_pairs={{0,4},{1,5},{2,6},{3,7},{4,0},{5,1},{6,2},{7,3},{8,12},{9,13},{10,... | collective-permute-start | bytes 1769480 | tf_op jit(solution)/shard_map/ppermute | solution.py:752
  184.1 7.6 %collective-permute-start.24 = (bf16[128,768]{1,0:T(8,128)(2,1)}, bf16[128,768]{1,0:T(8,128)(2,1)S(1)}, u32[]{:S(2)}, u32[]{:S(2)}) collective-permute-start(bf16[128,768]{1,0:T(8,128)(2,1)} %get-tuple-element.190), channel_id=1, source_target_pairs={{0,24},{8,0},{16,8},{24,16},{1,25},{9,1},{17,9},{25,17},{2,26},{10... | collective-permute-start | bytes 589832 | tf_op jit(solution)/shard_map/ppermute | solution.py:880
  186.1 16.2 %collective-permute-start.25 = (bf16[128,768]{1,0:T(8,128)(2,1)}, bf16[128,768]{1,0:T(8,128)(2,1)S(1)}, u32[]{:S(2)}, u32[]{:S(2)}) collective-permute-start(bf16[128,768]{1,0:T(8,128)(2,1)} %get-tuple-element.192), channel_id=1, source_target_pairs={{0,16},{8,24},{16,0},{24,8},{1,17},{9,25},{17,1},{25,9},{2,18},{10... | collective-permute-start | bytes 589832 | tf_op jit(solution)/shard_map/ppermute | solution.py:880
  186.1 16.2 %collective-permute-start.26 = (bf16[128,768]{1,0:T(8,128)(2,1)}, bf16[128,768]{1,0:T(8,128)(2,1)S(1)}, u32[]{:S(2)}, u32[]{:S(2)}) collective-permute-start(bf16[128,768]{1,0:T(8,128)(2,1)} %get-tuple-element.194), channel_id=1, source_target_pairs={{0,8},{8,16},{16,24},{24,0},{1,9},{9,17},{17,25},{25,1},{2,10},{10... | collective-permute-start | bytes 589832 | tf_op jit(solution)/shard_map/ppermute | solution.py:880
  216.5 54.9 %all-to-all-start.1 = ((bf16[4,2,128,768]{3,2,1,0:T(8,128)(2,1)}), bf16[4,2,128,768]{3,2,1,0:T(8,128)(2,1)S(1)}, u32[]{:S(2)}, u32[]{:S(2)}) async-start(bf16[4,2,128,768]{3,2,1,0:T(8,128)(2,1)} %get-tuple-element.222), calls=%async_computation.1 | async-start | bytes 3145728 | tf_op jit(solution)/shard_map/all_to_all | solution.py:875
  220.4 21.9 %collective-permute-start.31 = (bf16[96,3072]{1,0:T(8,128)(2,1)S(1)}, bf16[96,3072]{1,0:T(8,128)(2,1)S(1)}, u32[]{:S(2)}, u32[]{:S(2)}) collective-permute-start(bf16[96,3072]{1,0:T(8,128)(2,1)S(1)} %get-tuple-element.214), channel_id=1, source_target_pairs={{0,6},{1,7},{2,4},{3,5},{4,2},{5,3},{6,0},{7,1},{8,14},{9,15},{10,... | collective-permute-start | bytes 1769480 | tf_op jit(solution)/shard_map/ppermute | solution.py:752
  221.9 26.1 %collective-permute-start.32 = (bf16[384,768]{1,0:T(8,128)(2,1)}, bf16[384,768]{1,0:T(8,128)(2,1)S(1)}, u32[]{:S(2)}, u32[]{:S(2)}) collective-permute-start(bf16[384,768]{1,0:T(8,128)(2,1)} %get-tuple-element.215), channel_id=1, source_target_pairs={{0,2},{1,3},{2,0},{3,1},{4,6},{5,7},{6,4},{7,5},{8,10},{9,11},{10,... | collective-permute-start | bytes 1769480 | tf_op jit(solution)/shard_map/ppermute | solution.py:752
  222.9 26.0 %collective-permute-start.33 = (bf16[384,768]{1,0:T(8,128)(2,1)}, bf16[384,768]{1,0:T(8,128)(2,1)S(1)}, u32[]{:S(2)}, u32[]{:S(2)}) collective-permute-start(bf16[384,768]{1,0:T(8,128)(2,1)} %get-tuple-element.216), channel_id=1, source_target_pairs={{0,4},{1,5},{2,6},{3,7},{4,0},{5,1},{6,2},{7,3},{8,12},{9,13},{10,... | collective-permute-start | bytes 1769480 | tf_op jit(solution)/shard_map/ppermute | solution.py:752
  241.7 26.8 %collective-permute-start.35 = (bf16[4,4,3,24,384]{4,3,2,1,0:T(8,128)(2,1)}, bf16[4,4,3,24,384]{4,3,2,1,0:T(8,128)(2,1)S(1)}, u32[]{:S(2)}, u32[]{:S(2)}) collective-permute-start(bf16[4,4,3,24,384]{4,3,2,1,0:T(8,128)(2,1)} %get-tuple-element.225), channel_id=1, source_target_pairs={{0,1},{1,0},{2,3},{3,2},{4,5},{5,4},{6,7},{7,6},{8,9},{9,8},{10,11... | collective-permute-start | bytes 2654216 | tf_op jit(solution)/shard_map/ppermute | solution.py:752
  241.7 26.6 %collective-permute-start.36 = (bf16[4,4,2,24,384]{4,3,2,1,0:T(8,128)(2,1)}, bf16[4,4,2,24,384]{4,3,2,1,0:T(8,128)(2,1)S(1)}, u32[]{:S(2)}, u32[]{:S(2)}) collective-permute-start(bf16[4,4,2,24,384]{4,3,2,1,0:T(8,128)(2,1)} %get-tuple-element.227), channel_id=1, source_target_pairs={{0,1},{1,0},{2,3},{3,2},{4,5},{5,4},{6,7},{7,6},{8,9},{9,8},{10,11... | collective-permute-start | bytes 1769480 | tf_op jit(solution)/shard_map/ppermute | solution.py:752
  248.9 22.4 %collective-permute-start.34 = (bf16[384,768]{1,0:T(8,128)(2,1)S(1)}, bf16[384,768]{1,0:T(8,128)(2,1)}, u32[]{:S(2)}, u32[]{:S(2)}) collective-permute-start(bf16[384,768]{1,0:T(8,128)(2,1)S(1)} %copy-done.6), channel_id=1, source_target_pairs={{0,6},{1,7},{2,4},{3,5},{4,2},{5,3},{6,0},{7,1},{8,14},{9,15},{10,... | collective-permute-start | bytes 1769480 | tf_op jit(solution)/shard_map/ppermute | solution.py:752
  268.3 16.8 %collective-permute-start.41 = (bf16[4,4,3,24,384]{4,3,2,1,0:T(8,128)(2,1)}, bf16[4,4,3,24,384]{4,3,2,1,0:T(8,128)(2,1)}, u32[]{:S(2)}, u32[]{:S(2)}) collective-permute-start(bf16[4,4,3,24,384]{4,3,2,1,0:T(8,128)(2,1)} %get-tuple-element.239), channel_id=1, source_target_pairs={{0,1},{1,0},{2,3},{3,2},{4,5},{5,4},{6,7},{7,6},{8,9},{9,8},{10,11... | collective-permute-start | bytes 2654216 | tf_op jit(solution)/shard_map/ppermute | solution.py:752
  271.4 17.3 %collective-permute-start.37 = (bf16[4,5,24,384]{3,2,1,0:T(8,128)(2,1)}, bf16[4,5,24,384]{3,2,1,0:T(8,128)(2,1)S(1)}, u32[]{:S(2)}, u32[]{:S(2)}) collective-permute-start(bf16[4,5,24,384]{3,2,1,0:T(8,128)(2,1)} %pad_maximum_fusion.2), channel_id=1, source_target_pairs={{0,2},{1,3},{2,0},{3,1},{4,6},{5,7},{6,4},{7,5},{8,10},{9,11},{10,... | collective-permute-start | bytes 1105928 | tf_op jit(solution)/shard_map/ppermute | solution.py:752
  272.1 18.0 %collective-permute-start.38 = (bf16[4,5,24,384]{3,2,1,0:T(8,128)(2,1)}, bf16[4,5,24,384]{3,2,1,0:T(8,128)(2,1)S(1)}, u32[]{:S(2)}, u32[]{:S(2)}) collective-permute-start(bf16[4,5,24,384]{3,2,1,0:T(8,128)(2,1)} %pad_maximum_fusion.3), channel_id=1, source_target_pairs={{0,4},{1,5},{2,6},{3,7},{4,0},{5,1},{6,2},{7,3},{8,12},{9,13},{10,... | collective-permute-start | bytes 1105928 | tf_op jit(solution)/shard_map/ppermute | solution.py:752
  273.5 17.7 %collective-permute-start.39 = (bf16[4,5,24,384]{3,2,1,0:T(8,128)(2,1)S(1)}, bf16[4,5,24,384]{3,2,1,0:T(8,128)(2,1)S(1)}, u32[]{:S(2)}, u32[]{:S(2)}) collective-permute-start(bf16[4,5,24,384]{3,2,1,0:T(8,128)(2,1)S(1)} %pad_maximum_fusion.4), channel_id=1, source_target_pairs={{0,6},{1,7},{2,4},{3,5},{4,2},{5,3},{6,0},{7,1},{8,14},{9,15},{10,... | collective-permute-start | bytes 1105928 | tf_op jit(solution)/shard_map/ppermute | solution.py:752
  286.6 9.2 %collective-permute-start.42 = (bf16[4,3,24,384]{3,2,1,0:T(8,128)(2,1)S(1)}, bf16[4,3,24,384]{3,2,1,0:T(8,128)(2,1)S(1)}, u32[]{:S(2)}, u32[]{:S(2)}) collective-permute-start(bf16[4,3,24,384]{3,2,1,0:T(8,128)(2,1)S(1)} %get-tuple-element.241), channel_id=1, source_target_pairs={{0,2},{1,3},{2,0},{3,1},{4,6},{5,7},{6,4},{7,5},{8,10},{9,11},{10,... | collective-permute-start | bytes 663560 | tf_op jit(solution)/shard_map/ppermute | solution.py:752
  287.3 12.2 %collective-permute-start.43 = (bf16[4,3,24,384]{3,2,1,0:T(8,128)(2,1)S(1)}, bf16[4,3,24,384]{3,2,1,0:T(8,128)(2,1)S(1)}, u32[]{:S(2)}, u32[]{:S(2)}) collective-permute-start(bf16[4,3,24,384]{3,2,1,0:T(8,128)(2,1)S(1)} %get-tuple-element.242), channel_id=1, source_target_pairs={{0,4},{1,5},{2,6},{3,7},{4,0},{5,1},{6,2},{7,3},{8,12},{9,13},{10,... | collective-permute-start | bytes 663560 | tf_op jit(solution)/shard_map/ppermute | solution.py:752
  288.7 10.9 %collective-permute-start.44 = (bf16[4,3,24,384]{3,2,1,0:T(8,128)(2,1)S(1)}, bf16[4,3,24,384]{3,2,1,0:T(8,128)(2,1)S(1)}, u32[]{:S(2)}, u32[]{:S(2)}) collective-permute-start(bf16[4,3,24,384]{3,2,1,0:T(8,128)(2,1)S(1)} %get-tuple-element.243), channel_id=1, source_target_pairs={{0,6},{1,7},{2,4},{3,5},{4,2},{5,3},{6,0},{7,1},{8,14},{9,15},{10,... | collective-permute-start | bytes 663560 | tf_op jit(solution)/shard_map/ppermute | solution.py:752
  291.4 8.1 %collective-permute-start.40 = (bf16[2,5,24,384]{3,2,1,0:T(8,128)(2,1)S(1)}, bf16[2,5,24,384]{3,2,1,0:T(8,128)(2,1)S(1)}, u32[]{:S(2)}, u32[]{:S(2)}) collective-permute-start(bf16[2,5,24,384]{3,2,1,0:T(8,128)(2,1)S(1)} %get-tuple-element.301), channel_id=1, source_target_pairs={{0,8},{8,0},{16,24},{24,16},{1,9},{9,1},{17,25},{25,17},{2,10},{10... | collective-permute-start | bytes 552968 | tf_op jit(solution)/shard_map/ppermute | solution.py:757
  299.7 8.4 %collective-permute-start.46 = (bf16[2,3,24,384]{3,2,1,0:T(8,128)(2,1)S(1)}, bf16[2,3,24,384]{3,2,1,0:T(8,128)(2,1)S(1)}, u32[]{:S(2)}, u32[]{:S(2)}) collective-permute-start(bf16[2,3,24,384]{3,2,1,0:T(8,128)(2,1)S(1)} %get-tuple-element.303), channel_id=1, source_target_pairs={{0,8},{8,0},{16,24},{24,16},{1,9},{9,1},{17,25},{25,17},{2,10},{10... | collective-permute-start | bytes 331784 | tf_op jit(solution)/shard_map/ppermute | solution.py:757
  301.6 6.5 %collective-permute-start.45 = (bf16[1,5,24,384]{3,2,1,0:T(8,128)(2,1)S(1)}, bf16[1,5,24,384]{3,2,1,0:T(8,128)(2,1)S(1)}, u32[]{:S(2)}, u32[]{:S(2)}) collective-permute-start(bf16[1,5,24,384]{3,2,1,0:T(8,128)(2,1)S(1)} %get-tuple-element.305), channel_id=1, source_target_pairs={{0,16},{8,24},{16,0},{24,8},{1,17},{9,25},{17,1},{25,9},{2,18},{10... | collective-permute-start | bytes 276488 | tf_op jit(solution)/shard_map/ppermute | solution.py:757
  308.1 5.3 %collective-permute-start.48 = (bf16[1,3,24,384]{3,2,1,0:T(8,128)(2,1)S(1)}, bf16[1,3,24,384]{3,2,1,0:T(8,128)(2,1)S(1)}, u32[]{:S(2)}, u32[]{:S(2)}) collective-permute-start(bf16[1,3,24,384]{3,2,1,0:T(8,128)(2,1)S(1)} %get-tuple-element.307), channel_id=1, source_target_pairs={{0,16},{8,24},{16,0},{24,8},{1,17},{9,25},{17,1},{25,9},{2,18},{10... | collective-permute-start | bytes 165896 | tf_op jit(solution)/shard_map/ppermute | solution.py:757
  309.7 7.1 %collective-permute-start.47 = (bf16[5,24,384]{2,1,0:T(8,128)(2,1)S(1)}, bf16[5,24,384]{2,1,0:T(8,128)(2,1)S(1)}, u32[]{:S(2)}, u32[]{:S(2)}) collective-permute-start(bf16[5,24,384]{2,1,0:T(8,128)(2,1)S(1)} %fusion.21), channel_id=1, source_target_pairs={{0,16},{8,24},{16,0},{24,8},{1,17},{9,25},{17,1},{25,9},{2,18},{10... | collective-permute-start | bytes 276488 | tf_op jit(solution)/shard_map/ppermute | solution.py:757
  316.9 6.4 %collective-permute-start.49 = (bf16[2,5,24,384]{3,2,1,0:T(8,128)(2,1)S(1)}, bf16[2,5,24,384]{3,2,1,0:T(8,128)(2,1)S(1)}, u32[]{:S(2)}, u32[]{:S(2)}) collective-permute-start(bf16[2,5,24,384]{3,2,1,0:T(8,128)(2,1)S(1)} %pad_maximum_fusion.7), channel_id=1, source_target_pairs={{0,8},{8,0},{16,24},{24,16},{1,9},{9,1},{17,25},{25,17},{2,10},{10... | collective-permute-start | bytes 552968 | tf_op jit(solution)/shard_map/ppermute | solution.py:757
  317.0 5.4 %collective-permute-start.50 = (bf16[4,24,384]{2,1,0:T(8,128)(2,1)S(1)}, bf16[4,24,384]{2,1,0:T(8,128)(2,1)S(1)}, u32[]{:S(2)}, u32[]{:S(2)}) collective-permute-start(bf16[4,24,384]{2,1,0:T(8,128)(2,1)S(1)} %pad_maximum_fusion.9), channel_id=1, source_target_pairs={{0,16},{8,24},{16,0},{24,8},{1,17},{9,25},{17,1},{25,9},{2,18},{10... | collective-permute-start | bytes 221192 | tf_op jit(solution)/shard_map/ppermute | solution.py:757
  323.3 9.3 %collective-permute-start.52 = (bf16[20,24,384]{2,1,0:T(8,128)(2,1)S(1)}, bf16[20,24,384]{2,1,0:T(8,128)(2,1)S(1)}, u32[]{:S(2)}, u32[]{:S(2)}) collective-permute-start(bf16[20,24,384]{2,1,0:T(8,128)(2,1)S(1)} %bitcast.71), channel_id=1, source_target_pairs={{0,2},{1,3},{2,0},{3,1},{4,6},{5,7},{6,4},{7,5},{8,10},{9,11},{10,... | collective-permute-start | bytes 1105928 | tf_op jit(solution)/shard_map/ppermute | solution.py:752
  325.8 11.9 %collective-permute-start.54 = (bf16[20,24,384]{2,1,0:T(8,128)(2,1)S(1)}, bf16[20,24,384]{2,1,0:T(8,128)(2,1)S(1)}, u32[]{:S(2)}, u32[]{:S(2)}) collective-permute-start(bf16[20,24,384]{2,1,0:T(8,128)(2,1)S(1)} %bitcast.72), channel_id=1, source_target_pairs={{0,4},{1,5},{2,6},{3,7},{4,0},{5,1},{6,2},{7,3},{8,12},{9,13},{10,... | collective-permute-start | bytes 1105928 | tf_op jit(solution)/shard_map/ppermute | solution.py:752
  325.8 11.9 %collective-permute-start.56 = (bf16[20,24,384]{2,1,0:T(8,128)(2,1)S(1)}, bf16[20,24,384]{2,1,0:T(8,128)(2,1)S(1)}, u32[]{:S(2)}, u32[]{:S(2)}) collective-permute-start(bf16[20,24,384]{2,1,0:T(8,128)(2,1)S(1)} %bitcast.73), channel_id=1, source_target_pairs={{0,6},{1,7},{2,4},{3,5},{4,2},{5,3},{6,0},{7,1},{8,14},{9,15},{10,... | collective-permute-start | bytes 1105928 | tf_op jit(solution)/shard_map/ppermute | solution.py:752
  329.9 15.5 %collective-permute-start.51 = (bf16[20,24,384]{2,1,0:T(8,128)(2,1)S(1)}, bf16[20,24,384]{2,1,0:T(8,128)(2,1)S(1)}, u32[]{:S(2)}, u32[]{:S(2)}) collective-permute-start(bf16[20,24,384]{2,1,0:T(8,128)(2,1)S(1)} %bitcast.74), channel_id=1, source_target_pairs={{0,1},{1,0},{2,3},{3,2},{4,5},{5,4},{6,7},{7,6},{8,9},{9,8},{10,11... | collective-permute-start | bytes 1105928 | tf_op jit(solution)/shard_map/ppermute | solution.py:752
  329.9 14.4 %collective-permute-start.58 = (bf16[7,24,384]{2,1,0:T(8,128)(2,1)S(1)}, bf16[7,24,384]{2,1,0:T(8,128)(2,1)S(1)}, u32[]{:S(2)}, u32[]{:S(2)}) collective-permute-start(bf16[7,24,384]{2,1,0:T(8,128)(2,1)S(1)} %pad_maximum_fusion.8), channel_id=1, source_target_pairs={{0,8},{8,0},{16,24},{24,16},{1,9},{9,1},{17,25},{25,17},{2,10},{10... | collective-permute-start | bytes 387080 | tf_op jit(solution)/shard_map/ppermute | solution.py:757
  332.6 13.9 %collective-permute-start.53 = (bf16[20,24,384]{2,1,0:T(8,128)(2,1)S(1)}, bf16[20,24,384]{2,1,0:T(8,128)(2,1)S(1)}, u32[]{:S(2)}, u32[]{:S(2)}) collective-permute-start(bf16[20,24,384]{2,1,0:T(8,128)(2,1)S(1)} %collective-permute-done.52.refs_2_), channel_id=1, source_target_pairs={{0,1},{1,0},{2,3},{3,2},{4,5},{5,4},{6,7},{7,6},{8,9},{9,8},{10,11... | collective-permute-start | bytes 1105928 | tf_op jit(solution)/shard_map/ppermute | solution.py:752
  337.6 10.4 %collective-permute-start.55 = (bf16[20,24,384]{2,1,0:T(8,128)(2,1)S(1)}, bf16[20,24,384]{2,1,0:T(8,128)(2,1)S(1)}, u32[]{:S(2)}, u32[]{:S(2)}) collective-permute-start(bf16[20,24,384]{2,1,0:T(8,128)(2,1)S(1)} %collective-permute-done.54.refs_4_), channel_id=1, source_target_pairs={{0,1},{1,0},{2,3},{3,2},{4,5},{5,4},{6,7},{7,6},{8,9},{9,8},{10,11... | collective-permute-start | bytes 1105928 | tf_op jit(solution)/shard_map/ppermute | solution.py:752
  337.6 10.4 %collective-permute-start.57 = (bf16[20,24,384]{2,1,0:T(8,128)(2,1)S(1)}, bf16[20,24,384]{2,1,0:T(8,128)(2,1)S(1)}, u32[]{:S(2)}, u32[]{:S(2)}) collective-permute-start(bf16[20,24,384]{2,1,0:T(8,128)(2,1)S(1)} %collective-permute-done.56.refs_6_), channel_id=1, source_target_pairs={{0,1},{1,0},{2,3},{3,2},{4,5},{5,4},{6,7},{7,6},{8,9},{9,8},{10,11... | collective-permute-start | bytes 1105928 | tf_op jit(solution)/shard_map/ppermute | solution.py:752
  344.5 10.3 %collective-permute-start.59 = (bf16[13,24,384]{2,1,0:T(8,128)(2,1)S(1)}, bf16[13,24,384]{2,1,0:T(8,128)(2,1)S(1)}, u32[]{:S(2)}, u32[]{:S(2)}) collective-permute-start(bf16[13,24,384]{2,1,0:T(8,128)(2,1)S(1)} %pad_maximum_fusion.6.refs_0_), channel_id=1, source_target_pairs={{0,2},{1,3},{2,0},{3,1},{4,6},{5,7},{6,4},{7,5},{8,10},{9,11},{10,... | collective-permute-start | bytes 718856 | tf_op jit(solution)/shard_map/ppermute | solution.py:752
  345.3 12.7 %collective-permute-start.60 = (bf16[13,24,384]{2,1,0:T(8,128)(2,1)S(1)}, bf16[13,24,384]{2,1,0:T(8,128)(2,1)S(1)}, u32[]{:S(2)}, u32[]{:S(2)}) collective-permute-start(bf16[13,24,384]{2,1,0:T(8,128)(2,1)S(1)} %pad_maximum_fusion.6.refs_0_), channel_id=1, source_target_pairs={{0,4},{1,5},{2,6},{3,7},{4,0},{5,1},{6,2},{7,3},{8,12},{9,13},{10,... | collective-permute-start | bytes 718856 | tf_op jit(solution)/shard_map/ppermute | solution.py:752
  346.5 11.6 %collective-permute-start.61 = (bf16[13,24,384]{2,1,0:T(8,128)(2,1)S(1)}, bf16[13,24,384]{2,1,0:T(8,128)(2,1)S(1)}, u32[]{:S(2)}, u32[]{:S(2)}) collective-permute-start(bf16[13,24,384]{2,1,0:T(8,128)(2,1)S(1)} %pad_maximum_fusion.6.refs_0_), channel_id=1, source_target_pairs={{0,6},{1,7},{2,4},{3,5},{4,2},{5,3},{6,0},{7,1},{8,14},{9,15},{10,... | collective-permute-start | bytes 718856 | tf_op jit(solution)/shard_map/ppermute | solution.py:752
  358.1 3.4 collective-permute-start.62
  (62 other events, 612.9 us)

commit v4 on v3

--- a/solution.py
+++ b/solution.py
@@ -406,7 +406,7 @@
     )(*mixed, tokens, weight, scales, slots)
 
 
-def expert_kernel(trained, group, held, own_ref, *refs):
+def expert_kernel(trained, group, held, pick, own_ref, *refs):
     x_refs = refs[:group]
     g_ref, wr_ref, wrt_ref = refs[group : group + 3]
     in_refs = refs[group + 3 : group + 13]
@@ -419,7 +419,7 @@
     if trained:
         grad_refs = rest[:4]
         rest = rest[4:]
-    x_ref, dexp_ref, gate_ref, acc_ref, back_ref, xt_ref, win_ref, wout_ref, din_ref, dout_ref = rest
+    x_ref, dexp_ref, gate_ref, acc_ref, back_ref, xt_ref, win_ref, wout_ref, din_ref, dout_ref, sems = rest
     step = pl.program_id(0)
     capacity, width = back_refs[0].shape
     own = own_ref[0]
@@ -430,8 +430,32 @@
     def other_of(tail):
         return tail[:, 0:1].astype(F32).astype(jnp.int32) - own
 
+    def copies(step_chip):
+        made = []
+        chunk = win_ref.shape[2]
+        cols = pl.ds(pl.multiple_of((own_ref[2] ^ step_chip) * chunk, LANES), chunk)
+        for which in range(2):
+            core = own_ref[1] ^ which
+            for index, (chip, lower) in enumerate(PLACES):
+                piece = in_refs[5 * which + index]
+                tall = piece.shape[1]
+                at = ((own_ref[2] ^ chip) * 2 + core) * in_refs[0].shape[1] + lower * tall
+                rows = pl.ds(pl.multiple_of(at, 16), tall)
+                made.append((piece.at[pick, :, cols], win_ref.at[step_chip, rows, :]))
+                if chip == step_chip:
+                    piece = out_w_refs[5 * which + index]
+                    tall = piece.shape[1]
+                    rows = pl.ds(pl.multiple_of(core * out_w_refs[0].shape[1] + lower * tall, 16), tall)
+                    made.append((piece.at[pick], wout_ref.at[step_chip, rows, :]))
+        return [
+            pltpu.make_async_copy(src, dst, sems.at[step_chip, i]) for i, (src, dst) in enumerate(made)
+        ]
+
     @pl.when(step == 0)
     def _():
+        for chip in range(4):
+            for copy in copies(chip):
+                copy.start()
         for shift in range(group):
             span = slice(shift * capacity, (shift + 1) * capacity)
             rows = x_refs[shift][0]
@@ -450,22 +474,15 @@
         back_ref[...] = jnp.zeros_like(back_ref)
         xt_ref[...] = x_ref[...].astype(F32).T.astype(BF16)
 
-    for which in range(2):
-        core = own_ref[1] ^ which
-        for index, (chip, lower) in enumerate(PLACES):
-            piece = in_refs[5 * which + index]
-            tall = piece.shape[1]
-            at = ((own_ref[2] ^ chip) * 2 + core) * in_refs[0].shape[1] + lower * tall
-            win_ref[pl.ds(pl.multiple_of(at, 16), tall), :] = piece[0]
-
-            @pl.when(step == chip)
-            def _(piece=out_w_refs[5 * which + index], lower=lower, core=core):
-                tall = piece.shape[1]
-                at = core * out_w_refs[0].shape[1] + lower * tall
-                wout_ref[pl.ds(pl.multiple_of(at, 16), tall), :] = piece[0]
-
-    win = win_ref[...]
-    wout = wout_ref[...]
+    for chip in range(4):
+
+        @pl.when(step == chip)
+        def _(chip=chip):
+            for copy in copies(chip):
+                copy.wait()
+
+    win = win_ref[step]
+    wout = wout_ref[step]
     pre = dot_nn(x_ref[...], win)
     square = pre * pre
     tanh = jnp.tanh(0.7978845608028654 * (pre + 0.044715 * pre * square))
@@ -486,7 +503,7 @@
 
     @pl.when(step == pl.num_programs(0) - 1)
     def _():
-        router = jnp.zeros((width, LANES), F32)
+        router = jnp.zeros((LANES, width), F32)
         for shift in range(group):
             span = slice(shift * capacity, (shift + 1) * capacity)
             gate = gate_ref[span, 0:1]
@@ -499,7 +516,7 @@
             sign = jnp.where(lane == own, 1.0, 0.0) - jnp.where(lane == other, 1.0, 0.0)
             dlogits = (coef * sign).astype(BF16)
             back_refs[shift][...] = (back_ref[span, :] + dot_nn(dlogits, wrt_ref[...])).astype(BF16)
-            router = router + dot_nn(xt_ref[:, span], dlogits)
+            router = router + dot_tn(dlogits, x_ref[span, :])
         router_ref[...] = router
 
 
@@ -513,26 +530,24 @@
     many = group * capacity
     shard, deep = width // 8, inner // 8
     out_specs = [pl.BlockSpec((group, 1, capacity, width), lambda f, own: (0, place, 0, 0))]
-    out_specs += [full((capacity, width))] * group + [full((width, LANES))]
+    out_specs += [full((capacity, width))] * group + [full((LANES, width))]
     out_shape = [jax.ShapeDtypeStruct((group, local, capacity, width), BF16)]
     out_shape += [jax.ShapeDtypeStruct((capacity, width), BF16)] * group
-    out_shape += [jax.ShapeDtypeStruct((width, LANES), F32)]
+    out_shape += [jax.ShapeDtypeStruct((LANES, width), F32)]
     if trained:
         out_specs += [pl.BlockSpec((4, shard, chunk), lambda f, own: (0, 0, block(f, own)))] * 2
         out_specs += [pl.BlockSpec((1, deep, width), lambda f, own: (f, 0, 0))] * 2
         out_shape += [jax.ShapeDtypeStruct((4, shard, inner), BF16)] * 2
         out_shape += [jax.ShapeDtypeStruct((4, deep, width), BF16)] * 2
     return pl.pallas_call(
-        functools.partial(expert_kernel, trained, group, len(held)),
+        functools.partial(expert_kernel, trained, group, len(held), pick),
         grid_spec=pltpu.PrefetchScalarGridSpec(
             num_scalar_prefetch=1,
             grid=(4,),
             in_specs=[pl.BlockSpec((1, capacity, width), lambda f, own: (place, 0, 0))] * group
             + [pl.BlockSpec((group, 1, capacity, wide), lambda f, own: (0, place, 0, 0))]
             + [full((width, LANES)), full((LANES, width))]
-            + [pl.BlockSpec((1, w.shape[1], chunk), lambda f, own: (pick, 0, block(f, own))) for w in w_in]
-            + [pl.BlockSpec((1, w.shape[1], width), lambda f, own: (pick, 0, 0)) for w in w_out]
-            + [pl.BlockSpec(memory_space=pl.ANY)] * len(held),
+            + [pl.BlockSpec(memory_space=pl.ANY)] * (len(w_in) + len(w_out) + len(held)),
             out_specs=out_specs,
             scratch_shapes=[
             pltpu.VMEM((many, width), BF16),
@@ -541,10 +556,11 @@
             pltpu.VMEM((many, width), F32),
             pltpu.VMEM((many, width), F32),
             pltpu.VMEM((width, many), BF16),
-            pltpu.VMEM((width, chunk), BF16),
-            pltpu.VMEM((chunk, width), BF16),
+            pltpu.VMEM((4, width, chunk), BF16),
+            pltpu.VMEM((4, chunk, width), BF16),
             pltpu.VMEM((8, shard, chunk) if trained else (8, LANES), BF16),
             pltpu.VMEM((2, deep, width) if trained else (8, LANES), BF16),
+            pltpu.SemaphoreType.DMA((4, 14)),
             ],
         ),
         out_shape=out_shape,
@@ -706,10 +722,14 @@
 
     def put(out_ref):
         for index, piece in enumerate(pieces):
-            for far in range(4):
-                place = (at_ref[0] ^ index) * 4 + (at_ref[1] ^ FAR[far])
+
+            def each(far, carry, index=index, piece=piece):
+                place = (at_ref[0] ^ index) * 4 + (at_ref[1] ^ ((far >> 1) | ((far & 1) << 1)))
                 rows = pl.ds(pl.multiple_of(place * tall, 8), tall)
                 out_ref[rows, :] = piece[far * parts + part].astype(F32)
+                return carry
+
+            lax.fori_loop(0, 4, each, 0)
 
     @pl.when(part < 3)
     def _():
@@ -829,8 +849,14 @@
     return [piece for block in blocks for piece in (block, swap(block, 1))]
 
 
-def scatter_core(keep, send):
-    return [added(mine, other).astype(BF16) for mine, other in zip(keep, swap(send, 1))]
+def packed(small):
+    half = small.shape[1] // 2
+    return jnp.concatenate([small[:, :half], small[:, half:]])
+
+
+def unpacked(small):
+    half = small.shape[0] // 2
+    return jnp.concatenate([small[:half], small[half:]], axis=1)
 
 
 def natural(keep, send):
@@ -959,18 +985,20 @@
                 in_keep, in_send, out_keep, out_send = got[group + 2 :]
     returned = [backs[p][shift] for shift in range(group) for p in range(local)]
     if fast:
-        in_rs = scatter_core(in_keep, in_send)
-        out_rs = scatter_core(out_keep, out_send)
+        in_other, out_other = swap(in_send, 1), swap(out_send, 1)
+        outs[0], in_keep, out_keep, in_other, out_other = tie(outs[0], in_keep, out_keep, in_other, out_other)
+        in_rs = [total(pair) for pair in zip(in_keep, in_other)]
+        out_rs = [total(pair) for pair in zip(out_keep, out_other)]
         in_got = [swap(in_rs[chip], 2 * chip) for chip in (1, 2)]
-        tied = tie(*returned, *in_got, *in_rs, *out_rs)
-        returned, in_got, in_rs, out_rs = tied[:-10], tied[-10:-8], tied[-8:-4], tied[-4:]
+        tied = tie(*returned, in_rs[3], *out_rs)
+        returned, in_rs[3], out_rs = tied[:-5], tied[-5], tied[-4:]
         in_got.append(swap(in_rs[3], 6))
-        out_got = [swap(out_rs[chip], 2 * chip) for chip in (1, 2)]
     dres, dmixed, proj_keep, proj_send, sums2 = middle_call(
         slots_t, residual, cot_rows, scales, mixed, w_proj, at, returned
     )
     if fast:
-        dmixed, outs[0] = tie(dmixed, outs[0])
+        dmixed, outs[0], in_got[0], in_got[1], *out_rs = tie(dmixed, outs[0], in_got[0], in_got[1], *out_rs)
+        out_got = [swap(out_rs[chip], 2 * chip) for chip in (1, 2)]
     else:
         natural_in = natural(in_keep, in_send)
         natural_out = natural(out_keep, out_send)
@@ -988,29 +1016,29 @@
         lengths, qkv, dmixed, mixed_high, lse_high, normed1, at, *halves[1]
     )
     if fast:
-        dq_high, keep_high, back_outs, out_got[2], *halves_low = tie(
-            dq_high, keep_high, back_outs, out_got[2], *halves_low
-        )
+        dq_high, keep_high, back_outs, *halves_low = tie(dq_high, keep_high, back_outs, *halves_low)
         low = to_chips(halves_low)
         halves_high = sum_core((keep_high,), (send_high,))
     input_grad, sums1 = last_call((dq_low, dq_high), token_rows, dres, scales, w_qkv)
     if fast:
         sums1, *halves_high = tie(sums1, *halves_high)
         high = to_chips(halves_high)
-        small = jnp.concatenate([router_sum.T[:experts], sums1[:2], sums2[:2]], axis=0)
+        small = jnp.concatenate([router_sum[:experts], sums1[:2], sums2[:2]], axis=0)
         low = give(total(low), 1)
         tied = tie(*low, *high)
         low = give(total(tied[:2]), 2)
         high = give(total(tied[2:]), 1)
-        tied = tie(*low, *high)
+        new_in_grad = added(in_rs[0], *in_got)
+        new_in_grad, *tied = tie(new_in_grad, *low, *high)
         own_low = total(tied[:2])[0]
         low = [own_low, across(own_low, 2)]
         high = give(total(tied[2:]), 2)
-        tied = tie(*low, *high)
+        new_out_grad = added(out_rs[0], *out_got)
+        new_out_grad, *tied = tie(new_out_grad, *low, *high)
         low = jnp.stack(tied[:2])
         low = [low, across(low, 1)]
         own_high = total(tied[2:])[0]
-        mine = small.astype(BF16).reshape(1, *own_high.shape[1:])
+        mine = packed(small).astype(BF16)[None]
         high = [jnp.concatenate([own_high, mine])]
         high.append(across(high[0], 2))
         tied = tie(*low, *high)
@@ -1022,22 +1050,22 @@
         high = [high, across(high, 1)]
         mine = total([block[2 * parts :] for block in high])
         chips_high = spread_chips(jnp.concatenate([block[: 2 * parts] for block in high] + [mine]))
+        output = combine_call(me_one, slots_t, residual, back_outs)
+        output, *chips_low = tie(output, *chips_low)
         pieces_low = spread_cores(chips_low)
         qkv_grad, proj_grad = unpack_call(at, pieces_low, 0)
         qkv_grad, *chips_high = tie(qkv_grad, *chips_high)
         pieces_high = spread_cores(chips_high)
-        small = added(*[piece[4 * parts] for piece in pieces_high]).reshape(small.shape)
-        new_in_grad = added(in_rs[0], *in_got)
-        new_out_grad = added(out_rs[0], *out_got)
+        small = unpacked(added(*[piece[4 * parts] for piece in pieces_high]))
     else:
         pieces_low = sum_all((keep_low, proj_keep), (send_low, proj_send))
         pieces_high = sum_all((keep_high,), (send_high,))
-        small = jnp.concatenate([router_sum.T[:experts], sums1[:2], sums2[:2]], axis=0)
+        small = jnp.concatenate([router_sum[:experts], sums1[:2], sums2[:2]], axis=0)
         small = jnp.sum(lax.all_gather(small, ("expert", "batch"), axis=0), axis=0)
         new_in_grad = lax.psum_scatter(natural_in, "batch", scatter_dimension=0, tiled=True)
         new_out_grad = lax.psum_scatter(natural_out, "batch", scatter_dimension=0, tiled=True)
-    output = combine_call(me_one, slots_t, residual, back_outs)
     if not fast:
+        output = combine_call(me_one, slots_t, residual, back_outs)
         qkv_grad, proj_grad = unpack_call(at, pieces_low, 0)
     (qkv_grad,) = unpack_call(at, pieces_high, 1, qkv_grad)
     return (

time: 373 us -> 364 us (0.976)
  waiting for transfers between devices: 94.2 us -> 89 us
    add x3 -> x5, other arithmetic: 0.39 us -> 6.95 us  [added(): total = total + block.astype(F32)]
    broadcast_in_dim x2 -> x0, other arithmetic: 4.9 us -> none  [the longest x1 2.56 us: body(): new_in_grad.astype(F32)[None]]
    ppermute x6, waiting for transfers between devices: 15.3 us -> 10.5 us  [come(): lax.ppermute(block, 'expert', [(i, (i - shift) % group) for i in range(gr...]
    convert_element_type x2 -> x0, other arithmetic: 4.04 us -> none  [scatter_core(): added(mine, other).astype(BF16)]
  transfers between devices with their start and end apart: 68 -> 68, of which waited for: 25 -> 25; matrix products, arithmetic and copies ran while one was open for 7% -> 7% of each run, Pallas kernels for 34% -> 39%
where the time goes in v4:
time: 364 us; the launch traced here: 360 us
  Pallas kernels  169 us (46%)
  waiting for transfers between devices  89 us (24%)
  starting transfers between devices  65.3 us (18%)
  other arithmetic  17.8 us (5%)
  local copies, waits for them, and re-layouts  15.6 us (4%)
    pallas_call x2, Pallas kernels, expert_call(): pl.pallas_call(functools.partial(expert_kernel, trained, group, len(held)...  44.6 us
    pallas_call x2, Pallas kernels, attend_back_call(): pl.pallas_call(attend_back_kernel, grid=(count,), in_specs=[smem()] + [pl...  35.7 us
    ppermute x49, starting transfers between devices, swap(): return lax.ppermute(block, 'batch', [(i, i ^ bits) for i in range(size)])  35.5 us
    ppermute x3, waiting for transfers between devices, go(): lax.ppermute(block, 'expert', [(i, (i + shift) % group) for i in range(gr...  35.4 us
    ppermute x49, waiting for transfers between devices, swap(): return lax.ppermute(block, 'batch', [(i, i ^ bits) for i in range(size)])  27 us
    pallas_call x2, Pallas kernels, attend_call(): pl.pallas_call(attend_kernel, grid=(count,), in_specs=[smem()] + [pl.Bloc...  26.1 us
    ppermute x8, waiting for transfers between devices, across(): return lax.ppermute(block, 'expert', [(i, i ^ bits) for i in range(size)])  16.2 us
    pallas_call x1, Pallas kernels, middle_call(): pl.pallas_call(functools.partial(middle_kernel, len(parts)), grid=(seq //...  13.4 us
  transfers between devices with their start and end apart: 68, of which 25 were waited for; matrix products, arithmetic and copies ran while one was open for 7% of the time, Pallas kernels for 39%

profile of v4, /device:TPU:0, one launch (start us, length us, event | category | flops | bytes accessed | tf_op | source)
XLA Modules:
  0.0 359.5 jit_solution(6099573939083473800)
XLA Ops:
  0.7 2.0 constant_dynamic-update-slice_fusion.1
  3.5 3.0 collective-permute-start.1
  6.5 1.5 collective-permute-start
  9.7 6.0 %route.1 = (s32[8,1024]{1,0:T(8,128)}, s32[1024,128]{1,0:T(8,128)}, bf16[4,2,128,896]{3,2,1,0:T(8,128)(2,1)}) custom-call(s32[1]{0:T(128)S(6)} %copy.34.len_ref, s32[1]{0:T(128)} %bitcast.me_ref, s32[2,1024]{1,0:T(2,128)} %copy.29.route_ref, s32[1024,2]{1,0:T(8,128)} %bitcast.76, bf16[1024,768]{1,0:T(8,128)(2,1)} %bitcast.87), custom_call_target="tpu_custom_call" | custom-call | flops 6270000128 | bytes 17100000 | tf_op jit(solution)/shard_map/route/pallas_call | solution.py:347
  15.7 5.2 %all-to-all-start = ((bf16[4,2,128,896]{3,2,1,0:T(8,128)(2,1)}), bf16[4,2,128,896]{3,2,1,0:T(8,128)(2,1)S(1)}, u32[]{:S(2)}, u32[]{:S(2)}) async-start(bf16[4,2,128,896]{3,2,1,0:T(8,128)(2,1)} %get-tuple-element.184), calls=%async_computation | async-start | bytes 3670016 | tf_op jit(solution)/shard_map/all_to_all | solution.py:901
  21.0 1.4 pad_maximum_fusion.refs_17_
  23.1 8.4 %norm_qkv.1 = (bf16[1024,768]{1,0:T(8,128)(2,1)}, bf16[1024,2304]{1,0:T(8,128)(2,1)}) custom-call(bf16[1024,768]{1,0:T(8,128)(2,1)} %bitcast.89, f32[4,768]{1,0:T(4,128)} %pad_maximum_fusion.10.scale_ref.gain_ref, bf16[768,2304]{1,0:T(8,128)(2,1)} %w_ref.7), custom_call_target="tpu_custom_call" | custom-call | flops 9569999872 | bytes 26100000 | tf_op jit(solution)/shard_map/norm_qkv/pallas_call | solution.py:80
  31.5 13.1 %attend.2 = (bf16[1024,384]{1,0:T(8,128)(2,1)}, f32[3,8,1024]{2,1,0:T(8,128)}) custom-call(s32[1]{0:T(128)S(6)} %copy.34.len_ref, bf16[1024,2304]{1,0:T(8,128)(2,1)} %get-tuple-element.166.q_ref.k_ref.v_ref, bf16[1024,2304]{1,0:T(8,128)(2,1)} %get-tuple-element.166.q_ref.k_ref.v_ref, bf16[1024,2304]{1,0:T(8,128)(2,1)} %get-tuple-element.166.q_ref.k_ref.v_ref), custom_call_target="tpu_custom_call" | custom-call | flops 13200000000 | bytes 36000000 | tf_op jit(solution)/shard_map/attend/pallas_call | solution.py:152
  44.6 1.1 slice.190
  45.8 1.1 slice.191
  48.5 13.0 %attend.3 = (bf16[1024,384]{1,0:T(8,128)(2,1)}, f32[3,8,1024]{2,1,0:T(8,128)}) custom-call(s32[1]{0:T(128)S(6)} %copy.34.len_ref, bf16[1024,2304]{1,0:T(8,128)(2,1)} %get-tuple-element.166.q_ref.k_ref.v_ref, bf16[1024,2304]{1,0:T(8,128)(2,1)} %get-tuple-element.166.q_ref.k_ref.v_ref, bf16[1024,2304]{1,0:T(8,128)(2,1)} %get-tuple-element.166.q_ref.k_ref.v_ref), custom_call_target="tpu_custom_call" | custom-call | flops 13200000000 | bytes 36000000 | tf_op jit(solution)/shard_map/attend/pallas_call | solution.py:152
  61.5 1.4 collective-permute-done.3.refs_11_
  63.1 1.6 collective-permute-start.10
  65.2 8.8 %project_dispatch.1 = (f32[1024,768]{1,0:T(8,128)}, bf16[2,128,768]{2,1,0:T(8,128)(2,1)}, bf16[2,128,768]{2,1,0:T(8,128)(2,1)}, bf16[2,128,768]{2,1,0:T(8,128)(2,1)}, bf16[2,128,768]{2,1,0:T(8,128)(2,1)}) custom-call(bf16[1024,384]{1,0:T(8,128)(2,1)} %get-tuple-element.165.low_ref.o_ref, bf16[1024,384]{1,0:T(8,128)(2,1)} %get-tuple-element.172.high_ref.o_ref, ...), custom_call_target="tpu_custom_call" | custom-call | flops 9680000000 | bytes 26400000 | tf_op jit(solution)/shard_map/project_dispatch/pallas_call | solution.py:395
  74.1 2.1 collective-permute-start.7
  76.1 2.4 collective-permute-start.8
  78.5 9.7 %collective-permute-done.7.refs_1_ = bf16[2,128,768]{2,1,0:T(8,128)(2,1)S(1)} collective-permute-done((bf16[2,128,768]{2,1,0:T(8,128)(2,1)}, bf16[2,128,768]{2,1,0:T(8,128)(2,1)S(1)}, u32[]{:S(2)}, u32[]{:S(2)}) %collective-permute-start.7) | collective-permute-done | bytes 393248 | tf_op jit(solution)/shard_map/ppermute | solution.py:898
  88.2 7.0 %collective-permute-done.8.refs_3_ = bf16[2,128,768]{2,1,0:T(8,128)(2,1)S(1)} collective-permute-done((bf16[2,128,768]{2,1,0:T(8,128)(2,1)}, bf16[2,128,768]{2,1,0:T(8,128)(2,1)S(1)}, u32[]{:S(2)}, u32[]{:S(2)}) %collective-permute-start.8) | collective-permute-done | bytes 393248 | tf_op jit(solution)/shard_map/ppermute | solution.py:898
  98.8 1.2 collective-permute-start.15
  101.0 18.7 %collective-permute-done.11.refs_2_ = bf16[2,128,768]{2,1,0:T(8,128)(2,1)S(1)} collective-permute-done((bf16[2,128,768]{2,1,0:T(8,128)(2,1)S(1)}, bf16[2,128,768]{2,1,0:T(8,128)(2,1)S(1)}, u32[]{:S(2)}, u32[]{:S(2)}) %collective-permute-start.11) | collective-permute-done | bytes 393248 | tf_op jit(solution)/shard_map/ppermute | solution.py:898
  124.5 1.8 collective-permute-done.19.refs_25_
  127.2 25.6 %experts_new.1 = (bf16[4,2,128,768]{3,2,1,0:T(8,128)(2,1)}, bf16[128,768]{1,0:T(8,128)(2,1)}, bf16[128,768]{1,0:T(8,128)(2,1)}, bf16[128,768]{1,0:T(8,128)(2,1)}...) custom-call(s32[4]{0:T(128)} %get-tuple-element.345.own_ref, ...), custom_call_target="tpu_custom_call" | custom-call | flops 25300000768 | bytes 69000000 | tf_op jit(solution)/shard_map/experts_new/pallas_call | solution.py:542
  154.3 1.7 collective-permute-start.23
  156.0 19.0 %experts_old.1 = (bf16[4,2,128,768]{3,2,1,0:T(8,128)(2,1)}, bf16[128,768]{1,0:T(8,128)(2,1)}, bf16[128,768]{1,0:T(8,128)(2,1)}, bf16[128,768]{1,0:T(8,128)(2,1)}...) custom-call(s32[4]{0:T(128)} %get-tuple-element.344.own_ref, ...), custom_call_target="tpu_custom_call", output_to_operand_aliasing={{0}: (28, {})} | custom-call | flops 18699999232 | bytes 51000000 | tf_op jit(solution)/shard_map/experts_old/pallas_call | solution.py:542
  175.1 2.6 collective-permute-start.24
  178.6 1.8 collective-permute-start.26
  180.4 1.6 fusion.8
  183.5 1.6 fusion.6
  185.1 10.5 %collective-permute-done.25.refs_4_ = bf16[128,768]{1,0:T(8,128)(2,1)} collective-permute-done((bf16[128,768]{1,0:T(8,128)(2,1)}, bf16[128,768]{1,0:T(8,128)(2,1)}, u32[]{:S(2)}, u32[]{:S(2)}) %collective-permute-start.25) | collective-permute-done | bytes 196640 | tf_op jit(solution)/shard_map/ppermute | solution.py:906
  196.5 1.5 collective-permute-start.29
  198.0 13.4 %middle_back.1 = (f32[1024,768]{1,0:T(8,128)}, bf16[1024,768]{1,0:T(8,128)(2,1)}, bf16[4,4,2,24,384]{4,3,2,1,0:T(8,128)(2,1)}, bf16[4,4,2,24,384]{4,3,2,1,0:T(8,128)(2,1)}, f32[8,768]{1,0:T(8,128)}) custom-call(s32[1024,128]{1,0:T(8,128)} %get-tuple-element.160.slot_ref, f32[1024,768]{1,0:T(8,128)} %get-tuple-element.174.res_ref, ...), custom_call_target="tpu_custom_call" | custom-call | flops 14300000256 | bytes 39000000 | tf_op jit(solution)/shard_map/middle_back/pallas_call | solution.py:647
  214.1 4.4 %all-to-all-start.1 = ((bf16[4,2,128,768]{3,2,1,0:T(8,128)(2,1)}), bf16[4,2,128,768]{3,2,1,0:T(8,128)(2,1)}, u32[]{:S(2)}, u32[]{:S(2)}) async-start(bf16[4,2,128,768]{3,2,1,0:T(8,128)(2,1)} %get-tuple-element.245), calls=%async_computation.1 | async-start | bytes 3145728 | tf_op jit(solution)/shard_map/all_to_all | solution.py:901
  219.4 1.5 collective-permute-start.33
  220.9 17.9 %attend_back.2 = (bf16[3,1024,384]{2,1,0:T(8,128)(2,1)}, bf16[4,4,3,24,384]{4,3,2,1,0:T(8,128)(2,1)}, bf16[4,4,3,24,384]{4,3,2,1,0:T(8,128)(2,1)}) custom-call(s32[1]{0:T(128)S(6)} %copy.34.len_ref, bf16[1024,2304]{1,0:T(8,128)(2,1)} %get-tuple-element.166.q_ref.k_ref.v_ref, bf16[1024,2304]{1,0:T(8,128)(2,1)} %get-tuple-element.166.q_ref.k_ref.v_ref, ...), custom_call_target="tpu_custom_call" | custom-call | flops 5500000256 | bytes 15000000 | tf_op jit(solution)/shard_map/attend_back/pallas_call | solution.py:256
  238.8 1.3 fusion.21
  242.8 17.9 %attend_back.3 = (bf16[3,1024,384]{2,1,0:T(8,128)(2,1)}, bf16[4,4,3,24,384]{4,3,2,1,0:T(8,128)(2,1)}, bf16[4,4,3,24,384]{4,3,2,1,0:T(8,128)(2,1)}) custom-call(s32[1]{0:T(128)S(6)} %copy.34.len_ref, bf16[1024,2304]{1,0:T(8,128)(2,1)} %get-tuple-element.166.q_ref.k_ref.v_ref, bf16[1024,2304]{1,0:T(8,128)(2,1)} %get-tuple-element.166.q_ref.k_ref.v_ref, ...), custom_call_target="tpu_custom_call" | custom-call | flops 5500000256 | bytes 15000000 | tf_op jit(solution)/shard_map/attend_back/pallas_call | solution.py:256
  260.8 3.1 fusion.1
  264.3 1.1 collective-permute-start.37
  265.4 1.4 collective-permute-start.38
  267.9 10.1 %last_back.1 = (f32[1024,768]{1,0:T(8,128)}, f32[8,768]{1,0:T(8,128)}) custom-call(bf16[3,1024,384]{2,1,0:T(8,128)(2,1)} %get-tuple-element.262.low_ref, bf16[3,1024,384]{2,1,0:T(8,128)(2,1)} %get-tuple-element.263.high_ref, bf16[1024,768]{1,0:T(8,128)(2,1)} %bitcast.91, f32[1024,768]{1,0:T(8,128)} %get-tuple-element.264.dres_ref, ...), custom_call_target="tpu_custom_call" | custom-call | flops 5500000256 | bytes 15000000 | tf_op jit(solution)/shard_map/last_back/pallas_call | solution.py:695
  278.0 1.5 fusion.17
  279.5 1.1 collective-permute-start.42
  280.6 1.3 collective-permute-start.43
  282.0 2.3 collective-permute-done.38
  285.8 2.3 convert_add_fusion.1
  288.9 4.5 %collective-permute-done.43 = bf16[4,3,24,384]{3,2,1,0:T(8,128)(2,1)S(1)} collective-permute-done((bf16[4,3,24,384]{3,2,1,0:T(8,128)(2,1)S(1)}, bf16[4,3,24,384]{3,2,1,0:T(8,128)(2,1)S(1)}, u32[]{:S(2)}, u32[]{:S(2)}) %collective-permute-start.43) | collective-permute-done | bytes 221216 | tf_op jit(solution)/shard_map/ppermute | solution.py:772
  293.5 2.5 collective-permute-start.45
  296.4 3.7 %collective-permute-done.45 = bf16[1,5,24,384]{3,2,1,0:T(8,128)(2,1)S(1)} collective-permute-done((bf16[1,5,24,384]{3,2,1,0:T(8,128)(2,1)S(1)}, bf16[1,5,24,384]{3,2,1,0:T(8,128)(2,1)S(1)}, u32[]{:S(2)}, u32[]{:S(2)}) %collective-permute-start.45) | collective-permute-done | bytes 92192 | tf_op jit(solution)/shard_map/ppermute | solution.py:777
  300.1 1.4 collective-permute-done.46
  302.1 2.6 collective-permute-start.48
  304.7 5.3 %collective-permute-done.48 = bf16[1,3,24,384]{3,2,1,0:T(8,128)(2,1)S(1)} collective-permute-done((bf16[1,3,24,384]{3,2,1,0:T(8,128)(2,1)S(1)}, bf16[1,3,24,384]{3,2,1,0:T(8,128)(2,1)S(1)}, u32[]{:S(2)}, u32[]{:S(2)}) %collective-permute-start.48) | collective-permute-done | bytes 55328 | tf_op jit(solution)/shard_map/ppermute | solution.py:777
  310.1 1.5 collective-permute-start.50
  311.6 4.4 %collective-permute-done.50 = bf16[4,24,384]{2,1,0:T(8,128)(2,1)S(1)} collective-permute-done((bf16[4,24,384]{2,1,0:T(8,128)(2,1)S(1)}, bf16[4,24,384]{2,1,0:T(8,128)(2,1)S(1)}, u32[]{:S(2)}, u32[]{:S(2)}) %collective-permute-start.50) | collective-permute-done | bytes 73760 | tf_op jit(solution)/shard_map/ppermute | solution.py:777
  316.0 1.4 collective-permute-done.49
  317.5 1.4 collective-permute-start.53
  318.9 1.5 collective-permute-start.52
  321.2 6.2 %combine.1 = f32[1024,768]{1,0:T(8,128)} custom-call(s32[1]{0:T(128)} %bitcast.me_ref, s32[1024,128]{1,0:T(8,128)} %get-tuple-element.160.slot_ref, f32[1024,768]{1,0:T(8,128)} %get-tuple-element.174.res_ref, bf16[4,2,128,768]{3,2,1,0:T(8,128)(2,1)} %all-to-all-done.1.part_ref), custom_call_target="tpu_custom_call" | custom-call | flops 6819999744 | bytes 18600000 | tf_op jit(solution)/shard_map/combine/pallas_call | solution.py:597
  327.4 2.6 collective-permute-done.53.refs_6_
  329.9 5.9 %collective-permute-done.52.refs_4_ = bf16[20,24,384]{2,1,0:T(8,128)(2,1)S(1)} collective-permute-done((bf16[20,24,384]{2,1,0:T(8,128)(2,1)S(1)}, bf16[20,24,384]{2,1,0:T(8,128)(2,1)S(1)}, u32[]{:S(2)}, u32[]{:S(2)}) %collective-permute-start.52) | collective-permute-done | bytes 368672 | tf_op jit(solution)/shard_map/ppermute | solution.py:772
  337.1 1.4 collective-permute-start.61
  339.2 1.5 collective-permute-start.59
  342.1 5.8 %unpack.2 = (f32[768,2304]{1,0:T(8,128)}, f32[768,768]{1,0:T(8,128)}) custom-call(s32[2]{0:T(128)} %pad_add_fusion.at_ref, bf16[20,24,384]{2,1,0:T(8,128)(2,1)} %bitcast.83, bf16[20,24,384]{2,1,0:T(8,128)(2,1)} %copy-done.39, bf16[20,24,384]{2,1,0:T(8,128)(2,1)} %copy-done.38, bf16[20,24,384]{2,1,0:T(8,128)(2,1)} %copy-done.40, ...), custom_call_target="tpu_custom_call" | custom-call | flops 4400000000 | bytes 12000000 | tf_op jit(solution)/shard_map/unpack/pallas_call | solution.py:755
  347.9 3.1 collective-permute-done.60.refs_4_
  354.9 4.4 %unpack.3 = f32[768,2304]{1,0:T(8,128)} custom-call(s32[2]{0:T(128)} %pad_add_fusion.at_ref, bf16[13,24,384]{2,1,0:T(8,128)(2,1)} %copy-done.15, bf16[13,24,384]{2,1,0:T(8,128)(2,1)} %copy-done.25, bf16[13,24,384]{2,1,0:T(8,128)(2,1)} %copy-done.24, bf16[13,24,384]{2,1,0:T(8,128)(2,1)} %copy-done.26, ...), custom_call_target="tpu_custom_call", output_to_operand_aliasing={{}: (9, {})} | custom-call | flops 4400000000 | bytes 12000000 | tf_op jit(solution)/shard_map/unpack/pallas_call | solution.py:755
  (237 shorter events, 39.7 us)
Async XLA Ops:
  3.5 41.1 %collective-permute-start.1 = (bf16[2,96,3072]{2,1,0:T(8,128)(2,1)}, bf16[2,96,3072]{2,1,0:T(8,128)(2,1)}, u32[]{:S(2)}, u32[]{:S(2)}) collective-permute-start(bf16[2,96,3072]{2,1,0:T(8,128)(2,1)} %constant_dynamic-update-slice_fusion.refs_7_), channel_id=1, source_target_pairs={{0,4},{1,5},{2,6},{3,7},{4,0},{5,1},{6,2},{7,3},{8,12},{9,13},{10,... | collective-permute-start | bytes 3538952 | tf_op jit(solution)/shard_map/ppermute | solution.py:772
  6.5 38.1 %collective-permute-start = (bf16[2,96,3072]{2,1,0:T(8,128)(2,1)}, bf16[2,96,3072]{2,1,0:T(8,128)(2,1)}, u32[]{:S(2)}, u32[]{:S(2)}) collective-permute-start(bf16[2,96,3072]{2,1,0:T(8,128)(2,1)} %constant_dynamic-update-slice_fusion.refs_7_), channel_id=1, source_target_pairs={{0,2},{1,3},{2,0},{3,1},{4,6},{5,7},{6,4},{7,5},{8,10},{9,11},{10,... | collective-permute-start | bytes 3538952 | tf_op jit(solution)/shard_map/ppermute | solution.py:772
  15.7 108.8 %all-to-all-start = ((bf16[4,2,128,896]{3,2,1,0:T(8,128)(2,1)}), bf16[4,2,128,896]{3,2,1,0:T(8,128)(2,1)S(1)}, u32[]{:S(2)}, u32[]{:S(2)}) async-start(bf16[4,2,128,896]{3,2,1,0:T(8,128)(2,1)} %get-tuple-element.184), calls=%async_computation | async-start | bytes 3670016 | tf_op jit(solution)/shard_map/all_to_all | solution.py:901
  45.7 17.4 %collective-permute-start.6 = (bf16[2,96,3072]{2,1,0:T(8,128)(2,1)}, bf16[2,96,3072]{2,1,0:T(8,128)(2,1)S(1)}, u32[]{:S(2)}, u32[]{:S(2)}) collective-permute-start(bf16[2,96,3072]{2,1,0:T(8,128)(2,1)} %collective-permute-done.1.refs_9_), channel_id=1, source_target_pairs={{0,1},{1,0},{2,3},{3,2},{4,5},{5,4},{6,7},{7,6},{8,9},{9,8},{10,11... | collective-permute-start | bytes 3538952 | tf_op jit(solution)/shard_map/ppermute | solution.py:772
  46.9 16.2 %collective-permute-start.5 = (bf16[2,96,3072]{2,1,0:T(8,128)(2,1)}, bf16[2,96,3072]{2,1,0:T(8,128)(2,1)S(1)}, u32[]{:S(2)}, u32[]{:S(2)}) collective-permute-start(bf16[2,96,3072]{2,1,0:T(8,128)(2,1)} %collective-permute-done.refs_8_), channel_id=1, source_target_pairs={{0,1},{1,0},{2,3},{3,2},{4,5},{5,4},{6,7},{7,6},{8,9},{9,8},{10,11... | collective-permute-start | bytes 3538952 | tf_op jit(solution)/shard_map/ppermute | solution.py:772
  47.4 15.4 %collective-permute-start.3 = (bf16[2,48,3072]{2,1,0:T(8,128)(2,1)S(1)}, bf16[2,48,3072]{2,1,0:T(8,128)(2,1)}, u32[]{:S(2)}, u32[]{:S(2)}) collective-permute-start(bf16[2,48,3072]{2,1,0:T(8,128)(2,1)S(1)} %slice.191), channel_id=1, source_target_pairs={{0,4},{1,5},{2,6},{3,7},{4,0},{5,1},{6,2},{7,3},{8,12},{9,13},{10,... | collective-permute-start | bytes 1769480 | tf_op jit(solution)/shard_map/ppermute | solution.py:772
  47.9 15.1 %collective-permute-start.2 = (bf16[2,48,3072]{2,1,0:T(8,128)(2,1)S(1)}, bf16[2,48,3072]{2,1,0:T(8,128)(2,1)}, u32[]{:S(2)}, u32[]{:S(2)}) collective-permute-start(bf16[2,48,3072]{2,1,0:T(8,128)(2,1)S(1)} %slice.190), channel_id=1, source_target_pairs={{0,2},{1,3},{2,0},{3,1},{4,6},{5,7},{6,4},{7,5},{8,10},{9,11},{10,... | collective-permute-start | bytes 1769480 | tf_op jit(solution)/shard_map/ppermute | solution.py:772
  48.5 14.6 %collective-permute-start.4 = (bf16[2,96,3072]{2,1,0:T(8,128)(2,1)}, bf16[2,96,3072]{2,1,0:T(8,128)(2,1)S(1)}, u32[]{:S(2)}, u32[]{:S(2)}) collective-permute-start(bf16[2,96,3072]{2,1,0:T(8,128)(2,1)} %constant_dynamic-update-slice_fusion.refs_7_), channel_id=1, source_target_pairs={{0,1},{1,0},{2,3},{3,2},{4,5},{5,4},{6,7},{7,6},{8,9},{9,8},{10,11... | collective-permute-start | bytes 3538952 | tf_op jit(solution)/shard_map/ppermute | solution.py:772
  63.1 32.1 %collective-permute-start.10 = (bf16[2,384,768]{2,1,0:T(8,128)(2,1)S(1)}, bf16[2,384,768]{2,1,0:T(8,128)(2,1)}, u32[]{:S(2)}, u32[]{:S(2)}) collective-permute-start(bf16[2,384,768]{2,1,0:T(8,128)(2,1)S(1)} %pad_maximum_fusion.refs_17_), channel_id=1, source_target_pairs={{0,4},{1,5},{2,6},{3,7},{4,0},{5,1},{6,2},{7,3},{8,12},{9,13},{10,... | collective-permute-start | bytes 3538952 | tf_op jit(solution)/shard_map/ppermute | solution.py:772
  64.7 31.2 %collective-permute-start.9 = (bf16[2,384,768]{2,1,0:T(8,128)(2,1)S(1)}, bf16[2,384,768]{2,1,0:T(8,128)(2,1)}, u32[]{:S(2)}, u32[]{:S(2)}) collective-permute-start(bf16[2,384,768]{2,1,0:T(8,128)(2,1)S(1)} %pad_maximum_fusion.refs_17_), channel_id=1, source_target_pairs={{0,2},{1,3},{2,0},{3,1},{4,6},{5,7},{6,4},{7,5},{8,10},{9,11},{10,... | collective-permute-start | bytes 3538952 | tf_op jit(solution)/shard_map/ppermute | solution.py:772
  74.1 14.1 %collective-permute-start.7 = (bf16[2,128,768]{2,1,0:T(8,128)(2,1)}, bf16[2,128,768]{2,1,0:T(8,128)(2,1)S(1)}, u32[]{:S(2)}, u32[]{:S(2)}) collective-permute-start(bf16[2,128,768]{2,1,0:T(8,128)(2,1)} %get-tuple-element.176), channel_id=1, source_target_pairs={{0,8},{8,16},{16,24},{24,0},{1,9},{9,17},{17,25},{25,1},{2,10},{10... | collective-permute-start | bytes 1179656 | tf_op jit(solution)/shard_map/ppermute | solution.py:898
  76.1 19.0 %collective-permute-start.8 = (bf16[2,128,768]{2,1,0:T(8,128)(2,1)}, bf16[2,128,768]{2,1,0:T(8,128)(2,1)S(1)}, u32[]{:S(2)}, u32[]{:S(2)}) collective-permute-start(bf16[2,128,768]{2,1,0:T(8,128)(2,1)} %get-tuple-element.177), channel_id=1, source_target_pairs={{0,24},{8,0},{16,8},{24,16},{1,25},{9,1},{17,9},{25,17},{2,26},{10... | collective-permute-start | bytes 1179656 | tf_op jit(solution)/shard_map/ppermute | solution.py:898
  97.0 22.7 %collective-permute-start.14 = (bf16[2,192,768]{2,1,0:T(8,128)(2,1)S(1)}, bf16[2,192,768]{2,1,0:T(8,128)(2,1)}, u32[]{:S(2)}, u32[]{:S(2)}) collective-permute-start(bf16[2,192,768]{2,1,0:T(8,128)(2,1)S(1)} %slice.192), channel_id=1, source_target_pairs={{0,2},{1,3},{2,0},{3,1},{4,6},{5,7},{6,4},{7,5},{8,10},{9,11},{10,... | collective-permute-start | bytes 1769480 | tf_op jit(solution)/shard_map/ppermute | solution.py:772
  98.8 21.5 %collective-permute-start.15 = (bf16[2,192,768]{2,1,0:T(8,128)(2,1)S(1)}, bf16[2,192,768]{2,1,0:T(8,128)(2,1)}, u32[]{:S(2)}, u32[]{:S(2)}) collective-permute-start(bf16[2,192,768]{2,1,0:T(8,128)(2,1)S(1)} %slice.193), channel_id=1, source_target_pairs={{0,4},{1,5},{2,6},{3,7},{4,0},{5,1},{6,2},{7,3},{8,12},{9,13},{10,... | collective-permute-start | bytes 1769480 | tf_op jit(solution)/shard_map/ppermute | solution.py:772
  99.9 19.8 %collective-permute-start.11 = (bf16[2,128,768]{2,1,0:T(8,128)(2,1)S(1)}, bf16[2,128,768]{2,1,0:T(8,128)(2,1)S(1)}, u32[]{:S(2)}, u32[]{:S(2)}) collective-permute-start(bf16[2,128,768]{2,1,0:T(8,128)(2,1)S(1)} %copy-done.35), channel_id=1, source_target_pairs={{0,16},{8,24},{16,0},{24,8},{1,17},{9,25},{17,1},{25,9},{2,18},{10... | collective-permute-start | bytes 1179656 | tf_op jit(solution)/shard_map/ppermute | solution.py:898
  100.5 26.6 %collective-permute-start.17 = (bf16[2,384,768]{2,1,0:T(8,128)(2,1)}, bf16[2,384,768]{2,1,0:T(8,128)(2,1)}, u32[]{:S(2)}, u32[]{:S(2)}) collective-permute-start(bf16[2,384,768]{2,1,0:T(8,128)(2,1)} %collective-permute-done.9.refs_18_), channel_id=1, source_target_pairs={{0,1},{1,0},{2,3},{3,2},{4,5},{5,4},{6,7},{7,6},{8,9},{9,8},{10,11... | collective-permute-start | bytes 3538952 | tf_op jit(solution)/shard_map/ppermute | solution.py:772
  100.5 20.0 %collective-permute-start.12 = (bf16[2,48,3072]{2,1,0:T(8,128)(2,1)}, bf16[2,48,3072]{2,1,0:T(8,128)(2,1)}, u32[]{:S(2)}, u32[]{:S(2)}) collective-permute-start(bf16[2,48,3072]{2,1,0:T(8,128)(2,1)} %collective-permute-done.2.refs_10_), channel_id=1, source_target_pairs={{0,1},{1,0},{2,3},{3,2},{4,5},{5,4},{6,7},{7,6},{8,9},{9,8},{10,11... | collective-permute-start | bytes 1769480 | tf_op jit(solution)/shard_map/ppermute | solution.py:772
  119.7 2.3 collective-permute-start.13
  119.8 7.4 %collective-permute-start.16 = (bf16[2,384,768]{2,1,0:T(8,128)(2,1)S(1)}, bf16[2,384,768]{2,1,0:T(8,128)(2,1)}, u32[]{:S(2)}, u32[]{:S(2)}) collective-permute-start(bf16[2,384,768]{2,1,0:T(8,128)(2,1)S(1)} %pad_maximum_fusion.refs_17_), channel_id=1, source_target_pairs={{0,1},{1,0},{2,3},{3,2},{4,5},{5,4},{6,7},{7,6},{8,9},{9,8},{10,11... | collective-permute-start | bytes 3538952 | tf_op jit(solution)/shard_map/ppermute | solution.py:772
  120.5 6.7 %collective-permute-start.18 = (bf16[2,384,768]{2,1,0:T(8,128)(2,1)}, bf16[2,384,768]{2,1,0:T(8,128)(2,1)}, u32[]{:S(2)}, u32[]{:S(2)}) collective-permute-start(bf16[2,384,768]{2,1,0:T(8,128)(2,1)} %collective-permute-done.10.refs_19_), channel_id=1, source_target_pairs={{0,1},{1,0},{2,3},{3,2},{4,5},{5,4},{6,7},{7,6},{8,9},{9,8},{10,11... | collective-permute-start | bytes 3538952 | tf_op jit(solution)/shard_map/ppermute | solution.py:772
  120.5 5.8 %collective-permute-start.19 = (bf16[2,192,768]{2,1,0:T(8,128)(2,1)}, bf16[2,192,768]{2,1,0:T(8,128)(2,1)}, u32[]{:S(2)}, u32[]{:S(2)}) collective-permute-start(bf16[2,192,768]{2,1,0:T(8,128)(2,1)} %collective-permute-done.14.refs_20_), channel_id=1, source_target_pairs={{0,1},{1,0},{2,3},{3,2},{4,5},{5,4},{6,7},{7,6},{8,9},{9,8},{10,11... | collective-permute-start | bytes 1769480 | tf_op jit(solution)/shard_map/ppermute | solution.py:772
  122.1 5.1 %collective-permute-start.20 = (bf16[2,192,768]{2,1,0:T(8,128)(2,1)}, bf16[2,192,768]{2,1,0:T(8,128)(2,1)}, u32[]{:S(2)}, u32[]{:S(2)}) collective-permute-start(bf16[2,192,768]{2,1,0:T(8,128)(2,1)} %collective-permute-done.15.refs_21_), channel_id=1, source_target_pairs={{0,1},{1,0},{2,3},{3,2},{4,5},{5,4},{6,7},{7,6},{8,9},{9,8},{10,11... | collective-permute-start | bytes 1769480 | tf_op jit(solution)/shard_map/ppermute | solution.py:772
  152.8 27.6 %collective-permute-start.27 = (bf16[4,96,3072]{2,1,0:T(8,128)(2,1)}, bf16[4,96,3072]{2,1,0:T(8,128)(2,1)S(1)}, u32[]{:S(2)}, u32[]{:S(2)}) collective-permute-start(bf16[4,96,3072]{2,1,0:T(8,128)(2,1)} %get-tuple-element.213), channel_id=1, source_target_pairs={{0,1},{1,0},{2,3},{3,2},{4,5},{5,4},{6,7},{7,6},{8,9},{9,8},{10,11... | collective-permute-start | bytes 7077896 | tf_op jit(solution)/shard_map/ppermute | solution.py:772
  153.0 27.4 %collective-permute-start.28 = (bf16[4,384,768]{2,1,0:T(8,128)(2,1)}, bf16[4,384,768]{2,1,0:T(8,128)(2,1)S(1)}, u32[]{:S(2)}, u32[]{:S(2)}) collective-permute-start(bf16[4,384,768]{2,1,0:T(8,128)(2,1)} %get-tuple-element.214), channel_id=1, source_target_pairs={{0,1},{1,0},{2,3},{3,2},{4,5},{5,4},{6,7},{7,6},{8,9},{9,8},{10,11... | collective-permute-start | bytes 7077896 | tf_op jit(solution)/shard_map/ppermute | solution.py:772
  154.0 21.1 %collective-permute-start.21 = (bf16[128,768]{1,0:T(8,128)(2,1)}, bf16[128,768]{1,0:T(8,128)(2,1)S(1)}, u32[]{:S(2)}, u32[]{:S(2)}) collective-permute-start(bf16[128,768]{1,0:T(8,128)(2,1)} %get-tuple-element.199), channel_id=1, source_target_pairs={{0,24},{8,0},{16,8},{24,16},{1,25},{9,1},{17,9},{25,17},{2,26},{10... | collective-permute-start | bytes 589832 | tf_op jit(solution)/shard_map/ppermute | solution.py:906
  154.3 20.8 %collective-permute-start.22 = (bf16[128,768]{1,0:T(8,128)(2,1)}, bf16[128,768]{1,0:T(8,128)(2,1)S(1)}, u32[]{:S(2)}, u32[]{:S(2)}) collective-permute-start(bf16[128,768]{1,0:T(8,128)(2,1)} %get-tuple-element.200), channel_id=1, source_target_pairs={{0,16},{8,24},{16,0},{24,8},{1,17},{9,25},{17,1},{25,9},{2,18},{10... | collective-permute-start | bytes 589832 | tf_op jit(solution)/shard_map/ppermute | solution.py:906
  154.3 20.8 %collective-permute-start.23 = (bf16[128,768]{1,0:T(8,128)(2,1)}, bf16[128,768]{1,0:T(8,128)(2,1)S(1)}, u32[]{:S(2)}, u32[]{:S(2)}) collective-permute-start(bf16[128,768]{1,0:T(8,128)(2,1)} %get-tuple-element.201), channel_id=1, source_target_pairs={{0,8},{8,16},{16,24},{24,0},{1,9},{9,17},{17,25},{25,1},{2,10},{10... | collective-permute-start | bytes 589832 | tf_op jit(solution)/shard_map/ppermute | solution.py:906
  175.1 10.0 %collective-permute-start.24 = (bf16[128,768]{1,0:T(8,128)(2,1)}, bf16[128,768]{1,0:T(8,128)(2,1)}, u32[]{:S(2)}, u32[]{:S(2)}) collective-permute-start(bf16[128,768]{1,0:T(8,128)(2,1)} %get-tuple-element.204), channel_id=1, source_target_pairs={{0,24},{8,0},{16,8},{24,16},{1,25},{9,1},{17,9},{25,17},{2,26},{10... | collective-permute-start | bytes 589832 | tf_op jit(solution)/shard_map/ppermute | solution.py:906
  177.7 17.9 %collective-permute-start.25 = (bf16[128,768]{1,0:T(8,128)(2,1)}, bf16[128,768]{1,0:T(8,128)(2,1)}, u32[]{:S(2)}, u32[]{:S(2)}) collective-permute-start(bf16[128,768]{1,0:T(8,128)(2,1)} %get-tuple-element.206), channel_id=1, source_target_pairs={{0,16},{8,24},{16,0},{24,8},{1,17},{9,25},{17,1},{25,9},{2,18},{10... | collective-permute-start | bytes 589832 | tf_op jit(solution)/shard_map/ppermute | solution.py:906
  178.6 17.0 %collective-permute-start.26 = (bf16[128,768]{1,0:T(8,128)(2,1)}, bf16[128,768]{1,0:T(8,128)(2,1)}, u32[]{:S(2)}, u32[]{:S(2)}) collective-permute-start(bf16[128,768]{1,0:T(8,128)(2,1)} %get-tuple-element.208), channel_id=1, source_target_pairs={{0,8},{8,16},{16,24},{24,0},{1,9},{9,17},{17,25},{25,1},{2,10},{10... | collective-permute-start | bytes 589832 | tf_op jit(solution)/shard_map/ppermute | solution.py:906
  195.6 18.4 %collective-permute-start.30 = (bf16[96,3072]{1,0:T(8,128)(2,1)}, bf16[96,3072]{1,0:T(8,128)(2,1)}, u32[]{:S(2)}, u32[]{:S(2)}) collective-permute-start(bf16[96,3072]{1,0:T(8,128)(2,1)} %get-tuple-element.313), channel_id=1, source_target_pairs={{0,4},{1,5},{2,6},{3,7},{4,0},{5,1},{6,2},{7,3},{8,12},{9,13},{10,... | collective-permute-start | bytes 1769480 | tf_op jit(solution)/shard_map/ppermute | solution.py:772
  196.5 17.5 %collective-permute-start.29 = (bf16[96,3072]{1,0:T(8,128)(2,1)}, bf16[96,3072]{1,0:T(8,128)(2,1)}, u32[]{:S(2)}, u32[]{:S(2)}) collective-permute-start(bf16[96,3072]{1,0:T(8,128)(2,1)} %get-tuple-element.314), channel_id=1, source_target_pairs={{0,2},{1,3},{2,0},{3,1},{4,6},{5,7},{6,4},{7,5},{8,10},{9,11},{10,... | collective-permute-start | bytes 1769480 | tf_op jit(solution)/shard_map/ppermute | solution.py:772
  211.4 27.4 %collective-permute-start.35 = (bf16[4,4,2,24,384]{4,3,2,1,0:T(8,128)(2,1)}, bf16[4,4,2,24,384]{4,3,2,1,0:T(8,128)(2,1)}, u32[]{:S(2)}, u32[]{:S(2)}) collective-permute-start(bf16[4,4,2,24,384]{4,3,2,1,0:T(8,128)(2,1)} %get-tuple-element.249), channel_id=1, source_target_pairs={{0,1},{1,0},{2,3},{3,2},{4,5},{5,4},{6,7},{7,6},{8,9},{9,8},{10,11... | collective-permute-start | bytes 1769480 | tf_op jit(solution)/shard_map/ppermute | solution.py:772
  212.2 27.8 %collective-permute-start.31 = (bf16[96,3072]{1,0:T(8,128)(2,1)}, bf16[96,3072]{1,0:T(8,128)(2,1)}, u32[]{:S(2)}, u32[]{:S(2)}) collective-permute-start(bf16[96,3072]{1,0:T(8,128)(2,1)} %get-tuple-element.237), channel_id=1, source_target_pairs={{0,6},{1,7},{2,4},{3,5},{4,2},{5,3},{6,0},{7,1},{8,14},{9,15},{10,... | collective-permute-start | bytes 1769480 | tf_op jit(solution)/shard_map/ppermute | solution.py:772
  214.1 50.2 %all-to-all-start.1 = ((bf16[4,2,128,768]{3,2,1,0:T(8,128)(2,1)}), bf16[4,2,128,768]{3,2,1,0:T(8,128)(2,1)}, u32[]{:S(2)}, u32[]{:S(2)}) async-start(bf16[4,2,128,768]{3,2,1,0:T(8,128)(2,1)} %get-tuple-element.245), calls=%async_computation.1 | async-start | bytes 3145728 | tf_op jit(solution)/shard_map/all_to_all | solution.py:901
  218.4 22.3 %collective-permute-start.32 = (bf16[384,768]{1,0:T(8,128)(2,1)}, bf16[384,768]{1,0:T(8,128)(2,1)S(1)}, u32[]{:S(2)}, u32[]{:S(2)}) collective-permute-start(bf16[384,768]{1,0:T(8,128)(2,1)} %get-tuple-element.238), channel_id=1, source_target_pairs={{0,2},{1,3},{2,0},{3,1},{4,6},{5,7},{6,4},{7,5},{8,10},{9,11},{10,... | collective-permute-start | bytes 1769480 | tf_op jit(solution)/shard_map/ppermute | solution.py:772
  219.4 22.3 %collective-permute-start.33 = (bf16[384,768]{1,0:T(8,128)(2,1)}, bf16[384,768]{1,0:T(8,128)(2,1)S(1)}, u32[]{:S(2)}, u32[]{:S(2)}) collective-permute-start(bf16[384,768]{1,0:T(8,128)(2,1)} %get-tuple-element.239), channel_id=1, source_target_pairs={{0,4},{1,5},{2,6},{3,7},{4,0},{5,1},{6,2},{7,3},{8,12},{9,13},{10,... | collective-permute-start | bytes 1769480 | tf_op jit(solution)/shard_map/ppermute | solution.py:772
  238.7 25.1 %collective-permute-start.34 = (bf16[4,4,3,24,384]{4,3,2,1,0:T(8,128)(2,1)}, bf16[4,4,3,24,384]{4,3,2,1,0:T(8,128)(2,1)S(1)}, u32[]{:S(2)}, u32[]{:S(2)}) collective-permute-start(bf16[4,4,3,24,384]{4,3,2,1,0:T(8,128)(2,1)} %get-tuple-element.247), channel_id=1, source_target_pairs={{0,1},{1,0},{2,3},{3,2},{4,5},{5,4},{6,7},{7,6},{8,9},{9,8},{10,11... | collective-permute-start | bytes 2654216 | tf_op jit(solution)/shard_map/ppermute | solution.py:772
  241.7 44.1 %collective-permute-start.36 = (bf16[384,768]{1,0:T(8,128)(2,1)S(1)}, bf16[384,768]{1,0:T(8,128)(2,1)}, u32[]{:S(2)}, u32[]{:S(2)}) collective-permute-start(bf16[384,768]{1,0:T(8,128)(2,1)S(1)} %get-tuple-element.254), channel_id=1, source_target_pairs={{0,6},{1,7},{2,4},{3,5},{4,2},{5,3},{6,0},{7,1},{8,14},{9,15},{10,... | collective-permute-start | bytes 1769480 | tf_op jit(solution)/shard_map/ppermute | solution.py:772
  260.7 17.3 %collective-permute-start.41 = (bf16[4,4,3,24,384]{4,3,2,1,0:T(8,128)(2,1)}, bf16[4,4,3,24,384]{4,3,2,1,0:T(8,128)(2,1)}, u32[]{:S(2)}, u32[]{:S(2)}) collective-permute-start(bf16[4,4,3,24,384]{4,3,2,1,0:T(8,128)(2,1)} %get-tuple-element.267), channel_id=1, source_target_pairs={{0,1},{1,0},{2,3},{3,2},{4,5},{5,4},{6,7},{7,6},{8,9},{9,8},{10,11... | collective-permute-start | bytes 2654216 | tf_op jit(solution)/shard_map/ppermute | solution.py:772
  264.3 16.3 %collective-permute-start.37 = (bf16[4,5,24,384]{3,2,1,0:T(8,128)(2,1)S(1)}, bf16[4,5,24,384]{3,2,1,0:T(8,128)(2,1)S(1)}, u32[]{:S(2)}, u32[]{:S(2)}) collective-permute-start(bf16[4,5,24,384]{3,2,1,0:T(8,128)(2,1)S(1)} %pad_maximum_fusion.2), channel_id=1, source_target_pairs={{0,2},{1,3},{2,0},{3,1},{4,6},{5,7},{6,4},{7,5},{8,10},{9,11},{10,... | collective-permute-start | bytes 1105928 | tf_op jit(solution)/shard_map/ppermute | solution.py:772
  265.4 18.8 %collective-permute-start.38 = (bf16[4,5,24,384]{3,2,1,0:T(8,128)(2,1)S(1)}, bf16[4,5,24,384]{3,2,1,0:T(8,128)(2,1)S(1)}, u32[]{:S(2)}, u32[]{:S(2)}) collective-permute-start(bf16[4,5,24,384]{3,2,1,0:T(8,128)(2,1)S(1)} %pad_maximum_fusion.3), channel_id=1, source_target_pairs={{0,4},{1,5},{2,6},{3,7},{4,0},{5,1},{6,2},{7,3},{8,12},{9,13},{10,... | collective-permute-start | bytes 1105928 | tf_op jit(solution)/shard_map/ppermute | solution.py:772
  266.8 18.2 %collective-permute-start.39 = (bf16[4,5,24,384]{3,2,1,0:T(8,128)(2,1)S(1)}, bf16[4,5,24,384]{3,2,1,0:T(8,128)(2,1)S(1)}, u32[]{:S(2)}, u32[]{:S(2)}) collective-permute-start(bf16[4,5,24,384]{3,2,1,0:T(8,128)(2,1)S(1)} %pad_maximum_fusion.4), channel_id=1, source_target_pairs={{0,6},{1,7},{2,4},{3,5},{4,2},{5,3},{6,0},{7,1},{8,14},{9,15},{10,... | collective-permute-start | bytes 1105928 | tf_op jit(solution)/shard_map/ppermute | solution.py:772
  279.5 9.4 %collective-permute-start.42 = (bf16[4,3,24,384]{3,2,1,0:T(8,128)(2,1)S(1)}, bf16[4,3,24,384]{3,2,1,0:T(8,128)(2,1)S(1)}, u32[]{:S(2)}, u32[]{:S(2)}) collective-permute-start(bf16[4,3,24,384]{3,2,1,0:T(8,128)(2,1)S(1)} %get-tuple-element.269), channel_id=1, source_target_pairs={{0,2},{1,3},{2,0},{3,1},{4,6},{5,7},{6,4},{7,5},{8,10},{9,11},{10,... | collective-permute-start | bytes 663560 | tf_op jit(solution)/shard_map/ppermute | solution.py:772
  280.6 12.8 %collective-permute-start.43 = (bf16[4,3,24,384]{3,2,1,0:T(8,128)(2,1)S(1)}, bf16[4,3,24,384]{3,2,1,0:T(8,128)(2,1)S(1)}, u32[]{:S(2)}, u32[]{:S(2)}) collective-permute-start(bf16[4,3,24,384]{3,2,1,0:T(8,128)(2,1)S(1)} %get-tuple-element.270), channel_id=1, source_target_pairs={{0,4},{1,5},{2,6},{3,7},{4,0},{5,1},{6,2},{7,3},{8,12},{9,13},{10,... | collective-permute-start | bytes 663560 | tf_op jit(solution)/shard_map/ppermute | solution.py:772
  284.3 9.2 %collective-permute-start.44 = (bf16[4,3,24,384]{3,2,1,0:T(8,128)(2,1)S(1)}, bf16[4,3,24,384]{3,2,1,0:T(8,128)(2,1)S(1)}, u32[]{:S(2)}, u32[]{:S(2)}) collective-permute-start(bf16[4,3,24,384]{3,2,1,0:T(8,128)(2,1)S(1)} %get-tuple-element.271), channel_id=1, source_target_pairs={{0,6},{1,7},{2,4},{3,5},{4,2},{5,3},{6,0},{7,1},{8,14},{9,15},{10,... | collective-permute-start | bytes 663560 | tf_op jit(solution)/shard_map/ppermute | solution.py:772
  285.2 8.2 %collective-permute-start.40 = (bf16[2,5,24,384]{3,2,1,0:T(8,128)(2,1)S(1)}, bf16[2,5,24,384]{3,2,1,0:T(8,128)(2,1)S(1)}, u32[]{:S(2)}, u32[]{:S(2)}) collective-permute-start(bf16[2,5,24,384]{3,2,1,0:T(8,128)(2,1)S(1)} %get-tuple-element.332), channel_id=1, source_target_pairs={{0,8},{8,0},{16,24},{24,16},{1,9},{9,1},{17,25},{25,17},{2,10},{10... | collective-permute-start | bytes 552968 | tf_op jit(solution)/shard_map/ppermute | solution.py:777
  293.5 6.6 %collective-permute-start.45 = (bf16[1,5,24,384]{3,2,1,0:T(8,128)(2,1)S(1)}, bf16[1,5,24,384]{3,2,1,0:T(8,128)(2,1)S(1)}, u32[]{:S(2)}, u32[]{:S(2)}) collective-permute-start(bf16[1,5,24,384]{3,2,1,0:T(8,128)(2,1)S(1)} %get-tuple-element.336), channel_id=1, source_target_pairs={{0,16},{8,24},{16,0},{24,8},{1,17},{9,25},{17,1},{25,9},{2,18},{10... | collective-permute-start | bytes 276488 | tf_op jit(solution)/shard_map/ppermute | solution.py:777
  296.1 5.4 %collective-permute-start.46 = (bf16[2,3,24,384]{3,2,1,0:T(8,128)(2,1)S(1)}, bf16[2,3,24,384]{3,2,1,0:T(8,128)(2,1)S(1)}, u32[]{:S(2)}, u32[]{:S(2)}) collective-permute-start(bf16[2,3,24,384]{3,2,1,0:T(8,128)(2,1)S(1)} %get-tuple-element.334), channel_id=1, source_target_pairs={{0,8},{8,0},{16,24},{24,16},{1,9},{9,1},{17,25},{25,17},{2,10},{10... | collective-permute-start | bytes 331784 | tf_op jit(solution)/shard_map/ppermute | solution.py:777
  301.5 8.4 %collective-permute-start.47 = (bf16[5,24,384]{2,1,0:T(8,128)(2,1)S(1)}, bf16[5,24,384]{2,1,0:T(8,128)(2,1)S(1)}, u32[]{:S(2)}, u32[]{:S(2)}) collective-permute-start(bf16[5,24,384]{2,1,0:T(8,128)(2,1)S(1)} %fusion.22), channel_id=1, source_target_pairs={{0,16},{8,24},{16,0},{24,8},{1,17},{9,25},{17,1},{25,9},{2,18},{10... | collective-permute-start | bytes 276488 | tf_op jit(solution)/shard_map/ppermute | solution.py:777
  302.1 7.9 %collective-permute-start.48 = (bf16[1,3,24,384]{3,2,1,0:T(8,128)(2,1)S(1)}, bf16[1,3,24,384]{3,2,1,0:T(8,128)(2,1)S(1)}, u32[]{:S(2)}, u32[]{:S(2)}) collective-permute-start(bf16[1,3,24,384]{3,2,1,0:T(8,128)(2,1)S(1)} %get-tuple-element.338), channel_id=1, source_target_pairs={{0,16},{8,24},{16,0},{24,8},{1,17},{9,25},{17,1},{25,9},{2,18},{10... | collective-permute-start | bytes 165896 | tf_op jit(solution)/shard_map/ppermute | solution.py:777
  310.0 7.4 %collective-permute-start.49 = (bf16[2,5,24,384]{3,2,1,0:T(8,128)(2,1)S(1)}, bf16[2,5,24,384]{3,2,1,0:T(8,128)(2,1)S(1)}, u32[]{:S(2)}, u32[]{:S(2)}) collective-permute-start(bf16[2,5,24,384]{3,2,1,0:T(8,128)(2,1)S(1)} %pad_maximum_fusion.7), channel_id=1, source_target_pairs={{0,8},{8,0},{16,24},{24,16},{1,9},{9,1},{17,25},{25,17},{2,10},{10... | collective-permute-start | bytes 552968 | tf_op jit(solution)/shard_map/ppermute | solution.py:777
  310.1 5.9 %collective-permute-start.50 = (bf16[4,24,384]{2,1,0:T(8,128)(2,1)S(1)}, bf16[4,24,384]{2,1,0:T(8,128)(2,1)S(1)}, u32[]{:S(2)}, u32[]{:S(2)}) collective-permute-start(bf16[4,24,384]{2,1,0:T(8,128)(2,1)S(1)} %maximum_maximum_fusion), channel_id=1, source_target_pairs={{0,16},{8,24},{16,0},{24,8},{1,17},{9,25},{17,1},{25,9},{2,18},{10... | collective-permute-start | bytes 221192 | tf_op jit(solution)/shard_map/ppermute | solution.py:777
  317.5 12.4 %collective-permute-start.53 = (bf16[20,24,384]{2,1,0:T(8,128)(2,1)S(1)}, bf16[20,24,384]{2,1,0:T(8,128)(2,1)S(1)}, u32[]{:S(2)}, u32[]{:S(2)}) collective-permute-start(bf16[20,24,384]{2,1,0:T(8,128)(2,1)S(1)} %bitcast.79), channel_id=1, source_target_pairs={{0,6},{1,7},{2,4},{3,5},{4,2},{5,3},{6,0},{7,1},{8,14},{9,15},{10,... | collective-permute-start | bytes 1105928 | tf_op jit(solution)/shard_map/ppermute | solution.py:772
  318.9 16.9 %collective-permute-start.52 = (bf16[20,24,384]{2,1,0:T(8,128)(2,1)S(1)}, bf16[20,24,384]{2,1,0:T(8,128)(2,1)S(1)}, u32[]{:S(2)}, u32[]{:S(2)}) collective-permute-start(bf16[20,24,384]{2,1,0:T(8,128)(2,1)S(1)} %bitcast.80), channel_id=1, source_target_pairs={{0,4},{1,5},{2,6},{3,7},{4,0},{5,1},{6,2},{7,3},{8,12},{9,13},{10,... | collective-permute-start | bytes 1105928 | tf_op jit(solution)/shard_map/ppermute | solution.py:772
  320.4 15.5 %collective-permute-start.51 = (bf16[20,24,384]{2,1,0:T(8,128)(2,1)S(1)}, bf16[20,24,384]{2,1,0:T(8,128)(2,1)S(1)}, u32[]{:S(2)}, u32[]{:S(2)}) collective-permute-start(bf16[20,24,384]{2,1,0:T(8,128)(2,1)S(1)} %bitcast.81), channel_id=1, source_target_pairs={{0,2},{1,3},{2,0},{3,1},{4,6},{5,7},{6,4},{7,5},{8,10},{9,11},{10,... | collective-permute-start | bytes 1105928 | tf_op jit(solution)/shard_map/ppermute | solution.py:772
  321.1 15.9 %collective-permute-start.58 = (bf16[7,24,384]{2,1,0:T(8,128)(2,1)S(1)}, bf16[7,24,384]{2,1,0:T(8,128)(2,1)S(1)}, u32[]{:S(2)}, u32[]{:S(2)}) collective-permute-start(bf16[7,24,384]{2,1,0:T(8,128)(2,1)S(1)} %pad_maximum_fusion.8), channel_id=1, source_target_pairs={{0,8},{8,0},{16,24},{24,16},{1,9},{9,1},{17,25},{25,17},{2,10},{10... | collective-permute-start | bytes 387080 | tf_op jit(solution)/shard_map/ppermute | solution.py:777
  335.9 2.6 collective-permute-start.54
  335.9 3.2 collective-permute-start.55
  336.4 4.2 %collective-permute-start.56 = (bf16[20,24,384]{2,1,0:T(8,128)(2,1)S(1)}, bf16[20,24,384]{2,1,0:T(8,128)(2,1)S(1)}, u32[]{:S(2)}, u32[]{:S(2)}) collective-permute-start(bf16[20,24,384]{2,1,0:T(8,128)(2,1)S(1)} %collective-permute-done.52.refs_4_), channel_id=1, source_target_pairs={{0,1},{1,0},{2,3},{3,2},{4,5},{5,4},{6,7},{7,6},{8,9},{9,8},{10,11... | collective-permute-start | bytes 1105928 | tf_op jit(solution)/shard_map/ppermute | solution.py:772
  336.5 4.1 %collective-permute-start.57 = (bf16[20,24,384]{2,1,0:T(8,128)(2,1)S(1)}, bf16[20,24,384]{2,1,0:T(8,128)(2,1)S(1)}, u32[]{:S(2)}, u32[]{:S(2)}) collective-permute-start(bf16[20,24,384]{2,1,0:T(8,128)(2,1)S(1)} %collective-permute-done.53.refs_6_), channel_id=1, source_target_pairs={{0,1},{1,0},{2,3},{3,2},{4,5},{5,4},{6,7},{7,6},{8,9},{9,8},{10,11... | collective-permute-start | bytes 1105928 | tf_op jit(solution)/shard_map/ppermute | solution.py:772
  337.1 10.8 %collective-permute-start.61 = (bf16[13,24,384]{2,1,0:T(8,128)(2,1)S(1)}, bf16[13,24,384]{2,1,0:T(8,128)(2,1)S(1)}, u32[]{:S(2)}, u32[]{:S(2)}) collective-permute-start(bf16[13,24,384]{2,1,0:T(8,128)(2,1)S(1)} %pad_maximum_fusion.6.refs_0_), channel_id=1, source_target_pairs={{0,6},{1,7},{2,4},{3,5},{4,2},{5,3},{6,0},{7,1},{8,14},{9,15},{10,... | collective-permute-start | bytes 718856 | tf_op jit(solution)/shard_map/ppermute | solution.py:772
  338.5 12.5 %collective-permute-start.60 = (bf16[13,24,384]{2,1,0:T(8,128)(2,1)S(1)}, bf16[13,24,384]{2,1,0:T(8,128)(2,1)S(1)}, u32[]{:S(2)}, u32[]{:S(2)}) collective-permute-start(bf16[13,24,384]{2,1,0:T(8,128)(2,1)S(1)} %pad_maximum_fusion.6.refs_0_), channel_id=1, source_target_pairs={{0,4},{1,5},{2,6},{3,7},{4,0},{5,1},{6,2},{7,3},{8,12},{9,13},{10,... | collective-permute-start | bytes 718856 | tf_op jit(solution)/shard_map/ppermute | solution.py:772
  339.2 11.8 %collective-permute-start.59 = (bf16[13,24,384]{2,1,0:T(8,128)(2,1)S(1)}, bf16[13,24,384]{2,1,0:T(8,128)(2,1)S(1)}, u32[]{:S(2)}, u32[]{:S(2)}) collective-permute-start(bf16[13,24,384]{2,1,0:T(8,128)(2,1)S(1)} %pad_maximum_fusion.6.refs_0_), channel_id=1, source_target_pairs={{0,2},{1,3},{2,0},{3,1},{4,6},{5,7},{6,4},{7,5},{8,10},{9,11},{10,... | collective-permute-start | bytes 718856 | tf_op jit(solution)/shard_map/ppermute | solution.py:772
  (50 other events, 460.8 us)

commit v5 on v4

--- a/solution.py
+++ b/solution.py
@@ -938,8 +938,12 @@
         mixed, token_rows, w_proj, scales, slots, group, local, capacity
     )
     rows = [go(sent_rows[shift], shift) for shift in range(group)]
+    router = jnp.pad(w_router, ((0, 0), (0, LANES - experts)))
+    router_t = jnp.pad(w_router.T, ((0, LANES - experts), (0, 0)))
     if fast:
-        rows[1], rows[3], pair_out, *tied = tie(rows[1], rows[3], pair_out, *out_full, *in_half)
+        rows[1], rows[3], router, router_t, pair_out, *tied = tie(
+            rows[1], rows[3], router, router_t, pair_out, *out_full, *in_half
+        )
         out_full, in_half = tied[:2], tied[2:]
         out_half = relay(*out_full)
         in_parts = [pair_in, *in_full, *in_half]
@@ -953,8 +957,6 @@
             for trained, w_in, w_out in ((True, new_in, new_out), (False, old_in, old_out))
         }
     core, chip = (at[0] & 1, at[0] >> 1) if fast else (0, 0)
-    router = jnp.pad(w_router, ((0, 0), (0, LANES - experts)))
-    router_t = jnp.pad(w_router.T, ((0, LANES - experts), (0, 0)))
     outs, backs, router_sum = [], {}, 0.0
     half = experts // 2
     for trained in (True, False):

time: 364 us -> 363 us (level)
  no operation moved by 1% of the time
where the time goes in v5:
time: 363 us; the launch traced here: 359 us
  Pallas kernels  169 us (47%)
  waiting for transfers between devices  89.4 us (25%)
  starting transfers between devices  65.3 us (18%)
  other arithmetic  17.8 us (5%)
  local copies, waits for them, and re-layouts  14.6 us (4%)
    pallas_call x2, Pallas kernels, expert_call(): pl.pallas_call(functools.partial(expert_kernel, trained, group, len(held)...  44.6 us
    pallas_call x2, Pallas kernels, attend_back_call(): pl.pallas_call(attend_back_kernel, grid=(count,), in_specs=[smem()] + [pl...  35.6 us
    ppermute x49, starting transfers between devices, swap(): return lax.ppermute(block, 'batch', [(i, i ^ bits) for i in range(size)])  35.6 us
    ppermute x3, waiting for transfers between devices, go(): lax.ppermute(block, 'expert', [(i, (i + shift) % group) for i in range(gr...  33.9 us
    ppermute x49, waiting for transfers between devices, swap(): return lax.ppermute(block, 'batch', [(i, i ^ bits) for i in range(size)])  28.8 us
    pallas_call x2, Pallas kernels, attend_call(): pl.pallas_call(attend_kernel, grid=(count,), in_specs=[smem()] + [pl.Bloc...  26 us
    ppermute x8, waiting for transfers between devices, across(): return lax.ppermute(block, 'expert', [(i, i ^ bits) for i in range(size)])  16.2 us
    pallas_call x1, Pallas kernels, middle_call(): pl.pallas_call(functools.partial(middle_kernel, len(parts)), grid=(seq //...  13.4 us
  transfers between devices with their start and end apart: 68, of which 25 were waited for; matrix products, arithmetic and copies ran while one was open for 7% of the time, Pallas kernels for 39%

profile of v5, /device:TPU:0, one launch (start us, length us, event | category | flops | bytes accessed | tf_op | source)
XLA Modules:
  0.0 358.8 jit_solution(6875878670920423113)
XLA Ops:
  0.7 2.0 constant_dynamic-update-slice_fusion.1
  3.5 3.0 collective-permute-start.1
  6.5 1.5 collective-permute-start
  9.7 6.0 %route.1 = (s32[8,1024]{1,0:T(8,128)}, s32[1024,128]{1,0:T(8,128)}, bf16[4,2,128,896]{3,2,1,0:T(8,128)(2,1)}) custom-call(s32[1]{0:T(128)S(6)} %copy.34.len_ref, s32[1]{0:T(128)} %bitcast.me_ref, s32[2,1024]{1,0:T(2,128)} %copy.29.route_ref, s32[1024,2]{1,0:T(8,128)} %bitcast.76, bf16[1024,768]{1,0:T(8,128)(2,1)} %bitcast.87), custom_call_target="tpu_custom_call" | custom-call | flops 6270000128 | bytes 17100000 | tf_op jit(solution)/shard_map/route/pallas_call | solution.py:347
  15.7 5.2 %all-to-all-start = ((bf16[4,2,128,896]{3,2,1,0:T(8,128)(2,1)}), bf16[4,2,128,896]{3,2,1,0:T(8,128)(2,1)S(1)}, u32[]{:S(2)}, u32[]{:S(2)}) async-start(bf16[4,2,128,896]{3,2,1,0:T(8,128)(2,1)} %get-tuple-element.186), calls=%async_computation | async-start | bytes 3670016 | tf_op jit(solution)/shard_map/all_to_all | solution.py:901
  21.0 1.4 pad_maximum_fusion.refs_17_
  23.0 8.4 %norm_qkv.1 = (bf16[1024,768]{1,0:T(8,128)(2,1)}, bf16[1024,2304]{1,0:T(8,128)(2,1)}) custom-call(bf16[1024,768]{1,0:T(8,128)(2,1)} %bitcast.89, f32[4,768]{1,0:T(4,128)} %pad_maximum_fusion.10.scale_ref.gain_ref, bf16[768,2304]{1,0:T(8,128)(2,1)} %w_ref.7), custom_call_target="tpu_custom_call" | custom-call | flops 9569999872 | bytes 26100000 | tf_op jit(solution)/shard_map/norm_qkv/pallas_call | solution.py:80
  31.5 13.0 %attend.2 = (bf16[1024,384]{1,0:T(8,128)(2,1)}, f32[3,8,1024]{2,1,0:T(8,128)}) custom-call(s32[1]{0:T(128)S(6)} %copy.34.len_ref, bf16[1024,2304]{1,0:T(8,128)(2,1)} %get-tuple-element.168.q_ref.k_ref.v_ref, bf16[1024,2304]{1,0:T(8,128)(2,1)} %get-tuple-element.168.q_ref.k_ref.v_ref, bf16[1024,2304]{1,0:T(8,128)(2,1)} %get-tuple-element.168.q_ref.k_ref.v_ref), custom_call_target="tpu_custom_call" | custom-call | flops 13200000000 | bytes 36000000 | tf_op jit(solution)/shard_map/attend/pallas_call | solution.py:152
  44.5 1.1 slice.190
  45.7 1.1 slice.191
  48.4 13.0 %attend.3 = (bf16[1024,384]{1,0:T(8,128)(2,1)}, f32[3,8,1024]{2,1,0:T(8,128)}) custom-call(s32[1]{0:T(128)S(6)} %copy.34.len_ref, bf16[1024,2304]{1,0:T(8,128)(2,1)} %get-tuple-element.168.q_ref.k_ref.v_ref, bf16[1024,2304]{1,0:T(8,128)(2,1)} %get-tuple-element.168.q_ref.k_ref.v_ref, bf16[1024,2304]{1,0:T(8,128)(2,1)} %get-tuple-element.168.q_ref.k_ref.v_ref), custom_call_target="tpu_custom_call" | custom-call | flops 13200000000 | bytes 36000000 | tf_op jit(solution)/shard_map/attend/pallas_call | solution.py:152
  61.4 1.4 collective-permute-done.3.refs_11_
  63.0 1.6 collective-permute-start.10
  65.2 8.8 %project_dispatch.1 = (f32[1024,768]{1,0:T(8,128)}, bf16[2,128,768]{2,1,0:T(8,128)(2,1)}, bf16[2,128,768]{2,1,0:T(8,128)(2,1)}, bf16[2,128,768]{2,1,0:T(8,128)(2,1)}, bf16[2,128,768]{2,1,0:T(8,128)(2,1)}) custom-call(bf16[1024,384]{1,0:T(8,128)(2,1)} %get-tuple-element.167.low_ref.o_ref, bf16[1024,384]{1,0:T(8,128)(2,1)} %get-tuple-element.174.high_ref.o_ref, ...), custom_call_target="tpu_custom_call" | custom-call | flops 9680000000 | bytes 26400000 | tf_op jit(solution)/shard_map/project_dispatch/pallas_call | solution.py:395
  74.0 2.1 collective-permute-start.7
  76.1 2.3 collective-permute-start.8
  80.0 8.2 %collective-permute-done.7.refs_1_ = bf16[2,128,768]{2,1,0:T(8,128)(2,1)} collective-permute-done((bf16[2,128,768]{2,1,0:T(8,128)(2,1)}, bf16[2,128,768]{2,1,0:T(8,128)(2,1)}, u32[]{:S(2)}, u32[]{:S(2)}) %collective-permute-start.7) | collective-permute-done | bytes 393248 | tf_op jit(solution)/shard_map/ppermute | solution.py:898
  88.2 7.0 %collective-permute-done.8.refs_3_ = bf16[2,128,768]{2,1,0:T(8,128)(2,1)} collective-permute-done((bf16[2,128,768]{2,1,0:T(8,128)(2,1)}, bf16[2,128,768]{2,1,0:T(8,128)(2,1)}, u32[]{:S(2)}, u32[]{:S(2)}) %collective-permute-start.8) | collective-permute-done | bytes 393248 | tf_op jit(solution)/shard_map/ppermute | solution.py:898
  98.1 1.2 collective-permute-start.15
  100.3 18.7 %collective-permute-done.11.refs_2_ = bf16[2,128,768]{2,1,0:T(8,128)(2,1)S(1)} collective-permute-done((bf16[2,128,768]{2,1,0:T(8,128)(2,1)S(1)}, bf16[2,128,768]{2,1,0:T(8,128)(2,1)S(1)}, u32[]{:S(2)}, u32[]{:S(2)}) %collective-permute-start.11) | collective-permute-done | bytes 393248 | tf_op jit(solution)/shard_map/ppermute | solution.py:898
  120.1 1.3 collective-permute-done.13.refs_16_
  122.2 3.4 collective-permute-done.19.refs_25_
  126.5 25.6 %experts_new.1 = (bf16[4,2,128,768]{3,2,1,0:T(8,128)(2,1)}, bf16[128,768]{1,0:T(8,128)(2,1)}, bf16[128,768]{1,0:T(8,128)(2,1)}, bf16[128,768]{1,0:T(8,128)(2,1)}...) custom-call(s32[4]{0:T(128)} %get-tuple-element.349.own_ref, ...), custom_call_target="tpu_custom_call" | custom-call | flops 25300000768 | bytes 69000000 | tf_op jit(solution)/shard_map/experts_new/pallas_call | solution.py:542
  153.6 1.7 collective-permute-start.23
  155.4 19.0 %experts_old.1 = (bf16[4,2,128,768]{3,2,1,0:T(8,128)(2,1)}, bf16[128,768]{1,0:T(8,128)(2,1)}, bf16[128,768]{1,0:T(8,128)(2,1)}, bf16[128,768]{1,0:T(8,128)(2,1)}...) custom-call(s32[4]{0:T(128)} %get-tuple-element.348.own_ref, ...), custom_call_target="tpu_custom_call", output_to_operand_aliasing={{0}: (28, {})} | custom-call | flops 18699999232 | bytes 51000000 | tf_op jit(solution)/shard_map/experts_old/pallas_call | solution.py:542
  174.5 2.6 collective-permute-start.24
  177.9 1.7 collective-permute-start.26
  179.7 1.6 fusion.8
  182.8 1.6 fusion.6
  184.4 10.5 %collective-permute-done.25.refs_4_ = bf16[128,768]{1,0:T(8,128)(2,1)} collective-permute-done((bf16[128,768]{1,0:T(8,128)(2,1)}, bf16[128,768]{1,0:T(8,128)(2,1)}, u32[]{:S(2)}, u32[]{:S(2)}) %collective-permute-start.25) | collective-permute-done | bytes 196640 | tf_op jit(solution)/shard_map/ppermute | solution.py:906
  195.9 1.5 collective-permute-start.29
  197.3 13.4 %middle_back.1 = (f32[1024,768]{1,0:T(8,128)}, bf16[1024,768]{1,0:T(8,128)(2,1)}, bf16[4,4,2,24,384]{4,3,2,1,0:T(8,128)(2,1)}, bf16[4,4,2,24,384]{4,3,2,1,0:T(8,128)(2,1)}, f32[8,768]{1,0:T(8,128)}) custom-call(s32[1024,128]{1,0:T(8,128)} %get-tuple-element.162.slot_ref, f32[1024,768]{1,0:T(8,128)} %get-tuple-element.176.res_ref, ...), custom_call_target="tpu_custom_call" | custom-call | flops 14300000256 | bytes 39000000 | tf_op jit(solution)/shard_map/middle_back/pallas_call | solution.py:647
  213.4 4.3 %all-to-all-start.1 = ((bf16[4,2,128,768]{3,2,1,0:T(8,128)(2,1)}), bf16[4,2,128,768]{3,2,1,0:T(8,128)(2,1)}, u32[]{:S(2)}, u32[]{:S(2)}) async-start(bf16[4,2,128,768]{3,2,1,0:T(8,128)(2,1)} %get-tuple-element.249), calls=%async_computation.1 | async-start | bytes 3145728 | tf_op jit(solution)/shard_map/all_to_all | solution.py:901
  218.7 1.5 collective-permute-start.33
  220.2 17.8 %attend_back.2 = (bf16[3,1024,384]{2,1,0:T(8,128)(2,1)}, bf16[4,4,3,24,384]{4,3,2,1,0:T(8,128)(2,1)}, bf16[4,4,3,24,384]{4,3,2,1,0:T(8,128)(2,1)}) custom-call(s32[1]{0:T(128)S(6)} %copy.34.len_ref, bf16[1024,2304]{1,0:T(8,128)(2,1)} %get-tuple-element.168.q_ref.k_ref.v_ref, bf16[1024,2304]{1,0:T(8,128)(2,1)} %get-tuple-element.168.q_ref.k_ref.v_ref, ...), custom_call_target="tpu_custom_call" | custom-call | flops 5500000256 | bytes 15000000 | tf_op jit(solution)/shard_map/attend_back/pallas_call | solution.py:256
  238.1 1.3 fusion.21
  242.1 17.8 %attend_back.3 = (bf16[3,1024,384]{2,1,0:T(8,128)(2,1)}, bf16[4,4,3,24,384]{4,3,2,1,0:T(8,128)(2,1)}, bf16[4,4,3,24,384]{4,3,2,1,0:T(8,128)(2,1)}) custom-call(s32[1]{0:T(128)S(6)} %copy.34.len_ref, bf16[1024,2304]{1,0:T(8,128)(2,1)} %get-tuple-element.168.q_ref.k_ref.v_ref, bf16[1024,2304]{1,0:T(8,128)(2,1)} %get-tuple-element.168.q_ref.k_ref.v_ref, ...), custom_call_target="tpu_custom_call" | custom-call | flops 5500000256 | bytes 15000000 | tf_op jit(solution)/shard_map/attend_back/pallas_call | solution.py:256
  260.1 3.1 fusion.1
  264.7 1.4 collective-permute-start.38
  267.1 10.1 %last_back.1 = (f32[1024,768]{1,0:T(8,128)}, f32[8,768]{1,0:T(8,128)}) custom-call(bf16[3,1024,384]{2,1,0:T(8,128)(2,1)} %get-tuple-element.266.low_ref, bf16[3,1024,384]{2,1,0:T(8,128)(2,1)} %get-tuple-element.267.high_ref, bf16[1024,768]{1,0:T(8,128)(2,1)} %bitcast.91, f32[1024,768]{1,0:T(8,128)} %get-tuple-element.268.dres_ref, ...), custom_call_target="tpu_custom_call" | custom-call | flops 5500000256 | bytes 15000000 | tf_op jit(solution)/shard_map/last_back/pallas_call | solution.py:695
  277.3 1.5 fusion.17
  278.8 1.1 collective-permute-start.42
  279.9 1.4 collective-permute-start.43
  281.3 2.3 collective-permute-done.38
  285.1 2.3 convert_add_fusion.1
  288.2 4.5 %collective-permute-done.43 = bf16[4,3,24,384]{3,2,1,0:T(8,128)(2,1)S(1)} collective-permute-done((bf16[4,3,24,384]{3,2,1,0:T(8,128)(2,1)S(1)}, bf16[4,3,24,384]{3,2,1,0:T(8,128)(2,1)S(1)}, u32[]{:S(2)}, u32[]{:S(2)}) %collective-permute-start.43) | collective-permute-done | bytes 221216 | tf_op jit(solution)/shard_map/ppermute | solution.py:772
  292.8 2.5 collective-permute-start.45
  295.6 3.8 %collective-permute-done.45 = bf16[1,5,24,384]{3,2,1,0:T(8,128)(2,1)S(1)} collective-permute-done((bf16[1,5,24,384]{3,2,1,0:T(8,128)(2,1)S(1)}, bf16[1,5,24,384]{3,2,1,0:T(8,128)(2,1)S(1)}, u32[]{:S(2)}, u32[]{:S(2)}) %collective-permute-start.45) | collective-permute-done | bytes 92192 | tf_op jit(solution)/shard_map/ppermute | solution.py:777
  299.4 1.4 collective-permute-done.46
  301.3 2.6 collective-permute-start.48
  304.0 5.3 %collective-permute-done.48 = bf16[1,3,24,384]{3,2,1,0:T(8,128)(2,1)S(1)} collective-permute-done((bf16[1,3,24,384]{3,2,1,0:T(8,128)(2,1)S(1)}, bf16[1,3,24,384]{3,2,1,0:T(8,128)(2,1)S(1)}, u32[]{:S(2)}, u32[]{:S(2)}) %collective-permute-start.48) | collective-permute-done | bytes 55328 | tf_op jit(solution)/shard_map/ppermute | solution.py:777
  309.4 1.5 collective-permute-start.50
  310.9 4.4 %collective-permute-done.50 = bf16[4,24,384]{2,1,0:T(8,128)(2,1)S(1)} collective-permute-done((bf16[4,24,384]{2,1,0:T(8,128)(2,1)S(1)}, bf16[4,24,384]{2,1,0:T(8,128)(2,1)S(1)}, u32[]{:S(2)}, u32[]{:S(2)}) %collective-permute-start.50) | collective-permute-done | bytes 73760 | tf_op jit(solution)/shard_map/ppermute | solution.py:777
  315.3 1.4 collective-permute-done.49
  316.8 1.4 collective-permute-start.53
  318.2 1.4 collective-permute-start.52
  320.5 6.2 %combine.1 = f32[1024,768]{1,0:T(8,128)} custom-call(s32[1]{0:T(128)} %bitcast.me_ref, s32[1024,128]{1,0:T(8,128)} %get-tuple-element.162.slot_ref, f32[1024,768]{1,0:T(8,128)} %get-tuple-element.176.res_ref, bf16[4,2,128,768]{3,2,1,0:T(8,128)(2,1)} %all-to-all-done.1.part_ref), custom_call_target="tpu_custom_call" | custom-call | flops 6819999744 | bytes 18600000 | tf_op jit(solution)/shard_map/combine/pallas_call | solution.py:597
  326.6 2.5 collective-permute-done.53.refs_6_
  329.2 5.9 %collective-permute-done.52.refs_4_ = bf16[20,24,384]{2,1,0:T(8,128)(2,1)S(1)} collective-permute-done((bf16[20,24,384]{2,1,0:T(8,128)(2,1)S(1)}, bf16[20,24,384]{2,1,0:T(8,128)(2,1)S(1)}, u32[]{:S(2)}, u32[]{:S(2)}) %collective-permute-start.52) | collective-permute-done | bytes 368672 | tf_op jit(solution)/shard_map/ppermute | solution.py:772
  336.3 1.4 collective-permute-start.61
  338.4 1.5 collective-permute-start.59
  341.4 5.8 %unpack.2 = (f32[768,2304]{1,0:T(8,128)}, f32[768,768]{1,0:T(8,128)}) custom-call(s32[2]{0:T(128)} %pad_add_fusion.at_ref, bf16[20,24,384]{2,1,0:T(8,128)(2,1)} %bitcast.83, bf16[20,24,384]{2,1,0:T(8,128)(2,1)} %copy-done.37, bf16[20,24,384]{2,1,0:T(8,128)(2,1)} %copy-done.36, bf16[20,24,384]{2,1,0:T(8,128)(2,1)} %copy-done.38, ...), custom_call_target="tpu_custom_call" | custom-call | flops 4400000000 | bytes 12000000 | tf_op jit(solution)/shard_map/unpack/pallas_call | solution.py:755
  347.1 3.1 collective-permute-done.60.refs_4_
  354.2 4.4 %unpack.3 = f32[768,2304]{1,0:T(8,128)} custom-call(s32[2]{0:T(128)} %pad_add_fusion.at_ref, bf16[13,24,384]{2,1,0:T(8,128)(2,1)} %copy-done.15, bf16[13,24,384]{2,1,0:T(8,128)(2,1)} %copy-done.25, bf16[13,24,384]{2,1,0:T(8,128)(2,1)} %copy-done.24, bf16[13,24,384]{2,1,0:T(8,128)(2,1)} %copy-done.26, ...), custom_call_target="tpu_custom_call", output_to_operand_aliasing={{}: (9, {})} | custom-call | flops 4400000000 | bytes 12000000 | tf_op jit(solution)/shard_map/unpack/pallas_call | solution.py:755
  (233 shorter events, 38.8 us)
Async XLA Ops:
  3.5 41.0 %collective-permute-start.1 = (bf16[2,96,3072]{2,1,0:T(8,128)(2,1)}, bf16[2,96,3072]{2,1,0:T(8,128)(2,1)}, u32[]{:S(2)}, u32[]{:S(2)}) collective-permute-start(bf16[2,96,3072]{2,1,0:T(8,128)(2,1)} %constant_dynamic-update-slice_fusion.refs_7_), channel_id=1, source_target_pairs={{0,4},{1,5},{2,6},{3,7},{4,0},{5,1},{6,2},{7,3},{8,12},{9,13},{10,... | collective-permute-start | bytes 3538952 | tf_op jit(solution)/shard_map/ppermute | solution.py:772
  6.5 38.0 %collective-permute-start = (bf16[2,96,3072]{2,1,0:T(8,128)(2,1)}, bf16[2,96,3072]{2,1,0:T(8,128)(2,1)}, u32[]{:S(2)}, u32[]{:S(2)}) collective-permute-start(bf16[2,96,3072]{2,1,0:T(8,128)(2,1)} %constant_dynamic-update-slice_fusion.refs_7_), channel_id=1, source_target_pairs={{0,2},{1,3},{2,0},{3,1},{4,6},{5,7},{6,4},{7,5},{8,10},{9,11},{10,... | collective-permute-start | bytes 3538952 | tf_op jit(solution)/shard_map/ppermute | solution.py:772
  15.7 106.5 %all-to-all-start = ((bf16[4,2,128,896]{3,2,1,0:T(8,128)(2,1)}), bf16[4,2,128,896]{3,2,1,0:T(8,128)(2,1)S(1)}, u32[]{:S(2)}, u32[]{:S(2)}) async-start(bf16[4,2,128,896]{3,2,1,0:T(8,128)(2,1)} %get-tuple-element.186), calls=%async_computation | async-start | bytes 3670016 | tf_op jit(solution)/shard_map/all_to_all | solution.py:901
  45.6 17.4 %collective-permute-start.6 = (bf16[2,96,3072]{2,1,0:T(8,128)(2,1)}, bf16[2,96,3072]{2,1,0:T(8,128)(2,1)S(1)}, u32[]{:S(2)}, u32[]{:S(2)}) collective-permute-start(bf16[2,96,3072]{2,1,0:T(8,128)(2,1)} %collective-permute-done.1.refs_9_), channel_id=1, source_target_pairs={{0,1},{1,0},{2,3},{3,2},{4,5},{5,4},{6,7},{7,6},{8,9},{9,8},{10,11... | collective-permute-start | bytes 3538952 | tf_op jit(solution)/shard_map/ppermute | solution.py:772
  46.8 16.2 %collective-permute-start.5 = (bf16[2,96,3072]{2,1,0:T(8,128)(2,1)}, bf16[2,96,3072]{2,1,0:T(8,128)(2,1)S(1)}, u32[]{:S(2)}, u32[]{:S(2)}) collective-permute-start(bf16[2,96,3072]{2,1,0:T(8,128)(2,1)} %collective-permute-done.refs_8_), channel_id=1, source_target_pairs={{0,1},{1,0},{2,3},{3,2},{4,5},{5,4},{6,7},{7,6},{8,9},{9,8},{10,11... | collective-permute-start | bytes 3538952 | tf_op jit(solution)/shard_map/ppermute | solution.py:772
  47.3 15.4 %collective-permute-start.3 = (bf16[2,48,3072]{2,1,0:T(8,128)(2,1)S(1)}, bf16[2,48,3072]{2,1,0:T(8,128)(2,1)}, u32[]{:S(2)}, u32[]{:S(2)}) collective-permute-start(bf16[2,48,3072]{2,1,0:T(8,128)(2,1)S(1)} %slice.191), channel_id=1, source_target_pairs={{0,4},{1,5},{2,6},{3,7},{4,0},{5,1},{6,2},{7,3},{8,12},{9,13},{10,... | collective-permute-start | bytes 1769480 | tf_op jit(solution)/shard_map/ppermute | solution.py:772
  47.8 15.1 %collective-permute-start.2 = (bf16[2,48,3072]{2,1,0:T(8,128)(2,1)S(1)}, bf16[2,48,3072]{2,1,0:T(8,128)(2,1)}, u32[]{:S(2)}, u32[]{:S(2)}) collective-permute-start(bf16[2,48,3072]{2,1,0:T(8,128)(2,1)S(1)} %slice.190), channel_id=1, source_target_pairs={{0,2},{1,3},{2,0},{3,1},{4,6},{5,7},{6,4},{7,5},{8,10},{9,11},{10,... | collective-permute-start | bytes 1769480 | tf_op jit(solution)/shard_map/ppermute | solution.py:772
  48.4 14.6 %collective-permute-start.4 = (bf16[2,96,3072]{2,1,0:T(8,128)(2,1)}, bf16[2,96,3072]{2,1,0:T(8,128)(2,1)S(1)}, u32[]{:S(2)}, u32[]{:S(2)}) collective-permute-start(bf16[2,96,3072]{2,1,0:T(8,128)(2,1)} %constant_dynamic-update-slice_fusion.refs_7_), channel_id=1, source_target_pairs={{0,1},{1,0},{2,3},{3,2},{4,5},{5,4},{6,7},{7,6},{8,9},{9,8},{10,11... | collective-permute-start | bytes 3538952 | tf_op jit(solution)/shard_map/ppermute | solution.py:772
  63.0 32.2 %collective-permute-start.10 = (bf16[2,384,768]{2,1,0:T(8,128)(2,1)S(1)}, bf16[2,384,768]{2,1,0:T(8,128)(2,1)}, u32[]{:S(2)}, u32[]{:S(2)}) collective-permute-start(bf16[2,384,768]{2,1,0:T(8,128)(2,1)S(1)} %pad_maximum_fusion.refs_17_), channel_id=1, source_target_pairs={{0,4},{1,5},{2,6},{3,7},{4,0},{5,1},{6,2},{7,3},{8,12},{9,13},{10,... | collective-permute-start | bytes 3538952 | tf_op jit(solution)/shard_map/ppermute | solution.py:772
  64.6 30.6 %collective-permute-start.9 = (bf16[2,384,768]{2,1,0:T(8,128)(2,1)S(1)}, bf16[2,384,768]{2,1,0:T(8,128)(2,1)}, u32[]{:S(2)}, u32[]{:S(2)}) collective-permute-start(bf16[2,384,768]{2,1,0:T(8,128)(2,1)S(1)} %pad_maximum_fusion.refs_17_), channel_id=1, source_target_pairs={{0,2},{1,3},{2,0},{3,1},{4,6},{5,7},{6,4},{7,5},{8,10},{9,11},{10,... | collective-permute-start | bytes 3538952 | tf_op jit(solution)/shard_map/ppermute | solution.py:772
  74.0 14.2 %collective-permute-start.7 = (bf16[2,128,768]{2,1,0:T(8,128)(2,1)}, bf16[2,128,768]{2,1,0:T(8,128)(2,1)}, u32[]{:S(2)}, u32[]{:S(2)}) collective-permute-start(bf16[2,128,768]{2,1,0:T(8,128)(2,1)} %get-tuple-element.178), channel_id=1, source_target_pairs={{0,8},{8,16},{16,24},{24,0},{1,9},{9,17},{17,25},{25,1},{2,10},{10... | collective-permute-start | bytes 1179656 | tf_op jit(solution)/shard_map/ppermute | solution.py:898
  76.1 19.1 %collective-permute-start.8 = (bf16[2,128,768]{2,1,0:T(8,128)(2,1)}, bf16[2,128,768]{2,1,0:T(8,128)(2,1)}, u32[]{:S(2)}, u32[]{:S(2)}) collective-permute-start(bf16[2,128,768]{2,1,0:T(8,128)(2,1)} %get-tuple-element.179), channel_id=1, source_target_pairs={{0,24},{8,0},{16,8},{24,16},{1,25},{9,1},{17,9},{25,17},{2,26},{10... | collective-permute-start | bytes 1179656 | tf_op jit(solution)/shard_map/ppermute | solution.py:898
  96.3 22.7 %collective-permute-start.14 = (bf16[2,192,768]{2,1,0:T(8,128)(2,1)S(1)}, bf16[2,192,768]{2,1,0:T(8,128)(2,1)}, u32[]{:S(2)}, u32[]{:S(2)}) collective-permute-start(bf16[2,192,768]{2,1,0:T(8,128)(2,1)S(1)} %slice.192), channel_id=1, source_target_pairs={{0,2},{1,3},{2,0},{3,1},{4,6},{5,7},{6,4},{7,5},{8,10},{9,11},{10,... | collective-permute-start | bytes 1769480 | tf_op jit(solution)/shard_map/ppermute | solution.py:772
  98.1 21.5 %collective-permute-start.15 = (bf16[2,192,768]{2,1,0:T(8,128)(2,1)S(1)}, bf16[2,192,768]{2,1,0:T(8,128)(2,1)}, u32[]{:S(2)}, u32[]{:S(2)}) collective-permute-start(bf16[2,192,768]{2,1,0:T(8,128)(2,1)S(1)} %slice.193), channel_id=1, source_target_pairs={{0,4},{1,5},{2,6},{3,7},{4,0},{5,1},{6,2},{7,3},{8,12},{9,13},{10,... | collective-permute-start | bytes 1769480 | tf_op jit(solution)/shard_map/ppermute | solution.py:772
  99.2 19.8 %collective-permute-start.11 = (bf16[2,128,768]{2,1,0:T(8,128)(2,1)S(1)}, bf16[2,128,768]{2,1,0:T(8,128)(2,1)S(1)}, u32[]{:S(2)}, u32[]{:S(2)}) collective-permute-start(bf16[2,128,768]{2,1,0:T(8,128)(2,1)S(1)} %copy-done.33), channel_id=1, source_target_pairs={{0,16},{8,24},{16,0},{24,8},{1,17},{9,25},{17,1},{25,9},{2,18},{10... | collective-permute-start | bytes 1179656 | tf_op jit(solution)/shard_map/ppermute | solution.py:898
  99.8 26.6 %collective-permute-start.17 = (bf16[2,384,768]{2,1,0:T(8,128)(2,1)}, bf16[2,384,768]{2,1,0:T(8,128)(2,1)}, u32[]{:S(2)}, u32[]{:S(2)}) collective-permute-start(bf16[2,384,768]{2,1,0:T(8,128)(2,1)} %collective-permute-done.9.refs_18_), channel_id=1, source_target_pairs={{0,1},{1,0},{2,3},{3,2},{4,5},{5,4},{6,7},{7,6},{8,9},{9,8},{10,11... | collective-permute-start | bytes 3538952 | tf_op jit(solution)/shard_map/ppermute | solution.py:772
  99.8 19.8 %collective-permute-start.12 = (bf16[2,48,3072]{2,1,0:T(8,128)(2,1)}, bf16[2,48,3072]{2,1,0:T(8,128)(2,1)}, u32[]{:S(2)}, u32[]{:S(2)}) collective-permute-start(bf16[2,48,3072]{2,1,0:T(8,128)(2,1)} %collective-permute-done.2.refs_10_), channel_id=1, source_target_pairs={{0,1},{1,0},{2,3},{3,2},{4,5},{5,4},{6,7},{7,6},{8,9},{9,8},{10,11... | collective-permute-start | bytes 1769480 | tf_op jit(solution)/shard_map/ppermute | solution.py:772
  119.0 2.3 collective-permute-start.13
  119.1 7.4 %collective-permute-start.16 = (bf16[2,384,768]{2,1,0:T(8,128)(2,1)S(1)}, bf16[2,384,768]{2,1,0:T(8,128)(2,1)}, u32[]{:S(2)}, u32[]{:S(2)}) collective-permute-start(bf16[2,384,768]{2,1,0:T(8,128)(2,1)S(1)} %pad_maximum_fusion.refs_17_), channel_id=1, source_target_pairs={{0,1},{1,0},{2,3},{3,2},{4,5},{5,4},{6,7},{7,6},{8,9},{9,8},{10,11... | collective-permute-start | bytes 3538952 | tf_op jit(solution)/shard_map/ppermute | solution.py:772
  119.6 6.9 %collective-permute-start.18 = (bf16[2,384,768]{2,1,0:T(8,128)(2,1)}, bf16[2,384,768]{2,1,0:T(8,128)(2,1)}, u32[]{:S(2)}, u32[]{:S(2)}) collective-permute-start(bf16[2,384,768]{2,1,0:T(8,128)(2,1)} %collective-permute-done.10.refs_19_), channel_id=1, source_target_pairs={{0,1},{1,0},{2,3},{3,2},{4,5},{5,4},{6,7},{7,6},{8,9},{9,8},{10,11... | collective-permute-start | bytes 3538952 | tf_op jit(solution)/shard_map/ppermute | solution.py:772
  119.6 6.0 %collective-permute-start.19 = (bf16[2,192,768]{2,1,0:T(8,128)(2,1)}, bf16[2,192,768]{2,1,0:T(8,128)(2,1)}, u32[]{:S(2)}, u32[]{:S(2)}) collective-permute-start(bf16[2,192,768]{2,1,0:T(8,128)(2,1)} %collective-permute-done.14.refs_20_), channel_id=1, source_target_pairs={{0,1},{1,0},{2,3},{3,2},{4,5},{5,4},{6,7},{7,6},{8,9},{9,8},{10,11... | collective-permute-start | bytes 1769480 | tf_op jit(solution)/shard_map/ppermute | solution.py:772
  121.4 5.1 %collective-permute-start.20 = (bf16[2,192,768]{2,1,0:T(8,128)(2,1)}, bf16[2,192,768]{2,1,0:T(8,128)(2,1)}, u32[]{:S(2)}, u32[]{:S(2)}) collective-permute-start(bf16[2,192,768]{2,1,0:T(8,128)(2,1)} %collective-permute-done.15.refs_21_), channel_id=1, source_target_pairs={{0,1},{1,0},{2,3},{3,2},{4,5},{5,4},{6,7},{7,6},{8,9},{9,8},{10,11... | collective-permute-start | bytes 1769480 | tf_op jit(solution)/shard_map/ppermute | solution.py:772
  152.1 27.6 %collective-permute-start.27 = (bf16[4,96,3072]{2,1,0:T(8,128)(2,1)}, bf16[4,96,3072]{2,1,0:T(8,128)(2,1)S(1)}, u32[]{:S(2)}, u32[]{:S(2)}) collective-permute-start(bf16[4,96,3072]{2,1,0:T(8,128)(2,1)} %get-tuple-element.217), channel_id=1, source_target_pairs={{0,1},{1,0},{2,3},{3,2},{4,5},{5,4},{6,7},{7,6},{8,9},{9,8},{10,11... | collective-permute-start | bytes 7077896 | tf_op jit(solution)/shard_map/ppermute | solution.py:772
  152.3 27.4 %collective-permute-start.28 = (bf16[4,384,768]{2,1,0:T(8,128)(2,1)}, bf16[4,384,768]{2,1,0:T(8,128)(2,1)S(1)}, u32[]{:S(2)}, u32[]{:S(2)}) collective-permute-start(bf16[4,384,768]{2,1,0:T(8,128)(2,1)} %get-tuple-element.218), channel_id=1, source_target_pairs={{0,1},{1,0},{2,3},{3,2},{4,5},{5,4},{6,7},{7,6},{8,9},{9,8},{10,11... | collective-permute-start | bytes 7077896 | tf_op jit(solution)/shard_map/ppermute | solution.py:772
  153.3 21.1 %collective-permute-start.21 = (bf16[128,768]{1,0:T(8,128)(2,1)}, bf16[128,768]{1,0:T(8,128)(2,1)S(1)}, u32[]{:S(2)}, u32[]{:S(2)}) collective-permute-start(bf16[128,768]{1,0:T(8,128)(2,1)} %get-tuple-element.203), channel_id=1, source_target_pairs={{0,24},{8,0},{16,8},{24,16},{1,25},{9,1},{17,9},{25,17},{2,26},{10... | collective-permute-start | bytes 589832 | tf_op jit(solution)/shard_map/ppermute | solution.py:906
  153.6 20.8 %collective-permute-start.22 = (bf16[128,768]{1,0:T(8,128)(2,1)}, bf16[128,768]{1,0:T(8,128)(2,1)S(1)}, u32[]{:S(2)}, u32[]{:S(2)}) collective-permute-start(bf16[128,768]{1,0:T(8,128)(2,1)} %get-tuple-element.204), channel_id=1, source_target_pairs={{0,16},{8,24},{16,0},{24,8},{1,17},{9,25},{17,1},{25,9},{2,18},{10... | collective-permute-start | bytes 589832 | tf_op jit(solution)/shard_map/ppermute | solution.py:906
  153.6 20.8 %collective-permute-start.23 = (bf16[128,768]{1,0:T(8,128)(2,1)}, bf16[128,768]{1,0:T(8,128)(2,1)S(1)}, u32[]{:S(2)}, u32[]{:S(2)}) collective-permute-start(bf16[128,768]{1,0:T(8,128)(2,1)} %get-tuple-element.205), channel_id=1, source_target_pairs={{0,8},{8,16},{16,24},{24,0},{1,9},{9,17},{17,25},{25,1},{2,10},{10... | collective-permute-start | bytes 589832 | tf_op jit(solution)/shard_map/ppermute | solution.py:906
  174.5 10.0 %collective-permute-start.24 = (bf16[128,768]{1,0:T(8,128)(2,1)}, bf16[128,768]{1,0:T(8,128)(2,1)}, u32[]{:S(2)}, u32[]{:S(2)}) collective-permute-start(bf16[128,768]{1,0:T(8,128)(2,1)} %get-tuple-element.208), channel_id=1, source_target_pairs={{0,24},{8,0},{16,8},{24,16},{1,25},{9,1},{17,9},{25,17},{2,26},{10... | collective-permute-start | bytes 589832 | tf_op jit(solution)/shard_map/ppermute | solution.py:906
  177.1 17.9 %collective-permute-start.25 = (bf16[128,768]{1,0:T(8,128)(2,1)}, bf16[128,768]{1,0:T(8,128)(2,1)}, u32[]{:S(2)}, u32[]{:S(2)}) collective-permute-start(bf16[128,768]{1,0:T(8,128)(2,1)} %get-tuple-element.210), channel_id=1, source_target_pairs={{0,16},{8,24},{16,0},{24,8},{1,17},{9,25},{17,1},{25,9},{2,18},{10... | collective-permute-start | bytes 589832 | tf_op jit(solution)/shard_map/ppermute | solution.py:906
  177.9 17.0 %collective-permute-start.26 = (bf16[128,768]{1,0:T(8,128)(2,1)}, bf16[128,768]{1,0:T(8,128)(2,1)}, u32[]{:S(2)}, u32[]{:S(2)}) collective-permute-start(bf16[128,768]{1,0:T(8,128)(2,1)} %get-tuple-element.212), channel_id=1, source_target_pairs={{0,8},{8,16},{16,24},{24,0},{1,9},{9,17},{17,25},{25,1},{2,10},{10... | collective-permute-start | bytes 589832 | tf_op jit(solution)/shard_map/ppermute | solution.py:906
  194.9 18.5 %collective-permute-start.30 = (bf16[96,3072]{1,0:T(8,128)(2,1)}, bf16[96,3072]{1,0:T(8,128)(2,1)}, u32[]{:S(2)}, u32[]{:S(2)}) collective-permute-start(bf16[96,3072]{1,0:T(8,128)(2,1)} %get-tuple-element.317), channel_id=1, source_target_pairs={{0,4},{1,5},{2,6},{3,7},{4,0},{5,1},{6,2},{7,3},{8,12},{9,13},{10,... | collective-permute-start | bytes 1769480 | tf_op jit(solution)/shard_map/ppermute | solution.py:772
  195.9 17.5 %collective-permute-start.29 = (bf16[96,3072]{1,0:T(8,128)(2,1)}, bf16[96,3072]{1,0:T(8,128)(2,1)}, u32[]{:S(2)}, u32[]{:S(2)}) collective-permute-start(bf16[96,3072]{1,0:T(8,128)(2,1)} %get-tuple-element.318), channel_id=1, source_target_pairs={{0,2},{1,3},{2,0},{3,1},{4,6},{5,7},{6,4},{7,5},{8,10},{9,11},{10,... | collective-permute-start | bytes 1769480 | tf_op jit(solution)/shard_map/ppermute | solution.py:772
  210.7 27.3 %collective-permute-start.35 = (bf16[4,4,2,24,384]{4,3,2,1,0:T(8,128)(2,1)}, bf16[4,4,2,24,384]{4,3,2,1,0:T(8,128)(2,1)}, u32[]{:S(2)}, u32[]{:S(2)}) collective-permute-start(bf16[4,4,2,24,384]{4,3,2,1,0:T(8,128)(2,1)} %get-tuple-element.253), channel_id=1, source_target_pairs={{0,1},{1,0},{2,3},{3,2},{4,5},{5,4},{6,7},{7,6},{8,9},{9,8},{10,11... | collective-permute-start | bytes 1769480 | tf_op jit(solution)/shard_map/ppermute | solution.py:772
  211.6 27.8 %collective-permute-start.31 = (bf16[96,3072]{1,0:T(8,128)(2,1)}, bf16[96,3072]{1,0:T(8,128)(2,1)}, u32[]{:S(2)}, u32[]{:S(2)}) collective-permute-start(bf16[96,3072]{1,0:T(8,128)(2,1)} %get-tuple-element.241), channel_id=1, source_target_pairs={{0,6},{1,7},{2,4},{3,5},{4,2},{5,3},{6,0},{7,1},{8,14},{9,15},{10,... | collective-permute-start | bytes 1769480 | tf_op jit(solution)/shard_map/ppermute | solution.py:772
  213.4 50.2 %all-to-all-start.1 = ((bf16[4,2,128,768]{3,2,1,0:T(8,128)(2,1)}), bf16[4,2,128,768]{3,2,1,0:T(8,128)(2,1)}, u32[]{:S(2)}, u32[]{:S(2)}) async-start(bf16[4,2,128,768]{3,2,1,0:T(8,128)(2,1)} %get-tuple-element.249), calls=%async_computation.1 | async-start | bytes 3145728 | tf_op jit(solution)/shard_map/all_to_all | solution.py:901
  217.8 22.3 %collective-permute-start.32 = (bf16[384,768]{1,0:T(8,128)(2,1)}, bf16[384,768]{1,0:T(8,128)(2,1)S(1)}, u32[]{:S(2)}, u32[]{:S(2)}) collective-permute-start(bf16[384,768]{1,0:T(8,128)(2,1)} %get-tuple-element.242), channel_id=1, source_target_pairs={{0,2},{1,3},{2,0},{3,1},{4,6},{5,7},{6,4},{7,5},{8,10},{9,11},{10,... | collective-permute-start | bytes 1769480 | tf_op jit(solution)/shard_map/ppermute | solution.py:772
  218.7 22.4 %collective-permute-start.33 = (bf16[384,768]{1,0:T(8,128)(2,1)}, bf16[384,768]{1,0:T(8,128)(2,1)S(1)}, u32[]{:S(2)}, u32[]{:S(2)}) collective-permute-start(bf16[384,768]{1,0:T(8,128)(2,1)} %get-tuple-element.243), channel_id=1, source_target_pairs={{0,4},{1,5},{2,6},{3,7},{4,0},{5,1},{6,2},{7,3},{8,12},{9,13},{10,... | collective-permute-start | bytes 1769480 | tf_op jit(solution)/shard_map/ppermute | solution.py:772
  238.0 25.1 %collective-permute-start.34 = (bf16[4,4,3,24,384]{4,3,2,1,0:T(8,128)(2,1)}, bf16[4,4,3,24,384]{4,3,2,1,0:T(8,128)(2,1)S(1)}, u32[]{:S(2)}, u32[]{:S(2)}) collective-permute-start(bf16[4,4,3,24,384]{4,3,2,1,0:T(8,128)(2,1)} %get-tuple-element.251), channel_id=1, source_target_pairs={{0,1},{1,0},{2,3},{3,2},{4,5},{5,4},{6,7},{7,6},{8,9},{9,8},{10,11... | collective-permute-start | bytes 2654216 | tf_op jit(solution)/shard_map/ppermute | solution.py:772
  241.0 44.1 %collective-permute-start.36 = (bf16[384,768]{1,0:T(8,128)(2,1)S(1)}, bf16[384,768]{1,0:T(8,128)(2,1)}, u32[]{:S(2)}, u32[]{:S(2)}) collective-permute-start(bf16[384,768]{1,0:T(8,128)(2,1)S(1)} %get-tuple-element.258), channel_id=1, source_target_pairs={{0,6},{1,7},{2,4},{3,5},{4,2},{5,3},{6,0},{7,1},{8,14},{9,15},{10,... | collective-permute-start | bytes 1769480 | tf_op jit(solution)/shard_map/ppermute | solution.py:772
  260.0 17.3 %collective-permute-start.41 = (bf16[4,4,3,24,384]{4,3,2,1,0:T(8,128)(2,1)}, bf16[4,4,3,24,384]{4,3,2,1,0:T(8,128)(2,1)}, u32[]{:S(2)}, u32[]{:S(2)}) collective-permute-start(bf16[4,4,3,24,384]{4,3,2,1,0:T(8,128)(2,1)} %get-tuple-element.271), channel_id=1, source_target_pairs={{0,1},{1,0},{2,3},{3,2},{4,5},{5,4},{6,7},{7,6},{8,9},{9,8},{10,11... | collective-permute-start | bytes 2654216 | tf_op jit(solution)/shard_map/ppermute | solution.py:772
  263.6 16.3 %collective-permute-start.37 = (bf16[4,5,24,384]{3,2,1,0:T(8,128)(2,1)S(1)}, bf16[4,5,24,384]{3,2,1,0:T(8,128)(2,1)S(1)}, u32[]{:S(2)}, u32[]{:S(2)}) collective-permute-start(bf16[4,5,24,384]{3,2,1,0:T(8,128)(2,1)S(1)} %pad_maximum_fusion.2), channel_id=1, source_target_pairs={{0,2},{1,3},{2,0},{3,1},{4,6},{5,7},{6,4},{7,5},{8,10},{9,11},{10,... | collective-permute-start | bytes 1105928 | tf_op jit(solution)/shard_map/ppermute | solution.py:772
  264.7 18.8 %collective-permute-start.38 = (bf16[4,5,24,384]{3,2,1,0:T(8,128)(2,1)S(1)}, bf16[4,5,24,384]{3,2,1,0:T(8,128)(2,1)S(1)}, u32[]{:S(2)}, u32[]{:S(2)}) collective-permute-start(bf16[4,5,24,384]{3,2,1,0:T(8,128)(2,1)S(1)} %pad_maximum_fusion.3), channel_id=1, source_target_pairs={{0,4},{1,5},{2,6},{3,7},{4,0},{5,1},{6,2},{7,3},{8,12},{9,13},{10,... | collective-permute-start | bytes 1105928 | tf_op jit(solution)/shard_map/ppermute | solution.py:772
  266.1 18.3 %collective-permute-start.39 = (bf16[4,5,24,384]{3,2,1,0:T(8,128)(2,1)S(1)}, bf16[4,5,24,384]{3,2,1,0:T(8,128)(2,1)S(1)}, u32[]{:S(2)}, u32[]{:S(2)}) collective-permute-start(bf16[4,5,24,384]{3,2,1,0:T(8,128)(2,1)S(1)} %pad_maximum_fusion.4), channel_id=1, source_target_pairs={{0,6},{1,7},{2,4},{3,5},{4,2},{5,3},{6,0},{7,1},{8,14},{9,15},{10,... | collective-permute-start | bytes 1105928 | tf_op jit(solution)/shard_map/ppermute | solution.py:772
  278.8 9.4 %collective-permute-start.42 = (bf16[4,3,24,384]{3,2,1,0:T(8,128)(2,1)S(1)}, bf16[4,3,24,384]{3,2,1,0:T(8,128)(2,1)S(1)}, u32[]{:S(2)}, u32[]{:S(2)}) collective-permute-start(bf16[4,3,24,384]{3,2,1,0:T(8,128)(2,1)S(1)} %get-tuple-element.273), channel_id=1, source_target_pairs={{0,2},{1,3},{2,0},{3,1},{4,6},{5,7},{6,4},{7,5},{8,10},{9,11},{10,... | collective-permute-start | bytes 663560 | tf_op jit(solution)/shard_map/ppermute | solution.py:772
  279.9 12.8 %collective-permute-start.43 = (bf16[4,3,24,384]{3,2,1,0:T(8,128)(2,1)S(1)}, bf16[4,3,24,384]{3,2,1,0:T(8,128)(2,1)S(1)}, u32[]{:S(2)}, u32[]{:S(2)}) collective-permute-start(bf16[4,3,24,384]{3,2,1,0:T(8,128)(2,1)S(1)} %get-tuple-element.274), channel_id=1, source_target_pairs={{0,4},{1,5},{2,6},{3,7},{4,0},{5,1},{6,2},{7,3},{8,12},{9,13},{10,... | collective-permute-start | bytes 663560 | tf_op jit(solution)/shard_map/ppermute | solution.py:772
  283.5 9.2 %collective-permute-start.44 = (bf16[4,3,24,384]{3,2,1,0:T(8,128)(2,1)S(1)}, bf16[4,3,24,384]{3,2,1,0:T(8,128)(2,1)S(1)}, u32[]{:S(2)}, u32[]{:S(2)}) collective-permute-start(bf16[4,3,24,384]{3,2,1,0:T(8,128)(2,1)S(1)} %get-tuple-element.275), channel_id=1, source_target_pairs={{0,6},{1,7},{2,4},{3,5},{4,2},{5,3},{6,0},{7,1},{8,14},{9,15},{10,... | collective-permute-start | bytes 663560 | tf_op jit(solution)/shard_map/ppermute | solution.py:772
  284.6 8.2 %collective-permute-start.40 = (bf16[2,5,24,384]{3,2,1,0:T(8,128)(2,1)S(1)}, bf16[2,5,24,384]{3,2,1,0:T(8,128)(2,1)S(1)}, u32[]{:S(2)}, u32[]{:S(2)}) collective-permute-start(bf16[2,5,24,384]{3,2,1,0:T(8,128)(2,1)S(1)} %get-tuple-element.336), channel_id=1, source_target_pairs={{0,8},{8,0},{16,24},{24,16},{1,9},{9,1},{17,25},{25,17},{2,10},{10... | collective-permute-start | bytes 552968 | tf_op jit(solution)/shard_map/ppermute | solution.py:777
  292.8 6.6 %collective-permute-start.45 = (bf16[1,5,24,384]{3,2,1,0:T(8,128)(2,1)S(1)}, bf16[1,5,24,384]{3,2,1,0:T(8,128)(2,1)S(1)}, u32[]{:S(2)}, u32[]{:S(2)}) collective-permute-start(bf16[1,5,24,384]{3,2,1,0:T(8,128)(2,1)S(1)} %get-tuple-element.340), channel_id=1, source_target_pairs={{0,16},{8,24},{16,0},{24,8},{1,17},{9,25},{17,1},{25,9},{2,18},{10... | collective-permute-start | bytes 276488 | tf_op jit(solution)/shard_map/ppermute | solution.py:777
  295.4 5.4 %collective-permute-start.46 = (bf16[2,3,24,384]{3,2,1,0:T(8,128)(2,1)S(1)}, bf16[2,3,24,384]{3,2,1,0:T(8,128)(2,1)S(1)}, u32[]{:S(2)}, u32[]{:S(2)}) collective-permute-start(bf16[2,3,24,384]{3,2,1,0:T(8,128)(2,1)S(1)} %get-tuple-element.338), channel_id=1, source_target_pairs={{0,8},{8,0},{16,24},{24,16},{1,9},{9,1},{17,25},{25,17},{2,10},{10... | collective-permute-start | bytes 331784 | tf_op jit(solution)/shard_map/ppermute | solution.py:777
  300.8 8.4 %collective-permute-start.47 = (bf16[5,24,384]{2,1,0:T(8,128)(2,1)S(1)}, bf16[5,24,384]{2,1,0:T(8,128)(2,1)S(1)}, u32[]{:S(2)}, u32[]{:S(2)}) collective-permute-start(bf16[5,24,384]{2,1,0:T(8,128)(2,1)S(1)} %fusion.22), channel_id=1, source_target_pairs={{0,16},{8,24},{16,0},{24,8},{1,17},{9,25},{17,1},{25,9},{2,18},{10... | collective-permute-start | bytes 276488 | tf_op jit(solution)/shard_map/ppermute | solution.py:777
  301.3 7.9 %collective-permute-start.48 = (bf16[1,3,24,384]{3,2,1,0:T(8,128)(2,1)S(1)}, bf16[1,3,24,384]{3,2,1,0:T(8,128)(2,1)S(1)}, u32[]{:S(2)}, u32[]{:S(2)}) collective-permute-start(bf16[1,3,24,384]{3,2,1,0:T(8,128)(2,1)S(1)} %get-tuple-element.342), channel_id=1, source_target_pairs={{0,16},{8,24},{16,0},{24,8},{1,17},{9,25},{17,1},{25,9},{2,18},{10... | collective-permute-start | bytes 165896 | tf_op jit(solution)/shard_map/ppermute | solution.py:777
  309.2 7.4 %collective-permute-start.49 = (bf16[2,5,24,384]{3,2,1,0:T(8,128)(2,1)S(1)}, bf16[2,5,24,384]{3,2,1,0:T(8,128)(2,1)S(1)}, u32[]{:S(2)}, u32[]{:S(2)}) collective-permute-start(bf16[2,5,24,384]{3,2,1,0:T(8,128)(2,1)S(1)} %pad_maximum_fusion.7), channel_id=1, source_target_pairs={{0,8},{8,0},{16,24},{24,16},{1,9},{9,1},{17,25},{25,17},{2,10},{10... | collective-permute-start | bytes 552968 | tf_op jit(solution)/shard_map/ppermute | solution.py:777
  309.4 5.9 %collective-permute-start.50 = (bf16[4,24,384]{2,1,0:T(8,128)(2,1)S(1)}, bf16[4,24,384]{2,1,0:T(8,128)(2,1)S(1)}, u32[]{:S(2)}, u32[]{:S(2)}) collective-permute-start(bf16[4,24,384]{2,1,0:T(8,128)(2,1)S(1)} %maximum_maximum_fusion), channel_id=1, source_target_pairs={{0,16},{8,24},{16,0},{24,8},{1,17},{9,25},{17,1},{25,9},{2,18},{10... | collective-permute-start | bytes 221192 | tf_op jit(solution)/shard_map/ppermute | solution.py:777
  316.8 12.4 %collective-permute-start.53 = (bf16[20,24,384]{2,1,0:T(8,128)(2,1)S(1)}, bf16[20,24,384]{2,1,0:T(8,128)(2,1)S(1)}, u32[]{:S(2)}, u32[]{:S(2)}) collective-permute-start(bf16[20,24,384]{2,1,0:T(8,128)(2,1)S(1)} %bitcast.79), channel_id=1, source_target_pairs={{0,6},{1,7},{2,4},{3,5},{4,2},{5,3},{6,0},{7,1},{8,14},{9,15},{10,... | collective-permute-start | bytes 1105928 | tf_op jit(solution)/shard_map/ppermute | solution.py:772
  318.2 16.9 %collective-permute-start.52 = (bf16[20,24,384]{2,1,0:T(8,128)(2,1)S(1)}, bf16[20,24,384]{2,1,0:T(8,128)(2,1)S(1)}, u32[]{:S(2)}, u32[]{:S(2)}) collective-permute-start(bf16[20,24,384]{2,1,0:T(8,128)(2,1)S(1)} %bitcast.80), channel_id=1, source_target_pairs={{0,4},{1,5},{2,6},{3,7},{4,0},{5,1},{6,2},{7,3},{8,12},{9,13},{10,... | collective-permute-start | bytes 1105928 | tf_op jit(solution)/shard_map/ppermute | solution.py:772
  319.6 15.5 %collective-permute-start.51 = (bf16[20,24,384]{2,1,0:T(8,128)(2,1)S(1)}, bf16[20,24,384]{2,1,0:T(8,128)(2,1)S(1)}, u32[]{:S(2)}, u32[]{:S(2)}) collective-permute-start(bf16[20,24,384]{2,1,0:T(8,128)(2,1)S(1)} %bitcast.81), channel_id=1, source_target_pairs={{0,2},{1,3},{2,0},{3,1},{4,6},{5,7},{6,4},{7,5},{8,10},{9,11},{10,... | collective-permute-start | bytes 1105928 | tf_op jit(solution)/shard_map/ppermute | solution.py:772
  320.3 15.9 %collective-permute-start.58 = (bf16[7,24,384]{2,1,0:T(8,128)(2,1)S(1)}, bf16[7,24,384]{2,1,0:T(8,128)(2,1)S(1)}, u32[]{:S(2)}, u32[]{:S(2)}) collective-permute-start(bf16[7,24,384]{2,1,0:T(8,128)(2,1)S(1)} %pad_maximum_fusion.8), channel_id=1, source_target_pairs={{0,8},{8,0},{16,24},{24,16},{1,9},{9,1},{17,25},{25,17},{2,10},{10... | collective-permute-start | bytes 387080 | tf_op jit(solution)/shard_map/ppermute | solution.py:777
  335.1 2.6 collective-permute-start.54
  335.2 3.2 collective-permute-start.55
  335.7 4.2 %collective-permute-start.56 = (bf16[20,24,384]{2,1,0:T(8,128)(2,1)S(1)}, bf16[20,24,384]{2,1,0:T(8,128)(2,1)S(1)}, u32[]{:S(2)}, u32[]{:S(2)}) collective-permute-start(bf16[20,24,384]{2,1,0:T(8,128)(2,1)S(1)} %collective-permute-done.52.refs_4_), channel_id=1, source_target_pairs={{0,1},{1,0},{2,3},{3,2},{4,5},{5,4},{6,7},{7,6},{8,9},{9,8},{10,11... | collective-permute-start | bytes 1105928 | tf_op jit(solution)/shard_map/ppermute | solution.py:772
  335.8 4.1 %collective-permute-start.57 = (bf16[20,24,384]{2,1,0:T(8,128)(2,1)S(1)}, bf16[20,24,384]{2,1,0:T(8,128)(2,1)S(1)}, u32[]{:S(2)}, u32[]{:S(2)}) collective-permute-start(bf16[20,24,384]{2,1,0:T(8,128)(2,1)S(1)} %collective-permute-done.53.refs_6_), channel_id=1, source_target_pairs={{0,1},{1,0},{2,3},{3,2},{4,5},{5,4},{6,7},{7,6},{8,9},{9,8},{10,11... | collective-permute-start | bytes 1105928 | tf_op jit(solution)/shard_map/ppermute | solution.py:772
  336.3 10.8 %collective-permute-start.61 = (bf16[13,24,384]{2,1,0:T(8,128)(2,1)S(1)}, bf16[13,24,384]{2,1,0:T(8,128)(2,1)S(1)}, u32[]{:S(2)}, u32[]{:S(2)}) collective-permute-start(bf16[13,24,384]{2,1,0:T(8,128)(2,1)S(1)} %pad_maximum_fusion.6.refs_0_), channel_id=1, source_target_pairs={{0,6},{1,7},{2,4},{3,5},{4,2},{5,3},{6,0},{7,1},{8,14},{9,15},{10,... | collective-permute-start | bytes 718856 | tf_op jit(solution)/shard_map/ppermute | solution.py:772
  337.7 12.5 %collective-permute-start.60 = (bf16[13,24,384]{2,1,0:T(8,128)(2,1)S(1)}, bf16[13,24,384]{2,1,0:T(8,128)(2,1)S(1)}, u32[]{:S(2)}, u32[]{:S(2)}) collective-permute-start(bf16[13,24,384]{2,1,0:T(8,128)(2,1)S(1)} %pad_maximum_fusion.6.refs_0_), channel_id=1, source_target_pairs={{0,4},{1,5},{2,6},{3,7},{4,0},{5,1},{6,2},{7,3},{8,12},{9,13},{10,... | collective-permute-start | bytes 718856 | tf_op jit(solution)/shard_map/ppermute | solution.py:772
  338.4 11.8 %collective-permute-start.59 = (bf16[13,24,384]{2,1,0:T(8,128)(2,1)S(1)}, bf16[13,24,384]{2,1,0:T(8,128)(2,1)S(1)}, u32[]{:S(2)}, u32[]{:S(2)}) collective-permute-start(bf16[13,24,384]{2,1,0:T(8,128)(2,1)S(1)} %pad_maximum_fusion.6.refs_0_), channel_id=1, source_target_pairs={{0,2},{1,3},{2,0},{3,1},{4,6},{5,7},{6,4},{7,5},{8,10},{9,11},{10,... | collective-permute-start | bytes 718856 | tf_op jit(solution)/shard_map/ppermute | solution.py:772
  (48 other events, 425.3 us)
